TPU v7x, 256 devices: a whole 4x4x8 slice. The times are simulated.
256 devices in a mesh: row: 8 (over y, core), col: 16 (over z_hi, x), layer: 2 (over z_lo).
Axes of the slice: x: 4, y: 4, z: 8 (z_hi: 4, z_lo: 2; z = z_hi * 2 + z_lo), core: 2. Of those that a mesh axis runs over, the one named last changes fastest.
Arguments:
- tile_values: float32 [8, 32, 2, 6, 128, 128], P('row', ('col', 'layer')), may hold values from -1.8 to 1.8
- tile_rows: int32 [8, 32, 2, 6], P('row', ('col', 'layer')), may hold values from 0 to 255, as said below
- tile_cols: int32 [8, 32, 2, 6], P('row', ('col', 'layer')), may hold values from 0 to 255, as said below
- tile_counts: int32 [8, 32, 2], P('row', ('col', 'layer')), may hold values from 1 to 6, as said below
- out_rows: int32 [8, 16, 2, 12], P('row', 'col'), may hold values from 0 to 255, as said below
- out_cols: int32 [8, 16, 2, 12], P('row', 'col'), may hold values from 0 to 255, as said below
Outputs:
- squared: float32 [8, 32, 12, 128, 128], P('row', ('col', 'layer'))
Inputs may be any that keep to these rules, and one draw needn't show every extreme that they name: `tile_rows`: entry [r, s, h, q] lies in row band r (the 32 block rows from r * 32), in a run of 8 block rows whose index is congruent to h modulo 2; within one list [r, s, h] the 6 slots have distinct rows. `tile_cols`: entry [r, s, h, q] lies in sub-band s: block columns s * 8 to s * 8 + 7. Slots q < tile_counts[r, s, h] of list [r, s, h] hold tiles; values and coordinates in later slots mean nothing. Some list holds 6 tiles in every draw. out_rows[r, c, l, o] and out_cols[r, c, l, o] place the o-th kept tile of row band r and sub-band c * 2 + l; the row lies in row band r, the column in that sub-band, and the 12 positions of one [r, c, l] are distinct. `out_cols`: see out_rows.
All inputs are finite; a program needn't handle non-finite values.
Results may differ from a plain program's by a relative error of at most 0.0003.
Values sent between devices are 32-bit elements; how exact they have to be, the bound alone decides.
No kernel may reach another device: no remote copies, remote signals or barrier semaphores. Data moves between devices by JAX's collectives and lax.ppermute only.
A program may use at most 128 MiB of HBM per device.

v0:
```python
import jax
import jax.numpy as jnp
from jax import lax
from jax.sharding import PartitionSpec as P


def live_slots(counts, capacity):
    slot_ids = jnp.arange(capacity, dtype=jnp.int32)
    return slot_ids < counts[..., None]


def flatten_list(listed):
    values, list_rows, list_cols, counts = listed
    tile_order = values.shape[-1]
    capacity = values.shape[-3]
    live_mask = live_slots(counts, capacity)
    return (
        values.reshape(-1, tile_order, tile_order),
        list_rows.reshape(-1),
        list_cols.reshape(-1),
        live_mask.reshape(-1),
    )


def tile_products(running, one_shard, column_panel, target_rows, target_cols):
    left_values, left_rows, left_cols, left_live = one_shard
    right_values, right_rows, right_cols, right_live = column_panel
    left_hits = (left_live[None, :] & (left_rows[None, :] == target_rows[:, None])).astype(
        jnp.int32
    )
    left_pick = jnp.argmax(left_hits, axis=1)
    inner_index = jnp.take(left_cols, left_pick)
    right_hits = (
        right_live[None, :]
        & (right_rows[None, :] == inner_index[:, None])
        & (right_cols[None, :] == target_cols[:, None])
    ).astype(jnp.int32)
    right_pick = jnp.argmax(right_hits, axis=1)
    weight = (jnp.max(left_hits, axis=1) * jnp.max(right_hits, axis=1)).astype(jnp.float32)
    left_tiles = jnp.take(left_values, left_pick, axis=0)
    right_tiles = jnp.take(right_values, right_pick, axis=0)
    products = jnp.einsum(
        "opq,oqr->opr",
        left_tiles,
        right_tiles,
        precision=lax.Precision.HIGHEST,
        preferred_element_type=jnp.float32,
    )
    return running + products * weight[:, None, None]


def column_panel_of(listed):
    return flatten_list(lax.all_gather(listed, "row", axis=0, tiled=True))


def fold_over(column_panel, target_rows, target_cols, running, arrived):
    values, piece_rows, piece_cols, counts = arrived
    pieces_count = values.shape[1]
    tile_order = values.shape[-1]
    capacity = values.shape[-3]
    live_mask = live_slots(counts, capacity)
    shards = (
        values.reshape(pieces_count, -1, tile_order, tile_order),
        piece_rows.reshape(pieces_count, -1),
        piece_cols.reshape(pieces_count, -1),
        live_mask.reshape(pieces_count, -1),
    )

    def advance(carried, one_shard):
        return (tile_products(carried, one_shard, column_panel, target_rows, target_cols), None)

    running, unused = lax.scan(advance, running, shards)
    return running


def local(tile_values, tile_rows, tile_cols, tile_counts, out_rows, out_cols):
    tile_order = tile_values.shape[-1]
    own_list = (tile_values, tile_rows, tile_cols, tile_counts)
    column_panel = column_panel_of(own_list)
    layer_index = lax.axis_index("layer")
    target_rows = lax.dynamic_index_in_dim(out_rows[0, 0], layer_index, 0, keepdims=False)
    target_cols = lax.dynamic_index_in_dim(out_cols[0, 0], layer_index, 0, keepdims=False)
    empty_sums = jnp.zeros((target_rows.shape[0], tile_order, tile_order), jnp.float32)
    summed = fold_over(
        column_panel,
        target_rows,
        target_cols,
        empty_sums,
        (
            lax.all_gather(own_list[0], ("col", "layer"), axis=1, tiled=True),
            lax.all_gather(own_list[1], ("col", "layer"), axis=1, tiled=True),
            lax.all_gather(own_list[2], ("col", "layer"), axis=1, tiled=True),
            lax.all_gather(own_list[3], ("col", "layer"), axis=1, tiled=True),
        ),
    )
    result = summed.reshape(1, 1, -1, tile_order, tile_order)
    return result


def solution(mesh):
    in_specs = (
        P("row", ("col", "layer"), None, None, None, None),
        P("row", ("col", "layer"), None, None),
        P("row", ("col", "layer"), None, None),
        P("row", ("col", "layer"), None),
        P("row", "col", None, None),
        P("row", "col", None, None),
    )
    out_specs = P("row", ("col", "layer"), None, None, None)
    return jax.shard_map(local, mesh=mesh, in_specs=in_specs, out_specs=out_specs, check_vma=False)
```

profile of v0, /device:TPU:4, one launch (start us, length us, event | category | flops | bytes accessed | tf_op | source)
XLA Modules:
  0.0 898.2 jit_solution(16524936345030754830)
XLA Ops:
  8.0 10.9 %all_gather.27 = s32[8,1,2]{2,1,0:T(1,128)S(1)} all-gather(s32[1,1,2]{2,1,0:T(1,128)} %param.11), channel_id=1, replica_groups=mesh['row'=8,'col'=16,'layer'=2] {'row'}, dimensions={0}, use_global_device_ids=true | all-gather | bytes 72 | tf_op jit(solution)/shard_map/all_gather | solution.py:53
  18.9 8.3 all_gather.30
  27.4 9.8 %all_gather.28 = s32[8,1,2,6]{3,2,1,0:T(2,128)S(1)} all-gather(s32[1,1,2,6]{3,2,1,0:T(2,128)} %param.9), channel_id=1, replica_groups=mesh['row'=8,'col'=16,'layer'=2] {'row'}, dimensions={0}, use_global_device_ids=true | all-gather | bytes 432 | tf_op jit(solution)/shard_map/all_gather | solution.py:53
  37.2 69.7 %all_gather.25 = s32[1,32,2,6]{3,2,0,1:T(2,128)S(1)} all-gather(s32[1,1,2,6]{3,2,0,1:T(2,128)} %bitcast.52), channel_id=1, replica_groups=mesh['row'=8,'col'=16,'layer'=2] {'col','layer'}, dimensions={1}, use_global_device_ids=true | all-gather | bytes 1584 | tf_op jit(solution)/shard_map/all_gather | solution.py:91
  107.0 68.5 %all_gather.29 = s32[1,32,2,6]{3,2,0,1:T(2,128)S(1)} all-gather(s32[1,1,2,6]{3,2,0,1:T(2,128)} %bitcast.53), channel_id=1, replica_groups=mesh['row'=8,'col'=16,'layer'=2] {'col','layer'}, dimensions={1}, use_global_device_ids=true | all-gather | bytes 1584 | tf_op jit(solution)/shard_map/all_gather | solution.py:92
  175.6 69.7 %all_gather.24 = s32[1,32,2]{2,0,1:T(1,128)S(1)} all-gather(s32[1,1,2]{2,0,1:T(1,128)} %bitcast.55), channel_id=1, replica_groups=mesh['row'=8,'col'=16,'layer'=2] {'col','layer'}, dimensions={1}, use_global_device_ids=true | all-gather | bytes 264 | tf_op jit(solution)/shard_map/all_gather | solution.py:93
  246.4 349.6 %all-gather.3.cloned.1.call-done = f32[1,32,2,6,128,128]{5,4,3,2,0,1:T(8,128)} async-done(((f32[1,1,2,6,128,128]{5,4,3,2,0,1:T(8,128)}), f32[1,32,2,6,128,128]{5,4,3,2,0,1:T(8,128)}) %all-gather.3.cloned.1.call-update) | async-done | bytes 25165840 | tf_op jit(solution)/shard_map/all_gather | solution.py:90
  596.0 294.5 %while.12 = (s32[]{:T(128)}, f32[12,128,128]{2,1,0:T(8,128)S(1)}, pred[32,12]{1,0:T(8,128)(4,1)S(1)}, s32[32,12]{1,0:T(8,128)S(1)}, s32[12]{0:T(128)S(1)}, /*ind...) while((s32[]{:T(128)}, f32[12,128,128]{2,1,0:T(8,128)S(1)}, ...), condition=%wide.wide.region_5.6_spmd.clone, body=%wide.wide.region_0.5_spmd.clone.sunk | while | flops 302997888 | bytes 7876635 | solution.py:72
  598.4 3.4 gather_fusion.1
  607.6 3.4 gather_fusion.1
  616.9 3.4 gather_fusion.1
  626.1 3.4 gather_fusion.1
  635.3 3.4 gather_fusion.1
  644.5 3.4 gather_fusion.1
  653.7 3.4 gather_fusion.1
  662.9 3.4 gather_fusion.1
  672.1 3.4 gather_fusion.1
  681.3 3.4 gather_fusion.1
  764.1 3.4 gather_fusion.1
  782.5 3.4 gather_fusion.1
  800.9 3.4 gather_fusion.1
  819.3 3.4 gather_fusion.1
  837.8 3.4 gather_fusion.1
  856.2 3.4 gather_fusion.1
  (648 shorter events, 241.6 us)
Async XLA Ops:
  6.5 239.8 %all-gather.5.cloned.1.call-start = ((), (), s32[]{:S(2)}) async-start(), calls=%async_computation.1 | async-start | bytes 7077888 | tf_op jit(solution)/shard_map/all_gather | solution.py:53
  7.3 588.7 %all-gather.3.cloned.1.call-start = ((), (), s32[]{:S(2)}) async-start(), calls=%async_computation | async-start | bytes 25952256 | tf_op jit(solution)/shard_map/all_gather | solution.py:90
  27.3 568.7 %copy-start.1 = (s32[8,1,2,6]{3,2,1,0:T(2,128)}, s32[8,1,2,6]{3,2,1,0:T(2,128)S(1)}, u32[]{:S(2)}) copy-start(s32[8,1,2,6]{3,2,1,0:T(2,128)S(1)} %all_gather.30) | copy-start | bytes 1156
  37.1 558.9 %copy-start.2 = (s32[8,1,2,6]{3,2,1,0:T(2,128)}, s32[8,1,2,6]{3,2,1,0:T(2,128)S(1)}, u32[]{:S(2)}) copy-start(s32[8,1,2,6]{3,2,1,0:T(2,128)S(1)} %all_gather.28) | copy-start | bytes 1156
  890.5 0.9 copy-start
Sparse Core Ops, SparseCore 0:
  9.2 46.4 all-gather.4
  57.5 538.4 all-gather.2
where the time goes:
time: 902 us; the launch traced here: 898 us
  waiting for transfers between devices  351 us (39%)
  blocking collectives  237 us (26%)
  local copies, waits for them, and re-layouts  193 us (21%)
  other arithmetic  65.1 us (7%)
  matrix products  36.4 us (4%)
  between operations  13.4 us (1%)
    all_gather x1, waiting for transfers between devices, local(): lax.all_gather(own_list[0], ('col', 'layer'), axis=1, tiled=True)  350 us
    gather x32, local copies, waits for them, and re-layouts, tile_products(): right_tiles = jnp.take(right_values, right_pick, axis=0)  108 us
    all_gather x1, blocking collectives, local(): lax.all_gather(own_list[1], ('col', 'layer'), axis=1, tiled=True)  69.7 us
    all_gather x1, blocking collectives, local(): lax.all_gather(own_list[3], ('col', 'layer'), axis=1, tiled=True)  69.7 us
    all_gather x1, blocking collectives, local(): lax.all_gather(own_list[2], ('col', 'layer'), axis=1, tiled=True)  68.5 us
    squeeze x32, local copies, waits for them, and re-layouts, fold_over(): running, unused = lax.scan(advance, running, shards)  38.1 us
    dot_general x32, matrix products, tile_products(): jnp.einsum('opq,oqr->opr', left_tiles, right_tiles, precision=lax.Precisi...  36.4 us
    all_gather x3, blocking collectives, column_panel_of(): return flatten_list(lax.all_gather(listed, 'row', axis=0, tiled=True))  29 us
  transfers between devices with their start and end apart: 2, of which 1 were waited for; matrix products, arithmetic and copies ran while one was open for 0% of the time, Pallas kernels for 0%

commit v1 on v0

v1 whole, which is shorter than its diff:
```python
import functools

import jax
import jax.numpy as jnp
from jax import lax
from jax.experimental import pallas as pl
from jax.experimental.pallas import tpu as pltpu
from jax.sharding import PartitionSpec as P

GROUP = ("col", "layer")
LANES = 128
SLOT_PITCH = 16
ROUND_CAP = 20


def pack_body(tiles_ref, meta_ref, out_ref):
    peers, per_peer, strip, _ = out_ref.shape

    def one_tile(tile, carry):
        for peer in range(peers):
            out_ref[peer, tile] = tiles_ref[tile, peer * strip:(peer + 1) * strip, :]
        return carry

    lax.fori_loop(0, per_peer - 1, one_tile, 0)
    for peer in range(peers):
        out_ref[peer, per_peer - 1] = meta_ref[...]


def plan_body(scalars, strips_ref, send_ref, codes_ref, counts_ref, table, picks, codes_smem, sem):
    row_index, base = scalars[0], scalars[1]
    peers, cap = send_ref.shape[:2]
    per_peer = strips_ref.shape[0] // peers
    band = 8
    blocks = peers * band
    groups = peers * SLOT_PITCH // LANES
    peers_per_group = LANES // SLOT_PITCH
    f32, bf16 = jnp.float32, jnp.bfloat16

    tall = lax.broadcasted_iota(jnp.int32, (blocks, LANES), 0).astype(f32) + 1.0
    short = lax.broadcasted_iota(jnp.int32, (band, LANES), 0).astype(f32) + 1.0
    names = lax.broadcasted_iota(jnp.int32, (band, LANES), 1).astype(f32) + 1.0
    targets = []
    for peer in range(peers):
        meta = strips_ref[peer * per_peer + per_peer - 1]
        row_hot = jnp.where(tall == meta[0:1, :], 1.0, 0.0).astype(bf16)
        col_hot = jnp.where(short + float(peer * band) == meta[1:2, :], names, 0.0).astype(bf16)
        table[peer * band:(peer + 1) * band, :] = lax.dot_general(
            col_hot, row_hot, (((1,), (1,)), ((), ())), preferred_element_type=f32
        )
        if peer % peers_per_group == 0:
            targets.append(meta)
        else:
            targets[-1] = targets[-1] + meta
    by_col = table[...]
    by_row = by_col.T.astype(bf16)
    by_col = by_col.astype(bf16)

    inner = lax.broadcasted_iota(jnp.int32, (blocks, LANES), 0)
    lane = lax.broadcasted_iota(jnp.int32, (blocks, LANES), 1)
    below = jnp.where(
        lax.broadcasted_iota(jnp.int32, (blocks, blocks), 0) >= lax.broadcasted_iota(jnp.int32, (blocks, blocks), 1),
        1.0, 0.0,
    ).astype(bf16)
    lane_from = lax.broadcasted_iota(jnp.int32, (LANES, LANES), 0)
    lane_to = lax.broadcasted_iota(jnp.int32, (LANES, LANES), 1)
    same_peer = lane_from // SLOT_PITCH == lane_to // SLOT_PITCH
    earlier = jnp.where(same_peer & (lane_from < lane_to), 1.0, 0.0).astype(bf16)
    together = jnp.where(same_peer, 1.0, 0.0)
    fixed_code = (inner // band) * per_peer - SLOT_PITCH * row_index - 1 - 512 + ((lane % SLOT_PITCH) << 16)

    counts = []
    for group in range(groups):
        left_hot = jnp.where(tall == targets[group][2:3, :], 1.0, 0.0).astype(bf16)
        right_hot = jnp.where(tall == targets[group][3:4, :], 1.0, 0.0).astype(bf16)
        left = jnp.dot(by_col, left_hot, preferred_element_type=f32)
        right = jnp.dot(by_row, right_hot, preferred_element_type=f32)
        hit = left * right > 0.0
        ranks = jnp.dot(below, jnp.where(hit, 1.0, 0.0).astype(bf16), preferred_element_type=f32)
        found = jnp.broadcast_to(ranks[blocks - 1:blocks, :], (band, LANES))
        ahead = jnp.dot(found.astype(bf16), earlier, preferred_element_type=f32)
        counts.append(jnp.dot(found.astype(bf16), together.astype(bf16), preferred_element_type=f32)[0:1, :])
        place = (ranks + ahead[0:1, :]).astype(jnp.int32) - 1 - base
        place = jnp.where(hit, place, -1)
        code = (fixed_code + left.astype(jnp.int32) + (right.astype(jnp.int32) << 9)).astype(f32)
        for at in range(cap):
            picks[group * cap + at:group * cap + at + 1, :] = jnp.sum(
                jnp.where(place == at, code, 0.0), axis=0, keepdims=True
            )
    spread = jnp.dot(picks[...], together, precision=lax.Precision.HIGHEST, preferred_element_type=f32).astype(jnp.int32)
    slot = lax.broadcasted_iota(jnp.int32, (1, LANES), 1) % SLOT_PITCH
    halves = pl.cdiv(cap, SLOT_PITCH)
    rows = []
    for group in range(groups):
        for half in range(halves):
            merged = jnp.zeros((1, LANES), jnp.int32)
            for at in range(half * SLOT_PITCH, min(cap, (half + 1) * SLOT_PITCH)):
                here = spread[group * cap + at:group * cap + at + 1, :]
                merged = jnp.where(slot == at % SLOT_PITCH, here, merged)
            rows.append(merged)
    codes_ref[...] = jnp.concatenate(rows, axis=0)
    counts_ref[...] = jnp.concatenate(counts + counts, axis=0)[0:8, :].astype(jnp.int32)
    copy = pltpu.make_async_copy(codes_ref, codes_smem, sem)
    copy.start()
    copy.wait()

    def one_peer(peer, carry):
        line = (peer // peers_per_group) * halves
        first = (peer % peers_per_group) * SLOT_PITCH
        for at in range(cap):
            found_at = codes_smem[line + at // SLOT_PITCH, first + at % SLOT_PITCH] & 511
            send_ref[peer, at] = strips_ref[found_at]
        return carry

    lax.fori_loop(0, peers, one_peer, 0)


def product_body(first, scalars, codes, counts, *refs):
    strips_ref = refs[0]
    panels = refs[1:9]
    if first:
        out_ref, right, left, sems = refs[9:]
    else:
        running_ref, out_ref, right, left, sems = refs[9:]
    row_index, base, own = scalars[0], scalars[1], scalars[2]
    peers, cap, strip, _ = strips_ref.shape
    halves = pl.cdiv(cap, SLOT_PITCH)
    peers_per_group = LANES // SLOT_PITCH
    line = (own // peers_per_group) * halves
    lane = (own % peers_per_group) * SLOT_PITCH
    todo = jnp.clip(counts[own // peers_per_group, lane] - base, 0, cap)
    bf16 = jnp.bfloat16

    def code_of(at):
        return codes[line + at // SLOT_PITCH, lane + at % SLOT_PITCH]

    def fetch(at, carry):
        name = (code_of(at) >> 9) & 127
        from_row, slot = name // SLOT_PITCH, name % SLOT_PITCH
        away = ((row_index // 2 - from_row // 2) & 3) + ((row_index ^ from_row) & 1) * 4
        for index, panel in enumerate(panels):
            @pl.when(away == index)
            def _():
                pltpu.make_async_copy(panel.at[slot], right.at[at], sems.at[at]).start()
        return carry

    lax.fori_loop(0, todo, fetch, 0)
    if first:
        out_ref[...] = jnp.zeros_like(out_ref)
    else:
        out_ref[...] = running_ref[...]

    def multiply(at, carry):
        for peer in range(peers):
            left[peer * strip:(peer + 1) * strip, :] = strips_ref[peer, at]
        pltpu.make_async_copy(panels[0].at[0], right.at[at], sems.at[at]).wait()
        a, b = left[...], right[at]
        a_high = a.astype(bf16)
        b_high = b.astype(bf16)
        a_low = (a - a_high.astype(jnp.float32)).astype(bf16)
        b_low = (b - b_high.astype(jnp.float32)).astype(bf16)
        product = jnp.dot(a_high, b_low, preferred_element_type=jnp.float32)
        product = product + jnp.dot(a_low, b_high, preferred_element_type=jnp.float32)
        product = product + jnp.dot(a_high, b_high, preferred_element_type=jnp.float32)
        target = code_of(at) >> 16
        out_ref[target] = out_ref[target] + product
        return carry

    lax.fori_loop(0, todo, multiply, 0)


def whole(shape):
    return pl.BlockSpec(shape, lambda i, *_: (0,) * len(shape))


def pack(tiles, meta, peers):
    count, order = tiles.shape[:2]
    shape = (peers, count + 1, order // peers, order)
    return pl.pallas_call(pack_body, out_shape=jax.ShapeDtypeStruct(shape, jnp.float32))(tiles, meta)


def plan(strips, row_index, base, peers, cap):
    strip, order = strips.shape[1:]
    groups = peers * SLOT_PITCH // LANES
    lines = groups * pl.cdiv(cap, SLOT_PITCH)
    send = (peers, cap, strip, order)
    return pl.pallas_call(
        plan_body,
        grid_spec=pltpu.PrefetchScalarGridSpec(
            num_scalar_prefetch=1,
            grid=(1,),
            in_specs=[whole(strips.shape)],
            out_specs=[whole(send), whole((lines, LANES)), whole((8, LANES))],
            scratch_shapes=[
                pltpu.VMEM((peers * 8, peers * 8), jnp.float32),
                pltpu.VMEM((groups * cap, LANES), jnp.float32),
                pltpu.SMEM((lines, LANES), jnp.int32),
                pltpu.SemaphoreType.DMA,
            ],
        ),
        out_shape=[
            jax.ShapeDtypeStruct(send, jnp.float32),
            jax.ShapeDtypeStruct((lines, LANES), jnp.int32),
            jax.ShapeDtypeStruct((8, LANES), jnp.int32),
        ],
    )(jnp.stack([row_index, base]), strips)


def multiply_round(strips, panels, codes, counts, row_index, base, own, running, kept):
    peers, cap, strip, order = strips.shape
    first = running is None
    tiles = (kept, order, order)
    operands = [strips, *panels] + ([] if first else [running])
    in_specs = [whole(strips.shape)] + [pl.BlockSpec(memory_space=pl.ANY)] * len(panels)
    if not first:
        in_specs.append(whole(tiles))
    return pl.pallas_call(
        functools.partial(product_body, first),
        grid_spec=pltpu.PrefetchScalarGridSpec(
            num_scalar_prefetch=3,
            grid=(1,),
            in_specs=in_specs,
            out_specs=whole(tiles),
            scratch_shapes=[
                pltpu.VMEM((cap, order, order), jnp.float32),
                pltpu.VMEM((order, order), jnp.float32),
                pltpu.SemaphoreType.DMA((cap,)),
            ],
        ),
        out_shape=jax.ShapeDtypeStruct(tiles, jnp.float32),
    )(jnp.stack([row_index, base, own]), codes, counts, *operands)


def shift_rows(array, rows, by):
    return lax.ppermute(array, "row", [(i, (i + by) % rows) for i in range(rows)])


def swap_rows(array, rows, by):
    return lax.ppermute(array, "row", [(i, i ^ by) for i in range(rows)])


def local(tile_values, tile_rows, tile_cols, tile_counts, out_rows, out_cols):
    order = tile_values.shape[-1]
    capacity = tile_rows.shape[-1]
    kept = out_rows.shape[-1]
    rows = lax.axis_size("row")
    peers = lax.axis_size(GROUP)
    row_index = lax.axis_index("row")
    own = lax.axis_index(GROUP)
    layer_index = lax.axis_index("layer")
    tiles = tile_values.reshape(-1, order, order)

    live = jnp.arange(capacity, dtype=jnp.int32) < tile_counts.reshape(-1, 1)
    own_rows = jnp.where(live, tile_rows[0, 0] + 1, 0).reshape(-1)
    own_cols = jnp.where(live, tile_cols[0, 0] + 1, 0).reshape(-1)
    lane = jnp.arange(LANES, dtype=jnp.int32)

    def at_lanes(values, group):
        spread = jnp.tile(jnp.pad(values, (0, SLOT_PITCH - values.shape[0])), LANES // SLOT_PITCH)
        return jnp.where(lane // SLOT_PITCH == group, spread, 0)

    listed = jnp.stack([at_lanes(own_rows, row_index), at_lanes(own_cols, row_index)]).astype(jnp.float32)
    in_group = own % (LANES // SLOT_PITCH)
    target_rows = lax.dynamic_index_in_dim(out_rows[0, 0], layer_index, 0, keepdims=False) + 1
    target_cols = lax.dynamic_index_in_dim(out_cols[0, 0], layer_index, 0, keepdims=False) + 1
    wanted = jnp.stack([at_lanes(target_rows, in_group), at_lanes(target_cols, in_group)]).astype(jnp.float32)
    for by in (1, 2, 4):
        listed = listed + swap_rows(listed, rows, by)
    meta = jnp.concatenate([listed, wanted])

    strips = pack(tiles, meta, peers)
    strips = lax.all_to_all(strips, GROUP, 0, 0, tiled=True)
    near = [tiles] + [shift_rows(tiles, rows, by) for by in (2, 4, 6)]
    strips = strips.reshape(-1, order // peers, order)

    zero = jnp.zeros((), jnp.int32)
    send, codes, counts = plan(strips, row_index, zero, peers, ROUND_CAP)
    send, near = lax.optimization_barrier((send, near))
    panels = near + [swap_rows(piece, rows, 1) for piece in near]
    most = jnp.max(counts)
    for by in (1, 2, 4):
        most = jnp.maximum(most, swap_rows(most, rows, by))
    received = lax.all_to_all(send, GROUP, 0, 0, tiled=True)
    summed = multiply_round(received, panels, codes, counts, row_index, zero, own, None, kept)

    def unfinished(state):
        return state[0] < most

    def further(state):
        base, running = state
        send, codes, counts = plan(strips, row_index, base, peers, ROUND_CAP)
        received = lax.all_to_all(send, GROUP, 0, 0, tiled=True)
        running = multiply_round(received, panels, codes, counts, row_index, base, own, running, kept)
        return base + ROUND_CAP, running

    unused, summed = lax.while_loop(unfinished, further, (jnp.int32(ROUND_CAP), summed))
    return summed.reshape(1, 1, kept, order, order)


def solution(mesh):
    in_specs = (
        P("row", GROUP, None, None, None, None),
        P("row", GROUP, None, None),
        P("row", GROUP, None, None),
        P("row", GROUP, None),
        P("row", "col", None, None),
        P("row", "col", None, None),
    )
    out_specs = P("row", GROUP, None, None, None)
    return jax.shard_map(local, mesh=mesh, in_specs=in_specs, out_specs=out_specs, check_vma=False)
```

time: 902 us -> 116 us (0.13)
  waiting for transfers between devices: 351 us -> 46.6 us
  blocking collectives: 237 us -> 0 us
  local copies, waits for them, and re-layouts: 193 us -> 1.69 us
  other arithmetic: 65.1 us -> 6 us
  starting transfers between devices: 0.04 us -> 40.2 us
  matrix products: 36.4 us -> 0 us
  Pallas kernels: 0 us -> 16 us
  between operations: 13.4 us -> 2.86 us
    all_gather x2 -> x0, waiting for transfers between devices: 350 us -> none  [the longest x1 350 us: local(): lax.all_gather(own_list[0], ('col', 'layer'), axis=1, tiled=True)]
    all_gather x6 -> x0, blocking collectives: 237 us -> none  [the longest x1 69.7 us: local(): lax.all_gather(own_list[1], ('col', 'layer'), axis=1, tiled=True)]
    gather x96 -> x0, local copies, waits for them, and re-layouts: 148 us -> none  [the longest x32 108 us: tile_products(): right_tiles = jnp.take(right_values, right_pick, axis=0)]
    another operation x64 -> x2, other arithmetic: 49.1 us -> 1.24 us  [the longest x1 0.66 us: multiply_round(): jnp.stack([row_index, base, own])]
    squeeze x33 -> x0, local copies, waits for them, and re-layouts: 38.8 us -> none  [the longest x32 38.1 us: fold_over(): running, unused = lax.scan(advance, running, shards)]
    dot_general x32 -> x0, matrix products: 36.4 us -> none  [tile_products(): jnp.einsum('opq,oqr->opr', left_tiles, right_tiles, precision=lax.Precisi...]
    all_to_all x0 -> x2, waiting for transfers between devices: none -> 29.6 us  [the longest x1 15.4 us: local(): strips = lax.all_to_all(strips, GROUP, 0, 0, tiled=True)]
    all_to_all x0 -> x2, starting transfers between devices: none -> 21.5 us  [the longest x1 11.6 us: local(): strips = lax.all_to_all(strips, GROUP, 0, 0, tiled=True)]
  transfers between devices with their start and end apart: 2 -> 15, of which waited for: 1 -> 8; matrix products, arithmetic and copies ran while one was open for 0% -> 3% of each run, Pallas kernels for 0% -> 7%
where the time goes in v1:
time: 116 us; the launch traced here: 114 us
  waiting for transfers between devices  46.6 us (40%)
  starting transfers between devices  40.2 us (35%)
  Pallas kernels  16 us (14%)
  other arithmetic  6 us (5%)
  between operations  2.86 us (2%)
  local copies, waits for them, and re-layouts  1.69 us (1%)
    all_to_all x1, waiting for transfers between devices, local(): strips = lax.all_to_all(strips, GROUP, 0, 0, tiled=True)  15.4 us
    all_to_all x1, waiting for transfers between devices, local(): received = lax.all_to_all(send, GROUP, 0, 0, tiled=True)  14.2 us
    ppermute x10, starting transfers between devices, swap_rows(): return lax.ppermute(array, 'row', [(i, i ^ by) for i in range(rows)])  12.8 us
    all_to_all x1, starting transfers between devices, local(): strips = lax.all_to_all(strips, GROUP, 0, 0, tiled=True)  11.6 us
    all_to_all x1, starting transfers between devices, local(): received = lax.all_to_all(send, GROUP, 0, 0, tiled=True)  9.92 us
    ppermute x10, waiting for transfers between devices, swap_rows(): return lax.ppermute(array, 'row', [(i, i ^ by) for i in range(rows)])  9.84 us
    pallas_call x1, Pallas kernels, plan(): pl.pallas_call(plan_body, grid_spec=pltpu.PrefetchScalarGridSpec(num_scal...  7.42 us
    ppermute x3, waiting for transfers between devices, shift_rows(): lax.ppermute(array, 'row', [(i, (i + by) % rows) for i in range(rows)])  7.19 us
  transfers between devices with their start and end apart: 15, of which 8 were waited for; matrix products, arithmetic and copies ran while one was open for 3% of the time, Pallas kernels for 7%

profile of v1, /device:TPU:4, one launch (start us, length us, event | category | flops | bytes accessed | tf_op | source)
XLA Modules:
  0.0 113.6 jit_solution(10385253440427258113)
XLA Ops:
  1.5 0.7 iota_compare_fusion
  2.7 0.7 add_bitcast_fusion.1
  3.4 0.7 add_bitcast_fusion
  4.3 1.7 %collective-permute-start.1 = (f32[2,128]{1,0:T(2,128)S(1)}, f32[2,128]{1,0:T(2,128)S(1)}, u32[]{:S(2)}, u32[]{:S(2)}) collective-permute-start(f32[2,128]{1,0:T(2,128)S(1)} %fusion), channel_id=1, source_target_pairs={{0,64},{32,96},{64,0},{96,32},{128,192},{160,224},{192,128},{224,1... | collective-permute-start | bytes 3080 | tf_op jit(solution)/shard_map/ppermute | solution.py:238
  5.9 2.0 %collective-permute-done.1 = f32[2,128]{1,0:T(2,128)S(1)} collective-permute-done((f32[2,128]{1,0:T(2,128)S(1)}, f32[2,128]{1,0:T(2,128)S(1)}, u32[]{:S(2)}, u32[]{:S(2)}) %collective-permute-start.1) | collective-permute-done | bytes 1056 | tf_op jit(solution)/shard_map/ppermute | solution.py:238
  7.9 3.3 %collective-permute-start.2 = (f32[2,128]{1,0:T(2,128)S(1)}, f32[2,128]{1,0:T(2,128)S(1)}, u32[]{:S(2)}, u32[]{:S(2)}) collective-permute-start(f32[2,128]{1,0:T(2,128)S(1)} %fusion.1), channel_id=1, source_target_pairs={{0,128},{32,160},{64,192},{96,224},{128,0},{160,32},{192,64},{224,... | collective-permute-start | bytes 3080 | tf_op jit(solution)/shard_map/ppermute | solution.py:238
  11.2 1.9 %collective-permute-done.2 = f32[2,128]{1,0:T(2,128)S(1)} collective-permute-done((f32[2,128]{1,0:T(2,128)S(1)}, f32[2,128]{1,0:T(2,128)S(1)}, u32[]{:S(2)}, u32[]{:S(2)}) %collective-permute-start.2) | collective-permute-done | bytes 1056 | tf_op jit(solution)/shard_map/ppermute | solution.py:238
  13.7 2.3 %shard_map.64 = f32[32,13,4,128]{3,2,1,0:T(4,128)} custom-call(f32[12,128,128]{2,1,0:T(8,128)} %bitcast.21, f32[4,128]{1,0:T(4,128)} %pad_maximum_fusion.meta_ref), custom_call_target="tpu_custom_call" | custom-call | tf_op jit(solution)/shard_map/pallas_call | solution.py:178
  16.0 11.6 %all-to-all-start.1 = ((f32[32,13,4,128]{3,2,1,0:T(4,128)}), f32[32,13,4,128]{3,2,1,0:T(4,128)S(1)}, u32[]{:S(2)}, u32[]{:S(2)}) async-start(f32[32,13,4,128]{3,2,1,0:T(4,128)} %shard_map.64), calls=%async_computation.1 | async-start | bytes 1703936 | tf_op jit(solution)/shard_map/all_to_all | solution.py:271
  27.6 1.7 %collective-permute-start.3 = (f32[12,128,128]{2,1,0:T(8,128)S(1)}, f32[12,128,128]{2,1,0:T(8,128)}, u32[]{:S(2)}, u32[]{:S(2)}) collective-permute-start(f32[12,128,128]{2,1,0:T(8,128)S(1)} %bitcast.22), channel_id=1, source_target_pairs={{0,64},{32,96},{64,128},{96,160},{128,192},{160,224},{192,0},{224,... | collective-permute-start | bytes 2359304 | tf_op jit(solution)/shard_map/ppermute | solution.py:234
  29.3 2.9 %collective-permute-start.4 = (f32[12,128,128]{2,1,0:T(8,128)S(1)}, f32[12,128,128]{2,1,0:T(8,128)}, u32[]{:S(2)}, u32[]{:S(2)}) collective-permute-start(f32[12,128,128]{2,1,0:T(8,128)S(1)} %bitcast.23), channel_id=1, source_target_pairs={{0,128},{32,160},{64,192},{96,224},{128,0},{160,32},{192,64},{224,... | collective-permute-start | bytes 2359304 | tf_op jit(solution)/shard_map/ppermute | solution.py:234
  32.2 1.3 %collective-permute-start.5 = (f32[12,128,128]{2,1,0:T(8,128)S(1)}, f32[12,128,128]{2,1,0:T(8,128)}, u32[]{:S(2)}, u32[]{:S(2)}) collective-permute-start(f32[12,128,128]{2,1,0:T(8,128)S(1)} %bitcast.24), channel_id=1, source_target_pairs={{0,192},{32,224},{64,0},{96,32},{128,64},{160,96},{192,128},{224,1... | collective-permute-start | bytes 2359304 | tf_op jit(solution)/shard_map/ppermute | solution.py:234
  34.1 15.4 %all-to-all-done.1 = f32[32,13,4,128]{3,2,1,0:T(4,128)S(1)} async-done(((f32[32,13,4,128]{3,2,1,0:T(4,128)}), f32[32,13,4,128]{3,2,1,0:T(4,128)S(1)}, u32[]{:S(2)}, u32[]{:S(2)}) %all-to-all-start.1) | async-done | bytes 852000 | tf_op jit(solution)/shard_map/all_to_all | solution.py:271
  49.6 7.4 %shard_map.65 = (f32[32,20,4,128]{3,2,1,0:T(4,128)}, s32[8,128]{1,0:T(8,128)}, s32[8,128]{1,0:T(8,128)}) custom-call(s32[2]{0:T(128)} %pad_add_fusion.3.scalars, f32[416,4,128]{2,1,0:T(4,128)S(1)} %bitcast.19), custom_call_target="tpu_custom_call" | custom-call | tf_op jit(solution)/shard_map/pallas_call | solution.py:186
  57.0 7.2 %collective-permute-done.4.refs_3_ = f32[12,128,128]{2,1,0:T(8,128)} collective-permute-done((f32[12,128,128]{2,1,0:T(8,128)S(1)}, f32[12,128,128]{2,1,0:T(8,128)}, u32[]{:S(2)}, u32[]{:S(2)}) %collective-permute-start.4) | collective-permute-done | bytes 786464 | tf_op jit(solution)/shard_map/ppermute | solution.py:234
  64.2 9.9 %all-to-all-start.2 = ((f32[32,20,4,128]{3,2,1,0:T(4,128)}), f32[32,20,4,128]{3,2,1,0:T(4,128)S(1)}, u32[]{:S(2)}, u32[]{:S(2)}) async-start(f32[32,20,4,128]{3,2,1,0:T(4,128)} %get-tuple-element.92), calls=%async_computation.2 | async-start | bytes 2621440 | tf_op jit(solution)/shard_map/all_to_all | solution.py:282
  76.6 3.6 %collective-permute-done.10 = s32[]{:T(128)} collective-permute-done((s32[]{:T(128)}, s32[]{:T(128)}, u32[]{:S(2)}, u32[]{:S(2)}) %collective-permute-start.10) | collective-permute-done | bytes 36 | tf_op jit(solution)/shard_map/ppermute | solution.py:238
  81.5 2.6 %collective-permute-start.11 = (s32[]{:T(128)}, s32[]{:T(128)}, u32[]{:S(2)}, u32[]{:S(2)}) collective-permute-start(s32[]{:T(128)} %max.9), channel_id=1, source_target_pairs={{0,64},{32,96},{64,0},{96,32},{128,192},{160,224},{192,128},{224,1... | collective-permute-start | bytes 20 | tf_op jit(solution)/shard_map/ppermute | solution.py:238
  84.1 1.1 collective-permute-done.11
  85.9 4.0 %collective-permute-start.12 = (s32[]{:T(128)}, s32[]{:T(128)}, u32[]{:S(2)}, u32[]{:S(2)}) collective-permute-start(s32[]{:T(128)} %max.10), channel_id=1, source_target_pairs={{0,128},{32,160},{64,192},{96,224},{128,0},{160,32},{192,64},{224,... | collective-permute-start | bytes 20 | tf_op jit(solution)/shard_map/ppermute | solution.py:238
  89.8 1.3 %collective-permute-done.12 = s32[]{:T(128)} collective-permute-done((s32[]{:T(128)}, s32[]{:T(128)}, u32[]{:S(2)}, u32[]{:S(2)}) %collective-permute-start.12) | collective-permute-done | bytes 36 | tf_op jit(solution)/shard_map/ppermute | solution.py:238
  91.8 14.2 %all-to-all-done.2.refs_0_ = f32[32,20,4,128]{3,2,1,0:T(4,128)S(1)} async-done(((f32[32,20,4,128]{3,2,1,0:T(4,128)}), f32[32,20,4,128]{3,2,1,0:T(4,128)S(1)}, u32[]{:S(2)}, u32[]{:S(2)}) %all-to-all-start.2) | async-done | bytes 1310752 | tf_op jit(solution)/shard_map/all_to_all | solution.py:282
  105.9 1.1 copy-done.2
  107.0 6.2 %shard_map.66 = f32[12,128,128]{2,1,0:T(8,128)} custom-call(s32[3]{0:T(128)} %pad_add_fusion.2.scalars, s32[8,128]{1,0:T(8,128)} %get-tuple-element.89.codes, s32[8,128]{1,0:T(8,128)} %get-tuple-element.90.counts, f32[32,20,4,128]{3,2,1,0:T(4,128)} %copy-done.2, f32[12,128,128]{2,1,0:T(8,128)S(1)} %bitcast.26, ...), custom_call_target="tpu_custom_call" | custom-call | tf_op jit(solution)/shard_map/pallas_call | solution.py:216
  (48 shorter events, 6.0 us)
Async XLA Ops:
  2.6 1.7 %collective-permute-start = (f32[2,128]{1,0:T(2,128)S(1)}, f32[2,128]{1,0:T(2,128)S(1)}, u32[]{:S(2)}, u32[]{:S(2)}) collective-permute-start(f32[2,128]{1,0:T(2,128)S(1)} %add_convert_fusion), channel_id=1, source_target_pairs={{0,32},{32,0},{64,96},{96,64},{128,160},{160,128},{192,224},{224,1... | collective-permute-start | bytes 3080 | tf_op jit(solution)/shard_map/ppermute | solution.py:238
  4.3 3.7 %collective-permute-start.1 = (f32[2,128]{1,0:T(2,128)S(1)}, f32[2,128]{1,0:T(2,128)S(1)}, u32[]{:S(2)}, u32[]{:S(2)}) collective-permute-start(f32[2,128]{1,0:T(2,128)S(1)} %fusion), channel_id=1, source_target_pairs={{0,64},{32,96},{64,0},{96,32},{128,192},{160,224},{192,128},{224,1... | collective-permute-start | bytes 3080 | tf_op jit(solution)/shard_map/ppermute | solution.py:238
  7.9 5.2 %collective-permute-start.2 = (f32[2,128]{1,0:T(2,128)S(1)}, f32[2,128]{1,0:T(2,128)S(1)}, u32[]{:S(2)}, u32[]{:S(2)}) collective-permute-start(f32[2,128]{1,0:T(2,128)S(1)} %fusion.1), channel_id=1, source_target_pairs={{0,128},{32,160},{64,192},{96,224},{128,0},{160,32},{192,64},{224,... | collective-permute-start | bytes 3080 | tf_op jit(solution)/shard_map/ppermute | solution.py:238
  13.7 13.9 %copy-start.1 = (f32[1,1,2,6,128,128]{5,4,3,2,1,0:T(8,128)S(1)}, f32[1,1,2,6,128,128]{5,4,3,2,1,0:T(8,128)}, u32[]{:S(2)}) copy-start(f32[1,1,2,6,128,128]{5,4,3,2,1,0:T(8,128)} %param.8) | copy-start | bytes 2359300
  16.0 33.5 %all-to-all-start.1 = ((f32[32,13,4,128]{3,2,1,0:T(4,128)}), f32[32,13,4,128]{3,2,1,0:T(4,128)S(1)}, u32[]{:S(2)}, u32[]{:S(2)}) async-start(f32[32,13,4,128]{3,2,1,0:T(4,128)} %shard_map.64), calls=%async_computation.1 | async-start | bytes 1703936 | tf_op jit(solution)/shard_map/all_to_all | solution.py:271
  27.6 29.4 %collective-permute-start.3 = (f32[12,128,128]{2,1,0:T(8,128)S(1)}, f32[12,128,128]{2,1,0:T(8,128)}, u32[]{:S(2)}, u32[]{:S(2)}) collective-permute-start(f32[12,128,128]{2,1,0:T(8,128)S(1)} %bitcast.22), channel_id=1, source_target_pairs={{0,64},{32,96},{64,128},{96,160},{128,192},{160,224},{192,0},{224,... | collective-permute-start | bytes 2359304 | tf_op jit(solution)/shard_map/ppermute | solution.py:234
  29.3 34.9 %collective-permute-start.4 = (f32[12,128,128]{2,1,0:T(8,128)S(1)}, f32[12,128,128]{2,1,0:T(8,128)}, u32[]{:S(2)}, u32[]{:S(2)}) collective-permute-start(f32[12,128,128]{2,1,0:T(8,128)S(1)} %bitcast.23), channel_id=1, source_target_pairs={{0,128},{32,160},{64,192},{96,224},{128,0},{160,32},{192,64},{224,... | collective-permute-start | bytes 2359304 | tf_op jit(solution)/shard_map/ppermute | solution.py:234
  32.2 32.0 %collective-permute-start.5 = (f32[12,128,128]{2,1,0:T(8,128)S(1)}, f32[12,128,128]{2,1,0:T(8,128)}, u32[]{:S(2)}, u32[]{:S(2)}) collective-permute-start(f32[12,128,128]{2,1,0:T(8,128)S(1)} %bitcast.24), channel_id=1, source_target_pairs={{0,192},{32,224},{64,0},{96,32},{128,64},{160,96},{192,128},{224,1... | collective-permute-start | bytes 2359304 | tf_op jit(solution)/shard_map/ppermute | solution.py:234
  64.2 11.7 %copy-start.3 = (s32[8,128]{1,0:T(8,128)S(1)}, s32[8,128]{1,0:T(8,128)}, u32[]{:S(2)}) copy-start(s32[8,128]{1,0:T(8,128)} %get-tuple-element.90.counts) | copy-start | bytes 12292
  64.2 41.7 %all-to-all-start.2 = ((f32[32,20,4,128]{3,2,1,0:T(4,128)}), f32[32,20,4,128]{3,2,1,0:T(4,128)S(1)}, u32[]{:S(2)}, u32[]{:S(2)}) async-start(f32[32,20,4,128]{3,2,1,0:T(4,128)} %get-tuple-element.92), calls=%async_computation.2 | async-start | bytes 2621440 | tf_op jit(solution)/shard_map/all_to_all | solution.py:282
  74.1 17.6 %collective-permute-start.6 = (f32[12,128,128]{2,1,0:T(8,128)S(1)}, f32[12,128,128]{2,1,0:T(8,128)}, u32[]{:S(2)}, u32[]{:S(2)}) collective-permute-start(f32[12,128,128]{2,1,0:T(8,128)S(1)} %bitcast.25), channel_id=1, source_target_pairs={{0,32},{32,0},{64,96},{96,64},{128,160},{160,128},{192,224},{224,1... | collective-permute-start | bytes 2359304 | tf_op jit(solution)/shard_map/ppermute | solution.py:238
  74.2 17.5 %collective-permute-start.7 = (f32[12,128,128]{2,1,0:T(8,128)}, f32[12,128,128]{2,1,0:T(8,128)}, u32[]{:S(2)}, u32[]{:S(2)}) collective-permute-start(f32[12,128,128]{2,1,0:T(8,128)} %collective-permute-done.3.refs_2_), channel_id=1, source_target_pairs={{0,32},{32,0},{64,96},{96,64},{128,160},{160,128},{192,224},{224,1... | collective-permute-start | bytes 2359304 | tf_op jit(solution)/shard_map/ppermute | solution.py:238
  74.7 17.0 %collective-permute-start.8 = (f32[12,128,128]{2,1,0:T(8,128)}, f32[12,128,128]{2,1,0:T(8,128)}, u32[]{:S(2)}, u32[]{:S(2)}) collective-permute-start(f32[12,128,128]{2,1,0:T(8,128)} %collective-permute-done.4.refs_3_), channel_id=1, source_target_pairs={{0,32},{32,0},{64,96},{96,64},{128,160},{160,128},{192,224},{224,1... | collective-permute-start | bytes 2359304 | tf_op jit(solution)/shard_map/ppermute | solution.py:238
  74.8 16.9 %collective-permute-start.9 = (f32[12,128,128]{2,1,0:T(8,128)}, f32[12,128,128]{2,1,0:T(8,128)}, u32[]{:S(2)}, u32[]{:S(2)}) collective-permute-start(f32[12,128,128]{2,1,0:T(8,128)} %collective-permute-done.5.refs_4_), channel_id=1, source_target_pairs={{0,32},{32,0},{64,96},{96,64},{128,160},{160,128},{192,224},{224,1... | collective-permute-start | bytes 2359304 | tf_op jit(solution)/shard_map/ppermute | solution.py:238
  76.5 3.7 %collective-permute-start.10 = (s32[]{:T(128)}, s32[]{:T(128)}, u32[]{:S(2)}, u32[]{:S(2)}) collective-permute-start(s32[]{:T(128)} %reduce_max.9), channel_id=1, source_target_pairs={{0,32},{32,0},{64,96},{96,64},{128,160},{160,128},{192,224},{224,1... | collective-permute-start | bytes 20 | tf_op jit(solution)/shard_map/ppermute | solution.py:238
  81.5 3.7 %collective-permute-start.11 = (s32[]{:T(128)}, s32[]{:T(128)}, u32[]{:S(2)}, u32[]{:S(2)}) collective-permute-start(s32[]{:T(128)} %max.9), channel_id=1, source_target_pairs={{0,64},{32,96},{64,0},{96,32},{128,192},{160,224},{192,128},{224,1... | collective-permute-start | bytes 20 | tf_op jit(solution)/shard_map/ppermute | solution.py:238
  85.9 5.2 %collective-permute-start.12 = (s32[]{:T(128)}, s32[]{:T(128)}, u32[]{:S(2)}, u32[]{:S(2)}) collective-permute-start(s32[]{:T(128)} %max.10), channel_id=1, source_target_pairs={{0,128},{32,160},{64,192},{96,224},{128,0},{160,32},{192,64},{224,... | collective-permute-start | bytes 20 | tf_op jit(solution)/shard_map/ppermute | solution.py:238
  105.9 1.1 copy-start.2

commit v2 on v1

v2 whole, which is shorter than its diff:
```python
import functools

import jax
import jax.numpy as jnp
from jax import lax
from jax.experimental import pallas as pl
from jax.experimental.pallas import tpu as pltpu
from jax.sharding import PartitionSpec as P

GROUP = ("col", "layer")
LANES = 128
SLOT_PITCH = 16
ROUND_CAP = 20
LIMIT = pltpu.CompilerParams(vmem_limit_bytes=20 * 2**20)


def label_body(tile_rows, tile_cols, counts, out_rows, out_cols, listed_ref, wanted_ref):
    lists, capacity = tile_rows.shape[2:]
    row_index, layer_index = lax.axis_index("row"), lax.axis_index("layer")
    in_group = lax.axis_index(GROUP) % (LANES // SLOT_PITCH)
    lane = lax.broadcasted_iota(jnp.int32, (1, LANES), 1)
    nothing = jnp.zeros((1, LANES), jnp.int32)
    rows, cols, kept_rows, kept_cols = nothing, nothing, nothing, nothing
    mate_rows, mate_cols = nothing, nothing
    for at in range(lists):
        for slot in range(capacity):
            live = slot < counts[0, 0, at]
            here = lane == jnp.where(live, row_index * SLOT_PITCH + at * capacity + slot, -1)
            rows = jnp.where(here, tile_rows[0, 0, at, slot] + 1, rows)
            cols = jnp.where(here, tile_cols[0, 0, at, slot] + 1, cols)
    for at in range(out_rows.shape[3]):
        here = lane == in_group * SLOT_PITCH + at
        kept_rows = jnp.where(here, out_rows[0, 0, layer_index, at] + 1, kept_rows)
        kept_cols = jnp.where(here, out_cols[0, 0, layer_index, at] + 1, kept_cols)
        here = lane == row_index * SLOT_PITCH + at
        mate_rows = jnp.where(here, out_rows[0, 0, layer_index, at] + 1, mate_rows)
        mate_cols = jnp.where(here, out_cols[0, 0, layer_index, at] + 1, mate_cols)
    listed_ref[...] = jnp.concatenate([rows, cols, mate_rows, mate_cols]).astype(jnp.float32)
    wanted_ref[...] = jnp.concatenate([kept_rows, kept_cols]).astype(jnp.float32)


def pack_body(tiles_ref, listed_ref, wanted_ref, out_ref):
    peers, per_peer, strip, _ = out_ref.shape

    def one_tile(tile, carry):
        for peer in range(peers):
            out_ref[peer, tile] = tiles_ref[tile, peer * strip:(peer + 1) * strip, :]
        return carry

    lax.fori_loop(0, per_peer - 1, one_tile, 0)
    for peer in range(peers):
        out_ref[peer, per_peer - 1, 0:2, :] = listed_ref[0:2, :]
        out_ref[peer, per_peer - 1, 2:4, :] = wanted_ref[...]


def pack_right_body(tiles_ref, *out_refs):
    count, strip, _ = out_refs[0].shape
    row_index = lax.axis_index("row")
    for away, out_ref in enumerate(out_refs):
        start = pl.multiple_of((row_index + away) % len(out_refs) * strip, strip)
        for tile in range(count):
            out_ref[tile] = tiles_ref[tile, pl.ds(start, strip), :]


def plan_body(rows, scalars, strips_ref, mates_ref, *refs):
    piece_refs, send_ref, right_refs = refs[:rows], refs[rows], refs[rows + 1:2 * rows + 1]
    codes_ref, counts_ref, table, picks, panel, codes_smem, sem = refs[2 * rows + 1:]
    row_index, base = scalars[0], scalars[1]
    peers, cap = send_ref.shape[:2]
    per_peer = strips_ref.shape[0] // peers
    band = 8
    blocks = peers * band
    groups = peers * SLOT_PITCH // LANES
    peers_per_group = LANES // SLOT_PITCH
    f32, bf16 = jnp.float32, jnp.bfloat16

    tall = lax.broadcasted_iota(jnp.int32, (blocks, LANES), 0).astype(f32) + 1.0
    short = lax.broadcasted_iota(jnp.int32, (band, LANES), 0).astype(f32) + 1.0
    names = lax.broadcasted_iota(jnp.int32, (band, LANES), 1).astype(f32) + 1.0
    targets = []
    for peer in range(peers):
        meta = strips_ref[peer * per_peer + per_peer - 1]
        row_hot = jnp.where(tall == meta[0:1, :], 1.0, 0.0).astype(bf16)
        col_hot = jnp.where(short + float(peer * band) == meta[1:2, :], names, 0.0).astype(bf16)
        table[peer * band:(peer + 1) * band, :] = lax.dot_general(
            col_hot, row_hot, (((1,), (1,)), ((), ())), preferred_element_type=f32
        )
        if peer % peers_per_group == 0:
            targets.append(meta)
        else:
            targets[-1] = targets[-1] + meta
    by_col = table[...]
    by_row = by_col.T.astype(bf16)
    by_col = by_col.astype(bf16)

    inner = lax.broadcasted_iota(jnp.int32, (blocks, LANES), 0)
    lane = lax.broadcasted_iota(jnp.int32, (blocks, LANES), 1)
    below = jnp.where(
        lax.broadcasted_iota(jnp.int32, (blocks, blocks), 0) >= lax.broadcasted_iota(jnp.int32, (blocks, blocks), 1),
        1.0, 0.0,
    ).astype(bf16)
    lane_from = lax.broadcasted_iota(jnp.int32, (LANES, LANES), 0)
    lane_to = lax.broadcasted_iota(jnp.int32, (LANES, LANES), 1)
    same_peer = lane_from // SLOT_PITCH == lane_to // SLOT_PITCH
    earlier = jnp.where(same_peer & (lane_from < lane_to), 1.0, 0.0).astype(bf16)
    together = jnp.where(same_peer, 1.0, 0.0)
    fixed_code = (inner // band) * per_peer - SLOT_PITCH * row_index - 1 - 512 + ((lane % SLOT_PITCH) << 16)

    targets = [(meta[2:3, :], meta[3:4, :]) for meta in targets]
    targets.append((mates_ref[2:3, :], mates_ref[3:4, :]))
    counts = []
    for group, (target_rows, target_cols) in enumerate(targets):
        left_hot = jnp.where(tall == target_rows, 1.0, 0.0).astype(bf16)
        right_hot = jnp.where(tall == target_cols, 1.0, 0.0).astype(bf16)
        left = jnp.dot(by_col, left_hot, preferred_element_type=f32)
        right = jnp.dot(by_row, right_hot, preferred_element_type=f32)
        hit = left * right > 0.0
        ranks = jnp.dot(below, jnp.where(hit, 1.0, 0.0).astype(bf16), preferred_element_type=f32)
        found = jnp.broadcast_to(ranks[blocks - 1:blocks, :], (band, LANES))
        ahead = jnp.dot(found.astype(bf16), earlier, preferred_element_type=f32)
        counts.append(jnp.dot(found.astype(bf16), together.astype(bf16), preferred_element_type=f32)[0:1, :])
        place = (ranks + ahead[0:1, :]).astype(jnp.int32) - 1 - base
        place = jnp.where(hit, place, -1)
        if group < groups:
            code = (fixed_code + left.astype(jnp.int32) + (right.astype(jnp.int32) << 9)).astype(f32)
        else:
            code = right - 1.0
        for at in range(cap):
            picks[group * cap + at:group * cap + at + 1, :] = jnp.sum(
                jnp.where(place == at, code, 0.0), axis=0, keepdims=True
            )
    spread = jnp.dot(picks[...], together, precision=lax.Precision.HIGHEST, preferred_element_type=f32).astype(jnp.int32)
    slot = lax.broadcasted_iota(jnp.int32, (1, LANES), 1) % SLOT_PITCH
    halves = pl.cdiv(cap, SLOT_PITCH)
    lines = []
    for group in range(groups + 1):
        for half in range(halves):
            merged = jnp.zeros((1, LANES), jnp.int32)
            for at in range(half * SLOT_PITCH, min(cap, (half + 1) * SLOT_PITCH)):
                here = spread[group * cap + at:group * cap + at + 1, :]
                merged = jnp.where(slot == at % SLOT_PITCH, here, merged)
            lines.append(merged)
    lines += lines[-1:] * (codes_ref.shape[0] - len(lines))
    codes_ref[...] = jnp.concatenate(lines, axis=0)
    counts += counts[-1:] * (counts_ref.shape[0] - len(counts))
    counts_ref[...] = jnp.concatenate(counts, axis=0).astype(jnp.int32)
    copy = pltpu.make_async_copy(codes_ref, codes_smem, sem)
    copy.start()
    for away, piece_ref in enumerate(piece_refs):
        panel[(row_index + rows - away) % rows] = piece_ref[...]
    copy.wait()

    def one_peer(peer, carry):
        line = (peer // peers_per_group) * halves
        first = (peer % peers_per_group) * SLOT_PITCH
        for at in range(cap):
            found_at = codes_smem[line + at // SLOT_PITCH, first + at % SLOT_PITCH] & 511
            send_ref[peer, at] = strips_ref[found_at]
        return carry

    lax.fori_loop(0, peers, one_peer, 0)

    for away, right_ref in enumerate(right_refs):
        lane_at = (row_index + away) % rows * SLOT_PITCH
        for at in range(cap):
            name = codes_smem[groups * halves + at // SLOT_PITCH, lane_at + at % SLOT_PITCH]
            right_ref[at] = panel[name // SLOT_PITCH, name % SLOT_PITCH]


def product_body(first, rows, scalars, codes, counts, left_ref, *refs):
    right_refs, refs = refs[:rows], refs[rows:]
    if first:
        out_ref, left, right = refs
        out_ref[...] = jnp.zeros_like(out_ref)
    else:
        running_ref, out_ref, left, right = refs
        out_ref[...] = running_ref[...]
    base, own = scalars[0], scalars[1]
    row_index = lax.axis_index("row")
    peers, cap, strip, _ = left_ref.shape
    tall_strip = right_refs[0].shape[1]
    halves = pl.cdiv(cap, SLOT_PITCH)
    peers_per_group = LANES // SLOT_PITCH
    line = (own // peers_per_group) * halves
    lane = (own % peers_per_group) * SLOT_PITCH
    todo = jnp.clip(counts[own // peers_per_group, lane] - base, 0, cap)
    bf16 = jnp.bfloat16

    def multiply(at, carry):
        for peer in range(peers):
            left[peer * strip:(peer + 1) * strip, :] = left_ref[peer, at]
        for away, right_ref in enumerate(right_refs):
            start = pl.multiple_of((row_index + rows - away) % rows * tall_strip, tall_strip)
            right[pl.ds(start, tall_strip), :] = right_ref[at]
        a, b = left[...], right[...]
        a_high = a.astype(bf16)
        b_high = b.astype(bf16)
        a_low = (a - a_high.astype(jnp.float32)).astype(bf16)
        b_low = (b - b_high.astype(jnp.float32)).astype(bf16)
        product = jnp.dot(a_high, b_low, preferred_element_type=jnp.float32)
        product = product + jnp.dot(a_low, b_high, preferred_element_type=jnp.float32)
        product = product + jnp.dot(a_high, b_high, preferred_element_type=jnp.float32)
        target = codes[line + at // SLOT_PITCH, lane + at % SLOT_PITCH] >> 16
        out_ref[target] = out_ref[target] + product
        return carry

    lax.fori_loop(0, todo, multiply, 0)


def whole(shape):
    return pl.BlockSpec(shape, lambda i, *_: (0,) * len(shape))


def pack(tiles, listed, wanted, peers):
    count, order = tiles.shape[:2]
    shape = (peers, count + 1, order // peers, order)
    return pl.pallas_call(
        pack_body, out_shape=jax.ShapeDtypeStruct(shape, jnp.float32), compiler_params=LIMIT
    )(tiles, listed, wanted)


def pack_right(tiles, rows):
    count, order = tiles.shape[:2]
    shape = (count, order // rows, order)
    return pl.pallas_call(
        pack_right_body, out_shape=[jax.ShapeDtypeStruct(shape, jnp.float32)] * rows, compiler_params=LIMIT
    )(tiles)


def plan(strips, mates, pieces, row_index, base, peers, cap):
    strip, order = strips.shape[1:]
    rows = len(pieces)
    count, tall_strip, _ = pieces[0].shape
    groups = peers * SLOT_PITCH // LANES
    lines = 8 * pl.cdiv((groups + 1) * pl.cdiv(cap, SLOT_PITCH), 8)
    send, right = (peers, cap, strip, order), (cap, tall_strip, order)
    return pl.pallas_call(
        functools.partial(plan_body, rows),
        grid_spec=pltpu.PrefetchScalarGridSpec(
            num_scalar_prefetch=1,
            grid=(1,),
            in_specs=[whole(operand.shape) for operand in (strips, mates, *pieces)],
            out_specs=[whole(send)] + [whole(right)] * rows + [whole((lines, LANES)), whole((8, LANES))],
            scratch_shapes=[
                pltpu.VMEM((peers * 8, peers * 8), jnp.float32),
                pltpu.VMEM(((groups + 1) * cap, LANES), jnp.float32),
                pltpu.VMEM((rows, count, tall_strip, order), jnp.float32),
                pltpu.SMEM((lines, LANES), jnp.int32),
                pltpu.SemaphoreType.DMA,
            ],
        ),
        out_shape=[
            jax.ShapeDtypeStruct(send, jnp.float32),
            *[jax.ShapeDtypeStruct(right, jnp.float32)] * rows,
            jax.ShapeDtypeStruct((lines, LANES), jnp.int32),
            jax.ShapeDtypeStruct((8, LANES), jnp.int32),
        ],
        compiler_params=LIMIT,
    )(jnp.stack([row_index, base]), strips, mates, *pieces)


def multiply_round(left, right, codes, counts, base, own, running, kept):
    order = left.shape[-1]
    first = running is None
    tiles = (kept, order, order)
    operands = [left, *right] + ([] if first else [running])
    return pl.pallas_call(
        functools.partial(product_body, first, len(right)),
        grid_spec=pltpu.PrefetchScalarGridSpec(
            num_scalar_prefetch=3,
            grid=(1,),
            in_specs=[whole(operand.shape) for operand in operands],
            out_specs=whole(tiles),
            scratch_shapes=[pltpu.VMEM((order, order), jnp.float32)] * 2,
        ),
        out_shape=jax.ShapeDtypeStruct(tiles, jnp.float32),
        compiler_params=LIMIT,
    )(jnp.stack([base, own]), codes, counts, *operands)


def shift_all(pieces):
    rows = len(pieces)
    return [pieces[0]] + [
        lax.ppermute(pieces[by], "row", [(i, (i + by) % rows) for i in range(rows)]) for by in range(1, rows)
    ]


def swap_rows(array, rows, by):
    return lax.ppermute(array, "row", [(i, i ^ by) for i in range(rows)])


def local(tile_values, tile_rows, tile_cols, tile_counts, out_rows, out_cols):
    order = tile_values.shape[-1]
    kept = out_rows.shape[-1]
    rows = lax.axis_size("row")
    peers = lax.axis_size(GROUP)
    row_index = lax.axis_index("row")
    own = lax.axis_index(GROUP)
    tiles = tile_values.reshape(-1, order, order)

    listed, wanted = pl.pallas_call(
        label_body,
        in_specs=[pl.BlockSpec(memory_space=pltpu.SMEM)] * 5,
        out_shape=[jax.ShapeDtypeStruct((n, LANES), jnp.float32) for n in (4, 2)],
        compiler_params=LIMIT,
    )(tile_rows, tile_cols, tile_counts, out_rows, out_cols)
    for by in (1, 2, 4):
        listed = listed + swap_rows(listed, rows, by)
    pieces = shift_all(pack_right(tiles, rows))
    strips = pack(tiles, listed, wanted, peers)
    strips = lax.all_to_all(strips, GROUP, 0, 0, tiled=True)
    strips = strips.reshape(-1, order // peers, order)

    zero = jnp.zeros((), jnp.int32)
    send, *right, codes, counts = plan(strips, listed, pieces, row_index, zero, peers, ROUND_CAP)
    most = jnp.max(counts)
    for by in (1, 2, 4):
        most = jnp.maximum(most, swap_rows(most, rows, by))
    left = lax.all_to_all(send, GROUP, 0, 0, tiled=True)
    right = shift_all(right)
    summed = multiply_round(left, right, codes, counts, zero, own, None, kept)

    def unfinished(state):
        return state[0] < most

    def further(state):
        base, running = state
        send, *right, codes, counts = plan(strips, listed, pieces, row_index, base, peers, ROUND_CAP)
        left = lax.all_to_all(send, GROUP, 0, 0, tiled=True)
        right = shift_all(right)
        running = multiply_round(left, right, codes, counts, base, own, running, kept)
        return base + ROUND_CAP, running

    unused, summed = lax.while_loop(unfinished, further, (jnp.int32(ROUND_CAP), summed))
    return summed.reshape(1, 1, kept, order, order)


def solution(mesh):
    in_specs = (
        P("row", GROUP, None, None, None, None),
        P("row", GROUP, None, None),
        P("row", GROUP, None, None),
        P("row", GROUP, None),
        P("row", "col", None, None),
        P("row", "col", None, None),
    )
    out_specs = P("row", GROUP, None, None, None)
    return jax.shard_map(local, mesh=mesh, in_specs=in_specs, out_specs=out_specs, check_vma=False)
```

time: 116 us -> 106 us (0.914); the launches traced: 114 us -> 105 us
  waiting for transfers between devices: 46.6 us -> 25.8 us
  starting transfers between devices: 40.2 us -> 51.9 us
  other arithmetic: 6 us -> 1.38 us
  local copies, waits for them, and re-layouts: 1.69 us -> 5.44 us
  Pallas kernels: 16 us -> 17.8 us
    all_to_all x1, waiting for transfers between devices: 14.2 us -> 0.01 us  [local(): left = lax.all_to_all(send, GROUP, 0, 0, tiled=True)]
    ppermute x3 -> x14, starting transfers between devices: 5.9 us -> 18.7 us  [shift_all(): lax.ppermute(pieces[by], 'row', [(i, (i + by) % rows) for i in range(rows)])]
    all_to_all x1, waiting for transfers between devices: 15.4 us -> 7.64 us  [local(): strips = lax.all_to_all(strips, GROUP, 0, 0, tiled=True)]
    ppermute x3 -> x14, waiting for transfers between devices: 7.19 us -> 12.1 us  [shift_all(): lax.ppermute(pieces[by], 'row', [(i, (i + by) % rows) for i in range(rows)])]
    unnamed x6 -> x16, local copies, waits for them, and re-layouts: 1.08 us -> 5.44 us
    all_to_all x1, starting transfers between devices: 9.92 us -> 5.59 us  [local(): left = lax.all_to_all(send, GROUP, 0, 0, tiled=True)]
    ppermute x10 -> x6, waiting for transfers between devices: 9.84 us -> 6.05 us  [swap_rows(): return lax.ppermute(array, 'row', [(i, i ^ by) for i in range(rows)])]
    ppermute x10 -> x6, starting transfers between devices: 12.8 us -> 16.1 us  [swap_rows(): return lax.ppermute(array, 'row', [(i, i ^ by) for i in range(rows)])]
  transfers between devices with their start and end apart: 15 -> 22, of which waited for: 8 -> 10; matrix products, arithmetic and copies ran while one was open for 3% -> 1% of each run, Pallas kernels for 7% -> 0%
where the time goes in v2:
time: 106 us; the launch traced here: 105 us
  starting transfers between devices  51.9 us (49%)
  waiting for transfers between devices  25.8 us (24%)
  Pallas kernels  17.8 us (17%)
  local copies, waits for them, and re-layouts  5.44 us (5%)
  between operations  2.71 us (3%)
  other arithmetic  1.38 us (1%)
    ppermute x14, starting transfers between devices, shift_all(): lax.ppermute(pieces[by], 'row', [(i, (i + by) % rows) for i in range(rows)])  18.7 us
    ppermute x6, starting transfers between devices, swap_rows(): return lax.ppermute(array, 'row', [(i, i ^ by) for i in range(rows)])  16.1 us
    ppermute x14, waiting for transfers between devices, shift_all(): lax.ppermute(pieces[by], 'row', [(i, (i + by) % rows) for i in range(rows)])  12.1 us
    all_to_all x1, starting transfers between devices, local(): strips = lax.all_to_all(strips, GROUP, 0, 0, tiled=True)  11.6 us
    pallas_call x1, Pallas kernels, plan(): pl.pallas_call(functools.partial(plan_body, rows), grid_spec=pltpu.Prefet...  10.8 us
    all_to_all x1, waiting for transfers between devices, local(): strips = lax.all_to_all(strips, GROUP, 0, 0, tiled=True)  7.64 us
    ppermute x6, waiting for transfers between devices, swap_rows(): return lax.ppermute(array, 'row', [(i, i ^ by) for i in range(rows)])  6.05 us
    all_to_all x1, starting transfers between devices, local(): left = lax.all_to_all(send, GROUP, 0, 0, tiled=True)  5.59 us
  transfers between devices with their start and end apart: 22, of which 10 were waited for; matrix products, arithmetic and copies ran while one was open for 1% of the time, Pallas kernels for 0%

profile of v2, /device:TPU:4, one launch (start us, length us, event | category | flops | bytes accessed | tf_op | source)
XLA Modules:
  0.0 105.0 jit_solution(17241526671024399807)
XLA Ops:
  5.3 1.6 %collective-permute-start.8 = (f32[4,128]{1,0:T(4,128)S(1)}, f32[4,128]{1,0:T(4,128)S(1)}, u32[]{:S(2)}, u32[]{:S(2)}) collective-permute-start(f32[4,128]{1,0:T(4,128)S(1)} %add.16), channel_id=1, source_target_pairs={{0,64},{32,96},{64,0},{96,32},{128,192},{160,224},{192,128},{224,1... | collective-permute-start | bytes 6152 | tf_op jit(solution)/shard_map/ppermute | solution.py:289
  6.9 2.0 %collective-permute-done.8 = f32[4,128]{1,0:T(4,128)S(1)} collective-permute-done((f32[4,128]{1,0:T(4,128)S(1)}, f32[4,128]{1,0:T(4,128)S(1)}, u32[]{:S(2)}, u32[]{:S(2)}) %collective-permute-start.8) | collective-permute-done | bytes 2080 | tf_op jit(solution)/shard_map/ppermute | solution.py:289
  8.9 3.2 %collective-permute-start.9 = (f32[4,128]{1,0:T(4,128)S(1)}, f32[4,128]{1,0:T(4,128)S(1)}, u32[]{:S(2)}, u32[]{:S(2)}) collective-permute-start(f32[4,128]{1,0:T(4,128)S(1)} %add.17), channel_id=1, source_target_pairs={{0,128},{32,160},{64,192},{96,224},{128,0},{160,32},{192,64},{224,... | collective-permute-start | bytes 6152 | tf_op jit(solution)/shard_map/ppermute | solution.py:289
  12.1 1.9 %collective-permute-done.9 = f32[4,128]{1,0:T(4,128)S(1)} collective-permute-done((f32[4,128]{1,0:T(4,128)S(1)}, f32[4,128]{1,0:T(4,128)S(1)}, u32[]{:S(2)}, u32[]{:S(2)}) %collective-permute-start.9) | collective-permute-done | bytes 2080 | tf_op jit(solution)/shard_map/ppermute | solution.py:289
  15.7 1.9 %shard_map.65 = f32[32,13,4,128]{3,2,1,0:T(4,128)} custom-call(f32[12,128,128]{2,1,0:T(8,128)S(1)} %bitcast.14, f32[4,128]{1,0:T(4,128)} %add.18.listed_ref.mates_ref, f32[2,128]{1,0:T(2,128)S(1)} %get-tuple-element.116.wanted_ref), custom_call_target="tpu_custom_call" | custom-call | tf_op jit(solution)/shard_map/pallas_call | solution.py:217
  17.6 11.6 %all-to-all-start.1 = ((f32[32,13,4,128]{3,2,1,0:T(4,128)}), f32[32,13,4,128]{3,2,1,0:T(4,128)S(1)}, u32[]{:S(2)}, u32[]{:S(2)}) async-start(f32[32,13,4,128]{3,2,1,0:T(4,128)} %shard_map.65), calls=%async_computation.1 | async-start | bytes 1703936 | tf_op jit(solution)/shard_map/all_to_all | solution.py:311
  29.3 1.7 %collective-permute-start.11 = (f32[12,16,128]{2,1,0:T(8,128)S(1)}, f32[12,16,128]{2,1,0:T(8,128)}, u32[]{:S(2)}, u32[]{:S(2)}) collective-permute-start(f32[12,16,128]{2,1,0:T(8,128)S(1)} %get-tuple-element.119), channel_id=1, source_target_pairs={{0,64},{32,96},{64,128},{96,160},{128,192},{160,224},{192,0},{224,... | collective-permute-start | bytes 294920 | tf_op jit(solution)/shard_map/ppermute | solution.py:284
  31.0 2.2 %collective-permute-start.12 = (f32[12,16,128]{2,1,0:T(8,128)S(1)}, f32[12,16,128]{2,1,0:T(8,128)}, u32[]{:S(2)}, u32[]{:S(2)}) collective-permute-start(f32[12,16,128]{2,1,0:T(8,128)S(1)} %get-tuple-element.120), channel_id=1, source_target_pairs={{0,96},{32,128},{64,160},{96,192},{128,224},{160,0},{192,32},{224,... | collective-permute-start | bytes 294920 | tf_op jit(solution)/shard_map/ppermute | solution.py:284
  33.2 1.8 %collective-permute-start.13 = (f32[12,16,128]{2,1,0:T(8,128)S(1)}, f32[12,16,128]{2,1,0:T(8,128)}, u32[]{:S(2)}, u32[]{:S(2)}) collective-permute-start(f32[12,16,128]{2,1,0:T(8,128)S(1)} %get-tuple-element.121), channel_id=1, source_target_pairs={{0,128},{32,160},{64,192},{96,224},{128,0},{160,32},{192,64},{224,... | collective-permute-start | bytes 294920 | tf_op jit(solution)/shard_map/ppermute | solution.py:284
  35.0 1.8 %collective-permute-start.14 = (f32[12,16,128]{2,1,0:T(8,128)S(1)}, f32[12,16,128]{2,1,0:T(8,128)}, u32[]{:S(2)}, u32[]{:S(2)}) collective-permute-start(f32[12,16,128]{2,1,0:T(8,128)S(1)} %get-tuple-element.122), channel_id=1, source_target_pairs={{0,160},{32,192},{64,224},{96,0},{128,32},{160,64},{192,96},{224,1... | collective-permute-start | bytes 294920 | tf_op jit(solution)/shard_map/ppermute | solution.py:284
  38.7 1.9 %collective-permute-done.12.refs_3_ = f32[12,16,128]{2,1,0:T(8,128)} collective-permute-done((f32[12,16,128]{2,1,0:T(8,128)S(1)}, f32[12,16,128]{2,1,0:T(8,128)}, u32[]{:S(2)}, u32[]{:S(2)}) %collective-permute-start.12) | collective-permute-done | bytes 98336 | tf_op jit(solution)/shard_map/ppermute | solution.py:284
  41.8 1.4 %collective-permute-done.15.refs_6_ = f32[12,16,128]{2,1,0:T(8,128)} collective-permute-done((f32[12,16,128]{2,1,0:T(8,128)S(1)}, f32[12,16,128]{2,1,0:T(8,128)}, u32[]{:S(2)}, u32[]{:S(2)}) %collective-permute-start.15) | collective-permute-done | bytes 98336 | tf_op jit(solution)/shard_map/ppermute | solution.py:284
  43.2 7.6 %all-to-all-done.1 = f32[32,13,4,128]{3,2,1,0:T(4,128)S(1)} async-done(((f32[32,13,4,128]{3,2,1,0:T(4,128)}), f32[32,13,4,128]{3,2,1,0:T(4,128)S(1)}, u32[]{:S(2)}, u32[]{:S(2)}) %all-to-all-start.1) | async-done | bytes 852000 | tf_op jit(solution)/shard_map/all_to_all | solution.py:311
  51.8 10.8 %shard_map.67 = (f32[32,20,4,128]{3,2,1,0:T(4,128)}, f32[20,16,128]{2,1,0:T(8,128)S(1)}, f32[20,16,128]{2,1,0:T(8,128)S(1)}, f32[20,16,128]{2,1,0:T(8,128)S(1)},...) custom-call(s32[2]{0:T(128)S(1)} %pad_add_fusion.3.scalars, ...), custom_call_target="tpu_custom_call" | custom-call | tf_op jit(solution)/shard_map/pallas_call | solution.py:237
  62.5 5.6 %all-to-all-start.2 = ((f32[32,20,4,128]{3,2,1,0:T(4,128)}), f32[32,20,4,128]{3,2,1,0:T(4,128)S(1)}, u32[]{:S(2)}, u32[]{:S(2)}) async-start(f32[32,20,4,128]{3,2,1,0:T(4,128)} %get-tuple-element.127), calls=%async_computation.2 | async-start | bytes 2621440 | tf_op jit(solution)/shard_map/all_to_all | solution.py:319
  68.2 1.8 %collective-permute-start.18 = (f32[20,16,128]{2,1,0:T(8,128)S(1)}, f32[20,16,128]{2,1,0:T(8,128)S(1)}, u32[]{:S(2)}, u32[]{:S(2)}) collective-permute-start(f32[20,16,128]{2,1,0:T(8,128)S(1)} %get-tuple-element.130), channel_id=1, source_target_pairs={{0,64},{32,96},{64,128},{96,160},{128,192},{160,224},{192,0},{224,... | collective-permute-start | bytes 491528 | tf_op jit(solution)/shard_map/ppermute | solution.py:284
  72.6 1.8 %collective-permute-start.20 = (f32[20,16,128]{2,1,0:T(8,128)S(1)}, f32[20,16,128]{2,1,0:T(8,128)S(1)}, u32[]{:S(2)}, u32[]{:S(2)}) collective-permute-start(f32[20,16,128]{2,1,0:T(8,128)S(1)} %get-tuple-element.132), channel_id=1, source_target_pairs={{0,128},{32,160},{64,192},{96,224},{128,0},{160,32},{192,64},{224,... | collective-permute-start | bytes 491528 | tf_op jit(solution)/shard_map/ppermute | solution.py:284
  75.8 5.9 %collective-permute-start.25 = (s32[]{:T(128)}, s32[]{:T(128)}, u32[]{:S(2)}, u32[]{:S(2)}) collective-permute-start(s32[]{:T(128)} %max.9), channel_id=1, source_target_pairs={{0,64},{32,96},{64,0},{96,32},{128,192},{160,224},{192,128},{224,1... | collective-permute-start | bytes 20 | tf_op jit(solution)/shard_map/ppermute | solution.py:289
  82.4 4.2 %collective-permute-start.26 = (s32[]{:T(128)}, s32[]{:T(128)}, u32[]{:S(2)}, u32[]{:S(2)}) collective-permute-start(s32[]{:T(128)} %max.10), channel_id=1, source_target_pairs={{0,128},{32,160},{64,192},{96,224},{128,0},{160,32},{192,64},{224,... | collective-permute-start | bytes 20 | tf_op jit(solution)/shard_map/ppermute | solution.py:289
  87.6 2.5 %collective-permute-start.21 = (f32[20,16,128]{2,1,0:T(8,128)S(1)}, f32[20,16,128]{2,1,0:T(8,128)S(1)}, u32[]{:S(2)}, u32[]{:S(2)}) collective-permute-start(f32[20,16,128]{2,1,0:T(8,128)S(1)} %get-tuple-element.133), channel_id=1, source_target_pairs={{0,160},{32,192},{64,224},{96,0},{128,32},{160,64},{192,96},{224,1... | collective-permute-start | bytes 491528 | tf_op jit(solution)/shard_map/ppermute | solution.py:284
  90.1 2.2 %collective-permute-start.22 = (f32[20,16,128]{2,1,0:T(8,128)S(1)}, f32[20,16,128]{2,1,0:T(8,128)S(1)}, u32[]{:S(2)}, u32[]{:S(2)}) collective-permute-start(f32[20,16,128]{2,1,0:T(8,128)S(1)} %get-tuple-element.134), channel_id=1, source_target_pairs={{0,192},{32,224},{64,0},{96,32},{128,64},{160,96},{192,128},{224,1... | collective-permute-start | bytes 491528 | tf_op jit(solution)/shard_map/ppermute | solution.py:284
  93.1 5.7 %collective-permute-done.22.refs_6_ = f32[20,16,128]{2,1,0:T(8,128)S(1)} collective-permute-done((f32[20,16,128]{2,1,0:T(8,128)S(1)}, f32[20,16,128]{2,1,0:T(8,128)S(1)}, u32[]{:S(2)}, u32[]{:S(2)}) %collective-permute-start.22) | collective-permute-done | bytes 163872 | tf_op jit(solution)/shard_map/ppermute | solution.py:284
  98.7 1.9 %collective-permute-done.23.refs_7_ = f32[20,16,128]{2,1,0:T(8,128)S(1)} collective-permute-done((f32[20,16,128]{2,1,0:T(8,128)S(1)}, f32[20,16,128]{2,1,0:T(8,128)S(1)}, u32[]{:S(2)}, u32[]{:S(2)}) %collective-permute-start.23) | collective-permute-done | bytes 163872 | tf_op jit(solution)/shard_map/ppermute | solution.py:284
  100.6 4.4 %shard_map.68 = f32[12,128,128]{2,1,0:T(8,128)} custom-call(s32[2]{0:T(128)S(1)} %pad_add_fusion.2.scalars, s32[16,128]{1,0:T(8,128)S(1)} %get-tuple-element.125.codes, s32[8,128]{1,0:T(8,128)S(1)} %get-tuple-element.126.counts, f32[32,20,4,128]{3,2,1,0:T(4,128)S(1)} %all-to-all-done.2.left_ref, f32[20,16,128]{2,1,0:T(8,128)S(1)} %get-tuple-element.128.refs_0_, ...), custom_call_target="tpu_custom_call" | custom-call | tf_op jit(solution)/shard_map/pallas_call | solution.py:267
  (48 shorter events, 14.9 us)
Async XLA Ops:
  4.1 1.2 %collective-permute-start.7 = (f32[4,128]{1,0:T(4,128)S(1)}, f32[4,128]{1,0:T(4,128)S(1)}, u32[]{:S(2)}, u32[]{:S(2)}) collective-permute-start(f32[4,128]{1,0:T(4,128)S(1)} %get-tuple-element.115), channel_id=1, source_target_pairs={{0,32},{32,0},{64,96},{96,64},{128,160},{160,128},{192,224},{224,1... | collective-permute-start | bytes 6152 | tf_op jit(solution)/shard_map/ppermute | solution.py:289
  5.3 3.6 %collective-permute-start.8 = (f32[4,128]{1,0:T(4,128)S(1)}, f32[4,128]{1,0:T(4,128)S(1)}, u32[]{:S(2)}, u32[]{:S(2)}) collective-permute-start(f32[4,128]{1,0:T(4,128)S(1)} %add.16), channel_id=1, source_target_pairs={{0,64},{32,96},{64,0},{96,32},{128,192},{160,224},{192,128},{224,1... | collective-permute-start | bytes 6152 | tf_op jit(solution)/shard_map/ppermute | solution.py:289
  8.9 5.1 %collective-permute-start.9 = (f32[4,128]{1,0:T(4,128)S(1)}, f32[4,128]{1,0:T(4,128)S(1)}, u32[]{:S(2)}, u32[]{:S(2)}) collective-permute-start(f32[4,128]{1,0:T(4,128)S(1)} %add.17), channel_id=1, source_target_pairs={{0,128},{32,160},{64,192},{96,224},{128,0},{160,32},{192,64},{224,... | collective-permute-start | bytes 6152 | tf_op jit(solution)/shard_map/ppermute | solution.py:289
  14.6 1.1 %copy-start = (f32[1,1,2,6,128,128]{5,4,3,2,1,0:T(8,128)S(1)}, f32[1,1,2,6,128,128]{5,4,3,2,1,0:T(8,128)}, u32[]{:S(2)}) copy-start(f32[1,1,2,6,128,128]{5,4,3,2,1,0:T(8,128)} %param.8) | copy-start | bytes 2359300
  15.7 13.5 %copy-start.1 = (f32[1,1,2,6,128,128]{5,4,3,2,1,0:T(8,128)S(1)}, f32[1,1,2,6,128,128]{5,4,3,2,1,0:T(8,128)}, u32[]{:S(2)}) copy-start(f32[1,1,2,6,128,128]{5,4,3,2,1,0:T(8,128)} %param.8) | copy-start | bytes 2359300
  17.6 33.2 %all-to-all-start.1 = ((f32[32,13,4,128]{3,2,1,0:T(4,128)}), f32[32,13,4,128]{3,2,1,0:T(4,128)S(1)}, u32[]{:S(2)}, u32[]{:S(2)}) async-start(f32[32,13,4,128]{3,2,1,0:T(4,128)} %shard_map.65), calls=%async_computation.1 | async-start | bytes 1703936 | tf_op jit(solution)/shard_map/all_to_all | solution.py:311
  29.3 7.6 %collective-permute-start.10 = (f32[12,16,128]{2,1,0:T(8,128)S(1)}, f32[12,16,128]{2,1,0:T(8,128)}, u32[]{:S(2)}, u32[]{:S(2)}) collective-permute-start(f32[12,16,128]{2,1,0:T(8,128)S(1)} %get-tuple-element.118), channel_id=1, source_target_pairs={{0,32},{32,64},{64,96},{96,128},{128,160},{160,192},{192,224},{224... | collective-permute-start | bytes 294920 | tf_op jit(solution)/shard_map/ppermute | solution.py:284
  29.3 8.9 %collective-permute-start.11 = (f32[12,16,128]{2,1,0:T(8,128)S(1)}, f32[12,16,128]{2,1,0:T(8,128)}, u32[]{:S(2)}, u32[]{:S(2)}) collective-permute-start(f32[12,16,128]{2,1,0:T(8,128)S(1)} %get-tuple-element.119), channel_id=1, source_target_pairs={{0,64},{32,96},{64,128},{96,160},{128,192},{160,224},{192,0},{224,... | collective-permute-start | bytes 294920 | tf_op jit(solution)/shard_map/ppermute | solution.py:284
  31.0 9.6 %collective-permute-start.12 = (f32[12,16,128]{2,1,0:T(8,128)S(1)}, f32[12,16,128]{2,1,0:T(8,128)}, u32[]{:S(2)}, u32[]{:S(2)}) collective-permute-start(f32[12,16,128]{2,1,0:T(8,128)S(1)} %get-tuple-element.120), channel_id=1, source_target_pairs={{0,96},{32,128},{64,160},{96,192},{128,224},{160,0},{192,32},{224,... | collective-permute-start | bytes 294920 | tf_op jit(solution)/shard_map/ppermute | solution.py:284
  33.2 8.6 %collective-permute-start.13 = (f32[12,16,128]{2,1,0:T(8,128)S(1)}, f32[12,16,128]{2,1,0:T(8,128)}, u32[]{:S(2)}, u32[]{:S(2)}) collective-permute-start(f32[12,16,128]{2,1,0:T(8,128)S(1)} %get-tuple-element.121), channel_id=1, source_target_pairs={{0,128},{32,160},{64,192},{96,224},{128,0},{160,32},{192,64},{224,... | collective-permute-start | bytes 294920 | tf_op jit(solution)/shard_map/ppermute | solution.py:284
  35.0 6.8 %collective-permute-start.14 = (f32[12,16,128]{2,1,0:T(8,128)S(1)}, f32[12,16,128]{2,1,0:T(8,128)}, u32[]{:S(2)}, u32[]{:S(2)}) collective-permute-start(f32[12,16,128]{2,1,0:T(8,128)S(1)} %get-tuple-element.122), channel_id=1, source_target_pairs={{0,160},{32,192},{64,224},{96,0},{128,32},{160,64},{192,96},{224,1... | collective-permute-start | bytes 294920 | tf_op jit(solution)/shard_map/ppermute | solution.py:284
  36.8 6.3 %collective-permute-start.15 = (f32[12,16,128]{2,1,0:T(8,128)S(1)}, f32[12,16,128]{2,1,0:T(8,128)}, u32[]{:S(2)}, u32[]{:S(2)}) collective-permute-start(f32[12,16,128]{2,1,0:T(8,128)S(1)} %get-tuple-element.123), channel_id=1, source_target_pairs={{0,192},{32,224},{64,0},{96,32},{128,64},{160,96},{192,128},{224,1... | collective-permute-start | bytes 294920 | tf_op jit(solution)/shard_map/ppermute | solution.py:284
  38.2 5.0 %collective-permute-start.16 = (f32[12,16,128]{2,1,0:T(8,128)S(1)}, f32[12,16,128]{2,1,0:T(8,128)}, u32[]{:S(2)}, u32[]{:S(2)}) collective-permute-start(f32[12,16,128]{2,1,0:T(8,128)S(1)} %get-tuple-element.124), channel_id=1, source_target_pairs={{0,224},{32,0},{64,32},{96,64},{128,96},{160,128},{192,160},{224,1... | collective-permute-start | bytes 294920 | tf_op jit(solution)/shard_map/ppermute | solution.py:284
  62.5 38.1 %all-to-all-start.2 = ((f32[32,20,4,128]{3,2,1,0:T(4,128)}), f32[32,20,4,128]{3,2,1,0:T(4,128)S(1)}, u32[]{:S(2)}, u32[]{:S(2)}) async-start(f32[32,20,4,128]{3,2,1,0:T(4,128)} %get-tuple-element.127), calls=%async_computation.2 | async-start | bytes 2621440 | tf_op jit(solution)/shard_map/all_to_all | solution.py:319
  68.1 22.0 %collective-permute-start.17 = (f32[20,16,128]{2,1,0:T(8,128)S(1)}, f32[20,16,128]{2,1,0:T(8,128)S(1)}, u32[]{:S(2)}, u32[]{:S(2)}) collective-permute-start(f32[20,16,128]{2,1,0:T(8,128)S(1)} %get-tuple-element.129), channel_id=1, source_target_pairs={{0,32},{32,64},{64,96},{96,128},{128,160},{160,192},{192,224},{224... | collective-permute-start | bytes 491528 | tf_op jit(solution)/shard_map/ppermute | solution.py:284
  68.2 24.2 %collective-permute-start.18 = (f32[20,16,128]{2,1,0:T(8,128)S(1)}, f32[20,16,128]{2,1,0:T(8,128)S(1)}, u32[]{:S(2)}, u32[]{:S(2)}) collective-permute-start(f32[20,16,128]{2,1,0:T(8,128)S(1)} %get-tuple-element.130), channel_id=1, source_target_pairs={{0,64},{32,96},{64,128},{96,160},{128,192},{160,224},{192,0},{224,... | collective-permute-start | bytes 491528 | tf_op jit(solution)/shard_map/ppermute | solution.py:284
  70.6 3.9 %collective-permute-start.24 = (s32[]{:T(128)}, s32[]{:T(128)}, u32[]{:S(2)}, u32[]{:S(2)}) collective-permute-start(s32[]{:T(128)} %reduce_max.9), channel_id=1, source_target_pairs={{0,32},{32,0},{64,96},{96,64},{128,160},{160,128},{192,224},{224,1... | collective-permute-start | bytes 20 | tf_op jit(solution)/shard_map/ppermute | solution.py:289
  71.8 21.3 %collective-permute-start.19 = (f32[20,16,128]{2,1,0:T(8,128)S(1)}, f32[20,16,128]{2,1,0:T(8,128)S(1)}, u32[]{:S(2)}, u32[]{:S(2)}) collective-permute-start(f32[20,16,128]{2,1,0:T(8,128)S(1)} %get-tuple-element.131), channel_id=1, source_target_pairs={{0,96},{32,128},{64,160},{96,192},{128,224},{160,0},{192,32},{224,... | collective-permute-start | bytes 491528 | tf_op jit(solution)/shard_map/ppermute | solution.py:284
  72.6 20.4 %collective-permute-start.20 = (f32[20,16,128]{2,1,0:T(8,128)S(1)}, f32[20,16,128]{2,1,0:T(8,128)S(1)}, u32[]{:S(2)}, u32[]{:S(2)}) collective-permute-start(f32[20,16,128]{2,1,0:T(8,128)S(1)} %get-tuple-element.132), channel_id=1, source_target_pairs={{0,128},{32,160},{64,192},{96,224},{128,0},{160,32},{192,64},{224,... | collective-permute-start | bytes 491528 | tf_op jit(solution)/shard_map/ppermute | solution.py:284
  75.8 5.9 %collective-permute-start.25 = (s32[]{:T(128)}, s32[]{:T(128)}, u32[]{:S(2)}, u32[]{:S(2)}) collective-permute-start(s32[]{:T(128)} %max.9), channel_id=1, source_target_pairs={{0,64},{32,96},{64,0},{96,32},{128,192},{160,224},{192,128},{224,1... | collective-permute-start | bytes 20 | tf_op jit(solution)/shard_map/ppermute | solution.py:289
  82.4 5.2 %collective-permute-start.26 = (s32[]{:T(128)}, s32[]{:T(128)}, u32[]{:S(2)}, u32[]{:S(2)}) collective-permute-start(s32[]{:T(128)} %max.10), channel_id=1, source_target_pairs={{0,128},{32,160},{64,192},{96,224},{128,0},{160,32},{192,64},{224,... | collective-permute-start | bytes 20 | tf_op jit(solution)/shard_map/ppermute | solution.py:289
  87.6 5.5 %collective-permute-start.21 = (f32[20,16,128]{2,1,0:T(8,128)S(1)}, f32[20,16,128]{2,1,0:T(8,128)S(1)}, u32[]{:S(2)}, u32[]{:S(2)}) collective-permute-start(f32[20,16,128]{2,1,0:T(8,128)S(1)} %get-tuple-element.133), channel_id=1, source_target_pairs={{0,160},{32,192},{64,224},{96,0},{128,32},{160,64},{192,96},{224,1... | collective-permute-start | bytes 491528 | tf_op jit(solution)/shard_map/ppermute | solution.py:284
  90.1 8.6 %collective-permute-start.22 = (f32[20,16,128]{2,1,0:T(8,128)S(1)}, f32[20,16,128]{2,1,0:T(8,128)S(1)}, u32[]{:S(2)}, u32[]{:S(2)}) collective-permute-start(f32[20,16,128]{2,1,0:T(8,128)S(1)} %get-tuple-element.134), channel_id=1, source_target_pairs={{0,192},{32,224},{64,0},{96,32},{128,64},{160,96},{192,128},{224,1... | collective-permute-start | bytes 491528 | tf_op jit(solution)/shard_map/ppermute | solution.py:284
  92.4 8.3 %collective-permute-start.23 = (f32[20,16,128]{2,1,0:T(8,128)S(1)}, f32[20,16,128]{2,1,0:T(8,128)S(1)}, u32[]{:S(2)}, u32[]{:S(2)}) collective-permute-start(f32[20,16,128]{2,1,0:T(8,128)S(1)} %get-tuple-element.135), channel_id=1, source_target_pairs={{0,224},{32,0},{64,32},{96,64},{128,96},{160,128},{192,160},{224,1... | collective-permute-start | bytes 491528 | tf_op jit(solution)/shard_map/ppermute | solution.py:284
  (6 other events, 4.3 us)

commit v3 on v2

v3 whole, which is shorter than its diff:
```python
import functools

import jax
import jax.numpy as jnp
from jax import lax
from jax.experimental import pallas as pl
from jax.experimental.pallas import tpu as pltpu
from jax.sharding import PartitionSpec as P

GROUP = ("col", "layer")
LANES = 128
SLOT_PITCH = 16
PER_GROUP = LANES // SLOT_PITCH
ROUND_CAP = 20
LIMIT = pltpu.CompilerParams(vmem_limit_bytes=20 * 2**20)
HBM = pl.BlockSpec(memory_space=pltpu.HBM)


def in_hbm(*arrays):
    return [pltpu.with_memory_space_constraint(array, pltpu.HBM) for array in arrays]


def padded(size, unit):
    return unit * pl.cdiv(size, unit)


def label_body(*refs):
    sources, listed_ref, wanted_ref, sems, copies = refs[:5], refs[5], refs[6], refs[7], refs[8:]
    moves = [pltpu.make_async_copy(a, b, sems.at[n]) for n, (a, b) in enumerate(zip(sources, copies))]
    for move in moves:
        move.start()
    for move in moves:
        move.wait()
    tile_rows, tile_cols, counts, out_rows, out_cols = copies
    lists, capacity = tile_rows.shape[2:]
    row_index, layer_index = lax.axis_index("row"), lax.axis_index("layer")
    in_group = lax.axis_index(GROUP) % PER_GROUP
    lane = lax.broadcasted_iota(jnp.int32, (1, LANES), 1)
    nothing = jnp.zeros((1, LANES), jnp.int32)
    rows, cols, kept_rows, kept_cols = nothing, nothing, nothing, nothing
    mate_rows, mate_cols = nothing, nothing
    for at in range(lists):
        for slot in range(capacity):
            live = slot < counts[0, 0, at]
            here = lane == jnp.where(live, row_index * SLOT_PITCH + at * capacity + slot, -1)
            rows = jnp.where(here, tile_rows[0, 0, at, slot] + 1, rows)
            cols = jnp.where(here, tile_cols[0, 0, at, slot] + 1, cols)
    for at in range(out_rows.shape[3]):
        target_row, target_col = out_rows[0, 0, layer_index, at] + 1, out_cols[0, 0, layer_index, at] + 1
        here = lane == in_group * SLOT_PITCH + at
        kept_rows = jnp.where(here, target_row, kept_rows)
        kept_cols = jnp.where(here, target_col, kept_cols)
        here = lane == row_index * SLOT_PITCH + at
        mate_rows = jnp.where(here, target_row, mate_rows)
        mate_cols = jnp.where(here, target_col, mate_cols)
    listed_ref[...] = jnp.concatenate([rows, cols, mate_rows, mate_cols]).astype(jnp.float32)
    wanted_ref[...] = jnp.concatenate([kept_rows, kept_cols]).astype(jnp.float32)


def label(tile_rows, tile_cols, tile_counts, out_rows, out_cols):
    operands = (tile_rows, tile_cols, tile_counts, out_rows, out_cols)
    return pl.pallas_call(
        label_body,
        in_specs=[HBM] * 5,
        out_shape=[jax.ShapeDtypeStruct((n, LANES), jnp.float32) for n in (4, 2)],
        scratch_shapes=[pltpu.SemaphoreType.DMA((5,))] + [pltpu.SMEM(x.shape, jnp.int32) for x in operands],
        compiler_params=LIMIT,
    )(*in_hbm(*operands))


def pack_body(tiles_hbm, out_ref, tiles, sems):
    peers, per_peer, strip, _ = out_ref.shape
    for tile in range(per_peer - 1):
        pltpu.make_async_copy(tiles_hbm.at[tile], tiles.at[tile], sems.at[tile]).start()

    def one_tile(tile, carry):
        pltpu.make_async_copy(tiles_hbm.at[tile], tiles.at[tile], sems.at[tile]).wait()
        for peer in range(peers):
            out_ref[peer, tile] = tiles[tile, peer * strip:(peer + 1) * strip, :]
        return carry

    lax.fori_loop(0, per_peer - 1, one_tile, 0)


def pack(tiles, peers):
    count, order = tiles.shape[:2]
    shape = (peers, count + 1, order // peers, order)
    return pl.pallas_call(
        pack_body,
        in_specs=[HBM],
        out_shape=pltpu.HBM(shape, jnp.float32),
        scratch_shapes=[pltpu.VMEM(tiles.shape, jnp.float32), pltpu.SemaphoreType.DMA((count,))],
        compiler_params=LIMIT,
    )(*in_hbm(tiles))


def stamp_body(one_ref, other_ref, wanted_ref, strips_in, strips_out, total_ref, meta, sem):
    peers, per_peer = strips_out.shape[:2]
    total = one_ref[...] + other_ref[...]
    total_ref[...] = total
    full = jnp.concatenate([total[0:2, :], wanted_ref[...]])
    for peer in range(peers):
        meta[peer] = full
    copy = pltpu.make_async_copy(meta, strips_out.at[:, per_peer - 1], sem)
    copy.start()
    copy.wait()


def stamp(one, other, wanted, strips):
    peers, _, strip, order = strips.shape
    vmem = pl.BlockSpec(memory_space=pltpu.VMEM)
    return pl.pallas_call(
        stamp_body,
        in_specs=[vmem, vmem, vmem, HBM],
        out_specs=[HBM, vmem],
        out_shape=[pltpu.HBM(strips.shape, jnp.float32), jax.ShapeDtypeStruct(one.shape, jnp.float32)],
        input_output_aliases={3: 0},
        scratch_shapes=[pltpu.VMEM((peers, strip, order), jnp.float32), pltpu.SemaphoreType.DMA],
        compiler_params=LIMIT,
    )(one, other, wanted, *in_hbm(strips))


def pack_right_body(tiles_ref, *out_refs):
    count, strip, _ = out_refs[0].shape
    row_index = lax.axis_index("row")
    for away, out_ref in enumerate(out_refs):
        start = pl.multiple_of((row_index + away) % len(out_refs) * strip, strip)
        for tile in range(count):
            out_ref[tile] = tiles_ref[tile, pl.ds(start, strip), :]


def pack_right(tiles, rows):
    count, order = tiles.shape[:2]
    shape = (count, order // rows, order)
    return pl.pallas_call(
        pack_right_body, out_shape=[jax.ShapeDtypeStruct(shape, jnp.float32)] * rows, compiler_params=LIMIT
    )(*in_hbm(tiles))


def plan_body(
    rows, base_ref, strips_ref, mates_ref,
    send_ref, codes_ref, counts_ref, peak_ref,
    table, values, keys, picks, places_vmem, send, places, sem, send_sems,
):
    row_index, base = lax.axis_index("row"), base_ref[0]
    peers, cap = send_ref.shape[:2]
    per_peer = strips_ref.shape[0] // peers
    band = 8
    blocks = peers * band
    band_rows = blocks // rows
    groups = peers // PER_GROUP
    deep = picks.shape[0] // (groups + 1)
    halves = pl.cdiv(cap, SLOT_PITCH)
    f32, bf16 = jnp.float32, jnp.bfloat16
    iota = functools.partial(lax.broadcasted_iota, jnp.int32)

    one, zero = jnp.ones((blocks, LANES), bf16), jnp.zeros((blocks, LANES), bf16)
    tall = (iota((blocks, LANES), 0) + 1).astype(f32).astype(bf16)
    in_band = iota((band_rows, LANES), 0).astype(f32)
    band_start = (iota((1, LANES), 1) // SLOT_PITCH * band_rows + 1).astype(f32)
    band_mask = jnp.where(iota((blocks, LANES), 0) // band_rows == iota((blocks, LANES), 1) // SLOT_PITCH, 1.0, 0.0)
    band_mask = band_mask.astype(bf16)
    short = iota((band, LANES), 0).astype(f32) + 1.0
    names = iota((band, LANES), 1).astype(f32) + 1.0
    targets = []
    for peer in range(peers):
        meta = strips_ref[peer * per_peer + per_peer - 1]
        row_hot = jnp.where(in_band == meta[0:1, :] - band_start, 1.0, 0.0).astype(bf16)
        row_hot = jnp.concatenate([row_hot] * rows, axis=0) * band_mask
        col_hot = jnp.where(short + float(peer * band) == meta[1:2, :], names, 0.0).astype(bf16)
        table[peer * band:(peer + 1) * band, :] = lax.dot_general(
            col_hot, row_hot, (((1,), (1,)), ((), ())), preferred_element_type=f32
        )
        if peer % PER_GROUP == 0:
            targets.append(meta)
        else:
            targets[-1] = targets[-1] + meta
    by_col = table[...]
    by_row = by_col.T.astype(bf16)
    by_col = by_col.astype(bf16)

    below = jnp.where(iota((blocks, blocks), 0) >= iota((blocks, blocks), 1), 1.0, 0.0).astype(bf16)
    lane_from, lane_to = iota((LANES, LANES), 0), iota((LANES, LANES), 1)
    same_peer = lane_from // SLOT_PITCH == lane_to // SLOT_PITCH
    earlier = jnp.where(same_peer & (lane_from < lane_to), 1.0, 0.0).astype(bf16)
    together = jnp.where(same_peer, 1.0, 0.0)
    fixed = iota((blocks, LANES), 0) // band * per_peer + ((iota((blocks, LANES), 1) % SLOT_PITCH) << 16)
    fixed = (fixed - (SLOT_PITCH * row_index + 1 + 512)).astype(f32)

    targets = [(meta[2:3, :], meta[3:4, :]) for meta in targets]
    targets.append((mates_ref[2:3, :], mates_ref[3:4, :]))
    everything = []
    for group, (target_rows, target_cols) in enumerate(targets):
        def hot(target):
            few = jnp.broadcast_to(target, (16, LANES)).astype(bf16)
            return jnp.where(tall == jnp.concatenate([few] * (blocks // 16), axis=0), one, zero)

        left = jnp.dot(by_col, hot(target_rows), preferred_element_type=f32)
        right = jnp.dot(by_row, hot(target_cols), preferred_element_type=f32)
        hit = left * right > 0.0
        ranks = jnp.dot(below, jnp.where(hit, 1.0, 0.0).astype(bf16), preferred_element_type=f32)
        everything.append(ranks[blocks - 1:blocks, :])
        keys[group * blocks:(group + 1) * blocks, :] = jnp.where(hit, ranks, 0.0)
        if group < groups:
            value = fixed + left + right * 512.0
        else:
            name = right.astype(jnp.int32) - 1
            value = (name - (SLOT_PITCH - per_peer + 1) * (name >> 4)).astype(f32)
        values[group * blocks:(group + 1) * blocks, :] = value
    found = jnp.concatenate(everything + everything[-1:] * (8 - len(everything)), axis=0)
    ahead = jnp.dot(found.astype(bf16), earlier, preferred_element_type=f32) - base.astype(f32)
    counts = jnp.dot(found.astype(bf16), together.astype(bf16), preferred_element_type=f32)
    counts_ref[...] = counts.astype(jnp.int32)
    peak_ref[...] = jnp.broadcast_to(jnp.max(jnp.max(counts[0:groups, :], axis=0, keepdims=True), axis=1, keepdims=True), (8, LANES))
    picks[...] = jnp.zeros_like(picks)
    depth = jnp.max(found).astype(jnp.int32)
    slot_at = iota((deep, LANES), 0).astype(f32)

    def one_depth(level, carry):
        level_f = level.astype(f32)
        for group in range(groups + 1):
            span = slice(group * blocks, (group + 1) * blocks)
            value = jnp.sum(jnp.where(keys[span, :] == level_f + 1.0, values[span, :], 0.0), axis=0, keepdims=True)
            place = jnp.where(found[group:group + 1, :] > level_f, ahead[group:group + 1, :] + level_f, -1.0)
            span = slice(group * deep, (group + 1) * deep)
            picks[span, :] = picks[span, :] + jnp.where(slot_at == place, value, 0.0)
        return carry

    lax.fori_loop(0, depth, one_depth, 0)
    spread = jnp.dot(picks[...], together, precision=lax.Precision.HIGHEST, preferred_element_type=f32)
    mine = iota((deep, LANES), 0) % SLOT_PITCH == iota((deep, LANES), 1) % SLOT_PITCH
    lines = []
    for group in range(groups + 1):
        chosen = jnp.where(mine, spread[group * deep:(group + 1) * deep, :], 0.0)
        for half in range(halves):
            lines.append(jnp.sum(chosen[half * SLOT_PITCH:(half + 1) * SLOT_PITCH, :], axis=0, keepdims=True))
    lines += lines[-1:] * (codes_ref.shape[0] - len(lines))
    codes = jnp.concatenate(lines, axis=0).astype(jnp.int32)
    codes_ref[...] = codes
    places_vmem[...] = codes & 511
    copy = pltpu.make_async_copy(places_vmem, places, sem)
    copy.start()
    copy.wait()

    def one_group(group):
        part = pl.ds(group * PER_GROUP, PER_GROUP)
        return pltpu.make_async_copy(send.at[part], send_ref.at[part], send_sems.at[group])

    def one_peer(peer, carry):
        line = (peer >> 3) * halves
        first = (peer & (PER_GROUP - 1)) * SLOT_PITCH
        for at in range(cap):
            send[peer, at] = strips_ref[places[line + at // SLOT_PITCH, first + at % SLOT_PITCH]]
        return carry

    for group in range(groups):
        lax.fori_loop(group * PER_GROUP, (group + 1) * PER_GROUP, one_peer, 0)
        one_group(group).start()
    for group in range(groups):
        one_group(group).wait()


def whole(shape):
    return pl.BlockSpec(shape, lambda i, *_: (0,) * len(shape))


def plan(strips, mates, base, rows, peers, cap):
    strip, order = strips.shape[1:]
    groups = peers // PER_GROUP
    lines = padded((groups + 1) * pl.cdiv(cap, SLOT_PITCH), 8)
    send = (peers, cap, strip, order)
    blocks = peers * 8
    shapes = [(send, jnp.float32), ((lines, LANES), jnp.int32), ((8, LANES), jnp.int32), ((8, LANES), jnp.float32)]
    return pl.pallas_call(
        functools.partial(plan_body, rows),
        grid_spec=pltpu.PrefetchScalarGridSpec(
            num_scalar_prefetch=1,
            grid=(1,),
            in_specs=[whole(strips.shape), whole(mates.shape)],
            out_specs=[HBM] + [whole(shape) for shape, _ in shapes[1:]],
            scratch_shapes=[
                pltpu.VMEM((blocks, blocks), jnp.float32),
                pltpu.VMEM(((groups + 1) * blocks, LANES), jnp.float32),
                pltpu.VMEM(((groups + 1) * blocks, LANES), jnp.float32),
                pltpu.VMEM(((groups + 1) * padded(cap, 8), LANES), jnp.float32),
                pltpu.VMEM((lines, LANES), jnp.int32),
                pltpu.VMEM(send, jnp.float32),
                pltpu.SMEM((lines, LANES), jnp.int32),
                pltpu.SemaphoreType.DMA,
                pltpu.SemaphoreType.DMA((groups,)),
            ],
        ),
        out_shape=[pltpu.HBM(*shapes[0])] + [jax.ShapeDtypeStruct(*shape) for shape in shapes[1:]],
        compiler_params=LIMIT,
    )(base.reshape(1), pltpu.with_memory_space_constraint(strips, pltpu.VMEM), mates)


def collect_body(rows, first_line, codes, peak_ref, *refs):
    piece_refs, right_refs, panel = refs[:rows], refs[rows:2 * rows], refs[2 * rows]
    row_index = lax.axis_index("row")
    count, strip, _ = piece_refs[0].shape
    cap = right_refs[0].shape[0] - 1
    for away, piece_ref in enumerate(piece_refs):
        start = (row_index + rows - away) % rows * count
        for tile in range(count):
            panel[start + tile] = piece_ref[tile]
    for away, right_ref in enumerate(right_refs):
        lane = (row_index + away) % rows * SLOT_PITCH
        for at in range(cap):
            right_ref[at] = panel[codes[first_line + at // SLOT_PITCH, lane + at % SLOT_PITCH]]
        right_ref[cap, 0:8, :] = peak_ref[...]
        right_ref[cap, 8:16, :] = peak_ref[...]


def collect(codes, peak, pieces, peers, cap):
    rows = len(pieces)
    count, strip, order = pieces[0].shape
    right = (cap + 1, strip, order)
    return pl.pallas_call(
        functools.partial(collect_body, rows, peers // PER_GROUP * pl.cdiv(cap, SLOT_PITCH)),
        grid_spec=pltpu.PrefetchScalarGridSpec(
            num_scalar_prefetch=1,
            grid=(1,),
            in_specs=[whole(operand.shape) for operand in (peak, *pieces)],
            out_specs=[whole(right)] * rows,
            scratch_shapes=[pltpu.VMEM((rows * count, strip, order), jnp.float32)],
        ),
        out_shape=[jax.ShapeDtypeStruct(right, jnp.float32)] * rows,
        compiler_params=LIMIT,
    )(codes, peak, *in_hbm(*pieces))


def product_body(first, rows, base_ref, codes, counts, left_ref, *refs):
    right_refs, refs = refs[:rows], refs[rows:]
    if first:
        out_ref, most_ref, left, right = refs
        out_ref[...] = jnp.zeros_like(out_ref)
    else:
        running_ref, out_ref, most_ref, left, right = refs
        out_ref[...] = running_ref[...]
    row_index, own, base = lax.axis_index("row"), lax.axis_index(GROUP), base_ref[0]
    peers, cap, strip, order = left_ref.shape
    tall_strip = right_refs[0].shape[1]
    line = (own >> 3) * pl.cdiv(cap, SLOT_PITCH)
    lane = (own & (PER_GROUP - 1)) * SLOT_PITCH
    todo = jnp.clip(counts[own >> 3, lane] - base, 0, cap)
    most = right_refs[0][cap, 0:8, :]
    for right_ref in right_refs[1:]:
        most = jnp.maximum(most, right_ref[cap, 0:8, :])
    most_ref[...] = most.astype(jnp.int32)
    bf16 = jnp.bfloat16

    def product(at, half):
        for peer in range(peers):
            left[half, peer * strip:(peer + 1) * strip, :] = left_ref[peer, at]
        for away, right_ref in enumerate(right_refs):
            start = pl.multiple_of((row_index + rows - away) % rows * tall_strip, tall_strip)
            right[half, pl.ds(start, tall_strip), :] = right_ref[at]
        a, b = left[half], right[half]
        a_high, b_high = a.astype(bf16), b.astype(bf16)
        a_low = (a - a_high.astype(jnp.float32)).astype(bf16)
        b_low = (b - b_high.astype(jnp.float32)).astype(bf16)
        both = jnp.concatenate([b_high, b_low], axis=1)
        sums = jnp.dot(
            jnp.concatenate([a_high, a_low], axis=1),
            jnp.concatenate([both, both], axis=0),
            preferred_element_type=jnp.float32,
        )
        return sums[:, :order] + sums[:, order:]

    def target(at):
        return codes[line + (at >> 4), lane + (at & (SLOT_PITCH - 1))] >> 16

    def two(pair, carry):
        at = 2 * pair
        one, other = product(at, 0), product(at + 1, 1)
        out_ref[target(at)] += one

        @pl.when(at + 1 < todo)
        def _():
            out_ref[target(at + 1)] += other

        return carry

    lax.fori_loop(0, (todo + 1) >> 1, two, 0)


def multiply_round(left, right, codes, counts, base, running, kept):
    order = left.shape[-1]
    first = running is None
    tiles = (kept, order, order)
    operands = [pltpu.with_memory_space_constraint(left, pltpu.VMEM), *right] + ([] if first else [running])
    return pl.pallas_call(
        functools.partial(product_body, first, len(right)),
        grid_spec=pltpu.PrefetchScalarGridSpec(
            num_scalar_prefetch=3,
            grid=(1,),
            in_specs=[whole(operand.shape) for operand in operands],
            out_specs=[whole(tiles), whole((8, LANES))],
            scratch_shapes=[pltpu.VMEM((2, order, order), jnp.float32)] * 2,
        ),
        out_shape=[jax.ShapeDtypeStruct(tiles, jnp.float32), jax.ShapeDtypeStruct((8, LANES), jnp.int32)],
        compiler_params=LIMIT,
    )(base.reshape(1), codes, counts, *operands)


def shift_all(pieces):
    rows = len(pieces)
    return [pieces[0]] + [
        lax.ppermute(pieces[by], "row", [(i, (i + by) % rows) for i in range(rows)]) for by in range(1, rows)
    ]


def swap_rows(array, rows, by):
    return lax.ppermute(array, "row", [(i, i ^ by) for i in range(rows)])


def local(tile_values, tile_rows, tile_cols, tile_counts, out_rows, out_cols):
    order = tile_values.shape[-1]
    kept = out_rows.shape[-1]
    rows = lax.axis_size("row")
    peers = lax.axis_size(GROUP)
    tiles = tile_values.reshape(-1, order, order)

    listed, wanted = label(tile_rows, tile_cols, tile_counts, out_rows, out_cols)
    for by in (1, 2):
        listed = listed + swap_rows(listed, rows, by)
    strips, mates = stamp(listed, swap_rows(listed, rows, 4), wanted, pack(tiles, peers))
    pieces = shift_all(pack_right(tiles, rows))
    strips = lax.all_to_all(strips, GROUP, 0, 0, tiled=True)
    strips, pieces = lax.optimization_barrier((strips, pieces))
    strips = strips.reshape(-1, order // peers, order)

    def one_round(base, running):
        send, codes, counts, peak = plan(strips, mates, base, rows, peers, ROUND_CAP)
        left = lax.all_to_all(send, GROUP, 0, 0, tiled=True)
        right = shift_all(collect(codes, peak, pieces, peers, ROUND_CAP))
        return multiply_round(left, right, codes, counts, base, running, kept)

    summed, most = one_round(jnp.zeros((), jnp.int32), None)

    def unfinished(state):
        return state[0] < most[0, 0]

    def further(state):
        return state[0] + ROUND_CAP, one_round(*state)[0]

    unused, summed = lax.while_loop(unfinished, further, (jnp.int32(ROUND_CAP), summed))
    return summed.reshape(1, 1, kept, order, order)


def solution(mesh):
    in_specs = (
        P("row", GROUP, None, None, None, None),
        P("row", GROUP, None, None),
        P("row", GROUP, None, None),
        P("row", GROUP, None),
        P("row", "col", None, None),
        P("row", "col", None, None),
    )
    out_specs = P("row", GROUP, None, None, None)
    return jax.shard_map(local, mesh=mesh, in_specs=in_specs, out_specs=out_specs, check_vma=False)
```

time: 106 us -> 96.1 us (0.907)
  starting transfers between devices: 51.9 us -> 40.7 us
  waiting for transfers between devices: 25.8 us -> 34.1 us
  local copies, waits for them, and re-layouts: 5.44 us -> 1.2 us
  between operations: 2.71 us -> 0.25 us
  other arithmetic: 1.38 us -> 0.01 us
    ppermute x6 -> x3, starting transfers between devices: 16.1 us -> 4.86 us  [swap_rows(): return lax.ppermute(array, 'row', [(i, i ^ by) for i in range(rows)])]
    all_to_all x1, waiting for transfers between devices: 0.01 us -> 9.68 us  [one_round(): left = lax.all_to_all(send, GROUP, 0, 0, tiled=True)]
    unnamed x16 -> x0, local copies, waits for them, and re-layouts: 5.44 us -> none
    pallas_call x1, Pallas kernels: 10.8 us -> 5.99 us  [plan(): pl.pallas_call(functools.partial(plan_body, rows), grid_spec=pltpu.Prefet...]
    pallas_call x2 -> x4, Pallas kernels: 2.56 us -> 6.81 us  [the longest x1 3.09 us: collect(): pl.pallas_call(functools.partial(collect_body, rows, peers // PER_GROUP *...]
    ppermute x6 -> x3, waiting for transfers between devices: 6.05 us -> 3.15 us  [swap_rows(): return lax.ppermute(array, 'row', [(i, i ^ by) for i in range(rows)])]
    ppermute x14, waiting for transfers between devices: 12.1 us -> 14.1 us  [shift_all(): lax.ppermute(pieces[by], 'row', [(i, (i + by) % rows) for i in range(rows)])]
    pallas_call x1, Pallas kernels: 0.07 us -> 1.84 us  [pack_right(): pl.pallas_call(pack_right_body, out_shape=[jax.ShapeDtypeStruct(shape, jn...]
  transfers between devices with their start and end apart: 22 -> 19, of which waited for: 10 -> 14; matrix products, arithmetic and copies ran while one was open for 1% -> 0% of each run, Pallas kernels for 0% -> 7%
where the time goes in v3:
time: 96.1 us; the launch traced here: 95.6 us
  starting transfers between devices  40.7 us (42%)
  waiting for transfers between devices  34.1 us (35%)
  Pallas kernels  18.7 us (19%)
  local copies, waits for them, and re-layouts  1.2 us (1%)
    ppermute x14, starting transfers between devices, shift_all(): lax.ppermute(pieces[by], 'row', [(i, (i + by) % rows) for i in range(rows)])  18.5 us
    ppermute x14, waiting for transfers between devices, shift_all(): lax.ppermute(pieces[by], 'row', [(i, (i + by) % rows) for i in range(rows)])  14.1 us
    all_to_all x1, starting transfers between devices, local(): strips = lax.all_to_all(strips, GROUP, 0, 0, tiled=True)  11.6 us
    all_to_all x1, waiting for transfers between devices, one_round(): left = lax.all_to_all(send, GROUP, 0, 0, tiled=True)  9.68 us
    all_to_all x1, waiting for transfers between devices, local(): strips = lax.all_to_all(strips, GROUP, 0, 0, tiled=True)  7.14 us
    pallas_call x1, Pallas kernels, plan(): pl.pallas_call(functools.partial(plan_body, rows), grid_spec=pltpu.Prefet...  5.99 us
    all_to_all x1, starting transfers between devices, one_round(): left = lax.all_to_all(send, GROUP, 0, 0, tiled=True)  5.71 us
    ppermute x3, starting transfers between devices, swap_rows(): return lax.ppermute(array, 'row', [(i, i ^ by) for i in range(rows)])  4.86 us
  transfers between devices with their start and end apart: 19, of which 14 were waited for; matrix products, arithmetic and copies ran while one was open for 0% of the time, Pallas kernels for 7%

profile of v3, /device:TPU:4, one launch (start us, length us, event | category | flops | bytes accessed | tf_op | source)
XLA Modules:
  0.0 95.6 jit_solution(4028180062726838754)
XLA Ops:
  2.1 1.6 %collective-permute-start.8 = (f32[4,128]{1,0:T(4,128)S(1)}, f32[4,128]{1,0:T(4,128)S(1)}, u32[]{:S(2)}, u32[]{:S(2)}) collective-permute-start(f32[4,128]{1,0:T(4,128)S(1)} %add.9), channel_id=1, source_target_pairs={{0,64},{32,96},{64,0},{96,32},{128,192},{160,224},{192,128},{224,1... | collective-permute-start | bytes 6152 | tf_op jit(solution)/shard_map/ppermute | solution.py:415
  3.7 2.0 %collective-permute-done.8 = f32[4,128]{1,0:T(4,128)S(1)} collective-permute-done((f32[4,128]{1,0:T(4,128)S(1)}, f32[4,128]{1,0:T(4,128)S(1)}, u32[]{:S(2)}, u32[]{:S(2)}) %collective-permute-start.8) | collective-permute-done | bytes 2080 | tf_op jit(solution)/shard_map/ppermute | solution.py:415
  5.7 3.2 %collective-permute-start.9 = (f32[4,128]{1,0:T(4,128)S(1)}, f32[4,128]{1,0:T(4,128)S(1)}, u32[]{:S(2)}, u32[]{:S(2)}) collective-permute-start(f32[4,128]{1,0:T(4,128)S(1)} %add.10.one_ref), channel_id=1, source_target_pairs={{0,128},{32,160},{64,192},{96,224},{128,0},{160,32},{192,64},{224,... | collective-permute-start | bytes 6152 | tf_op jit(solution)/shard_map/ppermute | solution.py:415
  8.9 2.2 %shard_map.65.strips_in = f32[32,13,4,128]{3,2,1,0:T(4,128)} custom-call(f32[12,128,128]{2,1,0:T(8,128)} %bitcast.10), custom_call_target="tpu_custom_call" | custom-call | tf_op jit(solution)/shard_map/pallas_call | solution.py:88
  11.8 11.6 %all-to-all-start.1 = ((f32[32,13,4,128]{3,2,1,0:T(4,128)}), f32[32,13,4,128]{3,2,1,0:T(4,128)S(1)}, u32[]{:S(2)}, u32[]{:S(2)}) async-start(f32[32,13,4,128]{3,2,1,0:T(4,128)} %get-tuple-element.123), calls=%async_computation.1 | async-start | bytes 1703936 | tf_op jit(solution)/shard_map/all_to_all | solution.py:430
  23.4 1.8 %shard_map.67 = (f32[12,16,128]{2,1,0:T(8,128)}, f32[12,16,128]{2,1,0:T(8,128)S(1)}, f32[12,16,128]{2,1,0:T(8,128)S(1)}, f32[12,16,128]{2,1,0:T(8,128)S(1)}, f32...) custom-call(f32[12,128,128]{2,1,0:T(8,128)} %bitcast.11), custom_call_target="tpu_custom_call" | custom-call | tf_op jit(solution)/shard_map/pallas_call | solution.py:135
  26.5 2.3 %collective-permute-start.12 = (f32[12,16,128]{2,1,0:T(8,128)S(1)}, f32[12,16,128]{2,1,0:T(8,128)}, u32[]{:S(2)}, u32[]{:S(2)}) collective-permute-start(f32[12,16,128]{2,1,0:T(8,128)S(1)} %get-tuple-element.127), channel_id=1, source_target_pairs={{0,96},{32,128},{64,160},{96,192},{128,224},{160,0},{192,32},{224,... | collective-permute-start | bytes 294920 | tf_op jit(solution)/shard_map/ppermute | solution.py:410
  28.8 1.8 %collective-permute-start.13 = (f32[12,16,128]{2,1,0:T(8,128)S(1)}, f32[12,16,128]{2,1,0:T(8,128)}, u32[]{:S(2)}, u32[]{:S(2)}) collective-permute-start(f32[12,16,128]{2,1,0:T(8,128)S(1)} %get-tuple-element.128), channel_id=1, source_target_pairs={{0,128},{32,160},{64,192},{96,224},{128,0},{160,32},{192,64},{224,... | collective-permute-start | bytes 294920 | tf_op jit(solution)/shard_map/ppermute | solution.py:410
  30.6 1.8 %collective-permute-start.14 = (f32[12,16,128]{2,1,0:T(8,128)S(1)}, f32[12,16,128]{2,1,0:T(8,128)}, u32[]{:S(2)}, u32[]{:S(2)}) collective-permute-start(f32[12,16,128]{2,1,0:T(8,128)S(1)} %get-tuple-element.129), channel_id=1, source_target_pairs={{0,160},{32,192},{64,224},{96,0},{128,32},{160,64},{192,96},{224,1... | collective-permute-start | bytes 294920 | tf_op jit(solution)/shard_map/ppermute | solution.py:410
  34.3 1.9 %collective-permute-done.12.refs_3_ = f32[12,16,128]{2,1,0:T(8,128)} collective-permute-done((f32[12,16,128]{2,1,0:T(8,128)S(1)}, f32[12,16,128]{2,1,0:T(8,128)}, u32[]{:S(2)}, u32[]{:S(2)}) %collective-permute-start.12) | collective-permute-done | bytes 98336 | tf_op jit(solution)/shard_map/ppermute | solution.py:410
  37.3 1.4 %collective-permute-done.15.refs_6_ = f32[12,16,128]{2,1,0:T(8,128)} collective-permute-done((f32[12,16,128]{2,1,0:T(8,128)S(1)}, f32[12,16,128]{2,1,0:T(8,128)}, u32[]{:S(2)}, u32[]{:S(2)}) %collective-permute-start.15) | collective-permute-done | bytes 98336 | tf_op jit(solution)/shard_map/ppermute | solution.py:410
  38.8 7.1 %all-to-all-done.1 = f32[32,13,4,128]{3,2,1,0:T(4,128)S(1)} async-done(((f32[32,13,4,128]{3,2,1,0:T(4,128)}), f32[32,13,4,128]{3,2,1,0:T(4,128)S(1)}, u32[]{:S(2)}, u32[]{:S(2)}) %all-to-all-start.1) | async-done | bytes 852000 | tf_op jit(solution)/shard_map/all_to_all | solution.py:430
  45.9 6.0 %shard_map.68 = (f32[32,20,4,128]{3,2,1,0:T(4,128)}, s32[16,128]{1,0:T(8,128)S(1)}, s32[8,128]{1,0:T(8,128)S(1)}, f32[8,128]{1,0:T(8,128)S(1)}) custom-call(s32[1]{0:T(128)} %constant.2.clone.1.base_ref, f32[416,4,128]{2,1,0:T(4,128)S(1)} %bitcast.8, f32[4,128]{1,0:T(4,128)S(1)} %get-tuple-element.293.mates_ref), custom_call_target="tpu_custom_call" | custom-call | tf_op jit(solution)/shard_map/pallas_call | solution.py:274
  51.9 5.7 %all-to-all-start.2 = ((f32[32,20,4,128]{3,2,1,0:T(4,128)}), f32[32,20,4,128]{3,2,1,0:T(4,128)S(1)}, u32[]{:S(2)}, u32[]{:S(2)}) async-start(f32[32,20,4,128]{3,2,1,0:T(4,128)} %get-tuple-element.136), calls=%async_computation.2 | async-start | bytes 2621440 | tf_op jit(solution)/shard_map/all_to_all | solution.py:436
  57.6 3.1 %shard_map.69 = (f32[21,16,128]{2,1,0:T(8,128)S(1)}, f32[21,16,128]{2,1,0:T(8,128)S(1)}, f32[21,16,128]{2,1,0:T(8,128)S(1)}, f32[21,16,128]{2,1,0:T(8,128)}, f32...) custom-call(s32[16,128]{1,0:T(8,128)S(1)} %get-tuple-element.134.codes, ...), custom_call_target="tpu_custom_call" | custom-call | tf_op jit(solution)/shard_map/pallas_call | solution.py:319
  61.4 1.8 %collective-permute-start.19 = (f32[21,16,128]{2,1,0:T(8,128)}, f32[21,16,128]{2,1,0:T(8,128)S(1)}, u32[]{:S(2)}, u32[]{:S(2)}) collective-permute-start(f32[21,16,128]{2,1,0:T(8,128)} %get-tuple-element.149), channel_id=1, source_target_pairs={{0,96},{32,128},{64,160},{96,192},{128,224},{160,0},{192,32},{224,... | collective-permute-start | bytes 516104 | tf_op jit(solution)/shard_map/ppermute | solution.py:410
  63.3 2.2 %collective-permute-start.20 = (f32[21,16,128]{2,1,0:T(8,128)}, f32[21,16,128]{2,1,0:T(8,128)S(1)}, u32[]{:S(2)}, u32[]{:S(2)}) collective-permute-start(f32[21,16,128]{2,1,0:T(8,128)} %get-tuple-element.150), channel_id=1, source_target_pairs={{0,128},{32,160},{64,192},{96,224},{128,0},{160,32},{192,64},{224,... | collective-permute-start | bytes 516104 | tf_op jit(solution)/shard_map/ppermute | solution.py:410
  65.5 1.4 %collective-permute-start.21 = (f32[21,16,128]{2,1,0:T(8,128)}, f32[21,16,128]{2,1,0:T(8,128)S(1)}, u32[]{:S(2)}, u32[]{:S(2)}) collective-permute-start(f32[21,16,128]{2,1,0:T(8,128)} %get-tuple-element.151), channel_id=1, source_target_pairs={{0,160},{32,192},{64,224},{96,0},{128,32},{160,64},{192,96},{224,1... | collective-permute-start | bytes 516104 | tf_op jit(solution)/shard_map/ppermute | solution.py:410
  69.2 2.8 %collective-permute-start.23 = (f32[21,16,128]{2,1,0:T(8,128)}, f32[21,16,128]{2,1,0:T(8,128)}, u32[]{:S(2)}, u32[]{:S(2)}) collective-permute-start(f32[21,16,128]{2,1,0:T(8,128)} %get-tuple-element.153), channel_id=1, source_target_pairs={{0,224},{32,0},{64,32},{96,64},{128,96},{160,128},{192,160},{224,1... | collective-permute-start | bytes 516104 | tf_op jit(solution)/shard_map/ppermute | solution.py:410
  71.9 3.5 %collective-permute-done.19.refs_3_ = f32[21,16,128]{2,1,0:T(8,128)S(1)} collective-permute-done((f32[21,16,128]{2,1,0:T(8,128)}, f32[21,16,128]{2,1,0:T(8,128)S(1)}, u32[]{:S(2)}, u32[]{:S(2)}) %collective-permute-start.19) | collective-permute-done | bytes 172064 | tf_op jit(solution)/shard_map/ppermute | solution.py:410
  76.7 2.2 %collective-permute-done.22.refs_6_ = f32[21,16,128]{2,1,0:T(8,128)S(1)} collective-permute-done((f32[21,16,128]{2,1,0:T(8,128)}, f32[21,16,128]{2,1,0:T(8,128)S(1)}, u32[]{:S(2)}, u32[]{:S(2)}) %collective-permute-start.22) | collective-permute-done | bytes 172064 | tf_op jit(solution)/shard_map/ppermute | solution.py:410
  79.8 9.7 %all-to-all-done.2.left_ref = f32[32,20,4,128]{3,2,1,0:T(4,128)S(1)} async-done(((f32[32,20,4,128]{3,2,1,0:T(4,128)}), f32[32,20,4,128]{3,2,1,0:T(4,128)S(1)}, u32[]{:S(2)}, u32[]{:S(2)}) %all-to-all-start.2) | async-done | bytes 1310752 | tf_op jit(solution)/shard_map/all_to_all | solution.py:436
  89.5 4.1 %shard_map.70 = (f32[12,128,128]{2,1,0:T(8,128)}, s32[8,128]{1,0:T(8,128)}) custom-call(s32[1]{0:T(128)} %constant.2.clone.1.base_ref, s32[16,128]{1,0:T(8,128)S(1)} %get-tuple-element.134.codes, s32[8,128]{1,0:T(8,128)S(1)} %get-tuple-element.135.counts, f32[32,20,4,128]{3,2,1,0:T(4,128)S(1)} %all-to-all-done.2.left_ref, ...), custom_call_target="tpu_custom_call" | custom-call | tf_op jit(solution)/shard_map/pallas_call | solution.py:393
  93.6 1.8 %while.10 = (s32[]{:T(128)}, f32[12,128,128]{2,1,0:T(8,128)}, s32[8,128]{1,0:T(8,128)}, f32[416,4,128]{2,1,0:T(4,128)S(1)}, f32[4,128]{1,0:T(4,128)S(1)}, /*inde...) while((s32[]{:T(128)}, f32[12,128,128]{2,1,0:T(8,128)}, ...), condition=%wide.region_1.0_spmd, body=%wide.region_0.0_spmd.sunk | while | flops 2 | bytes 10322381 | solution.py:448
  (25 shorter events, 13.5 us)
Async XLA Ops:
  0.9 1.2 %collective-permute-start.7 = (f32[4,128]{1,0:T(4,128)S(1)}, f32[4,128]{1,0:T(4,128)S(1)}, u32[]{:S(2)}, u32[]{:S(2)}) collective-permute-start(f32[4,128]{1,0:T(4,128)S(1)} %get-tuple-element.121), channel_id=1, source_target_pairs={{0,32},{32,0},{64,96},{96,64},{128,160},{160,128},{192,224},{224,1... | collective-permute-start | bytes 6152 | tf_op jit(solution)/shard_map/ppermute | solution.py:415
  2.1 3.6 %collective-permute-start.8 = (f32[4,128]{1,0:T(4,128)S(1)}, f32[4,128]{1,0:T(4,128)S(1)}, u32[]{:S(2)}, u32[]{:S(2)}) collective-permute-start(f32[4,128]{1,0:T(4,128)S(1)} %add.9), channel_id=1, source_target_pairs={{0,64},{32,96},{64,0},{96,32},{128,192},{160,224},{192,128},{224,1... | collective-permute-start | bytes 6152 | tf_op jit(solution)/shard_map/ppermute | solution.py:415
  5.7 5.4 %collective-permute-start.9 = (f32[4,128]{1,0:T(4,128)S(1)}, f32[4,128]{1,0:T(4,128)S(1)}, u32[]{:S(2)}, u32[]{:S(2)}) collective-permute-start(f32[4,128]{1,0:T(4,128)S(1)} %add.10.one_ref), channel_id=1, source_target_pairs={{0,128},{32,160},{64,192},{96,224},{128,0},{160,32},{192,64},{224,... | collective-permute-start | bytes 6152 | tf_op jit(solution)/shard_map/ppermute | solution.py:415
  11.8 34.1 %all-to-all-start.1 = ((f32[32,13,4,128]{3,2,1,0:T(4,128)}), f32[32,13,4,128]{3,2,1,0:T(4,128)S(1)}, u32[]{:S(2)}, u32[]{:S(2)}) async-start(f32[32,13,4,128]{3,2,1,0:T(4,128)} %get-tuple-element.123), calls=%async_computation.1 | async-start | bytes 1703936 | tf_op jit(solution)/shard_map/all_to_all | solution.py:430
  25.2 7.2 %collective-permute-start.10 = (f32[12,16,128]{2,1,0:T(8,128)S(1)}, f32[12,16,128]{2,1,0:T(8,128)}, u32[]{:S(2)}, u32[]{:S(2)}) collective-permute-start(f32[12,16,128]{2,1,0:T(8,128)S(1)} %get-tuple-element.125), channel_id=1, source_target_pairs={{0,32},{32,64},{64,96},{96,128},{128,160},{160,192},{192,224},{224... | collective-permute-start | bytes 294920 | tf_op jit(solution)/shard_map/ppermute | solution.py:410
  25.2 8.5 %collective-permute-start.11 = (f32[12,16,128]{2,1,0:T(8,128)S(1)}, f32[12,16,128]{2,1,0:T(8,128)}, u32[]{:S(2)}, u32[]{:S(2)}) collective-permute-start(f32[12,16,128]{2,1,0:T(8,128)S(1)} %get-tuple-element.126), channel_id=1, source_target_pairs={{0,64},{32,96},{64,128},{96,160},{128,192},{160,224},{192,0},{224,... | collective-permute-start | bytes 294920 | tf_op jit(solution)/shard_map/ppermute | solution.py:410
  26.5 9.7 %collective-permute-start.12 = (f32[12,16,128]{2,1,0:T(8,128)S(1)}, f32[12,16,128]{2,1,0:T(8,128)}, u32[]{:S(2)}, u32[]{:S(2)}) collective-permute-start(f32[12,16,128]{2,1,0:T(8,128)S(1)} %get-tuple-element.127), channel_id=1, source_target_pairs={{0,96},{32,128},{64,160},{96,192},{128,224},{160,0},{192,32},{224,... | collective-permute-start | bytes 294920 | tf_op jit(solution)/shard_map/ppermute | solution.py:410
  28.8 8.5 %collective-permute-start.13 = (f32[12,16,128]{2,1,0:T(8,128)S(1)}, f32[12,16,128]{2,1,0:T(8,128)}, u32[]{:S(2)}, u32[]{:S(2)}) collective-permute-start(f32[12,16,128]{2,1,0:T(8,128)S(1)} %get-tuple-element.128), channel_id=1, source_target_pairs={{0,128},{32,160},{64,192},{96,224},{128,0},{160,32},{192,64},{224,... | collective-permute-start | bytes 294920 | tf_op jit(solution)/shard_map/ppermute | solution.py:410
  30.6 6.7 %collective-permute-start.14 = (f32[12,16,128]{2,1,0:T(8,128)S(1)}, f32[12,16,128]{2,1,0:T(8,128)}, u32[]{:S(2)}, u32[]{:S(2)}) collective-permute-start(f32[12,16,128]{2,1,0:T(8,128)S(1)} %get-tuple-element.129), channel_id=1, source_target_pairs={{0,160},{32,192},{64,224},{96,0},{128,32},{160,64},{192,96},{224,1... | collective-permute-start | bytes 294920 | tf_op jit(solution)/shard_map/ppermute | solution.py:410
  32.4 6.3 %collective-permute-start.15 = (f32[12,16,128]{2,1,0:T(8,128)S(1)}, f32[12,16,128]{2,1,0:T(8,128)}, u32[]{:S(2)}, u32[]{:S(2)}) collective-permute-start(f32[12,16,128]{2,1,0:T(8,128)S(1)} %get-tuple-element.130), channel_id=1, source_target_pairs={{0,192},{32,224},{64,0},{96,32},{128,64},{160,96},{192,128},{224,1... | collective-permute-start | bytes 294920 | tf_op jit(solution)/shard_map/ppermute | solution.py:410
  33.8 5.0 %collective-permute-start.16 = (f32[12,16,128]{2,1,0:T(8,128)S(1)}, f32[12,16,128]{2,1,0:T(8,128)}, u32[]{:S(2)}, u32[]{:S(2)}) collective-permute-start(f32[12,16,128]{2,1,0:T(8,128)S(1)} %get-tuple-element.131), channel_id=1, source_target_pairs={{0,224},{32,0},{64,32},{96,64},{128,96},{160,128},{192,160},{224,1... | collective-permute-start | bytes 294920 | tf_op jit(solution)/shard_map/ppermute | solution.py:410
  51.9 37.6 %all-to-all-start.2 = ((f32[32,20,4,128]{3,2,1,0:T(4,128)}), f32[32,20,4,128]{3,2,1,0:T(4,128)S(1)}, u32[]{:S(2)}, u32[]{:S(2)}) async-start(f32[32,20,4,128]{3,2,1,0:T(4,128)} %get-tuple-element.136), calls=%async_computation.2 | async-start | bytes 2621440 | tf_op jit(solution)/shard_map/all_to_all | solution.py:436
  60.7 7.3 %collective-permute-start.17 = (f32[21,16,128]{2,1,0:T(8,128)S(1)}, f32[21,16,128]{2,1,0:T(8,128)S(1)}, u32[]{:S(2)}, u32[]{:S(2)}) collective-permute-start(f32[21,16,128]{2,1,0:T(8,128)S(1)} %get-tuple-element.147), channel_id=1, source_target_pairs={{0,32},{32,64},{64,96},{96,128},{128,160},{160,192},{192,224},{224... | collective-permute-start | bytes 516104 | tf_op jit(solution)/shard_map/ppermute | solution.py:410
  60.7 8.4 %collective-permute-start.18 = (f32[21,16,128]{2,1,0:T(8,128)S(1)}, f32[21,16,128]{2,1,0:T(8,128)S(1)}, u32[]{:S(2)}, u32[]{:S(2)}) collective-permute-start(f32[21,16,128]{2,1,0:T(8,128)S(1)} %get-tuple-element.148), channel_id=1, source_target_pairs={{0,64},{32,96},{64,128},{96,160},{128,192},{160,224},{192,0},{224,... | collective-permute-start | bytes 516104 | tf_op jit(solution)/shard_map/ppermute | solution.py:410
  61.4 14.0 %collective-permute-start.19 = (f32[21,16,128]{2,1,0:T(8,128)}, f32[21,16,128]{2,1,0:T(8,128)S(1)}, u32[]{:S(2)}, u32[]{:S(2)}) collective-permute-start(f32[21,16,128]{2,1,0:T(8,128)} %get-tuple-element.149), channel_id=1, source_target_pairs={{0,96},{32,128},{64,160},{96,192},{128,224},{160,0},{192,32},{224,... | collective-permute-start | bytes 516104 | tf_op jit(solution)/shard_map/ppermute | solution.py:410
  63.3 13.2 %collective-permute-start.20 = (f32[21,16,128]{2,1,0:T(8,128)}, f32[21,16,128]{2,1,0:T(8,128)S(1)}, u32[]{:S(2)}, u32[]{:S(2)}) collective-permute-start(f32[21,16,128]{2,1,0:T(8,128)} %get-tuple-element.150), channel_id=1, source_target_pairs={{0,128},{32,160},{64,192},{96,224},{128,0},{160,32},{192,64},{224,... | collective-permute-start | bytes 516104 | tf_op jit(solution)/shard_map/ppermute | solution.py:410
  65.5 11.2 %collective-permute-start.21 = (f32[21,16,128]{2,1,0:T(8,128)}, f32[21,16,128]{2,1,0:T(8,128)S(1)}, u32[]{:S(2)}, u32[]{:S(2)}) collective-permute-start(f32[21,16,128]{2,1,0:T(8,128)} %get-tuple-element.151), channel_id=1, source_target_pairs={{0,160},{32,192},{64,224},{96,0},{128,32},{160,64},{192,96},{224,1... | collective-permute-start | bytes 516104 | tf_op jit(solution)/shard_map/ppermute | solution.py:410
  68.0 10.9 %collective-permute-start.22 = (f32[21,16,128]{2,1,0:T(8,128)}, f32[21,16,128]{2,1,0:T(8,128)S(1)}, u32[]{:S(2)}, u32[]{:S(2)}) collective-permute-start(f32[21,16,128]{2,1,0:T(8,128)} %get-tuple-element.152), channel_id=1, source_target_pairs={{0,192},{32,224},{64,0},{96,32},{128,64},{160,96},{192,128},{224,1... | collective-permute-start | bytes 516104 | tf_op jit(solution)/shard_map/ppermute | solution.py:410
  69.2 10.7 %collective-permute-start.23 = (f32[21,16,128]{2,1,0:T(8,128)}, f32[21,16,128]{2,1,0:T(8,128)}, u32[]{:S(2)}, u32[]{:S(2)}) collective-permute-start(f32[21,16,128]{2,1,0:T(8,128)} %get-tuple-element.153), channel_id=1, source_target_pairs={{0,224},{32,0},{64,32},{96,64},{128,96},{160,128},{192,160},{224,1... | collective-permute-start | bytes 516104 | tf_op jit(solution)/shard_map/ppermute | solution.py:410

commit v4 on v3

--- a/solution.py
+++ b/solution.py
@@ -14,6 +14,15 @@
 ROUND_CAP = 20
 LIMIT = pltpu.CompilerParams(vmem_limit_bytes=20 * 2**20)
 HBM = pl.BlockSpec(memory_space=pltpu.HBM)
+
+
+NEAR, FAR = 4, 8
+
+
+def away_from(peer, near, far):
+    x = (((peer >> 1) & 3) + NEAR - near) & 3
+    z = (((peer >> 3) * 2 + (peer & 1)) + FAR - far) & 7
+    return ((z >> 1) << 3) + (x << 1) + (z & 1)
 
 
 def in_hbm(*arrays):
@@ -70,7 +79,7 @@
 
 def pack_body(tiles_hbm, out_ref, tiles, sems):
     peers, per_peer, strip, _ = out_ref.shape
-    for tile in range(per_peer - 1):
+    for tile in range(per_peer):
         pltpu.make_async_copy(tiles_hbm.at[tile], tiles.at[tile], sems.at[tile]).start()
 
     def one_tile(tile, carry):
@@ -79,12 +88,12 @@
             out_ref[peer, tile] = tiles[tile, peer * strip:(peer + 1) * strip, :]
         return carry
 
-    lax.fori_loop(0, per_peer - 1, one_tile, 0)
+    lax.fori_loop(0, per_peer, one_tile, 0)
 
 
 def pack(tiles, peers):
     count, order = tiles.shape[:2]
-    shape = (peers, count + 1, order // peers, order)
+    shape = (peers, count, order // peers, order)
     return pl.pallas_call(
         pack_body,
         in_specs=[HBM],
@@ -94,30 +103,22 @@
     )(*in_hbm(tiles))
 
 
-def stamp_body(one_ref, other_ref, wanted_ref, strips_in, strips_out, total_ref, meta, sem):
-    peers, per_peer = strips_out.shape[:2]
-    total = one_ref[...] + other_ref[...]
-    total_ref[...] = total
-    full = jnp.concatenate([total[0:2, :], wanted_ref[...]])
-    for peer in range(peers):
-        meta[peer] = full
-    copy = pltpu.make_async_copy(meta, strips_out.at[:, per_peer - 1], sem)
-    copy.start()
-    copy.wait()
-
-
-def stamp(one, other, wanted, strips):
-    peers, _, strip, order = strips.shape
-    vmem = pl.BlockSpec(memory_space=pltpu.VMEM)
-    return pl.pallas_call(
-        stamp_body,
-        in_specs=[vmem, vmem, vmem, HBM],
-        out_specs=[HBM, vmem],
-        out_shape=[pltpu.HBM(strips.shape, jnp.float32), jax.ShapeDtypeStruct(one.shape, jnp.float32)],
-        input_output_aliases={3: 0},
-        scratch_shapes=[pltpu.VMEM((peers, strip, order), jnp.float32), pltpu.SemaphoreType.DMA],
-        compiler_params=LIMIT,
-    )(one, other, wanted, *in_hbm(strips))
+def merge_body(*refs):
+    listed_refs, wanted_ref, meta_ref, mates_ref = refs[:-3], *refs[-3:]
+    total = listed_refs[0][...]
+    for listed_ref in listed_refs[1:]:
+        total = total + listed_ref[...]
+    meta_ref[0:2, :] = total[0:2, :]
+    meta_ref[2:4, :] = wanted_ref[...]
+    mates_ref[...] = total[2:4, :]
+
+
+def merge(listed, wanted):
+    return pl.pallas_call(
+        merge_body,
+        out_shape=[jax.ShapeDtypeStruct((n, LANES), jnp.float32) for n in (4, 2)],
+        compiler_params=LIMIT,
+    )(*listed, wanted)
 
 
 def pack_right_body(tiles_ref, *out_refs):
@@ -137,14 +138,10 @@
     )(*in_hbm(tiles))
 
 
-def plan_body(
-    rows, base_ref, strips_ref, mates_ref,
-    send_ref, codes_ref, counts_ref, peak_ref,
-    table, values, keys, picks, places_vmem, send, places, sem, send_sems,
-):
-    row_index, base = lax.axis_index("row"), base_ref[0]
-    peers, cap = send_ref.shape[:2]
-    per_peer = strips_ref.shape[0] // peers
+def plan_body(rows, peers, per_peer, cap, base_ref, *refs):
+    meta_refs, mates_ref = refs[:FAR], refs[FAR]
+    codes_ref, places_ref, counts_ref, peak_ref, table, wanted, values, keys, picks = refs[FAR + 1:]
+    row_index, own, base = lax.axis_index("row"), lax.axis_index(GROUP), base_ref[0]
     band = 8
     blocks = peers * band
     band_rows = blocks // rows
@@ -162,19 +159,18 @@
     band_mask = band_mask.astype(bf16)
     short = iota((band, LANES), 0).astype(f32) + 1.0
     names = iota((band, LANES), 1).astype(f32) + 1.0
-    targets = []
-    for peer in range(peers):
-        meta = strips_ref[peer * per_peer + per_peer - 1]
-        row_hot = jnp.where(in_band == meta[0:1, :] - band_start, 1.0, 0.0).astype(bf16)
-        row_hot = jnp.concatenate([row_hot] * rows, axis=0) * band_mask
-        col_hot = jnp.where(short + float(peer * band) == meta[1:2, :], names, 0.0).astype(bf16)
-        table[peer * band:(peer + 1) * band, :] = lax.dot_general(
-            col_hot, row_hot, (((1,), (1,)), ((), ())), preferred_element_type=f32
-        )
-        if peer % PER_GROUP == 0:
-            targets.append(meta)
-        else:
-            targets[-1] = targets[-1] + meta
+    wanted[...] = jnp.zeros_like(wanted)
+    for far in range(FAR):
+        for near in range(NEAR):
+            peer = away_from(own, near, far)
+            meta = meta_refs[far][near]
+            row_hot = jnp.where(in_band == meta[0:1, :] - band_start, 1.0, 0.0).astype(bf16)
+            row_hot = jnp.concatenate([row_hot] * rows, axis=0) * band_mask
+            col_hot = jnp.where(short + (peer * band).astype(f32) == meta[1:2, :], names, 0.0).astype(bf16)
+            table[pl.ds(pl.multiple_of(peer * band, band), band), :] = lax.dot_general(
+                col_hot, row_hot, (((1,), (1,)), ((), ())), preferred_element_type=f32
+            )
+            wanted[peer >> 3] = wanted[peer >> 3] + meta
     by_col = table[...]
     by_row = by_col.T.astype(bf16)
     by_col = by_col.astype(bf16)
@@ -187,8 +183,8 @@
     fixed = iota((blocks, LANES), 0) // band * per_peer + ((iota((blocks, LANES), 1) % SLOT_PITCH) << 16)
     fixed = (fixed - (SLOT_PITCH * row_index + 1 + 512)).astype(f32)
 
-    targets = [(meta[2:3, :], meta[3:4, :]) for meta in targets]
-    targets.append((mates_ref[2:3, :], mates_ref[3:4, :]))
+    targets = [(wanted[group, 2:3, :], wanted[group, 3:4, :]) for group in range(groups)]
+    targets.append((mates_ref[0:1, :], mates_ref[1:2, :]))
     everything = []
     for group, (target_rows, target_cols) in enumerate(targets):
         def hot(target):
@@ -205,7 +201,7 @@
             value = fixed + left + right * 512.0
         else:
             name = right.astype(jnp.int32) - 1
-            value = (name - (SLOT_PITCH - per_peer + 1) * (name >> 4)).astype(f32)
+            value = (name - (SLOT_PITCH - per_peer) * (name >> 4)).astype(f32)
         values[group * blocks:(group + 1) * blocks, :] = value
     found = jnp.concatenate(everything + everything[-1:] * (8 - len(everything)), axis=0)
     ahead = jnp.dot(found.astype(bf16), earlier, preferred_element_type=f32) - base.astype(f32)
@@ -237,14 +233,17 @@
     lines += lines[-1:] * (codes_ref.shape[0] - len(lines))
     codes = jnp.concatenate(lines, axis=0).astype(jnp.int32)
     codes_ref[...] = codes
-    places_vmem[...] = codes & 511
-    copy = pltpu.make_async_copy(places_vmem, places, sem)
-    copy.start()
-    copy.wait()
+    places_ref[...] = codes & 511
+
+
+def send_body(places, strips_ref, send_ref, send, sems):
+    peers, cap = send.shape[:2]
+    groups = peers // PER_GROUP
+    halves = pl.cdiv(cap, SLOT_PITCH)
 
     def one_group(group):
         part = pl.ds(group * PER_GROUP, PER_GROUP)
-        return pltpu.make_async_copy(send.at[part], send_ref.at[part], send_sems.at[group])
+        return pltpu.make_async_copy(send.at[part], send_ref.at[part], sems.at[group])
 
     def one_peer(peer, carry):
         line = (peer >> 3) * halves
@@ -264,35 +263,46 @@
     return pl.BlockSpec(shape, lambda i, *_: (0,) * len(shape))
 
 
-def plan(strips, mates, base, rows, peers, cap):
-    strip, order = strips.shape[1:]
+def plan(metas, mates, base, rows, peers, per_peer, cap):
     groups = peers // PER_GROUP
     lines = padded((groups + 1) * pl.cdiv(cap, SLOT_PITCH), 8)
-    send = (peers, cap, strip, order)
     blocks = peers * 8
-    shapes = [(send, jnp.float32), ((lines, LANES), jnp.int32), ((8, LANES), jnp.int32), ((8, LANES), jnp.float32)]
-    return pl.pallas_call(
-        functools.partial(plan_body, rows),
+    shapes = [((lines, LANES), jnp.int32)] * 2 + [((8, LANES), jnp.int32), ((8, LANES), jnp.float32)]
+    return pl.pallas_call(
+        functools.partial(plan_body, rows, peers, per_peer, cap),
         grid_spec=pltpu.PrefetchScalarGridSpec(
             num_scalar_prefetch=1,
             grid=(1,),
-            in_specs=[whole(strips.shape), whole(mates.shape)],
-            out_specs=[HBM] + [whole(shape) for shape, _ in shapes[1:]],
+            in_specs=[whole(operand.shape) for operand in (*metas, mates)],
+            out_specs=[whole(shape) for shape, _ in shapes],
             scratch_shapes=[
                 pltpu.VMEM((blocks, blocks), jnp.float32),
+                pltpu.VMEM((groups, 4, LANES), jnp.float32),
                 pltpu.VMEM(((groups + 1) * blocks, LANES), jnp.float32),
                 pltpu.VMEM(((groups + 1) * blocks, LANES), jnp.float32),
                 pltpu.VMEM(((groups + 1) * padded(cap, 8), LANES), jnp.float32),
-                pltpu.VMEM((lines, LANES), jnp.int32),
-                pltpu.VMEM(send, jnp.float32),
-                pltpu.SMEM((lines, LANES), jnp.int32),
-                pltpu.SemaphoreType.DMA,
-                pltpu.SemaphoreType.DMA((groups,)),
             ],
         ),
-        out_shape=[pltpu.HBM(*shapes[0])] + [jax.ShapeDtypeStruct(*shape) for shape in shapes[1:]],
-        compiler_params=LIMIT,
-    )(base.reshape(1), pltpu.with_memory_space_constraint(strips, pltpu.VMEM), mates)
+        out_shape=[jax.ShapeDtypeStruct(*shape) for shape in shapes],
+        compiler_params=LIMIT,
+    )(base.reshape(1), *metas, mates)
+
+
+def send_strips(places, strips, peers, cap):
+    strip, order = strips.shape[1:]
+    send = (peers, cap, strip, order)
+    return pl.pallas_call(
+        send_body,
+        grid_spec=pltpu.PrefetchScalarGridSpec(
+            num_scalar_prefetch=1,
+            grid=(1,),
+            in_specs=[whole(strips.shape)],
+            out_specs=HBM,
+            scratch_shapes=[pltpu.VMEM(send, jnp.float32), pltpu.SemaphoreType.DMA((peers // PER_GROUP,))],
+        ),
+        out_shape=pltpu.HBM(send, jnp.float32),
+        compiler_params=LIMIT,
+    )(places, pltpu.with_memory_space_constraint(strips, pltpu.VMEM))
 
 
 def collect_body(rows, first_line, codes, peak_ref, *refs):
@@ -411,6 +421,11 @@
     ]
 
 
+def from_peers(array, near, far, peers):
+    pairs = [(away_from(peer, near, far), peer) for peer in range(peers)]
+    return array if near + far == 0 else lax.ppermute(array, GROUP, pairs)
+
+
 def swap_rows(array, rows, by):
     return lax.ppermute(array, "row", [(i, i ^ by) for i in range(rows)])
 
@@ -423,16 +438,19 @@
     tiles = tile_values.reshape(-1, order, order)
 
     listed, wanted = label(tile_rows, tile_cols, tile_counts, out_rows, out_cols)
-    for by in (1, 2):
-        listed = listed + swap_rows(listed, rows, by)
-    strips, mates = stamp(listed, swap_rows(listed, rows, 4), wanted, pack(tiles, peers))
+    listed = listed + swap_rows(listed, rows, 1)
+    listed = [listed] + [lax.ppermute(listed, "row", [(i, (i + by) % rows) for i in range(rows)]) for by in (2, 4, 6)]
+    meta, mates = merge(listed, wanted)
+    metas = jnp.stack([from_peers(meta, near, 0, peers) for near in range(NEAR)])
+    metas = [from_peers(metas, 0, far, peers) for far in range(FAR)]
+    strips = lax.all_to_all(pack(tiles, peers), GROUP, 0, 0, tiled=True)
+    per_peer = strips.shape[1]
+    strips = strips.reshape(-1, order // peers, order)
     pieces = shift_all(pack_right(tiles, rows))
-    strips = lax.all_to_all(strips, GROUP, 0, 0, tiled=True)
-    strips, pieces = lax.optimization_barrier((strips, pieces))
-    strips = strips.reshape(-1, order // peers, order)
 
     def one_round(base, running):
-        send, codes, counts, peak = plan(strips, mates, base, rows, peers, ROUND_CAP)
+        codes, places, counts, peak = plan(metas, mates, base, rows, peers, per_peer, ROUND_CAP)
+        send = send_strips(places, strips, peers, ROUND_CAP)
         left = lax.all_to_all(send, GROUP, 0, 0, tiled=True)
         right = shift_all(collect(codes, peak, pieces, peers, ROUND_CAP))
         return multiply_round(left, right, codes, counts, base, running, kept)

time: 96.1 us -> 113 us (1.18)
  the two profiles are of different devices: /device:TPU:4 before, /device:TPU:1 now
where the time goes in v4:
time: 113 us
  starting transfers between devices  59.9 us (53%)
  waiting for transfers between devices  31.4 us (28%)
  Pallas kernels  18.3 us (16%)
  local copies, waits for them, and re-layouts  1.87 us (2%)
    ppermute x14, waiting for transfers between devices, shift_all(): lax.ppermute(pieces[by], 'row', [(i, (i + by) % rows) for i in range(rows)])  21.1 us
    ppermute x14, starting transfers between devices, shift_all(): lax.ppermute(pieces[by], 'row', [(i, (i + by) % rows) for i in range(rows)])  20.9 us
    ppermute x10, starting transfers between devices, from_peers(): return array if near + far == 0 else lax.ppermute(array, GROUP, pairs)  17.3 us
    all_to_all x1, starting transfers between devices, local(): strips = lax.all_to_all(pack(tiles, peers), GROUP, 0, 0, tiled=True)  11.9 us
    ppermute x10, waiting for transfers between devices, from_peers(): return array if near + far == 0 else lax.ppermute(array, GROUP, pairs)  6.2 us
    all_to_all x1, starting transfers between devices, one_round(): left = lax.all_to_all(send, GROUP, 0, 0, tiled=True)  4.96 us
    pallas_call x1, Pallas kernels, multiply_round(): pl.pallas_call(functools.partial(product_body, first, len(right)), grid_s...  4.3 us
    ppermute x3, starting transfers between devices, local(): lax.ppermute(listed, 'row', [(i, (i + by) % rows) for i in range(rows)])  3.77 us
  transfers between devices with their start and end apart: 30, of which 14 were waited for; matrix products, arithmetic and copies ran while one was open for 0% of the time, Pallas kernels for 8%

profile of v4, /device:TPU:1, one launch (start us, length us, event | category | flops | bytes accessed | tf_op | source)
XLA Modules:
  0.0 112.6 jit_solution(15935137105950706036)
XLA Ops:
  0.0 2.1 %shard_map.67 = f32[32,12,4,128]{3,2,1,0:T(4,128)} custom-call(f32[12,128,128]{2,1,0:T(8,128)} %bitcast.15), custom_call_target="tpu_custom_call" | custom-call | tf_op jit(solution)/shard_map/pallas_call | solution.py:97
  2.2 11.9 %all-to-all-start.1 = ((f32[32,12,4,128]{3,2,1,0:T(4,128)}), f32[32,12,4,128]{3,2,1,0:T(4,128)S(1)}, u32[]{:S(2)}, u32[]{:S(2)}) async-start(f32[32,12,4,128]{3,2,1,0:T(4,128)} %shard_map.67), calls=%async_computation.1 | async-start | bytes 1572864 | tf_op jit(solution)/shard_map/all_to_all | solution.py:446
  16.8 2.7 %collective-permute-start.10 = (f32[4,128]{1,0:T(4,128)S(1)}, f32[4,128]{1,0:T(4,128)S(1)}, u32[]{:S(2)}, u32[]{:S(2)}) collective-permute-start(f32[4,128]{1,0:T(4,128)S(1)} %add.6.refs_0_), channel_id=1, source_target_pairs={{0,192},{32,224},{64,0},{96,32},{128,64},{160,96},{192,128},{224,1... | collective-permute-start | bytes 6152 | tf_op jit(solution)/shard_map/ppermute | solution.py:442
  20.6 3.2 %collective-permute-done.9.refs_2_ = f32[4,128]{1,0:T(4,128)S(1)} collective-permute-done((f32[4,128]{1,0:T(4,128)S(1)}, f32[4,128]{1,0:T(4,128)S(1)}, u32[]{:S(2)}, u32[]{:S(2)}) %collective-permute-start.9) | collective-permute-done | bytes 2080 | tf_op jit(solution)/shard_map/ppermute | solution.py:442
  23.8 2.7 %collective-permute-start.13 = (f32[4,128]{1,0:T(4,128)S(1)}, f32[4,128]{1,0:T(4,128)S(1)}, u32[]{:S(2)}, u32[]{:S(2)}) collective-permute-start(f32[4,128]{1,0:T(4,128)S(1)} %get-tuple-element.154), channel_id=1, source_target_pairs={{2,0},{3,1},{4,2},{5,3},{6,4},{7,5},{0,6},{1,7},{10,8},{11,9},{12,... | collective-permute-start | bytes 6152 | tf_op jit(solution)/shard_map/ppermute | solution.py:426
  27.7 3.1 %collective-permute-done.12 = f32[4,128]{1,0:T(4,128)S(1)} collective-permute-done((f32[4,128]{1,0:T(4,128)S(1)}, f32[4,128]{1,0:T(4,128)S(1)}, u32[]{:S(2)}, u32[]{:S(2)}) %collective-permute-start.12) | collective-permute-done | bytes 2080 | tf_op jit(solution)/shard_map/ppermute | solution.py:426
  31.1 2.4 %collective-permute-start.20 = (f32[4,4,128]{2,1,0:T(4,128)S(1)}, f32[4,4,128]{2,1,0:T(4,128)S(1)}, u32[]{:S(2)}, u32[]{:S(2)}) collective-permute-start(f32[4,4,128]{2,1,0:T(4,128)S(1)} %pad_maximum_fusion.refs_0_), channel_id=1, source_target_pairs={{1,0},{8,1},{3,2},{10,3},{5,4},{12,5},{7,6},{14,7},{9,8},{16,9},{1... | collective-permute-start | bytes 24584 | tf_op jit(solution)/shard_map/ppermute | solution.py:426
  33.5 2.0 %collective-permute-start.19 = (f32[4,4,128]{2,1,0:T(4,128)S(1)}, f32[4,4,128]{2,1,0:T(4,128)S(1)}, u32[]{:S(2)}, u32[]{:S(2)}) collective-permute-start(f32[4,4,128]{2,1,0:T(4,128)S(1)} %pad_maximum_fusion.refs_0_), channel_id=1, source_target_pairs={{8,0},{9,1},{10,2},{11,3},{12,4},{13,5},{14,6},{15,7},{16,8},{17,9... | collective-permute-start | bytes 24584 | tf_op jit(solution)/shard_map/ppermute | solution.py:426
  36.8 3.3 %collective-permute-start.17 = (f32[4,4,128]{2,1,0:T(4,128)S(1)}, f32[4,4,128]{2,1,0:T(4,128)S(1)}, u32[]{:S(2)}, u32[]{:S(2)}) collective-permute-start(f32[4,4,128]{2,1,0:T(4,128)S(1)} %pad_maximum_fusion.refs_0_), channel_id=1, source_target_pairs={{16,0},{17,1},{18,2},{19,3},{20,4},{21,5},{22,6},{23,7},{24,8},{25... | collective-permute-start | bytes 24584 | tf_op jit(solution)/shard_map/ppermute | solution.py:426
  40.4 2.9 %collective-permute-start.15 = (f32[4,4,128]{2,1,0:T(4,128)S(1)}, f32[4,4,128]{2,1,0:T(4,128)S(1)}, u32[]{:S(2)}, u32[]{:S(2)}) collective-permute-start(f32[4,4,128]{2,1,0:T(4,128)S(1)} %pad_maximum_fusion.refs_0_), channel_id=1, source_target_pairs={{24,0},{25,1},{26,2},{27,3},{28,4},{29,5},{30,6},{31,7},{0,8},{1,9... | collective-permute-start | bytes 24584 | tf_op jit(solution)/shard_map/ppermute | solution.py:426
  47.3 3.0 %shard_map.66 = (s32[16,128]{1,0:T(8,128)S(1)}, s32[16,128]{1,0:T(8,128)S(1)}, s32[8,128]{1,0:T(8,128)S(1)}, f32[8,128]{1,0:T(8,128)S(1)}) custom-call(s32[1]{0:T(128)} %constant.2.clone.1.base_ref, f32[4,4,128]{2,1,0:T(4,128)S(1)} %pad_maximum_fusion.refs_0_, f32[4,4,128]{2,1,0:T(4,128)S(1)} %collective-permute-done.14.refs_1_, ...), custom_call_target="tpu_custom_call" | custom-call | tf_op jit(solution)/shard_map/pallas_call | solution.py:271
  50.3 3.0 %shard_map.68 = f32[32,20,4,128]{3,2,1,0:T(4,128)} custom-call(s32[16,128]{1,0:T(8,128)S(1)} %get-tuple-element.158.places, f32[384,4,128]{2,1,0:T(4,128)S(1)} %bitcast.12), custom_call_target="tpu_custom_call" | custom-call | tf_op jit(solution)/shard_map/pallas_call | solution.py:294
  53.4 5.0 %all-to-all-start.2 = ((f32[32,20,4,128]{3,2,1,0:T(4,128)}), f32[32,20,4,128]{3,2,1,0:T(4,128)S(1)}, u32[]{:S(2)}, u32[]{:S(2)}) async-start(f32[32,20,4,128]{3,2,1,0:T(4,128)} %shard_map.68), calls=%async_computation.2 | async-start | bytes 2621440 | tf_op jit(solution)/shard_map/all_to_all | solution.py:454
  60.2 5.4 %collective-permute-start.21 = (f32[12,16,128]{2,1,0:T(8,128)S(1)}, f32[12,16,128]{2,1,0:T(8,128)S(1)}, u32[]{:S(2)}, u32[]{:S(2)}) collective-permute-start(f32[12,16,128]{2,1,0:T(8,128)S(1)} %get-tuple-element.161), channel_id=1, source_target_pairs={{0,32},{32,64},{64,96},{96,128},{128,160},{160,192},{192,224},{224... | collective-permute-start | bytes 294920 | tf_op jit(solution)/shard_map/ppermute | solution.py:420
  70.0 2.6 %collective-permute-start.25 = (f32[12,16,128]{2,1,0:T(8,128)S(1)}, f32[12,16,128]{2,1,0:T(8,128)S(1)}, u32[]{:S(2)}, u32[]{:S(2)}) collective-permute-start(f32[12,16,128]{2,1,0:T(8,128)S(1)} %get-tuple-element.165), channel_id=1, source_target_pairs={{0,160},{32,192},{64,224},{96,0},{128,32},{160,64},{192,96},{224,1... | collective-permute-start | bytes 294920 | tf_op jit(solution)/shard_map/ppermute | solution.py:420
  72.7 5.3 %collective-permute-done.22.refs_2_ = f32[12,16,128]{2,1,0:T(8,128)S(1)} collective-permute-done((f32[12,16,128]{2,1,0:T(8,128)S(1)}, f32[12,16,128]{2,1,0:T(8,128)S(1)}, u32[]{:S(2)}, u32[]{:S(2)}) %collective-permute-start.22) | collective-permute-done | bytes 98336 | tf_op jit(solution)/shard_map/ppermute | solution.py:420
  78.5 3.7 %collective-permute-done.27.refs_7_ = f32[12,16,128]{2,1,0:T(8,128)S(1)} collective-permute-done((f32[12,16,128]{2,1,0:T(8,128)S(1)}, f32[12,16,128]{2,1,0:T(8,128)S(1)}, u32[]{:S(2)}, u32[]{:S(2)}) %collective-permute-start.27) | collective-permute-done | bytes 98336 | tf_op jit(solution)/shard_map/ppermute | solution.py:420
  82.9 3.1 %shard_map.70 = (f32[21,16,128]{2,1,0:T(8,128)S(1)}, f32[21,16,128]{2,1,0:T(8,128)S(1)}, f32[21,16,128]{2,1,0:T(8,128)S(1)}, f32[21,16,128]{2,1,0:T(8,128)}, f32...) custom-call(s32[16,128]{1,0:T(8,128)S(1)} %get-tuple-element.156.codes, ...), custom_call_target="tpu_custom_call" | custom-call | tf_op jit(solution)/shard_map/pallas_call | solution.py:329
  89.7 2.6 %collective-permute-start.33 = (f32[21,16,128]{2,1,0:T(8,128)}, f32[21,16,128]{2,1,0:T(8,128)S(1)}, u32[]{:S(2)}, u32[]{:S(2)}) collective-permute-start(f32[21,16,128]{2,1,0:T(8,128)} %get-tuple-element.174), channel_id=1, source_target_pairs={{0,192},{32,224},{64,0},{96,32},{128,64},{160,96},{192,128},{224,1... | collective-permute-start | bytes 516104 | tf_op jit(solution)/shard_map/ppermute | solution.py:420
  93.3 2.1 %collective-permute-start.34 = (f32[21,16,128]{2,1,0:T(8,128)}, f32[21,16,128]{2,1,0:T(8,128)}, u32[]{:S(2)}, u32[]{:S(2)}) collective-permute-start(f32[21,16,128]{2,1,0:T(8,128)} %get-tuple-element.175), channel_id=1, source_target_pairs={{0,224},{32,0},{64,32},{96,64},{128,96},{160,128},{192,160},{224,1... | collective-permute-start | bytes 516104 | tf_op jit(solution)/shard_map/ppermute | solution.py:420
  95.4 7.2 %collective-permute-done.30.refs_3_ = f32[21,16,128]{2,1,0:T(8,128)S(1)} collective-permute-done((f32[21,16,128]{2,1,0:T(8,128)}, f32[21,16,128]{2,1,0:T(8,128)S(1)}, u32[]{:S(2)}, u32[]{:S(2)}) %collective-permute-start.30) | collective-permute-done | bytes 172064 | tf_op jit(solution)/shard_map/ppermute | solution.py:420
  102.6 2.8 %collective-permute-done.33.refs_6_ = f32[21,16,128]{2,1,0:T(8,128)S(1)} collective-permute-done((f32[21,16,128]{2,1,0:T(8,128)}, f32[21,16,128]{2,1,0:T(8,128)S(1)}, u32[]{:S(2)}, u32[]{:S(2)}) %collective-permute-start.33) | collective-permute-done | bytes 172064 | tf_op jit(solution)/shard_map/ppermute | solution.py:420
  106.0 4.3 %shard_map.71 = (f32[12,128,128]{2,1,0:T(8,128)}, s32[8,128]{1,0:T(8,128)}) custom-call(s32[1]{0:T(128)} %constant.2.clone.1.base_ref, s32[16,128]{1,0:T(8,128)S(1)} %get-tuple-element.156.codes, s32[8,128]{1,0:T(8,128)S(1)} %get-tuple-element.157.counts, f32[32,20,4,128]{3,2,1,0:T(4,128)S(1)} %all-to-all-done.2.left_ref, ...), custom_call_target="tpu_custom_call" | custom-call | tf_op jit(solution)/shard_map/pallas_call | solution.py:403
  110.3 2.1 %while.10 = (s32[]{:T(128)}, f32[12,128,128]{2,1,0:T(8,128)}, s32[8,128]{1,0:T(8,128)}, f32[4,4,128]{2,1,0:T(4,128)S(1)}, f32[4,4,128]{2,1,0:T(4,128)S(1)}, /*in...) while((s32[]{:T(128)}, f32[12,128,128]{2,1,0:T(8,128)}, ...), condition=%wide.region_1.0_spmd, body=%wide.region_0.0_spmd.sunk | while | flops 2 | bytes 10322445 | solution.py:466
  (62 shorter events, 24.7 us)
Async XLA Ops:
  2.2 48.2 %all-to-all-start.1 = ((f32[32,12,4,128]{3,2,1,0:T(4,128)}), f32[32,12,4,128]{3,2,1,0:T(4,128)S(1)}, u32[]{:S(2)}, u32[]{:S(2)}) async-start(f32[32,12,4,128]{3,2,1,0:T(4,128)} %shard_map.67), calls=%async_computation.1 | async-start | bytes 1572864 | tf_op jit(solution)/shard_map/all_to_all | solution.py:446
  19.5 4.2 %collective-permute-start.9 = (f32[4,128]{1,0:T(4,128)S(1)}, f32[4,128]{1,0:T(4,128)S(1)}, u32[]{:S(2)}, u32[]{:S(2)}) collective-permute-start(f32[4,128]{1,0:T(4,128)S(1)} %add.6.refs_0_), channel_id=1, source_target_pairs={{0,128},{32,160},{64,192},{96,224},{128,0},{160,32},{192,64},{224,... | collective-permute-start | bytes 6152 | tf_op jit(solution)/shard_map/ppermute | solution.py:442
  26.6 4.2 %collective-permute-start.12 = (f32[4,128]{1,0:T(4,128)S(1)}, f32[4,128]{1,0:T(4,128)S(1)}, u32[]{:S(2)}, u32[]{:S(2)}) collective-permute-start(f32[4,128]{1,0:T(4,128)S(1)} %get-tuple-element.154), channel_id=1, source_target_pairs={{4,0},{5,1},{6,2},{7,3},{0,4},{1,5},{2,6},{3,7},{12,8},{13,9},{14,... | collective-permute-start | bytes 6152 | tf_op jit(solution)/shard_map/ppermute | solution.py:426
  31.1 9.3 %collective-permute-start.20 = (f32[4,4,128]{2,1,0:T(4,128)S(1)}, f32[4,4,128]{2,1,0:T(4,128)S(1)}, u32[]{:S(2)}, u32[]{:S(2)}) collective-permute-start(f32[4,4,128]{2,1,0:T(4,128)S(1)} %pad_maximum_fusion.refs_0_), channel_id=1, source_target_pairs={{1,0},{8,1},{3,2},{10,3},{5,4},{12,5},{7,6},{14,7},{9,8},{16,9},{1... | collective-permute-start | bytes 24584 | tf_op jit(solution)/shard_map/ppermute | solution.py:426
  33.5 9.8 %collective-permute-start.19 = (f32[4,4,128]{2,1,0:T(4,128)S(1)}, f32[4,4,128]{2,1,0:T(4,128)S(1)}, u32[]{:S(2)}, u32[]{:S(2)}) collective-permute-start(f32[4,4,128]{2,1,0:T(4,128)S(1)} %pad_maximum_fusion.refs_0_), channel_id=1, source_target_pairs={{8,0},{9,1},{10,2},{11,3},{12,4},{13,5},{14,6},{15,7},{16,8},{17,9... | collective-permute-start | bytes 24584 | tf_op jit(solution)/shard_map/ppermute | solution.py:426
  35.6 8.9 %collective-permute-start.18 = (f32[4,4,128]{2,1,0:T(4,128)S(1)}, f32[4,4,128]{2,1,0:T(4,128)S(1)}, u32[]{:S(2)}, u32[]{:S(2)}) collective-permute-start(f32[4,4,128]{2,1,0:T(4,128)S(1)} %pad_maximum_fusion.refs_0_), channel_id=1, source_target_pairs={{9,0},{16,1},{11,2},{18,3},{13,4},{20,5},{15,6},{22,7},{17,8},{24,... | collective-permute-start | bytes 24584 | tf_op jit(solution)/shard_map/ppermute | solution.py:426
  36.8 7.7 %collective-permute-start.17 = (f32[4,4,128]{2,1,0:T(4,128)S(1)}, f32[4,4,128]{2,1,0:T(4,128)S(1)}, u32[]{:S(2)}, u32[]{:S(2)}) collective-permute-start(f32[4,4,128]{2,1,0:T(4,128)S(1)} %pad_maximum_fusion.refs_0_), channel_id=1, source_target_pairs={{16,0},{17,1},{18,2},{19,3},{20,4},{21,5},{22,6},{23,7},{24,8},{25... | collective-permute-start | bytes 24584 | tf_op jit(solution)/shard_map/ppermute | solution.py:426
  40.1 5.5 %collective-permute-start.16 = (f32[4,4,128]{2,1,0:T(4,128)S(1)}, f32[4,4,128]{2,1,0:T(4,128)S(1)}, u32[]{:S(2)}, u32[]{:S(2)}) collective-permute-start(f32[4,4,128]{2,1,0:T(4,128)S(1)} %pad_maximum_fusion.refs_0_), channel_id=1, source_target_pairs={{17,0},{24,1},{19,2},{26,3},{21,4},{28,5},{23,6},{30,7},{25,8},{0,... | collective-permute-start | bytes 24584 | tf_op jit(solution)/shard_map/ppermute | solution.py:426
  40.4 5.2 %collective-permute-start.15 = (f32[4,4,128]{2,1,0:T(4,128)S(1)}, f32[4,4,128]{2,1,0:T(4,128)S(1)}, u32[]{:S(2)}, u32[]{:S(2)}) collective-permute-start(f32[4,4,128]{2,1,0:T(4,128)S(1)} %pad_maximum_fusion.refs_0_), channel_id=1, source_target_pairs={{24,0},{25,1},{26,2},{27,3},{28,4},{29,5},{30,6},{31,7},{0,8},{1,9... | collective-permute-start | bytes 24584 | tf_op jit(solution)/shard_map/ppermute | solution.py:426
  43.3 4.0 %collective-permute-start.14 = (f32[4,4,128]{2,1,0:T(4,128)S(1)}, f32[4,4,128]{2,1,0:T(4,128)S(1)}, u32[]{:S(2)}, u32[]{:S(2)}) collective-permute-start(f32[4,4,128]{2,1,0:T(4,128)S(1)} %pad_maximum_fusion.refs_0_), channel_id=1, source_target_pairs={{25,0},{0,1},{27,2},{2,3},{29,4},{4,5},{31,6},{6,7},{1,8},{8,9},{3... | collective-permute-start | bytes 24584 | tf_op jit(solution)/shard_map/ppermute | solution.py:426
  53.4 52.6 %all-to-all-start.2 = ((f32[32,20,4,128]{3,2,1,0:T(4,128)}), f32[32,20,4,128]{3,2,1,0:T(4,128)S(1)}, u32[]{:S(2)}, u32[]{:S(2)}) async-start(f32[32,20,4,128]{3,2,1,0:T(4,128)} %shard_map.68), calls=%async_computation.2 | async-start | bytes 2621440 | tf_op jit(solution)/shard_map/all_to_all | solution.py:454
  60.2 12.5 %collective-permute-start.21 = (f32[12,16,128]{2,1,0:T(8,128)S(1)}, f32[12,16,128]{2,1,0:T(8,128)S(1)}, u32[]{:S(2)}, u32[]{:S(2)}) collective-permute-start(f32[12,16,128]{2,1,0:T(8,128)S(1)} %get-tuple-element.161), channel_id=1, source_target_pairs={{0,32},{32,64},{64,96},{96,128},{128,160},{160,192},{192,224},{224... | collective-permute-start | bytes 294920 | tf_op jit(solution)/shard_map/ppermute | solution.py:420
  65.6 12.3 %collective-permute-start.22 = (f32[12,16,128]{2,1,0:T(8,128)S(1)}, f32[12,16,128]{2,1,0:T(8,128)S(1)}, u32[]{:S(2)}, u32[]{:S(2)}) collective-permute-start(f32[12,16,128]{2,1,0:T(8,128)S(1)} %get-tuple-element.162), channel_id=1, source_target_pairs={{0,64},{32,96},{64,128},{96,160},{128,192},{160,224},{192,0},{224,... | collective-permute-start | bytes 294920 | tf_op jit(solution)/shard_map/ppermute | solution.py:420
  67.3 11.2 %collective-permute-start.23 = (f32[12,16,128]{2,1,0:T(8,128)S(1)}, f32[12,16,128]{2,1,0:T(8,128)S(1)}, u32[]{:S(2)}, u32[]{:S(2)}) collective-permute-start(f32[12,16,128]{2,1,0:T(8,128)S(1)} %get-tuple-element.163), channel_id=1, source_target_pairs={{0,96},{32,128},{64,160},{96,192},{128,224},{160,0},{192,32},{224,... | collective-permute-start | bytes 294920 | tf_op jit(solution)/shard_map/ppermute | solution.py:420
  68.0 10.5 %collective-permute-start.24 = (f32[12,16,128]{2,1,0:T(8,128)S(1)}, f32[12,16,128]{2,1,0:T(8,128)S(1)}, u32[]{:S(2)}, u32[]{:S(2)}) collective-permute-start(f32[12,16,128]{2,1,0:T(8,128)S(1)} %get-tuple-element.164), channel_id=1, source_target_pairs={{0,128},{32,160},{64,192},{96,224},{128,0},{160,32},{192,64},{224,... | collective-permute-start | bytes 294920 | tf_op jit(solution)/shard_map/ppermute | solution.py:420
  70.0 8.5 %collective-permute-start.25 = (f32[12,16,128]{2,1,0:T(8,128)S(1)}, f32[12,16,128]{2,1,0:T(8,128)S(1)}, u32[]{:S(2)}, u32[]{:S(2)}) collective-permute-start(f32[12,16,128]{2,1,0:T(8,128)S(1)} %get-tuple-element.165), channel_id=1, source_target_pairs={{0,160},{32,192},{64,224},{96,0},{128,32},{160,64},{192,96},{224,1... | collective-permute-start | bytes 294920 | tf_op jit(solution)/shard_map/ppermute | solution.py:420
  72.6 5.9 %collective-permute-start.26 = (f32[12,16,128]{2,1,0:T(8,128)S(1)}, f32[12,16,128]{2,1,0:T(8,128)S(1)}, u32[]{:S(2)}, u32[]{:S(2)}) collective-permute-start(f32[12,16,128]{2,1,0:T(8,128)S(1)} %get-tuple-element.166), channel_id=1, source_target_pairs={{0,192},{32,224},{64,0},{96,32},{128,64},{160,96},{192,128},{224,1... | collective-permute-start | bytes 294920 | tf_op jit(solution)/shard_map/ppermute | solution.py:420
  77.9 4.3 %collective-permute-start.27 = (f32[12,16,128]{2,1,0:T(8,128)S(1)}, f32[12,16,128]{2,1,0:T(8,128)S(1)}, u32[]{:S(2)}, u32[]{:S(2)}) collective-permute-start(f32[12,16,128]{2,1,0:T(8,128)S(1)} %get-tuple-element.167), channel_id=1, source_target_pairs={{0,224},{32,0},{64,32},{96,64},{128,96},{160,128},{192,160},{224,1... | collective-permute-start | bytes 294920 | tf_op jit(solution)/shard_map/ppermute | solution.py:420
  86.0 7.2 %collective-permute-start.29 = (f32[21,16,128]{2,1,0:T(8,128)S(1)}, f32[21,16,128]{2,1,0:T(8,128)S(1)}, u32[]{:S(2)}, u32[]{:S(2)}) collective-permute-start(f32[21,16,128]{2,1,0:T(8,128)S(1)} %get-tuple-element.170), channel_id=1, source_target_pairs={{0,64},{32,96},{64,128},{96,160},{128,192},{160,224},{192,0},{224,... | collective-permute-start | bytes 516104 | tf_op jit(solution)/shard_map/ppermute | solution.py:420
  86.1 16.5 %collective-permute-start.30 = (f32[21,16,128]{2,1,0:T(8,128)}, f32[21,16,128]{2,1,0:T(8,128)S(1)}, u32[]{:S(2)}, u32[]{:S(2)}) collective-permute-start(f32[21,16,128]{2,1,0:T(8,128)} %get-tuple-element.171), channel_id=1, source_target_pairs={{0,96},{32,128},{64,160},{96,192},{128,224},{160,0},{192,32},{224,... | collective-permute-start | bytes 516104 | tf_op jit(solution)/shard_map/ppermute | solution.py:420
  87.7 14.8 %collective-permute-start.31 = (f32[21,16,128]{2,1,0:T(8,128)}, f32[21,16,128]{2,1,0:T(8,128)S(1)}, u32[]{:S(2)}, u32[]{:S(2)}) collective-permute-start(f32[21,16,128]{2,1,0:T(8,128)} %get-tuple-element.172), channel_id=1, source_target_pairs={{0,128},{32,160},{64,192},{96,224},{128,0},{160,32},{192,64},{224,... | collective-permute-start | bytes 516104 | tf_op jit(solution)/shard_map/ppermute | solution.py:420
  89.4 13.2 %collective-permute-start.32 = (f32[21,16,128]{2,1,0:T(8,128)}, f32[21,16,128]{2,1,0:T(8,128)S(1)}, u32[]{:S(2)}, u32[]{:S(2)}) collective-permute-start(f32[21,16,128]{2,1,0:T(8,128)} %get-tuple-element.173), channel_id=1, source_target_pairs={{0,160},{32,192},{64,224},{96,0},{128,32},{160,64},{192,96},{224,1... | collective-permute-start | bytes 516104 | tf_op jit(solution)/shard_map/ppermute | solution.py:420
  89.7 15.6 %collective-permute-start.33 = (f32[21,16,128]{2,1,0:T(8,128)}, f32[21,16,128]{2,1,0:T(8,128)S(1)}, u32[]{:S(2)}, u32[]{:S(2)}) collective-permute-start(f32[21,16,128]{2,1,0:T(8,128)} %get-tuple-element.174), channel_id=1, source_target_pairs={{0,192},{32,224},{64,0},{96,32},{128,64},{160,96},{192,128},{224,1... | collective-permute-start | bytes 516104 | tf_op jit(solution)/shard_map/ppermute | solution.py:420
  93.3 12.7 %collective-permute-start.34 = (f32[21,16,128]{2,1,0:T(8,128)}, f32[21,16,128]{2,1,0:T(8,128)}, u32[]{:S(2)}, u32[]{:S(2)}) collective-permute-start(f32[21,16,128]{2,1,0:T(8,128)} %get-tuple-element.175), channel_id=1, source_target_pairs={{0,224},{32,0},{64,32},{96,64},{128,96},{160,128},{192,160},{224,1... | collective-permute-start | bytes 516104 | tf_op jit(solution)/shard_map/ppermute | solution.py:420
  (13 other events, 50.9 us)

commit v5 on v3

--- a/solution.py
+++ b/solution.py
@@ -12,6 +12,7 @@
 SLOT_PITCH = 16
 PER_GROUP = LANES // SLOT_PITCH
 ROUND_CAP = 20
+TOGETHER = 2
 LIMIT = pltpu.CompilerParams(vmem_limit_bytes=20 * 2**20)
 HBM = pl.BlockSpec(memory_space=pltpu.HBM)
 
@@ -246,15 +247,11 @@
         part = pl.ds(group * PER_GROUP, PER_GROUP)
         return pltpu.make_async_copy(send.at[part], send_ref.at[part], send_sems.at[group])
 
-    def one_peer(peer, carry):
-        line = (peer >> 3) * halves
-        first = (peer & (PER_GROUP - 1)) * SLOT_PITCH
-        for at in range(cap):
-            send[peer, at] = strips_ref[places[line + at // SLOT_PITCH, first + at % SLOT_PITCH]]
-        return carry
-
     for group in range(groups):
-        lax.fori_loop(group * PER_GROUP, (group + 1) * PER_GROUP, one_peer, 0)
+        for peer in range(group * PER_GROUP, (group + 1) * PER_GROUP):
+            line, first = group * halves, peer % PER_GROUP * SLOT_PITCH
+            for at in range(cap):
+                send[peer, at] = strips_ref[places[line + at // SLOT_PITCH, first + at % SLOT_PITCH]]
         one_group(group).start()
     for group in range(groups):
         one_group(group).wait()
@@ -330,37 +327,76 @@
     )(codes, peak, *in_hbm(*pieces))
 
 
-def product_body(first, rows, base_ref, codes, counts, left_ref, *refs):
-    right_refs, refs = refs[:rows], refs[rows:]
-    if first:
-        out_ref, most_ref, left, right = refs
-        out_ref[...] = jnp.zeros_like(out_ref)
-    else:
-        running_ref, out_ref, most_ref, left, right = refs
-        out_ref[...] = running_ref[...]
-    row_index, own, base = lax.axis_index("row"), lax.axis_index(GROUP), base_ref[0]
-    peers, cap, strip, order = left_ref.shape
-    tall_strip = right_refs[0].shape[1]
-    line = (own >> 3) * pl.cdiv(cap, SLOT_PITCH)
-    lane = (own & (PER_GROUP - 1)) * SLOT_PITCH
-    todo = jnp.clip(counts[own >> 3, lane] - base, 0, cap)
+def ready_body(*refs):
+    right_refs, out_hbm, most_ref, right, out_ref, sem = refs[:-5], *refs[-5:]
+    rows, cap, order = len(right_refs), *out_ref.shape[:2]
+    row_index = lax.axis_index("row")
+    strip = right_refs[0].shape[1]
     most = right_refs[0][cap, 0:8, :]
     for right_ref in right_refs[1:]:
         most = jnp.maximum(most, right_ref[cap, 0:8, :])
     most_ref[...] = most.astype(jnp.int32)
-    bf16 = jnp.bfloat16
+
+    def one_tile(at, carry):
+        for away, right_ref in enumerate(right_refs):
+            start = pl.multiple_of((row_index + rows - away) % rows * strip, strip)
+            right[pl.ds(start, strip), :] = right_ref[at]
+        b = right[...]
+        b_high = b.astype(jnp.bfloat16)
+        out_ref[at, :, :order] = b_high
+        out_ref[at, :, order:] = (b - b_high.astype(jnp.float32)).astype(jnp.bfloat16)
+        return carry
+
+    lax.fori_loop(0, cap, one_tile, 0)
+    copy = pltpu.make_async_copy(out_ref, out_hbm, sem)
+    copy.start()
+    copy.wait()
+
+
+def ready(right):
+    cap, order = right[0].shape[0] - 1, right[0].shape[2]
+    vmem = pl.BlockSpec(memory_space=pltpu.VMEM)
+    rights, most = pl.pallas_call(
+        ready_body,
+        in_specs=[vmem] * len(right),
+        out_specs=[HBM, vmem],
+        out_shape=[pltpu.HBM((cap, order, 2 * order), jnp.bfloat16), jax.ShapeDtypeStruct((8, LANES), jnp.int32)],
+        scratch_shapes=[
+            pltpu.VMEM((order, order), jnp.float32),
+            pltpu.VMEM((cap, order, 2 * order), jnp.bfloat16),
+            pltpu.SemaphoreType.DMA,
+        ],
+        compiler_params=LIMIT,
+    )(*right)
+    return rights, most[0, 0]
+
+
+def product_body(first, scalars, codes, counts, left_ref, rights_ref, *refs):
+    out_ref, left, rights, sems = refs[-4:]
+    own, base = lax.axis_index(GROUP), scalars[0]
+    peers, cap, strip, order = left_ref.shape
+    line = (own >> 3) * pl.cdiv(cap, SLOT_PITCH)
+    lane = (own & (PER_GROUP - 1)) * SLOT_PITCH
+    todo = jnp.clip(counts[own >> 3, lane] - base, 0, cap)
+
+    def fetch(at):
+        return pltpu.make_async_copy(rights_ref.at[at], rights.at[at], sems.at[at])
+
+    for at in range(cap):
+        fetch(at).start()
+    if first:
+        out_ref[...] = jnp.zeros_like(out_ref)
+    else:
+        out_ref[...] = refs[0][...]
 
     def product(at, half):
+        fetch(at).wait()
         for peer in range(peers):
             left[half, peer * strip:(peer + 1) * strip, :] = left_ref[peer, at]
-        for away, right_ref in enumerate(right_refs):
-            start = pl.multiple_of((row_index + rows - away) % rows * tall_strip, tall_strip)
-            right[half, pl.ds(start, tall_strip), :] = right_ref[at]
-        a, b = left[half], right[half]
-        a_high, b_high = a.astype(bf16), b.astype(bf16)
-        a_low = (a - a_high.astype(jnp.float32)).astype(bf16)
-        b_low = (b - b_high.astype(jnp.float32)).astype(bf16)
-        both = jnp.concatenate([b_high, b_low], axis=1)
+        a = left[half]
+        a_high = a.astype(jnp.bfloat16)
+        a_low = (a - a_high.astype(jnp.float32)).astype(jnp.bfloat16)
+        both = rights[at]
         sums = jnp.dot(
             jnp.concatenate([a_high, a_low], axis=1),
             jnp.concatenate([both, both], axis=0),
@@ -371,37 +407,50 @@
     def target(at):
         return codes[line + (at >> 4), lane + (at & (SLOT_PITCH - 1))] >> 16
 
-    def two(pair, carry):
-        at = 2 * pair
-        one, other = product(at, 0), product(at + 1, 1)
-        out_ref[target(at)] += one
-
-        @pl.when(at + 1 < todo)
-        def _():
-            out_ref[target(at + 1)] += other
+    def several(step, carry):
+        at = TOGETHER * step
+        sums = [product(at + n, n) for n in range(TOGETHER)]
+        out_ref[target(at)] += sums[0]
+        for n in range(1, TOGETHER):
+            @pl.when(at + n < todo)
+            def _():
+                out_ref[target(at + n)] += sums[n]
 
         return carry
 
-    lax.fori_loop(0, (todo + 1) >> 1, two, 0)
+    def unused(at, carry):
+        fetch(at).wait()
+        return carry
+
+    steps = (todo + TOGETHER - 1) // TOGETHER
+    lax.fori_loop(0, steps, several, 0)
+    lax.fori_loop(TOGETHER * steps, cap, unused, 0)
 
 
 def multiply_round(left, right, codes, counts, base, running, kept):
     order = left.shape[-1]
     first = running is None
     tiles = (kept, order, order)
-    operands = [pltpu.with_memory_space_constraint(left, pltpu.VMEM), *right] + ([] if first else [running])
-    return pl.pallas_call(
-        functools.partial(product_body, first, len(right)),
+    rights, most = ready(right)
+    scalars = jnp.stack([base, most])
+    operands = [pltpu.with_memory_space_constraint(left, pltpu.VMEM), *in_hbm(rights)] + ([] if first else [running])
+    summed = pl.pallas_call(
+        functools.partial(product_body, first),
         grid_spec=pltpu.PrefetchScalarGridSpec(
             num_scalar_prefetch=3,
             grid=(1,),
-            in_specs=[whole(operand.shape) for operand in operands],
-            out_specs=[whole(tiles), whole((8, LANES))],
-            scratch_shapes=[pltpu.VMEM((2, order, order), jnp.float32)] * 2,
+            in_specs=[whole(left.shape), HBM] + ([] if first else [whole(tiles)]),
+            out_specs=whole(tiles),
+            scratch_shapes=[
+                pltpu.VMEM((TOGETHER, order, order), jnp.float32),
+                pltpu.VMEM(rights.shape, rights.dtype),
+                pltpu.SemaphoreType.DMA((rights.shape[0],)),
+            ],
         ),
-        out_shape=[jax.ShapeDtypeStruct(tiles, jnp.float32), jax.ShapeDtypeStruct((8, LANES), jnp.int32)],
-        compiler_params=LIMIT,
-    )(base.reshape(1), codes, counts, *operands)
+        out_shape=jax.ShapeDtypeStruct(tiles, jnp.float32),
+        compiler_params=LIMIT,
+    )(scalars, codes, counts, *operands)
+    return summed, most
 
 
 def shift_all(pieces):
@@ -425,7 +474,7 @@
     listed, wanted = label(tile_rows, tile_cols, tile_counts, out_rows, out_cols)
     for by in (1, 2):
         listed = listed + swap_rows(listed, rows, by)
-    strips, mates = stamp(listed, swap_rows(listed, rows, 4), wanted, pack(tiles, peers))
+    strips, mates = stamp(listed, swap_rows(listed, rows, rows - 2), wanted, pack(tiles, peers))
     pieces = shift_all(pack_right(tiles, rows))
     strips = lax.all_to_all(strips, GROUP, 0, 0, tiled=True)
     strips, pieces = lax.optimization_barrier((strips, pieces))
@@ -440,7 +489,7 @@
     summed, most = one_round(jnp.zeros((), jnp.int32), None)
 
     def unfinished(state):
-        return state[0] < most[0, 0]
+        return state[0] < most
 
     def further(state):
         return state[0] + ROUND_CAP, one_round(*state)[0]

time: 96.1 us -> 94.8 us (0.986)
  waiting for transfers between devices: 34.1 us -> 30.6 us
  Pallas kernels: 18.7 us -> 21.8 us
    all_to_all x1, waiting for transfers between devices: 9.68 us -> 5.5 us  [one_round(): left = lax.all_to_all(send, GROUP, 0, 0, tiled=True)]
    pallas_call x1 -> x2, Pallas kernels: 4.06 us -> 8.12 us  [the longest x1 5.29 us: multiply_round(): pl.pallas_call(functools.partial(product_body, first), grid_spec=pltpu.Pr...]
    pallas_call x1, Pallas kernels: 5.99 us -> 5.03 us  [plan(): pl.pallas_call(functools.partial(plan_body, rows), grid_spec=pltpu.Prefet...]
  transfers between devices with their start and end apart: 19 -> 19, of which waited for: 14 -> 15; matrix products, arithmetic and copies ran while one was open for 0% -> 1% of each run, Pallas kernels for 7% -> 10%
where the time goes in v5:
time: 94.8 us; the launch traced here: 94.5 us
  starting transfers between devices  39.8 us (42%)
  waiting for transfers between devices  30.6 us (32%)
  Pallas kernels  21.8 us (23%)
    ppermute x14, starting transfers between devices, shift_all(): lax.ppermute(pieces[by], 'row', [(i, (i + by) % rows) for i in range(rows)])  17.8 us
    ppermute x14, waiting for transfers between devices, shift_all(): lax.ppermute(pieces[by], 'row', [(i, (i + by) % rows) for i in range(rows)])  14.1 us
    all_to_all x1, starting transfers between devices, local(): strips = lax.all_to_all(strips, GROUP, 0, 0, tiled=True)  11.6 us
    all_to_all x1, waiting for transfers between devices, local(): strips = lax.all_to_all(strips, GROUP, 0, 0, tiled=True)  7.9 us
    all_to_all x1, starting transfers between devices, one_round(): left = lax.all_to_all(send, GROUP, 0, 0, tiled=True)  5.71 us
    all_to_all x1, waiting for transfers between devices, one_round(): left = lax.all_to_all(send, GROUP, 0, 0, tiled=True)  5.5 us
    pallas_call x1, Pallas kernels, multiply_round(): pl.pallas_call(functools.partial(product_body, first), grid_spec=pltpu.Pr...  5.29 us
    pallas_call x1, Pallas kernels, plan(): pl.pallas_call(functools.partial(plan_body, rows), grid_spec=pltpu.Prefet...  5.03 us
  transfers between devices with their start and end apart: 19, of which 15 were waited for; matrix products, arithmetic and copies ran while one was open for 1% of the time, Pallas kernels for 10%

profile of v5, /device:TPU:4, one launch (start us, length us, event | category | flops | bytes accessed | tf_op | source)
XLA Modules:
  0.0 94.5 jit_solution(18440448025804661914)
XLA Ops:
  2.1 1.6 %collective-permute-start.8 = (f32[4,128]{1,0:T(4,128)S(1)}, f32[4,128]{1,0:T(4,128)S(1)}, u32[]{:S(2)}, u32[]{:S(2)}) collective-permute-start(f32[4,128]{1,0:T(4,128)S(1)} %add.9), channel_id=1, source_target_pairs={{0,64},{32,96},{64,0},{96,32},{128,192},{160,224},{192,128},{224,1... | collective-permute-start | bytes 6152 | tf_op jit(solution)/shard_map/ppermute | solution.py:464
  3.7 2.0 %collective-permute-done.8 = f32[4,128]{1,0:T(4,128)S(1)} collective-permute-done((f32[4,128]{1,0:T(4,128)S(1)}, f32[4,128]{1,0:T(4,128)S(1)}, u32[]{:S(2)}, u32[]{:S(2)}) %collective-permute-start.8) | collective-permute-done | bytes 2080 | tf_op jit(solution)/shard_map/ppermute | solution.py:464
  5.7 3.0 %collective-permute-start.9 = (f32[4,128]{1,0:T(4,128)S(1)}, f32[4,128]{1,0:T(4,128)S(1)}, u32[]{:S(2)}, u32[]{:S(2)}) collective-permute-start(f32[4,128]{1,0:T(4,128)S(1)} %add.10.one_ref), channel_id=1, source_target_pairs={{0,192},{32,224},{64,128},{96,160},{128,64},{160,96},{192,0},{224,... | collective-permute-start | bytes 6152 | tf_op jit(solution)/shard_map/ppermute | solution.py:464
  8.7 2.2 %shard_map.65.strips_in = f32[32,13,4,128]{3,2,1,0:T(4,128)} custom-call(f32[12,128,128]{2,1,0:T(8,128)} %bitcast.13), custom_call_target="tpu_custom_call" | custom-call | tf_op jit(solution)/shard_map/pallas_call | solution.py:89
  11.6 11.6 %all-to-all-start.1 = ((f32[32,13,4,128]{3,2,1,0:T(4,128)}), f32[32,13,4,128]{3,2,1,0:T(4,128)S(1)}, u32[]{:S(2)}, u32[]{:S(2)}) async-start(f32[32,13,4,128]{3,2,1,0:T(4,128)} %get-tuple-element.124), calls=%async_computation.1 | async-start | bytes 1703936 | tf_op jit(solution)/shard_map/all_to_all | solution.py:479
  23.2 1.8 %shard_map.67 = (f32[12,16,128]{2,1,0:T(8,128)}, f32[12,16,128]{2,1,0:T(8,128)S(1)}, f32[12,16,128]{2,1,0:T(8,128)S(1)}, f32[12,16,128]{2,1,0:T(8,128)S(1)}, f32...) custom-call(f32[12,128,128]{2,1,0:T(8,128)} %bitcast.14), custom_call_target="tpu_custom_call" | custom-call | tf_op jit(solution)/shard_map/pallas_call | solution.py:136
  25.2 3.3 %collective-permute-start.12 = (f32[12,16,128]{2,1,0:T(8,128)S(1)}, f32[12,16,128]{2,1,0:T(8,128)S(1)}, u32[]{:S(2)}, u32[]{:S(2)}) collective-permute-start(f32[12,16,128]{2,1,0:T(8,128)S(1)} %get-tuple-element.128), channel_id=1, source_target_pairs={{0,96},{32,128},{64,160},{96,192},{128,224},{160,0},{192,32},{224,... | collective-permute-start | bytes 294920 | tf_op jit(solution)/shard_map/ppermute | solution.py:459
  29.5 2.6 %collective-permute-start.14 = (f32[12,16,128]{2,1,0:T(8,128)S(1)}, f32[12,16,128]{2,1,0:T(8,128)S(1)}, u32[]{:S(2)}, u32[]{:S(2)}) collective-permute-start(f32[12,16,128]{2,1,0:T(8,128)S(1)} %get-tuple-element.130), channel_id=1, source_target_pairs={{0,160},{32,192},{64,224},{96,0},{128,32},{160,64},{192,96},{224,1... | collective-permute-start | bytes 294920 | tf_op jit(solution)/shard_map/ppermute | solution.py:459
  32.3 1.8 %collective-permute-start.16 = (f32[12,16,128]{2,1,0:T(8,128)S(1)}, f32[12,16,128]{2,1,0:T(8,128)S(1)}, u32[]{:S(2)}, u32[]{:S(2)}) collective-permute-start(f32[12,16,128]{2,1,0:T(8,128)S(1)} %get-tuple-element.132), channel_id=1, source_target_pairs={{0,224},{32,0},{64,32},{96,64},{128,96},{160,128},{192,160},{224,1... | collective-permute-start | bytes 294920 | tf_op jit(solution)/shard_map/ppermute | solution.py:459
  34.0 1.8 %collective-permute-done.12.refs_3_ = f32[12,16,128]{2,1,0:T(8,128)S(1)} collective-permute-done((f32[12,16,128]{2,1,0:T(8,128)S(1)}, f32[12,16,128]{2,1,0:T(8,128)S(1)}, u32[]{:S(2)}, u32[]{:S(2)}) %collective-permute-start.12) | collective-permute-done | bytes 98336 | tf_op jit(solution)/shard_map/ppermute | solution.py:459
  37.8 7.9 %all-to-all-done.1 = f32[32,13,4,128]{3,2,1,0:T(4,128)S(1)} async-done(((f32[32,13,4,128]{3,2,1,0:T(4,128)}), f32[32,13,4,128]{3,2,1,0:T(4,128)S(1)}, u32[]{:S(2)}, u32[]{:S(2)}) %all-to-all-start.1) | async-done | bytes 852000 | tf_op jit(solution)/shard_map/all_to_all | solution.py:479
  45.7 5.0 %shard_map.68 = (f32[32,20,4,128]{3,2,1,0:T(4,128)}, s32[16,128]{1,0:T(8,128)S(1)}, s32[8,128]{1,0:T(8,128)S(1)}, f32[8,128]{1,0:T(8,128)S(1)}) custom-call(s32[1]{0:T(128)} %constant.2.clone.1.base_ref, f32[416,4,128]{2,1,0:T(4,128)S(1)} %bitcast.11, f32[4,128]{1,0:T(4,128)S(1)} %get-tuple-element.296.mates_ref), custom_call_target="tpu_custom_call" | custom-call | tf_op jit(solution)/shard_map/pallas_call | solution.py:271
  50.8 5.7 %all-to-all-start.2 = ((f32[32,20,4,128]{3,2,1,0:T(4,128)}), f32[32,20,4,128]{3,2,1,0:T(4,128)S(1)}, u32[]{:S(2)}, u32[]{:S(2)}) async-start(f32[32,20,4,128]{3,2,1,0:T(4,128)} %get-tuple-element.155), calls=%async_computation.2 | async-start | bytes 2621440 | tf_op jit(solution)/shard_map/all_to_all | solution.py:485
  56.5 3.1 %shard_map.69 = (f32[21,16,128]{2,1,0:T(8,128)S(1)}, f32[21,16,128]{2,1,0:T(8,128)S(1)}, f32[21,16,128]{2,1,0:T(8,128)S(1)}, f32[21,16,128]{2,1,0:T(8,128)}, f32...) custom-call(s32[16,128]{1,0:T(8,128)S(1)} %get-tuple-element.135.codes, ...), custom_call_target="tpu_custom_call" | custom-call | tf_op jit(solution)/shard_map/pallas_call | solution.py:316
  59.7 2.3 %collective-permute-start.19 = (f32[21,16,128]{2,1,0:T(8,128)}, f32[21,16,128]{2,1,0:T(8,128)S(1)}, u32[]{:S(2)}, u32[]{:S(2)}) collective-permute-start(f32[21,16,128]{2,1,0:T(8,128)} %get-tuple-element.148), channel_id=1, source_target_pairs={{0,96},{32,128},{64,160},{96,192},{128,224},{160,0},{192,32},{224,... | collective-permute-start | bytes 516104 | tf_op jit(solution)/shard_map/ppermute | solution.py:459
  62.0 2.1 %collective-permute-start.20 = (f32[21,16,128]{2,1,0:T(8,128)}, f32[21,16,128]{2,1,0:T(8,128)S(1)}, u32[]{:S(2)}, u32[]{:S(2)}) collective-permute-start(f32[21,16,128]{2,1,0:T(8,128)} %get-tuple-element.149), channel_id=1, source_target_pairs={{0,128},{32,160},{64,192},{96,224},{128,0},{160,32},{192,64},{224,... | collective-permute-start | bytes 516104 | tf_op jit(solution)/shard_map/ppermute | solution.py:459
  64.1 1.5 %collective-permute-start.21 = (f32[21,16,128]{2,1,0:T(8,128)}, f32[21,16,128]{2,1,0:T(8,128)S(1)}, u32[]{:S(2)}, u32[]{:S(2)}) collective-permute-start(f32[21,16,128]{2,1,0:T(8,128)} %get-tuple-element.150), channel_id=1, source_target_pairs={{0,160},{32,192},{64,224},{96,0},{128,32},{160,64},{192,96},{224,1... | collective-permute-start | bytes 516104 | tf_op jit(solution)/shard_map/ppermute | solution.py:459
  65.6 1.3 %collective-permute-done.17.refs_1_ = f32[21,16,128]{2,1,0:T(8,128)S(1)} collective-permute-done((f32[21,16,128]{2,1,0:T(8,128)S(1)}, f32[21,16,128]{2,1,0:T(8,128)S(1)}, u32[]{:S(2)}, u32[]{:S(2)}) %collective-permute-start.17) | collective-permute-done | bytes 172064 | tf_op jit(solution)/shard_map/ppermute | solution.py:459
  68.1 2.6 %collective-permute-start.23 = (f32[21,16,128]{2,1,0:T(8,128)}, f32[21,16,128]{2,1,0:T(8,128)}, u32[]{:S(2)}, u32[]{:S(2)}) collective-permute-start(f32[21,16,128]{2,1,0:T(8,128)} %get-tuple-element.152), channel_id=1, source_target_pairs={{0,224},{32,0},{64,32},{96,64},{128,96},{160,128},{192,160},{224,1... | collective-permute-start | bytes 516104 | tf_op jit(solution)/shard_map/ppermute | solution.py:459
  70.7 3.5 %collective-permute-done.19.refs_3_ = f32[21,16,128]{2,1,0:T(8,128)S(1)} collective-permute-done((f32[21,16,128]{2,1,0:T(8,128)}, f32[21,16,128]{2,1,0:T(8,128)S(1)}, u32[]{:S(2)}, u32[]{:S(2)}) %collective-permute-start.19) | collective-permute-done | bytes 172064 | tf_op jit(solution)/shard_map/ppermute | solution.py:459
  76.6 2.2 %collective-permute-done.23.refs_7_ = f32[21,16,128]{2,1,0:T(8,128)} collective-permute-done((f32[21,16,128]{2,1,0:T(8,128)}, f32[21,16,128]{2,1,0:T(8,128)}, u32[]{:S(2)}, u32[]{:S(2)}) %collective-permute-start.23) | collective-permute-done | bytes 172064 | tf_op jit(solution)/shard_map/ppermute | solution.py:459
  78.8 2.8 %shard_map.70 = (bf16[20,128,256]{2,1,0:T(8,128)(2,1)}, s32[8,128]{1,0:T(8,128)S(1)}) custom-call(f32[21,16,128]{2,1,0:T(8,128)S(1)} %get-tuple-element.145.refs_0_, f32[21,16,128]{2,1,0:T(8,128)S(1)} %collective-permute-done.17.refs_1_, f32[21,16,128]{2,1,0:T(8,128)S(1)} %collective-permute-done.18.refs_2_, ...), custom_call_target="tpu_custom_call" | custom-call | tf_op jit(solution)/shard_map/pallas_call | solution.py:359
  82.9 5.5 %all-to-all-done.2.left_ref = f32[32,20,4,128]{3,2,1,0:T(4,128)S(1)} async-done(((f32[32,20,4,128]{3,2,1,0:T(4,128)}), f32[32,20,4,128]{3,2,1,0:T(4,128)S(1)}, u32[]{:S(2)}, u32[]{:S(2)}) %all-to-all-start.2) | async-done | bytes 1310752 | tf_op jit(solution)/shard_map/all_to_all | solution.py:485
  88.4 5.3 %shard_map.71 = f32[12,128,128]{2,1,0:T(8,128)} custom-call(s32[2]{0:T(128)S(1)} %pad_add_fusion.1.scalars, s32[16,128]{1,0:T(8,128)S(1)} %get-tuple-element.135.codes, s32[8,128]{1,0:T(8,128)S(1)} %get-tuple-element.154.counts, f32[32,20,4,128]{3,2,1,0:T(4,128)S(1)} %all-to-all-done.2.left_ref, bf16[20,128,256]{2,1,0:T(8,128)(2,1)} %get-tuple-element.156.rights_ref), custom_call_target="tpu_custom_call" | custom-call | tf_op jit(solution)/shard_map/pallas_call | solution.py:437
  (41 shorter events, 11.6 us)
Async XLA Ops:
  0.9 1.2 %collective-permute-start.7 = (f32[4,128]{1,0:T(4,128)S(1)}, f32[4,128]{1,0:T(4,128)S(1)}, u32[]{:S(2)}, u32[]{:S(2)}) collective-permute-start(f32[4,128]{1,0:T(4,128)S(1)} %get-tuple-element.122), channel_id=1, source_target_pairs={{0,32},{32,0},{64,96},{96,64},{128,160},{160,128},{192,224},{224,1... | collective-permute-start | bytes 6152 | tf_op jit(solution)/shard_map/ppermute | solution.py:464
  2.1 3.6 %collective-permute-start.8 = (f32[4,128]{1,0:T(4,128)S(1)}, f32[4,128]{1,0:T(4,128)S(1)}, u32[]{:S(2)}, u32[]{:S(2)}) collective-permute-start(f32[4,128]{1,0:T(4,128)S(1)} %add.9), channel_id=1, source_target_pairs={{0,64},{32,96},{64,0},{96,32},{128,192},{160,224},{192,128},{224,1... | collective-permute-start | bytes 6152 | tf_op jit(solution)/shard_map/ppermute | solution.py:464
  5.7 5.2 %collective-permute-start.9 = (f32[4,128]{1,0:T(4,128)S(1)}, f32[4,128]{1,0:T(4,128)S(1)}, u32[]{:S(2)}, u32[]{:S(2)}) collective-permute-start(f32[4,128]{1,0:T(4,128)S(1)} %add.10.one_ref), channel_id=1, source_target_pairs={{0,192},{32,224},{64,128},{96,160},{128,64},{160,96},{192,0},{224,... | collective-permute-start | bytes 6152 | tf_op jit(solution)/shard_map/ppermute | solution.py:464
  11.6 34.1 %all-to-all-start.1 = ((f32[32,13,4,128]{3,2,1,0:T(4,128)}), f32[32,13,4,128]{3,2,1,0:T(4,128)S(1)}, u32[]{:S(2)}, u32[]{:S(2)}) async-start(f32[32,13,4,128]{3,2,1,0:T(4,128)} %get-tuple-element.124), calls=%async_computation.1 | async-start | bytes 1703936 | tf_op jit(solution)/shard_map/all_to_all | solution.py:479
  25.0 7.1 %collective-permute-start.10 = (f32[12,16,128]{2,1,0:T(8,128)S(1)}, f32[12,16,128]{2,1,0:T(8,128)S(1)}, u32[]{:S(2)}, u32[]{:S(2)}) collective-permute-start(f32[12,16,128]{2,1,0:T(8,128)S(1)} %get-tuple-element.126), channel_id=1, source_target_pairs={{0,32},{32,64},{64,96},{96,128},{128,160},{160,192},{192,224},{224... | collective-permute-start | bytes 294920 | tf_op jit(solution)/shard_map/ppermute | solution.py:459
  25.0 7.2 %collective-permute-start.11 = (f32[12,16,128]{2,1,0:T(8,128)S(1)}, f32[12,16,128]{2,1,0:T(8,128)S(1)}, u32[]{:S(2)}, u32[]{:S(2)}) collective-permute-start(f32[12,16,128]{2,1,0:T(8,128)S(1)} %get-tuple-element.127), channel_id=1, source_target_pairs={{0,64},{32,96},{64,128},{96,160},{128,192},{160,224},{192,0},{224,... | collective-permute-start | bytes 294920 | tf_op jit(solution)/shard_map/ppermute | solution.py:459
  25.2 10.6 %collective-permute-start.12 = (f32[12,16,128]{2,1,0:T(8,128)S(1)}, f32[12,16,128]{2,1,0:T(8,128)S(1)}, u32[]{:S(2)}, u32[]{:S(2)}) collective-permute-start(f32[12,16,128]{2,1,0:T(8,128)S(1)} %get-tuple-element.128), channel_id=1, source_target_pairs={{0,96},{32,128},{64,160},{96,192},{128,224},{160,0},{192,32},{224,... | collective-permute-start | bytes 294920 | tf_op jit(solution)/shard_map/ppermute | solution.py:459
  28.5 8.4 %collective-permute-start.13 = (f32[12,16,128]{2,1,0:T(8,128)S(1)}, f32[12,16,128]{2,1,0:T(8,128)S(1)}, u32[]{:S(2)}, u32[]{:S(2)}) collective-permute-start(f32[12,16,128]{2,1,0:T(8,128)S(1)} %get-tuple-element.129), channel_id=1, source_target_pairs={{0,128},{32,160},{64,192},{96,224},{128,0},{160,32},{192,64},{224,... | collective-permute-start | bytes 294920 | tf_op jit(solution)/shard_map/ppermute | solution.py:459
  29.5 7.4 %collective-permute-start.14 = (f32[12,16,128]{2,1,0:T(8,128)S(1)}, f32[12,16,128]{2,1,0:T(8,128)S(1)}, u32[]{:S(2)}, u32[]{:S(2)}) collective-permute-start(f32[12,16,128]{2,1,0:T(8,128)S(1)} %get-tuple-element.130), channel_id=1, source_target_pairs={{0,160},{32,192},{64,224},{96,0},{128,32},{160,64},{192,96},{224,1... | collective-permute-start | bytes 294920 | tf_op jit(solution)/shard_map/ppermute | solution.py:459
  32.1 18.7 %copy-start.1 = (f32[12,16,128]{2,1,0:T(8,128)}, f32[12,16,128]{2,1,0:T(8,128)S(1)}, u32[]{:S(2)}) copy-start(f32[12,16,128]{2,1,0:T(8,128)S(1)} %collective-permute-done.10.refs_1_) | copy-start | bytes 294916
  32.1 5.4 %collective-permute-start.15 = (f32[12,16,128]{2,1,0:T(8,128)S(1)}, f32[12,16,128]{2,1,0:T(8,128)S(1)}, u32[]{:S(2)}, u32[]{:S(2)}) collective-permute-start(f32[12,16,128]{2,1,0:T(8,128)S(1)} %get-tuple-element.131), channel_id=1, source_target_pairs={{0,192},{32,224},{64,0},{96,32},{128,64},{160,96},{192,128},{224,1... | collective-permute-start | bytes 294920 | tf_op jit(solution)/shard_map/ppermute | solution.py:459
  32.3 18.5 %copy-start.2 = (f32[12,16,128]{2,1,0:T(8,128)}, f32[12,16,128]{2,1,0:T(8,128)S(1)}, u32[]{:S(2)}) copy-start(f32[12,16,128]{2,1,0:T(8,128)S(1)} %collective-permute-done.11.refs_2_) | copy-start | bytes 294916
  32.3 5.6 %collective-permute-start.16 = (f32[12,16,128]{2,1,0:T(8,128)S(1)}, f32[12,16,128]{2,1,0:T(8,128)S(1)}, u32[]{:S(2)}, u32[]{:S(2)}) collective-permute-start(f32[12,16,128]{2,1,0:T(8,128)S(1)} %get-tuple-element.132), channel_id=1, source_target_pairs={{0,224},{32,0},{64,32},{96,64},{128,96},{160,128},{192,160},{224,1... | collective-permute-start | bytes 294920 | tf_op jit(solution)/shard_map/ppermute | solution.py:459
  35.8 15.0 %copy-start.3 = (f32[12,16,128]{2,1,0:T(8,128)}, f32[12,16,128]{2,1,0:T(8,128)S(1)}, u32[]{:S(2)}) copy-start(f32[12,16,128]{2,1,0:T(8,128)S(1)} %collective-permute-done.12.refs_3_) | copy-start | bytes 294916
  36.9 13.9 %copy-start.4 = (f32[12,16,128]{2,1,0:T(8,128)}, f32[12,16,128]{2,1,0:T(8,128)S(1)}, u32[]{:S(2)}) copy-start(f32[12,16,128]{2,1,0:T(8,128)S(1)} %collective-permute-done.13.refs_4_) | copy-start | bytes 294916
  36.9 13.9 %copy-start.5 = (f32[12,16,128]{2,1,0:T(8,128)}, f32[12,16,128]{2,1,0:T(8,128)S(1)}, u32[]{:S(2)}) copy-start(f32[12,16,128]{2,1,0:T(8,128)S(1)} %collective-permute-done.14.refs_5_) | copy-start | bytes 294916
  50.8 37.5 %all-to-all-start.2 = ((f32[32,20,4,128]{3,2,1,0:T(4,128)}), f32[32,20,4,128]{3,2,1,0:T(4,128)S(1)}, u32[]{:S(2)}, u32[]{:S(2)}) async-start(f32[32,20,4,128]{3,2,1,0:T(4,128)} %get-tuple-element.155), calls=%async_computation.2 | async-start | bytes 2621440 | tf_op jit(solution)/shard_map/all_to_all | solution.py:485
  59.6 7.3 %collective-permute-start.17 = (f32[21,16,128]{2,1,0:T(8,128)S(1)}, f32[21,16,128]{2,1,0:T(8,128)S(1)}, u32[]{:S(2)}, u32[]{:S(2)}) collective-permute-start(f32[21,16,128]{2,1,0:T(8,128)S(1)} %get-tuple-element.146), channel_id=1, source_target_pairs={{0,32},{32,64},{64,96},{96,128},{128,160},{160,192},{192,224},{224... | collective-permute-start | bytes 516104 | tf_op jit(solution)/shard_map/ppermute | solution.py:459
  59.6 8.4 %collective-permute-start.18 = (f32[21,16,128]{2,1,0:T(8,128)S(1)}, f32[21,16,128]{2,1,0:T(8,128)S(1)}, u32[]{:S(2)}, u32[]{:S(2)}) collective-permute-start(f32[21,16,128]{2,1,0:T(8,128)S(1)} %get-tuple-element.147), channel_id=1, source_target_pairs={{0,64},{32,96},{64,128},{96,160},{128,192},{160,224},{192,0},{224,... | collective-permute-start | bytes 516104 | tf_op jit(solution)/shard_map/ppermute | solution.py:459
  59.7 14.4 %collective-permute-start.19 = (f32[21,16,128]{2,1,0:T(8,128)}, f32[21,16,128]{2,1,0:T(8,128)S(1)}, u32[]{:S(2)}, u32[]{:S(2)}) collective-permute-start(f32[21,16,128]{2,1,0:T(8,128)} %get-tuple-element.148), channel_id=1, source_target_pairs={{0,96},{32,128},{64,160},{96,192},{128,224},{160,0},{192,32},{224,... | collective-permute-start | bytes 516104 | tf_op jit(solution)/shard_map/ppermute | solution.py:459
  62.0 13.3 %collective-permute-start.20 = (f32[21,16,128]{2,1,0:T(8,128)}, f32[21,16,128]{2,1,0:T(8,128)S(1)}, u32[]{:S(2)}, u32[]{:S(2)}) collective-permute-start(f32[21,16,128]{2,1,0:T(8,128)} %get-tuple-element.149), channel_id=1, source_target_pairs={{0,128},{32,160},{64,192},{96,224},{128,0},{160,32},{192,64},{224,... | collective-permute-start | bytes 516104 | tf_op jit(solution)/shard_map/ppermute | solution.py:459
  64.1 11.4 %collective-permute-start.21 = (f32[21,16,128]{2,1,0:T(8,128)}, f32[21,16,128]{2,1,0:T(8,128)S(1)}, u32[]{:S(2)}, u32[]{:S(2)}) collective-permute-start(f32[21,16,128]{2,1,0:T(8,128)} %get-tuple-element.150), channel_id=1, source_target_pairs={{0,160},{32,192},{64,224},{96,0},{128,32},{160,64},{192,96},{224,1... | collective-permute-start | bytes 516104 | tf_op jit(solution)/shard_map/ppermute | solution.py:459
  67.0 9.6 %collective-permute-start.22 = (f32[21,16,128]{2,1,0:T(8,128)}, f32[21,16,128]{2,1,0:T(8,128)S(1)}, u32[]{:S(2)}, u32[]{:S(2)}) collective-permute-start(f32[21,16,128]{2,1,0:T(8,128)} %get-tuple-element.151), channel_id=1, source_target_pairs={{0,192},{32,224},{64,0},{96,32},{128,64},{160,96},{192,128},{224,1... | collective-permute-start | bytes 516104 | tf_op jit(solution)/shard_map/ppermute | solution.py:459
  68.1 10.7 %collective-permute-start.23 = (f32[21,16,128]{2,1,0:T(8,128)}, f32[21,16,128]{2,1,0:T(8,128)}, u32[]{:S(2)}, u32[]{:S(2)}) collective-permute-start(f32[21,16,128]{2,1,0:T(8,128)} %get-tuple-element.152), channel_id=1, source_target_pairs={{0,224},{32,0},{64,32},{96,64},{128,96},{160,128},{192,160},{224,1... | collective-permute-start | bytes 516104 | tf_op jit(solution)/shard_map/ppermute | solution.py:459
  (2 other events, 26.3 us)

commit v6 on v3

--- a/solution.py
+++ b/solution.py
@@ -12,6 +12,7 @@
 SLOT_PITCH = 16
 PER_GROUP = LANES // SLOT_PITCH
 ROUND_CAP = 20
+TOGETHER = 2
 LIMIT = pltpu.CompilerParams(vmem_limit_bytes=20 * 2**20)
 HBM = pl.BlockSpec(memory_space=pltpu.HBM)
 
@@ -137,9 +138,64 @@
     )(*in_hbm(tiles))
 
 
+def list_products(by_col, by_row, targets, value_of, base, cap, values, keys, picks):
+    blocks = by_col.shape[0]
+    groups = len(targets)
+    deep = picks.shape[0] // groups
+    f32, bf16 = jnp.float32, jnp.bfloat16
+    iota = functools.partial(lax.broadcasted_iota, jnp.int32)
+    one, zero = jnp.ones((blocks, LANES), bf16), jnp.zeros((blocks, LANES), bf16)
+    tall = (iota((blocks, LANES), 0) + 1).astype(f32).astype(bf16)
+    below = jnp.where(iota((blocks, blocks), 0) >= iota((blocks, blocks), 1), 1.0, 0.0).astype(bf16)
+    lane_from, lane_to = iota((LANES, LANES), 0), iota((LANES, LANES), 1)
+    same_peer = lane_from // SLOT_PITCH == lane_to // SLOT_PITCH
+    earlier = jnp.where(same_peer & (lane_from < lane_to), 1.0, 0.0).astype(bf16)
+    together = jnp.where(same_peer, 1.0, 0.0)
+
+    everything = []
+    for group, (target_rows, target_cols) in enumerate(targets):
+        def hot(target):
+            few = jnp.broadcast_to(target, (16, LANES)).astype(bf16)
+            return jnp.where(tall == jnp.concatenate([few] * (blocks // 16), axis=0), one, zero)
+
+        left = jnp.dot(by_col, hot(target_rows), preferred_element_type=f32)
+        right = jnp.dot(by_row, hot(target_cols), preferred_element_type=f32)
+        hit = left * right > 0.0
+        ranks = jnp.dot(below, jnp.where(hit, 1.0, 0.0).astype(bf16), preferred_element_type=f32)
+        everything.append(ranks[blocks - 1:blocks, :])
+        keys[group * blocks:(group + 1) * blocks, :] = jnp.where(hit, ranks, 0.0)
+        values[group * blocks:(group + 1) * blocks, :] = value_of(left, right)
+    found = jnp.concatenate(everything + everything[-1:] * (8 - len(everything)), axis=0)
+    ahead = jnp.dot(found.astype(bf16), earlier, preferred_element_type=f32) - base.astype(f32)
+    counts = jnp.dot(found.astype(bf16), together.astype(bf16), preferred_element_type=f32)
+    picks[...] = jnp.zeros_like(picks)
+    depth = jnp.max(found).astype(jnp.int32)
+    slot_at = iota((deep, LANES), 0).astype(f32)
+
+    def one_depth(level, carry):
+        level_f = level.astype(f32)
+        for group in range(groups):
+            span = slice(group * blocks, (group + 1) * blocks)
+            value = jnp.sum(jnp.where(keys[span, :] == level_f + 1.0, values[span, :], 0.0), axis=0, keepdims=True)
+            place = jnp.where(found[group:group + 1, :] > level_f, ahead[group:group + 1, :] + level_f, -1.0)
+            span = slice(group * deep, (group + 1) * deep)
+            picks[span, :] = picks[span, :] + jnp.where(slot_at == place, value, 0.0)
+        return carry
+
+    lax.fori_loop(0, depth, one_depth, 0)
+    spread = jnp.dot(picks[...], together, precision=lax.Precision.HIGHEST, preferred_element_type=f32)
+    mine = iota((deep, LANES), 0) % SLOT_PITCH == iota((deep, LANES), 1) % SLOT_PITCH
+    lines = []
+    for group in range(groups):
+        chosen = jnp.where(mine, spread[group * deep:(group + 1) * deep, :], 0.0)
+        for half in range(pl.cdiv(cap, SLOT_PITCH)):
+            lines.append(jnp.sum(chosen[half * SLOT_PITCH:(half + 1) * SLOT_PITCH, :], axis=0, keepdims=True))
+    return lines, counts
+
+
 def plan_body(
-    rows, base_ref, strips_ref, mates_ref,
-    send_ref, codes_ref, counts_ref, peak_ref,
+    rows, base_ref, strips_ref,
+    send_ref, codes_ref, counts_ref, peak_ref, by_col_ref, by_row_ref,
     table, values, keys, picks, places_vmem, send, places, sem, send_sems,
 ):
     row_index, base = lax.axis_index("row"), base_ref[0]
@@ -149,13 +205,10 @@
     blocks = peers * band
     band_rows = blocks // rows
     groups = peers // PER_GROUP
-    deep = picks.shape[0] // (groups + 1)
     halves = pl.cdiv(cap, SLOT_PITCH)
     f32, bf16 = jnp.float32, jnp.bfloat16
     iota = functools.partial(lax.broadcasted_iota, jnp.int32)
 
-    one, zero = jnp.ones((blocks, LANES), bf16), jnp.zeros((blocks, LANES), bf16)
-    tall = (iota((blocks, LANES), 0) + 1).astype(f32).astype(bf16)
     in_band = iota((band_rows, LANES), 0).astype(f32)
     band_start = (iota((1, LANES), 1) // SLOT_PITCH * band_rows + 1).astype(f32)
     band_mask = jnp.where(iota((blocks, LANES), 0) // band_rows == iota((blocks, LANES), 1) // SLOT_PITCH, 1.0, 0.0)
@@ -178,83 +231,34 @@
     by_col = table[...]
     by_row = by_col.T.astype(bf16)
     by_col = by_col.astype(bf16)
-
-    below = jnp.where(iota((blocks, blocks), 0) >= iota((blocks, blocks), 1), 1.0, 0.0).astype(bf16)
-    lane_from, lane_to = iota((LANES, LANES), 0), iota((LANES, LANES), 1)
-    same_peer = lane_from // SLOT_PITCH == lane_to // SLOT_PITCH
-    earlier = jnp.where(same_peer & (lane_from < lane_to), 1.0, 0.0).astype(bf16)
-    together = jnp.where(same_peer, 1.0, 0.0)
+    by_col_ref[...] = by_col
+    by_row_ref[...] = by_row
+
     fixed = iota((blocks, LANES), 0) // band * per_peer + ((iota((blocks, LANES), 1) % SLOT_PITCH) << 16)
     fixed = (fixed - (SLOT_PITCH * row_index + 1 + 512)).astype(f32)
-
-    targets = [(meta[2:3, :], meta[3:4, :]) for meta in targets]
-    targets.append((mates_ref[2:3, :], mates_ref[3:4, :]))
-    everything = []
-    for group, (target_rows, target_cols) in enumerate(targets):
-        def hot(target):
-            few = jnp.broadcast_to(target, (16, LANES)).astype(bf16)
-            return jnp.where(tall == jnp.concatenate([few] * (blocks // 16), axis=0), one, zero)
-
-        left = jnp.dot(by_col, hot(target_rows), preferred_element_type=f32)
-        right = jnp.dot(by_row, hot(target_cols), preferred_element_type=f32)
-        hit = left * right > 0.0
-        ranks = jnp.dot(below, jnp.where(hit, 1.0, 0.0).astype(bf16), preferred_element_type=f32)
-        everything.append(ranks[blocks - 1:blocks, :])
-        keys[group * blocks:(group + 1) * blocks, :] = jnp.where(hit, ranks, 0.0)
-        if group < groups:
-            value = fixed + left + right * 512.0
-        else:
-            name = right.astype(jnp.int32) - 1
-            value = (name - (SLOT_PITCH - per_peer + 1) * (name >> 4)).astype(f32)
-        values[group * blocks:(group + 1) * blocks, :] = value
-    found = jnp.concatenate(everything + everything[-1:] * (8 - len(everything)), axis=0)
-    ahead = jnp.dot(found.astype(bf16), earlier, preferred_element_type=f32) - base.astype(f32)
-    counts = jnp.dot(found.astype(bf16), together.astype(bf16), preferred_element_type=f32)
-    counts_ref[...] = counts.astype(jnp.int32)
-    peak_ref[...] = jnp.broadcast_to(jnp.max(jnp.max(counts[0:groups, :], axis=0, keepdims=True), axis=1, keepdims=True), (8, LANES))
-    picks[...] = jnp.zeros_like(picks)
-    depth = jnp.max(found).astype(jnp.int32)
-    slot_at = iota((deep, LANES), 0).astype(f32)
-
-    def one_depth(level, carry):
-        level_f = level.astype(f32)
-        for group in range(groups + 1):
-            span = slice(group * blocks, (group + 1) * blocks)
-            value = jnp.sum(jnp.where(keys[span, :] == level_f + 1.0, values[span, :], 0.0), axis=0, keepdims=True)
-            place = jnp.where(found[group:group + 1, :] > level_f, ahead[group:group + 1, :] + level_f, -1.0)
-            span = slice(group * deep, (group + 1) * deep)
-            picks[span, :] = picks[span, :] + jnp.where(slot_at == place, value, 0.0)
-        return carry
-
-    lax.fori_loop(0, depth, one_depth, 0)
-    spread = jnp.dot(picks[...], together, precision=lax.Precision.HIGHEST, preferred_element_type=f32)
-    mine = iota((deep, LANES), 0) % SLOT_PITCH == iota((deep, LANES), 1) % SLOT_PITCH
-    lines = []
-    for group in range(groups + 1):
-        chosen = jnp.where(mine, spread[group * deep:(group + 1) * deep, :], 0.0)
-        for half in range(halves):
-            lines.append(jnp.sum(chosen[half * SLOT_PITCH:(half + 1) * SLOT_PITCH, :], axis=0, keepdims=True))
-    lines += lines[-1:] * (codes_ref.shape[0] - len(lines))
+    lines, counts = list_products(
+        by_col, by_row, [(meta[2:3, :], meta[3:4, :]) for meta in targets],
+        lambda left, right: fixed + left + right * 512.0, base, cap, values, keys, picks,
+    )
     codes = jnp.concatenate(lines, axis=0).astype(jnp.int32)
-    codes_ref[...] = codes
     places_vmem[...] = codes & 511
     copy = pltpu.make_async_copy(places_vmem, places, sem)
     copy.start()
+    codes_ref[...] = codes
+    counts_ref[...] = counts.astype(jnp.int32)
+    longest = jnp.max(jnp.max(counts[0:groups, :], axis=0, keepdims=True), axis=1, keepdims=True)
+    peak_ref[...] = jnp.broadcast_to(longest, (8, LANES))
     copy.wait()
 
     def one_group(group):
         part = pl.ds(group * PER_GROUP, PER_GROUP)
         return pltpu.make_async_copy(send.at[part], send_ref.at[part], send_sems.at[group])
 
-    def one_peer(peer, carry):
-        line = (peer >> 3) * halves
-        first = (peer & (PER_GROUP - 1)) * SLOT_PITCH
-        for at in range(cap):
-            send[peer, at] = strips_ref[places[line + at // SLOT_PITCH, first + at % SLOT_PITCH]]
-        return carry
-
     for group in range(groups):
-        lax.fori_loop(group * PER_GROUP, (group + 1) * PER_GROUP, one_peer, 0)
+        for peer in range(group * PER_GROUP, (group + 1) * PER_GROUP):
+            line, first = group * halves, peer % PER_GROUP * SLOT_PITCH
+            for at in range(cap):
+                send[peer, at] = strips_ref[places[line + at // SLOT_PITCH, first + at % SLOT_PITCH]]
         one_group(group).start()
     for group in range(groups):
         one_group(group).wait()
@@ -264,25 +268,31 @@
     return pl.BlockSpec(shape, lambda i, *_: (0,) * len(shape))
 
 
-def plan(strips, mates, base, rows, peers, cap):
+def list_scratch(groups, blocks, cap):
+    lists = pltpu.VMEM((groups * blocks, LANES), jnp.float32)
+    return [lists, lists, pltpu.VMEM((groups * padded(cap, 8), LANES), jnp.float32)]
+
+
+def plan(strips, base, rows, peers, cap):
     strip, order = strips.shape[1:]
     groups = peers // PER_GROUP
-    lines = padded((groups + 1) * pl.cdiv(cap, SLOT_PITCH), 8)
+    lines = groups * pl.cdiv(cap, SLOT_PITCH)
     send = (peers, cap, strip, order)
     blocks = peers * 8
-    shapes = [(send, jnp.float32), ((lines, LANES), jnp.int32), ((8, LANES), jnp.int32), ((8, LANES), jnp.float32)]
+    shapes = [
+        (send, jnp.float32), ((lines, LANES), jnp.int32), ((8, LANES), jnp.int32), ((8, LANES), jnp.float32),
+        ((blocks, blocks), jnp.bfloat16), ((blocks, blocks), jnp.bfloat16),
+    ]
     return pl.pallas_call(
         functools.partial(plan_body, rows),
         grid_spec=pltpu.PrefetchScalarGridSpec(
             num_scalar_prefetch=1,
             grid=(1,),
-            in_specs=[whole(strips.shape), whole(mates.shape)],
+            in_specs=[whole(strips.shape)],
             out_specs=[HBM] + [whole(shape) for shape, _ in shapes[1:]],
             scratch_shapes=[
                 pltpu.VMEM((blocks, blocks), jnp.float32),
-                pltpu.VMEM(((groups + 1) * blocks, LANES), jnp.float32),
-                pltpu.VMEM(((groups + 1) * blocks, LANES), jnp.float32),
-                pltpu.VMEM(((groups + 1) * padded(cap, 8), LANES), jnp.float32),
+                *list_scratch(groups, blocks, cap),
                 pltpu.VMEM((lines, LANES), jnp.int32),
                 pltpu.VMEM(send, jnp.float32),
                 pltpu.SMEM((lines, LANES), jnp.int32),
@@ -292,71 +302,92 @@
         ),
         out_shape=[pltpu.HBM(*shapes[0])] + [jax.ShapeDtypeStruct(*shape) for shape in shapes[1:]],
         compiler_params=LIMIT,
-    )(base.reshape(1), pltpu.with_memory_space_constraint(strips, pltpu.VMEM), mates)
-
-
-def collect_body(rows, first_line, codes, peak_ref, *refs):
-    piece_refs, right_refs, panel = refs[:rows], refs[rows:2 * rows], refs[2 * rows]
+    )(base.reshape(1), pltpu.with_memory_space_constraint(strips, pltpu.VMEM))
+
+
+def collect_body(rows, base_ref, by_col_ref, by_row_ref, mates_ref, peak_ref, *refs):
+    piece_refs, right_refs = refs[:rows], refs[rows:2 * rows]
+    values, keys, picks, places_vmem, panel, places, sem = refs[2 * rows:]
     row_index = lax.axis_index("row")
     count, strip, _ = piece_refs[0].shape
     cap = right_refs[0].shape[0] - 1
+
+    def place_of(left, right):
+        name = right.astype(jnp.int32) - 1
+        return (name - (SLOT_PITCH - count) * (name >> 4)).astype(jnp.float32)
+
+    lines, _ = list_products(
+        by_col_ref[...], by_row_ref[...], [(mates_ref[2:3, :], mates_ref[3:4, :])],
+        place_of, base_ref[0], cap, values, keys, picks,
+    )
+    lines += lines[-1:] * (places_vmem.shape[0] - len(lines))
+    places_vmem[...] = jnp.concatenate(lines, axis=0).astype(jnp.int32)
+    copy = pltpu.make_async_copy(places_vmem, places, sem)
+    copy.start()
     for away, piece_ref in enumerate(piece_refs):
         start = (row_index + rows - away) % rows * count
         for tile in range(count):
             panel[start + tile] = piece_ref[tile]
+    copy.wait()
     for away, right_ref in enumerate(right_refs):
         lane = (row_index + away) % rows * SLOT_PITCH
         for at in range(cap):
-            right_ref[at] = panel[codes[first_line + at // SLOT_PITCH, lane + at % SLOT_PITCH]]
+            right_ref[at] = panel[places[at // SLOT_PITCH, lane + at % SLOT_PITCH]]
         right_ref[cap, 0:8, :] = peak_ref[...]
         right_ref[cap, 8:16, :] = peak_ref[...]
 
 
-def collect(codes, peak, pieces, peers, cap):
+def collect(tables, mates, peak, pieces, base, cap):
     rows = len(pieces)
     count, strip, order = pieces[0].shape
     right = (cap + 1, strip, order)
-    return pl.pallas_call(
-        functools.partial(collect_body, rows, peers // PER_GROUP * pl.cdiv(cap, SLOT_PITCH)),
+    operands = (*tables, mates, peak, *pieces)
+    return pl.pallas_call(
+        functools.partial(collect_body, rows),
         grid_spec=pltpu.PrefetchScalarGridSpec(
             num_scalar_prefetch=1,
             grid=(1,),
-            in_specs=[whole(operand.shape) for operand in (peak, *pieces)],
+            in_specs=[whole(operand.shape) for operand in operands],
             out_specs=[whole(right)] * rows,
-            scratch_shapes=[pltpu.VMEM((rows * count, strip, order), jnp.float32)],
+            scratch_shapes=[
+                *list_scratch(1, tables[0].shape[0], cap),
+                pltpu.VMEM((8, LANES), jnp.int32),
+                pltpu.VMEM((rows * count, strip, order), jnp.float32),
+                pltpu.SMEM((8, LANES), jnp.int32),
+                pltpu.SemaphoreType.DMA,
+            ],
         ),
         out_shape=[jax.ShapeDtypeStruct(right, jnp.float32)] * rows,
         compiler_params=LIMIT,
-    )(codes, peak, *in_hbm(*pieces))
-
-
-def product_body(first, rows, base_ref, codes, counts, left_ref, *refs):
+    )(base.reshape(1), *tables, mates, peak, *in_hbm(*pieces))
+
+
+def peak_body(*refs):
+    *right_refs, most_ref = refs
+    cap = right_refs[0].shape[0] - 1
+    most = right_refs[0][cap, 0:8, :]
+    for right_ref in right_refs[1:]:
+        most = jnp.maximum(most, right_ref[cap, 0:8, :])
+    most_ref[...] = most.astype(jnp.int32)
+
+
+def product_body(first, rows, scalars, codes, counts, left_ref, *refs):
     right_refs, refs = refs[:rows], refs[rows:]
-    if first:
-        out_ref, most_ref, left, right = refs
-        out_ref[...] = jnp.zeros_like(out_ref)
-    else:
-        running_ref, out_ref, most_ref, left, right = refs
-        out_ref[...] = running_ref[...]
-    row_index, own, base = lax.axis_index("row"), lax.axis_index(GROUP), base_ref[0]
+    out_ref, right = refs[-2:]
+    out_ref[...] = jnp.zeros_like(out_ref) if first else refs[0][...]
+    row_index, own, base = lax.axis_index("row"), lax.axis_index(GROUP), scalars[0]
     peers, cap, strip, order = left_ref.shape
     tall_strip = right_refs[0].shape[1]
     line = (own >> 3) * pl.cdiv(cap, SLOT_PITCH)
     lane = (own & (PER_GROUP - 1)) * SLOT_PITCH
     todo = jnp.clip(counts[own >> 3, lane] - base, 0, cap)
-    most = right_refs[0][cap, 0:8, :]
-    for right_ref in right_refs[1:]:
-        most = jnp.maximum(most, right_ref[cap, 0:8, :])
-    most_ref[...] = most.astype(jnp.int32)
     bf16 = jnp.bfloat16
 
     def product(at, half):
-        for peer in range(peers):
-            left[half, peer * strip:(peer + 1) * strip, :] = left_ref[peer, at]
         for away, right_ref in enumerate(right_refs):
             start = pl.multiple_of((row_index + rows - away) % rows * tall_strip, tall_strip)
             right[half, pl.ds(start, tall_strip), :] = right_ref[at]
-        a, b = left[half], right[half]
+        a, b = jnp.concatenate([left_ref[peer, at] for peer in range(peers)], axis=0), right[half]
         a_high, b_high = a.astype(bf16), b.astype(bf16)
         a_low = (a - a_high.astype(jnp.float32)).astype(bf16)
         b_low = (b - b_high.astype(jnp.float32)).astype(bf16)
@@ -371,37 +402,41 @@
     def target(at):
         return codes[line + (at >> 4), lane + (at & (SLOT_PITCH - 1))] >> 16
 
-    def two(pair, carry):
-        at = 2 * pair
-        one, other = product(at, 0), product(at + 1, 1)
-        out_ref[target(at)] += one
-
-        @pl.when(at + 1 < todo)
-        def _():
-            out_ref[target(at + 1)] += other
+    def several(step, carry):
+        at = TOGETHER * step
+        sums = [product(at + n, n) for n in range(TOGETHER)]
+        out_ref[target(at)] += sums[0]
+        for n in range(1, TOGETHER):
+            @pl.when(at + n < todo)
+            def _():
+                out_ref[target(at + n)] += sums[n]
 
         return carry
 
-    lax.fori_loop(0, (todo + 1) >> 1, two, 0)
+    lax.fori_loop(0, (todo + TOGETHER - 1) // TOGETHER, several, 0)
 
 
 def multiply_round(left, right, codes, counts, base, running, kept):
     order = left.shape[-1]
     first = running is None
     tiles = (kept, order, order)
-    operands = [pltpu.with_memory_space_constraint(left, pltpu.VMEM), *right] + ([] if first else [running])
-    return pl.pallas_call(
+    most = pl.pallas_call(
+        peak_body, out_shape=jax.ShapeDtypeStruct((8, LANES), jnp.int32), compiler_params=LIMIT
+    )(*right)[0, 0]
+    operands = [pltpu.with_memory_space_constraint(x, pltpu.VMEM) for x in (left, *right)] + ([] if first else [running])
+    summed = pl.pallas_call(
         functools.partial(product_body, first, len(right)),
         grid_spec=pltpu.PrefetchScalarGridSpec(
             num_scalar_prefetch=3,
             grid=(1,),
             in_specs=[whole(operand.shape) for operand in operands],
-            out_specs=[whole(tiles), whole((8, LANES))],
-            scratch_shapes=[pltpu.VMEM((2, order, order), jnp.float32)] * 2,
+            out_specs=whole(tiles),
+            scratch_shapes=[pltpu.VMEM((TOGETHER, order, order), jnp.float32)],
         ),
-        out_shape=[jax.ShapeDtypeStruct(tiles, jnp.float32), jax.ShapeDtypeStruct((8, LANES), jnp.int32)],
-        compiler_params=LIMIT,
-    )(base.reshape(1), codes, counts, *operands)
+        out_shape=jax.ShapeDtypeStruct(tiles, jnp.float32),
+        compiler_params=LIMIT,
+    )(jnp.stack([base, most]), codes, counts, *operands)
+    return summed, most
 
 
 def shift_all(pieces):
@@ -425,22 +460,22 @@
     listed, wanted = label(tile_rows, tile_cols, tile_counts, out_rows, out_cols)
     for by in (1, 2):
         listed = listed + swap_rows(listed, rows, by)
-    strips, mates = stamp(listed, swap_rows(listed, rows, 4), wanted, pack(tiles, peers))
+    strips, mates = stamp(listed, swap_rows(listed, rows, rows - 2), wanted, pack(tiles, peers))
     pieces = shift_all(pack_right(tiles, rows))
     strips = lax.all_to_all(strips, GROUP, 0, 0, tiled=True)
     strips, pieces = lax.optimization_barrier((strips, pieces))
     strips = strips.reshape(-1, order // peers, order)
 
     def one_round(base, running):
-        send, codes, counts, peak = plan(strips, mates, base, rows, peers, ROUND_CAP)
+        send, codes, counts, peak, *tables = plan(strips, base, rows, peers, ROUND_CAP)
         left = lax.all_to_all(send, GROUP, 0, 0, tiled=True)
-        right = shift_all(collect(codes, peak, pieces, peers, ROUND_CAP))
+        right = shift_all(collect(tables, mates, peak, pieces, base, ROUND_CAP))
         return multiply_round(left, right, codes, counts, base, running, kept)
 
     summed, most = one_round(jnp.zeros((), jnp.int32), None)
 
     def unfinished(state):
-        return state[0] < most[0, 0]
+        return state[0] < most
 
     def further(state):
         return state[0] + ROUND_CAP, one_round(*state)[0]

time: 96.1 us -> 93.1 us (0.969)
  waiting for transfers between devices: 34.1 us -> 31.8 us
    all_to_all x1, waiting for transfers between devices: 9.68 us -> 6.81 us  [one_round(): left = lax.all_to_all(send, GROUP, 0, 0, tiled=True)]
    pallas_call x1, Pallas kernels: 5.99 us -> 4.37 us  [plan(): pl.pallas_call(functools.partial(plan_body, rows), grid_spec=pltpu.Prefet...]
    pallas_call x1 -> x2, Pallas kernels: 3.09 us -> 4.66 us  [the longest x1 3.73 us: collect(): pl.pallas_call(functools.partial(collect_body, rows), grid_spec=pltpu.Pre...]
  transfers between devices with their start and end apart: 19 -> 19, of which waited for: 14 -> 15; matrix products, arithmetic and copies ran while one was open for 0% -> 1% of each run, Pallas kernels for 7% -> 9%
where the time goes in v6:
time: 93.1 us; the launch traced here: 92.7 us
  starting transfers between devices  40 us (43%)
  waiting for transfers between devices  31.8 us (34%)
  Pallas kernels  18.8 us (20%)
    ppermute x14, starting transfers between devices, shift_all(): lax.ppermute(pieces[by], 'row', [(i, (i + by) % rows) for i in range(rows)])  18 us
    ppermute x14, waiting for transfers between devices, shift_all(): lax.ppermute(pieces[by], 'row', [(i, (i + by) % rows) for i in range(rows)])  14 us
    all_to_all x1, starting transfers between devices, local(): strips = lax.all_to_all(strips, GROUP, 0, 0, tiled=True)  11.6 us
    all_to_all x1, waiting for transfers between devices, local(): strips = lax.all_to_all(strips, GROUP, 0, 0, tiled=True)  7.9 us
    all_to_all x1, waiting for transfers between devices, one_round(): left = lax.all_to_all(send, GROUP, 0, 0, tiled=True)  6.81 us
    all_to_all x1, starting transfers between devices, one_round(): left = lax.all_to_all(send, GROUP, 0, 0, tiled=True)  5.71 us
    ppermute x3, starting transfers between devices, swap_rows(): return lax.ppermute(array, 'row', [(i, i ^ by) for i in range(rows)])  4.68 us
    pallas_call x1, Pallas kernels, plan(): pl.pallas_call(functools.partial(plan_body, rows), grid_spec=pltpu.Prefet...  4.37 us
  transfers between devices with their start and end apart: 19, of which 15 were waited for; matrix products, arithmetic and copies ran while one was open for 1% of the time, Pallas kernels for 9%

profile of v6, /device:TPU:4, one launch (start us, length us, event | category | flops | bytes accessed | tf_op | source)
XLA Modules:
  0.0 92.7 jit_solution(6114338968202604697)
XLA Ops:
  2.1 1.6 %collective-permute-start.8 = (f32[4,128]{1,0:T(4,128)S(1)}, f32[4,128]{1,0:T(4,128)S(1)}, u32[]{:S(2)}, u32[]{:S(2)}) collective-permute-start(f32[4,128]{1,0:T(4,128)S(1)} %add.9), channel_id=1, source_target_pairs={{0,64},{32,96},{64,0},{96,32},{128,192},{160,224},{192,128},{224,1... | collective-permute-start | bytes 6152 | tf_op jit(solution)/shard_map/ppermute | solution.py:450
  3.7 2.0 %collective-permute-done.8 = f32[4,128]{1,0:T(4,128)S(1)} collective-permute-done((f32[4,128]{1,0:T(4,128)S(1)}, f32[4,128]{1,0:T(4,128)S(1)}, u32[]{:S(2)}, u32[]{:S(2)}) %collective-permute-start.8) | collective-permute-done | bytes 2080 | tf_op jit(solution)/shard_map/ppermute | solution.py:450
  5.7 3.0 %collective-permute-start.9 = (f32[4,128]{1,0:T(4,128)S(1)}, f32[4,128]{1,0:T(4,128)S(1)}, u32[]{:S(2)}, u32[]{:S(2)}) collective-permute-start(f32[4,128]{1,0:T(4,128)S(1)} %add.10.one_ref), channel_id=1, source_target_pairs={{0,192},{32,224},{64,128},{96,160},{128,64},{160,96},{192,0},{224,... | collective-permute-start | bytes 6152 | tf_op jit(solution)/shard_map/ppermute | solution.py:450
  8.7 2.2 %shard_map.65.strips_in = f32[32,13,4,128]{3,2,1,0:T(4,128)} custom-call(f32[12,128,128]{2,1,0:T(8,128)} %bitcast.13), custom_call_target="tpu_custom_call" | custom-call | tf_op jit(solution)/shard_map/pallas_call | solution.py:89
  11.6 11.6 %all-to-all-start.1 = ((f32[32,13,4,128]{3,2,1,0:T(4,128)}), f32[32,13,4,128]{3,2,1,0:T(4,128)S(1)}, u32[]{:S(2)}, u32[]{:S(2)}) async-start(f32[32,13,4,128]{3,2,1,0:T(4,128)} %get-tuple-element.124), calls=%async_computation.1 | async-start | bytes 1703936 | tf_op jit(solution)/shard_map/all_to_all | solution.py:465
  23.2 1.8 %shard_map.67 = (f32[12,16,128]{2,1,0:T(8,128)}, f32[12,16,128]{2,1,0:T(8,128)S(1)}, f32[12,16,128]{2,1,0:T(8,128)S(1)}, f32[12,16,128]{2,1,0:T(8,128)S(1)}, f32...) custom-call(f32[12,128,128]{2,1,0:T(8,128)} %bitcast.14), custom_call_target="tpu_custom_call" | custom-call | tf_op jit(solution)/shard_map/pallas_call | solution.py:136
  25.2 3.3 %collective-permute-start.12 = (f32[12,16,128]{2,1,0:T(8,128)S(1)}, f32[12,16,128]{2,1,0:T(8,128)}, u32[]{:S(2)}, u32[]{:S(2)}) collective-permute-start(f32[12,16,128]{2,1,0:T(8,128)S(1)} %get-tuple-element.128), channel_id=1, source_target_pairs={{0,96},{32,128},{64,160},{96,192},{128,224},{160,0},{192,32},{224,... | collective-permute-start | bytes 294920 | tf_op jit(solution)/shard_map/ppermute | solution.py:445
  29.5 2.6 %collective-permute-start.14 = (f32[12,16,128]{2,1,0:T(8,128)S(1)}, f32[12,16,128]{2,1,0:T(8,128)}, u32[]{:S(2)}, u32[]{:S(2)}) collective-permute-start(f32[12,16,128]{2,1,0:T(8,128)S(1)} %get-tuple-element.130), channel_id=1, source_target_pairs={{0,160},{32,192},{64,224},{96,0},{128,32},{160,64},{192,96},{224,1... | collective-permute-start | bytes 294920 | tf_op jit(solution)/shard_map/ppermute | solution.py:445
  32.2 1.7 %collective-permute-start.16 = (f32[12,16,128]{2,1,0:T(8,128)S(1)}, f32[12,16,128]{2,1,0:T(8,128)}, u32[]{:S(2)}, u32[]{:S(2)}) collective-permute-start(f32[12,16,128]{2,1,0:T(8,128)S(1)} %get-tuple-element.132), channel_id=1, source_target_pairs={{0,224},{32,0},{64,32},{96,64},{128,96},{160,128},{192,160},{224,1... | collective-permute-start | bytes 294920 | tf_op jit(solution)/shard_map/ppermute | solution.py:445
  34.0 1.9 %collective-permute-done.12.refs_3_ = f32[12,16,128]{2,1,0:T(8,128)} collective-permute-done((f32[12,16,128]{2,1,0:T(8,128)S(1)}, f32[12,16,128]{2,1,0:T(8,128)}, u32[]{:S(2)}, u32[]{:S(2)}) %collective-permute-start.12) | collective-permute-done | bytes 98336 | tf_op jit(solution)/shard_map/ppermute | solution.py:445
  37.8 7.9 %all-to-all-done.1 = f32[32,13,4,128]{3,2,1,0:T(4,128)S(1)} async-done(((f32[32,13,4,128]{3,2,1,0:T(4,128)}), f32[32,13,4,128]{3,2,1,0:T(4,128)S(1)}, u32[]{:S(2)}, u32[]{:S(2)}) %all-to-all-start.1) | async-done | bytes 852000 | tf_op jit(solution)/shard_map/all_to_all | solution.py:465
  45.7 4.4 %shard_map.68 = (f32[32,20,4,128]{3,2,1,0:T(4,128)}, s32[8,128]{1,0:T(8,128)S(1)}, s32[8,128]{1,0:T(8,128)S(1)}, f32[8,128]{1,0:T(8,128)S(1)}, bf16[256,256]{1,0...) custom-call(s32[1]{0:T(128)} %constant.2.clone.1.base_ref, f32[416,4,128]{2,1,0:T(4,128)S(1)} %bitcast.11), custom_call_target="tpu_custom_call" | custom-call | tf_op jit(solution)/shard_map/pallas_call | solution.py:286
  50.1 5.7 %all-to-all-start.2 = ((f32[32,20,4,128]{3,2,1,0:T(4,128)}), f32[32,20,4,128]{3,2,1,0:T(4,128)S(1)}, u32[]{:S(2)}, u32[]{:S(2)}) async-start(f32[32,20,4,128]{3,2,1,0:T(4,128)} %get-tuple-element.156), calls=%async_computation.2 | async-start | bytes 2621440 | tf_op jit(solution)/shard_map/all_to_all | solution.py:471
  55.8 3.7 %shard_map.69 = (f32[21,16,128]{2,1,0:T(8,128)S(1)}, f32[21,16,128]{2,1,0:T(8,128)S(1)}, f32[21,16,128]{2,1,0:T(8,128)S(1)}, f32[21,16,128]{2,1,0:T(8,128)}, f32...) custom-call(s32[1]{0:T(128)} %constant.2.clone.1.base_ref, ...), custom_call_target="tpu_custom_call" | custom-call | tf_op jit(solution)/shard_map/pallas_call | solution.py:345
  59.8 2.2 %collective-permute-start.19 = (f32[21,16,128]{2,1,0:T(8,128)}, f32[21,16,128]{2,1,0:T(8,128)S(1)}, u32[]{:S(2)}, u32[]{:S(2)}) collective-permute-start(f32[21,16,128]{2,1,0:T(8,128)} %get-tuple-element.149), channel_id=1, source_target_pairs={{0,96},{32,128},{64,160},{96,192},{128,224},{160,0},{192,32},{224,... | collective-permute-start | bytes 516104 | tf_op jit(solution)/shard_map/ppermute | solution.py:445
  62.0 2.0 %collective-permute-start.20 = (f32[21,16,128]{2,1,0:T(8,128)}, f32[21,16,128]{2,1,0:T(8,128)S(1)}, u32[]{:S(2)}, u32[]{:S(2)}) collective-permute-start(f32[21,16,128]{2,1,0:T(8,128)} %get-tuple-element.150), channel_id=1, source_target_pairs={{0,128},{32,160},{64,192},{96,224},{128,0},{160,32},{192,64},{224,... | collective-permute-start | bytes 516104 | tf_op jit(solution)/shard_map/ppermute | solution.py:445
  64.0 1.6 %collective-permute-start.21 = (f32[21,16,128]{2,1,0:T(8,128)}, f32[21,16,128]{2,1,0:T(8,128)S(1)}, u32[]{:S(2)}, u32[]{:S(2)}) collective-permute-start(f32[21,16,128]{2,1,0:T(8,128)} %get-tuple-element.151), channel_id=1, source_target_pairs={{0,160},{32,192},{64,224},{96,0},{128,32},{160,64},{192,96},{224,1... | collective-permute-start | bytes 516104 | tf_op jit(solution)/shard_map/ppermute | solution.py:445
  65.7 1.2 %collective-permute-done.17.refs_1_ = f32[21,16,128]{2,1,0:T(8,128)S(1)} collective-permute-done((f32[21,16,128]{2,1,0:T(8,128)S(1)}, f32[21,16,128]{2,1,0:T(8,128)S(1)}, u32[]{:S(2)}, u32[]{:S(2)}) %collective-permute-start.17) | collective-permute-done | bytes 172064 | tf_op jit(solution)/shard_map/ppermute | solution.py:445
  68.0 2.6 %collective-permute-start.23 = (f32[21,16,128]{2,1,0:T(8,128)}, f32[21,16,128]{2,1,0:T(8,128)}, u32[]{:S(2)}, u32[]{:S(2)}) collective-permute-start(f32[21,16,128]{2,1,0:T(8,128)} %get-tuple-element.153), channel_id=1, source_target_pairs={{0,224},{32,0},{64,32},{96,64},{128,96},{160,128},{192,160},{224,1... | collective-permute-start | bytes 516104 | tf_op jit(solution)/shard_map/ppermute | solution.py:445
  70.6 3.5 %collective-permute-done.19.refs_3_ = f32[21,16,128]{2,1,0:T(8,128)S(1)} collective-permute-done((f32[21,16,128]{2,1,0:T(8,128)}, f32[21,16,128]{2,1,0:T(8,128)S(1)}, u32[]{:S(2)}, u32[]{:S(2)}) %collective-permute-start.19) | collective-permute-done | bytes 172064 | tf_op jit(solution)/shard_map/ppermute | solution.py:445
  74.1 1.2 %collective-permute-done.20.refs_4_ = f32[21,16,128]{2,1,0:T(8,128)S(1)} collective-permute-done((f32[21,16,128]{2,1,0:T(8,128)}, f32[21,16,128]{2,1,0:T(8,128)S(1)}, u32[]{:S(2)}, u32[]{:S(2)}) %collective-permute-start.20) | collective-permute-done | bytes 172064 | tf_op jit(solution)/shard_map/ppermute | solution.py:445
  76.5 2.2 %collective-permute-done.23.refs_7_ = f32[21,16,128]{2,1,0:T(8,128)} collective-permute-done((f32[21,16,128]{2,1,0:T(8,128)}, f32[21,16,128]{2,1,0:T(8,128)}, u32[]{:S(2)}, u32[]{:S(2)}) %collective-permute-start.23) | collective-permute-done | bytes 172064 | tf_op jit(solution)/shard_map/ppermute | solution.py:445
  80.9 6.8 %all-to-all-done.2.left_ref = f32[32,20,4,128]{3,2,1,0:T(4,128)S(1)} async-done(((f32[32,20,4,128]{3,2,1,0:T(4,128)}), f32[32,20,4,128]{3,2,1,0:T(4,128)S(1)}, u32[]{:S(2)}, u32[]{:S(2)}) %all-to-all-start.2) | async-done | bytes 1310752 | tf_op jit(solution)/shard_map/all_to_all | solution.py:471
  87.7 4.2 %shard_map.71 = f32[12,128,128]{2,1,0:T(8,128)} custom-call(s32[2]{0:T(128)S(1)} %pad_add_fusion.1.scalars, s32[8,128]{1,0:T(8,128)S(1)} %get-tuple-element.154.codes, s32[8,128]{1,0:T(8,128)S(1)} %get-tuple-element.155.counts, f32[32,20,4,128]{3,2,1,0:T(4,128)S(1)} %all-to-all-done.2.left_ref, f32[21,16,128]{2,1,0:T(8,128)S(1)} %get-tuple-element.146.refs_0_, ...), custom_call_target="tpu_custom_call" | custom-call | tf_op jit(solution)/shard_map/pallas_call | solution.py:427
  (27 shorter events, 11.5 us)
Async XLA Ops:
  0.9 1.2 %collective-permute-start.7 = (f32[4,128]{1,0:T(4,128)S(1)}, f32[4,128]{1,0:T(4,128)S(1)}, u32[]{:S(2)}, u32[]{:S(2)}) collective-permute-start(f32[4,128]{1,0:T(4,128)S(1)} %get-tuple-element.122), channel_id=1, source_target_pairs={{0,32},{32,0},{64,96},{96,64},{128,160},{160,128},{192,224},{224,1... | collective-permute-start | bytes 6152 | tf_op jit(solution)/shard_map/ppermute | solution.py:450
  2.1 3.6 %collective-permute-start.8 = (f32[4,128]{1,0:T(4,128)S(1)}, f32[4,128]{1,0:T(4,128)S(1)}, u32[]{:S(2)}, u32[]{:S(2)}) collective-permute-start(f32[4,128]{1,0:T(4,128)S(1)} %add.9), channel_id=1, source_target_pairs={{0,64},{32,96},{64,0},{96,32},{128,192},{160,224},{192,128},{224,1... | collective-permute-start | bytes 6152 | tf_op jit(solution)/shard_map/ppermute | solution.py:450
  5.7 5.2 %collective-permute-start.9 = (f32[4,128]{1,0:T(4,128)S(1)}, f32[4,128]{1,0:T(4,128)S(1)}, u32[]{:S(2)}, u32[]{:S(2)}) collective-permute-start(f32[4,128]{1,0:T(4,128)S(1)} %add.10.one_ref), channel_id=1, source_target_pairs={{0,192},{32,224},{64,128},{96,160},{128,64},{160,96},{192,0},{224,... | collective-permute-start | bytes 6152 | tf_op jit(solution)/shard_map/ppermute | solution.py:450
  11.6 34.1 %all-to-all-start.1 = ((f32[32,13,4,128]{3,2,1,0:T(4,128)}), f32[32,13,4,128]{3,2,1,0:T(4,128)S(1)}, u32[]{:S(2)}, u32[]{:S(2)}) async-start(f32[32,13,4,128]{3,2,1,0:T(4,128)} %get-tuple-element.124), calls=%async_computation.1 | async-start | bytes 1703936 | tf_op jit(solution)/shard_map/all_to_all | solution.py:465
  25.0 7.1 %collective-permute-start.10 = (f32[12,16,128]{2,1,0:T(8,128)S(1)}, f32[12,16,128]{2,1,0:T(8,128)}, u32[]{:S(2)}, u32[]{:S(2)}) collective-permute-start(f32[12,16,128]{2,1,0:T(8,128)S(1)} %get-tuple-element.126), channel_id=1, source_target_pairs={{0,32},{32,64},{64,96},{96,128},{128,160},{160,192},{192,224},{224... | collective-permute-start | bytes 294920 | tf_op jit(solution)/shard_map/ppermute | solution.py:445
  25.0 7.2 %collective-permute-start.11 = (f32[12,16,128]{2,1,0:T(8,128)S(1)}, f32[12,16,128]{2,1,0:T(8,128)}, u32[]{:S(2)}, u32[]{:S(2)}) collective-permute-start(f32[12,16,128]{2,1,0:T(8,128)S(1)} %get-tuple-element.127), channel_id=1, source_target_pairs={{0,64},{32,96},{64,128},{96,160},{128,192},{160,224},{192,0},{224,... | collective-permute-start | bytes 294920 | tf_op jit(solution)/shard_map/ppermute | solution.py:445
  25.2 10.7 %collective-permute-start.12 = (f32[12,16,128]{2,1,0:T(8,128)S(1)}, f32[12,16,128]{2,1,0:T(8,128)}, u32[]{:S(2)}, u32[]{:S(2)}) collective-permute-start(f32[12,16,128]{2,1,0:T(8,128)S(1)} %get-tuple-element.128), channel_id=1, source_target_pairs={{0,96},{32,128},{64,160},{96,192},{128,224},{160,0},{192,32},{224,... | collective-permute-start | bytes 294920 | tf_op jit(solution)/shard_map/ppermute | solution.py:445
  28.5 8.5 %collective-permute-start.13 = (f32[12,16,128]{2,1,0:T(8,128)S(1)}, f32[12,16,128]{2,1,0:T(8,128)}, u32[]{:S(2)}, u32[]{:S(2)}) collective-permute-start(f32[12,16,128]{2,1,0:T(8,128)S(1)} %get-tuple-element.129), channel_id=1, source_target_pairs={{0,128},{32,160},{64,192},{96,224},{128,0},{160,32},{192,64},{224,... | collective-permute-start | bytes 294920 | tf_op jit(solution)/shard_map/ppermute | solution.py:445
  29.5 7.5 %collective-permute-start.14 = (f32[12,16,128]{2,1,0:T(8,128)S(1)}, f32[12,16,128]{2,1,0:T(8,128)}, u32[]{:S(2)}, u32[]{:S(2)}) collective-permute-start(f32[12,16,128]{2,1,0:T(8,128)S(1)} %get-tuple-element.130), channel_id=1, source_target_pairs={{0,160},{32,192},{64,224},{96,0},{128,32},{160,64},{192,96},{224,1... | collective-permute-start | bytes 294920 | tf_op jit(solution)/shard_map/ppermute | solution.py:445
  32.1 5.5 %collective-permute-start.15 = (f32[12,16,128]{2,1,0:T(8,128)S(1)}, f32[12,16,128]{2,1,0:T(8,128)}, u32[]{:S(2)}, u32[]{:S(2)}) collective-permute-start(f32[12,16,128]{2,1,0:T(8,128)S(1)} %get-tuple-element.131), channel_id=1, source_target_pairs={{0,192},{32,224},{64,0},{96,32},{128,64},{160,96},{192,128},{224,1... | collective-permute-start | bytes 294920 | tf_op jit(solution)/shard_map/ppermute | solution.py:445
  32.2 5.5 %collective-permute-start.16 = (f32[12,16,128]{2,1,0:T(8,128)S(1)}, f32[12,16,128]{2,1,0:T(8,128)}, u32[]{:S(2)}, u32[]{:S(2)}) collective-permute-start(f32[12,16,128]{2,1,0:T(8,128)S(1)} %get-tuple-element.132), channel_id=1, source_target_pairs={{0,224},{32,0},{64,32},{96,64},{128,96},{160,128},{192,160},{224,1... | collective-permute-start | bytes 294920 | tf_op jit(solution)/shard_map/ppermute | solution.py:445
  50.1 37.6 %all-to-all-start.2 = ((f32[32,20,4,128]{3,2,1,0:T(4,128)}), f32[32,20,4,128]{3,2,1,0:T(4,128)S(1)}, u32[]{:S(2)}, u32[]{:S(2)}) async-start(f32[32,20,4,128]{3,2,1,0:T(4,128)} %get-tuple-element.156), calls=%async_computation.2 | async-start | bytes 2621440 | tf_op jit(solution)/shard_map/all_to_all | solution.py:471
  59.5 7.3 %collective-permute-start.17 = (f32[21,16,128]{2,1,0:T(8,128)S(1)}, f32[21,16,128]{2,1,0:T(8,128)S(1)}, u32[]{:S(2)}, u32[]{:S(2)}) collective-permute-start(f32[21,16,128]{2,1,0:T(8,128)S(1)} %get-tuple-element.147), channel_id=1, source_target_pairs={{0,32},{32,64},{64,96},{96,128},{128,160},{160,192},{192,224},{224... | collective-permute-start | bytes 516104 | tf_op jit(solution)/shard_map/ppermute | solution.py:445
  59.5 8.5 %collective-permute-start.18 = (f32[21,16,128]{2,1,0:T(8,128)S(1)}, f32[21,16,128]{2,1,0:T(8,128)S(1)}, u32[]{:S(2)}, u32[]{:S(2)}) collective-permute-start(f32[21,16,128]{2,1,0:T(8,128)S(1)} %get-tuple-element.148), channel_id=1, source_target_pairs={{0,64},{32,96},{64,128},{96,160},{128,192},{160,224},{192,0},{224,... | collective-permute-start | bytes 516104 | tf_op jit(solution)/shard_map/ppermute | solution.py:445
  59.8 14.3 %collective-permute-start.19 = (f32[21,16,128]{2,1,0:T(8,128)}, f32[21,16,128]{2,1,0:T(8,128)S(1)}, u32[]{:S(2)}, u32[]{:S(2)}) collective-permute-start(f32[21,16,128]{2,1,0:T(8,128)} %get-tuple-element.149), channel_id=1, source_target_pairs={{0,96},{32,128},{64,160},{96,192},{128,224},{160,0},{192,32},{224,... | collective-permute-start | bytes 516104 | tf_op jit(solution)/shard_map/ppermute | solution.py:445
  62.0 13.3 %collective-permute-start.20 = (f32[21,16,128]{2,1,0:T(8,128)}, f32[21,16,128]{2,1,0:T(8,128)S(1)}, u32[]{:S(2)}, u32[]{:S(2)}) collective-permute-start(f32[21,16,128]{2,1,0:T(8,128)} %get-tuple-element.150), channel_id=1, source_target_pairs={{0,128},{32,160},{64,192},{96,224},{128,0},{160,32},{192,64},{224,... | collective-permute-start | bytes 516104 | tf_op jit(solution)/shard_map/ppermute | solution.py:445
  64.0 11.4 %collective-permute-start.21 = (f32[21,16,128]{2,1,0:T(8,128)}, f32[21,16,128]{2,1,0:T(8,128)S(1)}, u32[]{:S(2)}, u32[]{:S(2)}) collective-permute-start(f32[21,16,128]{2,1,0:T(8,128)} %get-tuple-element.151), channel_id=1, source_target_pairs={{0,160},{32,192},{64,224},{96,0},{128,32},{160,64},{192,96},{224,1... | collective-permute-start | bytes 516104 | tf_op jit(solution)/shard_map/ppermute | solution.py:445
  66.9 9.7 %collective-permute-start.22 = (f32[21,16,128]{2,1,0:T(8,128)}, f32[21,16,128]{2,1,0:T(8,128)S(1)}, u32[]{:S(2)}, u32[]{:S(2)}) collective-permute-start(f32[21,16,128]{2,1,0:T(8,128)} %get-tuple-element.152), channel_id=1, source_target_pairs={{0,192},{32,224},{64,0},{96,32},{128,64},{160,96},{192,128},{224,1... | collective-permute-start | bytes 516104 | tf_op jit(solution)/shard_map/ppermute | solution.py:445
  68.0 10.7 %collective-permute-start.23 = (f32[21,16,128]{2,1,0:T(8,128)}, f32[21,16,128]{2,1,0:T(8,128)}, u32[]{:S(2)}, u32[]{:S(2)}) collective-permute-start(f32[21,16,128]{2,1,0:T(8,128)} %get-tuple-element.153), channel_id=1, source_target_pairs={{0,224},{32,0},{64,32},{96,64},{128,96},{160,128},{192,160},{224,1... | collective-permute-start | bytes 516104 | tf_op jit(solution)/shard_map/ppermute | solution.py:445

commit v7 on v6

--- a/solution.py
+++ b/solution.py
@@ -376,7 +376,7 @@
     out_ref, right = refs[-2:]
     out_ref[...] = jnp.zeros_like(out_ref) if first else refs[0][...]
     row_index, own, base = lax.axis_index("row"), lax.axis_index(GROUP), scalars[0]
-    peers, cap, strip, order = left_ref.shape
+    peers, cap = left_ref.shape[:2]
     tall_strip = right_refs[0].shape[1]
     line = (own >> 3) * pl.cdiv(cap, SLOT_PITCH)
     lane = (own & (PER_GROUP - 1)) * SLOT_PITCH
@@ -391,13 +391,11 @@
         a_high, b_high = a.astype(bf16), b.astype(bf16)
         a_low = (a - a_high.astype(jnp.float32)).astype(bf16)
         b_low = (b - b_high.astype(jnp.float32)).astype(bf16)
-        both = jnp.concatenate([b_high, b_low], axis=1)
-        sums = jnp.dot(
-            jnp.concatenate([a_high, a_low], axis=1),
-            jnp.concatenate([both, both], axis=0),
+        return jnp.dot(
+            jnp.concatenate([a_high, a_low, a_high], axis=1),
+            jnp.concatenate([b_high, b_high, b_low], axis=0),
             preferred_element_type=jnp.float32,
         )
-        return sums[:, :order] + sums[:, order:]
 
     def target(at):
         return codes[line + (at >> 4), lane + (at & (SLOT_PITCH - 1))] >> 16
@@ -460,7 +458,8 @@
     listed, wanted = label(tile_rows, tile_cols, tile_counts, out_rows, out_cols)
     for by in (1, 2):
         listed = listed + swap_rows(listed, rows, by)
-    strips, mates = stamp(listed, swap_rows(listed, rows, rows - 2), wanted, pack(tiles, peers))
+    listed, strips = lax.optimization_barrier((listed, pack(tiles, peers)))
+    strips, mates = stamp(listed, swap_rows(listed, rows, rows - 2), wanted, strips)
     pieces = shift_all(pack_right(tiles, rows))
     strips = lax.all_to_all(strips, GROUP, 0, 0, tiled=True)
     strips, pieces = lax.optimization_barrier((strips, pieces))

time: 93.1 us -> 93.1 us (level)
  waiting for transfers between devices: 31.8 us -> 30 us
  starting transfers between devices: 40 us -> 41.7 us
    ppermute x14, starting transfers between devices: 18 us -> 19.9 us  [shift_all(): lax.ppermute(pieces[by], 'row', [(i, (i + by) % rows) for i in range(rows)])]
    ppermute x14, waiting for transfers between devices: 14 us -> 12.1 us  [shift_all(): lax.ppermute(pieces[by], 'row', [(i, (i + by) % rows) for i in range(rows)])]
  transfers between devices with their start and end apart: 19 -> 19, of which waited for: 15 -> 14; matrix products, arithmetic and copies ran while one was open for 1% -> 1% of each run, Pallas kernels for 9% -> 9%
where the time goes in v7:
time: 93.1 us; the launch traced here: 92.6 us
  starting transfers between devices  41.7 us (45%)
  waiting for transfers between devices  30 us (32%)
  Pallas kernels  18.8 us (20%)
    ppermute x14, starting transfers between devices, shift_all(): lax.ppermute(pieces[by], 'row', [(i, (i + by) % rows) for i in range(rows)])  19.9 us
    ppermute x14, waiting for transfers between devices, shift_all(): lax.ppermute(pieces[by], 'row', [(i, (i + by) % rows) for i in range(rows)])  12.1 us
    all_to_all x1, starting transfers between devices, local(): strips = lax.all_to_all(strips, GROUP, 0, 0, tiled=True)  11.6 us
    all_to_all x1, waiting for transfers between devices, local(): strips = lax.all_to_all(strips, GROUP, 0, 0, tiled=True)  7.83 us
    all_to_all x1, waiting for transfers between devices, one_round(): left = lax.all_to_all(send, GROUP, 0, 0, tiled=True)  6.8 us
    all_to_all x1, starting transfers between devices, one_round(): left = lax.all_to_all(send, GROUP, 0, 0, tiled=True)  5.71 us
    ppermute x3, starting transfers between devices, swap_rows(): return lax.ppermute(array, 'row', [(i, i ^ by) for i in range(rows)])  4.49 us
    pallas_call x1, Pallas kernels, plan(): pl.pallas_call(functools.partial(plan_body, rows), grid_spec=pltpu.Prefet...  4.37 us
  transfers between devices with their start and end apart: 19, of which 14 were waited for; matrix products, arithmetic and copies ran while one was open for 1% of the time, Pallas kernels for 9%

profile of v7, /device:TPU:4, one launch (start us, length us, event | category | flops | bytes accessed | tf_op | source)
XLA Modules:
  0.0 92.6 jit_solution(11691452646333866365)
XLA Ops:
  2.1 1.6 %collective-permute-start.8 = (f32[4,128]{1,0:T(4,128)S(1)}, f32[4,128]{1,0:T(4,128)S(1)}, u32[]{:S(2)}, u32[]{:S(2)}) collective-permute-start(f32[4,128]{1,0:T(4,128)S(1)} %add.9), channel_id=1, source_target_pairs={{0,64},{32,96},{64,0},{96,32},{128,192},{160,224},{192,128},{224,1... | collective-permute-start | bytes 6152 | tf_op jit(solution)/shard_map/ppermute | solution.py:448
  3.7 2.2 %shard_map.65.strips_in = f32[32,13,4,128]{3,2,1,0:T(4,128)} custom-call(f32[12,128,128]{2,1,0:T(8,128)} %bitcast.13), custom_call_target="tpu_custom_call" | custom-call | tf_op jit(solution)/shard_map/pallas_call | solution.py:89
  5.9 2.8 %collective-permute-start.9 = (f32[4,128]{1,0:T(4,128)S(1)}, f32[4,128]{1,0:T(4,128)S(1)}, u32[]{:S(2)}, u32[]{:S(2)}) collective-permute-start(f32[4,128]{1,0:T(4,128)S(1)} %add.10.one_ref), channel_id=1, source_target_pairs={{0,192},{32,224},{64,128},{96,160},{128,64},{160,96},{192,0},{224,... | collective-permute-start | bytes 6152 | tf_op jit(solution)/shard_map/ppermute | solution.py:448
  8.7 2.1 %collective-permute-done.9.other_ref = f32[4,128]{1,0:T(4,128)S(1)} collective-permute-done((f32[4,128]{1,0:T(4,128)S(1)}, f32[4,128]{1,0:T(4,128)S(1)}, u32[]{:S(2)}, u32[]{:S(2)}) %collective-permute-start.9) | collective-permute-done | bytes 2080 | tf_op jit(solution)/shard_map/ppermute | solution.py:448
  11.4 11.6 %all-to-all-start.1 = ((f32[32,13,4,128]{3,2,1,0:T(4,128)}), f32[32,13,4,128]{3,2,1,0:T(4,128)S(1)}, u32[]{:S(2)}, u32[]{:S(2)}) async-start(f32[32,13,4,128]{3,2,1,0:T(4,128)} %get-tuple-element.128), calls=%async_computation.1 | async-start | bytes 1703936 | tf_op jit(solution)/shard_map/all_to_all | solution.py:464
  23.0 1.8 %shard_map.67 = (f32[12,16,128]{2,1,0:T(8,128)}, f32[12,16,128]{2,1,0:T(8,128)S(1)}, f32[12,16,128]{2,1,0:T(8,128)S(1)}, f32[12,16,128]{2,1,0:T(8,128)S(1)}, f32...) custom-call(f32[12,128,128]{2,1,0:T(8,128)} %bitcast.14), custom_call_target="tpu_custom_call" | custom-call | tf_op jit(solution)/shard_map/pallas_call | solution.py:136
  25.0 3.5 %collective-permute-start.12 = (f32[12,16,128]{2,1,0:T(8,128)S(1)}, f32[12,16,128]{2,1,0:T(8,128)}, u32[]{:S(2)}, u32[]{:S(2)}) collective-permute-start(f32[12,16,128]{2,1,0:T(8,128)S(1)} %get-tuple-element.132), channel_id=1, source_target_pairs={{0,96},{32,128},{64,160},{96,192},{128,224},{160,0},{192,32},{224,... | collective-permute-start | bytes 294920 | tf_op jit(solution)/shard_map/ppermute | solution.py:443
  29.3 2.7 %collective-permute-start.14 = (f32[12,16,128]{2,1,0:T(8,128)S(1)}, f32[12,16,128]{2,1,0:T(8,128)}, u32[]{:S(2)}, u32[]{:S(2)}) collective-permute-start(f32[12,16,128]{2,1,0:T(8,128)S(1)} %get-tuple-element.134), channel_id=1, source_target_pairs={{0,160},{32,192},{64,224},{96,0},{128,32},{160,64},{192,96},{224,1... | collective-permute-start | bytes 294920 | tf_op jit(solution)/shard_map/ppermute | solution.py:443
  32.2 1.7 %collective-permute-start.16 = (f32[12,16,128]{2,1,0:T(8,128)S(1)}, f32[12,16,128]{2,1,0:T(8,128)}, u32[]{:S(2)}, u32[]{:S(2)}) collective-permute-start(f32[12,16,128]{2,1,0:T(8,128)S(1)} %get-tuple-element.136), channel_id=1, source_target_pairs={{0,224},{32,0},{64,32},{96,64},{128,96},{160,128},{192,160},{224,1... | collective-permute-start | bytes 294920 | tf_op jit(solution)/shard_map/ppermute | solution.py:443
  34.0 1.9 %collective-permute-done.12.refs_3_ = f32[12,16,128]{2,1,0:T(8,128)} collective-permute-done((f32[12,16,128]{2,1,0:T(8,128)S(1)}, f32[12,16,128]{2,1,0:T(8,128)}, u32[]{:S(2)}, u32[]{:S(2)}) %collective-permute-start.12) | collective-permute-done | bytes 98336 | tf_op jit(solution)/shard_map/ppermute | solution.py:443
  37.7 7.8 %all-to-all-done.1 = f32[32,13,4,128]{3,2,1,0:T(4,128)S(1)} async-done(((f32[32,13,4,128]{3,2,1,0:T(4,128)}), f32[32,13,4,128]{3,2,1,0:T(4,128)S(1)}, u32[]{:S(2)}, u32[]{:S(2)}) %all-to-all-start.1) | async-done | bytes 852000 | tf_op jit(solution)/shard_map/all_to_all | solution.py:464
  45.5 4.4 %shard_map.68 = (f32[32,20,4,128]{3,2,1,0:T(4,128)}, s32[8,128]{1,0:T(8,128)S(1)}, s32[8,128]{1,0:T(8,128)S(1)}, f32[8,128]{1,0:T(8,128)S(1)}, bf16[256,256]{1,0...) custom-call(s32[1]{0:T(128)} %constant.2.clone.1.base_ref, f32[416,4,128]{2,1,0:T(4,128)S(1)} %bitcast.11), custom_call_target="tpu_custom_call" | custom-call | tf_op jit(solution)/shard_map/pallas_call | solution.py:286
  49.9 5.7 %all-to-all-start.2 = ((f32[32,20,4,128]{3,2,1,0:T(4,128)}), f32[32,20,4,128]{3,2,1,0:T(4,128)S(1)}, u32[]{:S(2)}, u32[]{:S(2)}) async-start(f32[32,20,4,128]{3,2,1,0:T(4,128)} %get-tuple-element.160), calls=%async_computation.2 | async-start | bytes 2621440 | tf_op jit(solution)/shard_map/all_to_all | solution.py:470
  55.6 3.7 %shard_map.69 = (f32[21,16,128]{2,1,0:T(8,128)S(1)}, f32[21,16,128]{2,1,0:T(8,128)S(1)}, f32[21,16,128]{2,1,0:T(8,128)S(1)}, f32[21,16,128]{2,1,0:T(8,128)}, f32...) custom-call(s32[1]{0:T(128)} %constant.2.clone.1.base_ref, ...), custom_call_target="tpu_custom_call" | custom-call | tf_op jit(solution)/shard_map/pallas_call | solution.py:345
  59.5 2.9 %collective-permute-start.19 = (f32[21,16,128]{2,1,0:T(8,128)}, f32[21,16,128]{2,1,0:T(8,128)S(1)}, u32[]{:S(2)}, u32[]{:S(2)}) collective-permute-start(f32[21,16,128]{2,1,0:T(8,128)} %get-tuple-element.153), channel_id=1, source_target_pairs={{0,96},{32,128},{64,160},{96,192},{128,224},{160,0},{192,32},{224,... | collective-permute-start | bytes 516104 | tf_op jit(solution)/shard_map/ppermute | solution.py:443
  62.4 1.4 %collective-permute-start.20 = (f32[21,16,128]{2,1,0:T(8,128)}, f32[21,16,128]{2,1,0:T(8,128)S(1)}, u32[]{:S(2)}, u32[]{:S(2)}) collective-permute-start(f32[21,16,128]{2,1,0:T(8,128)} %get-tuple-element.154), channel_id=1, source_target_pairs={{0,128},{32,160},{64,192},{96,224},{128,0},{160,32},{192,64},{224,... | collective-permute-start | bytes 516104 | tf_op jit(solution)/shard_map/ppermute | solution.py:443
  63.8 2.3 %collective-permute-start.21 = (f32[21,16,128]{2,1,0:T(8,128)}, f32[21,16,128]{2,1,0:T(8,128)S(1)}, u32[]{:S(2)}, u32[]{:S(2)}) collective-permute-start(f32[21,16,128]{2,1,0:T(8,128)} %get-tuple-element.155), channel_id=1, source_target_pairs={{0,160},{32,192},{64,224},{96,0},{128,32},{160,64},{192,96},{224,1... | collective-permute-start | bytes 516104 | tf_op jit(solution)/shard_map/ppermute | solution.py:443
  67.9 3.1 %collective-permute-start.23 = (f32[21,16,128]{2,1,0:T(8,128)}, f32[21,16,128]{2,1,0:T(8,128)}, u32[]{:S(2)}, u32[]{:S(2)}) collective-permute-start(f32[21,16,128]{2,1,0:T(8,128)} %get-tuple-element.157), channel_id=1, source_target_pairs={{0,224},{32,0},{64,32},{96,64},{128,96},{160,128},{192,160},{224,1... | collective-permute-start | bytes 516104 | tf_op jit(solution)/shard_map/ppermute | solution.py:443
  71.0 3.4 %collective-permute-done.19.refs_3_ = f32[21,16,128]{2,1,0:T(8,128)S(1)} collective-permute-done((f32[21,16,128]{2,1,0:T(8,128)}, f32[21,16,128]{2,1,0:T(8,128)S(1)}, u32[]{:S(2)}, u32[]{:S(2)}) %collective-permute-start.19) | collective-permute-done | bytes 172064 | tf_op jit(solution)/shard_map/ppermute | solution.py:443
  74.4 1.2 %collective-permute-done.20.refs_4_ = f32[21,16,128]{2,1,0:T(8,128)S(1)} collective-permute-done((f32[21,16,128]{2,1,0:T(8,128)}, f32[21,16,128]{2,1,0:T(8,128)S(1)}, u32[]{:S(2)}, u32[]{:S(2)}) %collective-permute-start.20) | collective-permute-done | bytes 172064 | tf_op jit(solution)/shard_map/ppermute | solution.py:443
  75.7 1.7 %collective-permute-done.22.refs_6_ = f32[21,16,128]{2,1,0:T(8,128)S(1)} collective-permute-done((f32[21,16,128]{2,1,0:T(8,128)}, f32[21,16,128]{2,1,0:T(8,128)S(1)}, u32[]{:S(2)}, u32[]{:S(2)}) %collective-permute-start.22) | collective-permute-done | bytes 172064 | tf_op jit(solution)/shard_map/ppermute | solution.py:443
  77.4 1.2 %collective-permute-done.23.refs_7_ = f32[21,16,128]{2,1,0:T(8,128)} collective-permute-done((f32[21,16,128]{2,1,0:T(8,128)}, f32[21,16,128]{2,1,0:T(8,128)}, u32[]{:S(2)}, u32[]{:S(2)}) %collective-permute-start.23) | collective-permute-done | bytes 172064 | tf_op jit(solution)/shard_map/ppermute | solution.py:443
  80.8 6.8 %all-to-all-done.2.left_ref = f32[32,20,4,128]{3,2,1,0:T(4,128)S(1)} async-done(((f32[32,20,4,128]{3,2,1,0:T(4,128)}), f32[32,20,4,128]{3,2,1,0:T(4,128)S(1)}, u32[]{:S(2)}, u32[]{:S(2)}) %all-to-all-start.2) | async-done | bytes 1310752 | tf_op jit(solution)/shard_map/all_to_all | solution.py:470
  87.6 4.2 %shard_map.71 = f32[12,128,128]{2,1,0:T(8,128)} custom-call(s32[2]{0:T(128)S(1)} %pad_add_fusion.1.scalars, s32[8,128]{1,0:T(8,128)S(1)} %get-tuple-element.158.codes, s32[8,128]{1,0:T(8,128)S(1)} %get-tuple-element.159.counts, f32[32,20,4,128]{3,2,1,0:T(4,128)S(1)} %all-to-all-done.2.left_ref, f32[21,16,128]{2,1,0:T(8,128)S(1)} %get-tuple-element.150.refs_0_, ...), custom_call_target="tpu_custom_call" | custom-call | tf_op jit(solution)/shard_map/pallas_call | solution.py:425
  (27 shorter events, 10.4 us)
Async XLA Ops:
  0.9 1.2 %collective-permute-start.7 = (f32[4,128]{1,0:T(4,128)S(1)}, f32[4,128]{1,0:T(4,128)S(1)}, u32[]{:S(2)}, u32[]{:S(2)}) collective-permute-start(f32[4,128]{1,0:T(4,128)S(1)} %get-tuple-element.124), channel_id=1, source_target_pairs={{0,32},{32,0},{64,96},{96,64},{128,160},{160,128},{192,224},{224,1... | collective-permute-start | bytes 6152 | tf_op jit(solution)/shard_map/ppermute | solution.py:448
  2.1 3.8 %collective-permute-start.8 = (f32[4,128]{1,0:T(4,128)S(1)}, f32[4,128]{1,0:T(4,128)S(1)}, u32[]{:S(2)}, u32[]{:S(2)}) collective-permute-start(f32[4,128]{1,0:T(4,128)S(1)} %add.9), channel_id=1, source_target_pairs={{0,64},{32,96},{64,0},{96,32},{128,192},{160,224},{192,128},{224,1... | collective-permute-start | bytes 6152 | tf_op jit(solution)/shard_map/ppermute | solution.py:448
  5.9 4.9 %collective-permute-start.9 = (f32[4,128]{1,0:T(4,128)S(1)}, f32[4,128]{1,0:T(4,128)S(1)}, u32[]{:S(2)}, u32[]{:S(2)}) collective-permute-start(f32[4,128]{1,0:T(4,128)S(1)} %add.10.one_ref), channel_id=1, source_target_pairs={{0,192},{32,224},{64,128},{96,160},{128,64},{160,96},{192,0},{224,... | collective-permute-start | bytes 6152 | tf_op jit(solution)/shard_map/ppermute | solution.py:448
  11.4 34.1 %all-to-all-start.1 = ((f32[32,13,4,128]{3,2,1,0:T(4,128)}), f32[32,13,4,128]{3,2,1,0:T(4,128)S(1)}, u32[]{:S(2)}, u32[]{:S(2)}) async-start(f32[32,13,4,128]{3,2,1,0:T(4,128)} %get-tuple-element.128), calls=%async_computation.1 | async-start | bytes 1703936 | tf_op jit(solution)/shard_map/all_to_all | solution.py:464
  24.9 7.2 %collective-permute-start.10 = (f32[12,16,128]{2,1,0:T(8,128)S(1)}, f32[12,16,128]{2,1,0:T(8,128)}, u32[]{:S(2)}, u32[]{:S(2)}) collective-permute-start(f32[12,16,128]{2,1,0:T(8,128)S(1)} %get-tuple-element.130), channel_id=1, source_target_pairs={{0,32},{32,64},{64,96},{96,128},{128,160},{160,192},{192,224},{224... | collective-permute-start | bytes 294920 | tf_op jit(solution)/shard_map/ppermute | solution.py:443
  24.9 7.4 %collective-permute-start.11 = (f32[12,16,128]{2,1,0:T(8,128)S(1)}, f32[12,16,128]{2,1,0:T(8,128)}, u32[]{:S(2)}, u32[]{:S(2)}) collective-permute-start(f32[12,16,128]{2,1,0:T(8,128)S(1)} %get-tuple-element.131), channel_id=1, source_target_pairs={{0,64},{32,96},{64,128},{96,160},{128,192},{160,224},{192,0},{224,... | collective-permute-start | bytes 294920 | tf_op jit(solution)/shard_map/ppermute | solution.py:443
  25.0 10.9 %collective-permute-start.12 = (f32[12,16,128]{2,1,0:T(8,128)S(1)}, f32[12,16,128]{2,1,0:T(8,128)}, u32[]{:S(2)}, u32[]{:S(2)}) collective-permute-start(f32[12,16,128]{2,1,0:T(8,128)S(1)} %get-tuple-element.132), channel_id=1, source_target_pairs={{0,96},{32,128},{64,160},{96,192},{128,224},{160,0},{192,32},{224,... | collective-permute-start | bytes 294920 | tf_op jit(solution)/shard_map/ppermute | solution.py:443
  28.5 8.5 %collective-permute-start.13 = (f32[12,16,128]{2,1,0:T(8,128)S(1)}, f32[12,16,128]{2,1,0:T(8,128)}, u32[]{:S(2)}, u32[]{:S(2)}) collective-permute-start(f32[12,16,128]{2,1,0:T(8,128)S(1)} %get-tuple-element.133), channel_id=1, source_target_pairs={{0,128},{32,160},{64,192},{96,224},{128,0},{160,32},{192,64},{224,... | collective-permute-start | bytes 294920 | tf_op jit(solution)/shard_map/ppermute | solution.py:443
  29.3 7.7 %collective-permute-start.14 = (f32[12,16,128]{2,1,0:T(8,128)S(1)}, f32[12,16,128]{2,1,0:T(8,128)}, u32[]{:S(2)}, u32[]{:S(2)}) collective-permute-start(f32[12,16,128]{2,1,0:T(8,128)S(1)} %get-tuple-element.134), channel_id=1, source_target_pairs={{0,160},{32,192},{64,224},{96,0},{128,32},{160,64},{192,96},{224,1... | collective-permute-start | bytes 294920 | tf_op jit(solution)/shard_map/ppermute | solution.py:443
  32.1 5.4 %collective-permute-start.15 = (f32[12,16,128]{2,1,0:T(8,128)S(1)}, f32[12,16,128]{2,1,0:T(8,128)}, u32[]{:S(2)}, u32[]{:S(2)}) collective-permute-start(f32[12,16,128]{2,1,0:T(8,128)S(1)} %get-tuple-element.135), channel_id=1, source_target_pairs={{0,192},{32,224},{64,0},{96,32},{128,64},{160,96},{192,128},{224,1... | collective-permute-start | bytes 294920 | tf_op jit(solution)/shard_map/ppermute | solution.py:443
  32.2 5.5 %collective-permute-start.16 = (f32[12,16,128]{2,1,0:T(8,128)S(1)}, f32[12,16,128]{2,1,0:T(8,128)}, u32[]{:S(2)}, u32[]{:S(2)}) collective-permute-start(f32[12,16,128]{2,1,0:T(8,128)S(1)} %get-tuple-element.136), channel_id=1, source_target_pairs={{0,224},{32,0},{64,32},{96,64},{128,96},{160,128},{192,160},{224,1... | collective-permute-start | bytes 294920 | tf_op jit(solution)/shard_map/ppermute | solution.py:443
  49.9 37.6 %all-to-all-start.2 = ((f32[32,20,4,128]{3,2,1,0:T(4,128)}), f32[32,20,4,128]{3,2,1,0:T(4,128)S(1)}, u32[]{:S(2)}, u32[]{:S(2)}) async-start(f32[32,20,4,128]{3,2,1,0:T(4,128)} %get-tuple-element.160), calls=%async_computation.2 | async-start | bytes 2621440 | tf_op jit(solution)/shard_map/all_to_all | solution.py:470
  59.4 7.3 %collective-permute-start.17 = (f32[21,16,128]{2,1,0:T(8,128)S(1)}, f32[21,16,128]{2,1,0:T(8,128)S(1)}, u32[]{:S(2)}, u32[]{:S(2)}) collective-permute-start(f32[21,16,128]{2,1,0:T(8,128)S(1)} %get-tuple-element.151), channel_id=1, source_target_pairs={{0,32},{32,64},{64,96},{96,128},{128,160},{160,192},{192,224},{224... | collective-permute-start | bytes 516104 | tf_op jit(solution)/shard_map/ppermute | solution.py:443
  59.4 8.5 %collective-permute-start.18 = (f32[21,16,128]{2,1,0:T(8,128)S(1)}, f32[21,16,128]{2,1,0:T(8,128)S(1)}, u32[]{:S(2)}, u32[]{:S(2)}) collective-permute-start(f32[21,16,128]{2,1,0:T(8,128)S(1)} %get-tuple-element.152), channel_id=1, source_target_pairs={{0,64},{32,96},{64,128},{96,160},{128,192},{160,224},{192,0},{224,... | collective-permute-start | bytes 516104 | tf_op jit(solution)/shard_map/ppermute | solution.py:443
  59.5 14.9 %collective-permute-start.19 = (f32[21,16,128]{2,1,0:T(8,128)}, f32[21,16,128]{2,1,0:T(8,128)S(1)}, u32[]{:S(2)}, u32[]{:S(2)}) collective-permute-start(f32[21,16,128]{2,1,0:T(8,128)} %get-tuple-element.153), channel_id=1, source_target_pairs={{0,96},{32,128},{64,160},{96,192},{128,224},{160,0},{192,32},{224,... | collective-permute-start | bytes 516104 | tf_op jit(solution)/shard_map/ppermute | solution.py:443
  62.4 13.2 %collective-permute-start.20 = (f32[21,16,128]{2,1,0:T(8,128)}, f32[21,16,128]{2,1,0:T(8,128)S(1)}, u32[]{:S(2)}, u32[]{:S(2)}) collective-permute-start(f32[21,16,128]{2,1,0:T(8,128)} %get-tuple-element.154), channel_id=1, source_target_pairs={{0,128},{32,160},{64,192},{96,224},{128,0},{160,32},{192,64},{224,... | collective-permute-start | bytes 516104 | tf_op jit(solution)/shard_map/ppermute | solution.py:443
  63.8 11.8 %collective-permute-start.21 = (f32[21,16,128]{2,1,0:T(8,128)}, f32[21,16,128]{2,1,0:T(8,128)S(1)}, u32[]{:S(2)}, u32[]{:S(2)}) collective-permute-start(f32[21,16,128]{2,1,0:T(8,128)} %get-tuple-element.155), channel_id=1, source_target_pairs={{0,160},{32,192},{64,224},{96,0},{128,32},{160,64},{192,96},{224,1... | collective-permute-start | bytes 516104 | tf_op jit(solution)/shard_map/ppermute | solution.py:443
  66.7 10.7 %collective-permute-start.22 = (f32[21,16,128]{2,1,0:T(8,128)}, f32[21,16,128]{2,1,0:T(8,128)S(1)}, u32[]{:S(2)}, u32[]{:S(2)}) collective-permute-start(f32[21,16,128]{2,1,0:T(8,128)} %get-tuple-element.156), channel_id=1, source_target_pairs={{0,192},{32,224},{64,0},{96,32},{128,64},{160,96},{192,128},{224,1... | collective-permute-start | bytes 516104 | tf_op jit(solution)/shard_map/ppermute | solution.py:443
  67.9 10.7 %collective-permute-start.23 = (f32[21,16,128]{2,1,0:T(8,128)}, f32[21,16,128]{2,1,0:T(8,128)}, u32[]{:S(2)}, u32[]{:S(2)}) collective-permute-start(f32[21,16,128]{2,1,0:T(8,128)} %get-tuple-element.157), channel_id=1, source_target_pairs={{0,224},{32,0},{64,32},{96,64},{128,96},{160,128},{192,160},{224,1... | collective-permute-start | bytes 516104 | tf_op jit(solution)/shard_map/ppermute | solution.py:443

commit v8 on v7

--- a/solution.py
+++ b/solution.py
@@ -141,12 +141,13 @@
 def list_products(by_col, by_row, targets, value_of, base, cap, values, keys, picks):
     blocks = by_col.shape[0]
     groups = len(targets)
+    bands = values.shape[0] // groups
     deep = picks.shape[0] // groups
     f32, bf16 = jnp.float32, jnp.bfloat16
     iota = functools.partial(lax.broadcasted_iota, jnp.int32)
     one, zero = jnp.ones((blocks, LANES), bf16), jnp.zeros((blocks, LANES), bf16)
     tall = (iota((blocks, LANES), 0) + 1).astype(f32).astype(bf16)
-    below = jnp.where(iota((blocks, blocks), 0) >= iota((blocks, blocks), 1), 1.0, 0.0).astype(bf16)
+    below = jnp.where(iota((bands, bands), 0) >= iota((bands, bands), 1), 1.0, 0.0).astype(bf16)
     lane_from, lane_to = iota((LANES, LANES), 0), iota((LANES, LANES), 1)
     same_peer = lane_from // SLOT_PITCH == lane_to // SLOT_PITCH
     earlier = jnp.where(same_peer & (lane_from < lane_to), 1.0, 0.0).astype(bf16)
@@ -160,11 +161,15 @@
 
         left = jnp.dot(by_col, hot(target_rows), preferred_element_type=f32)
         right = jnp.dot(by_row, hot(target_cols), preferred_element_type=f32)
-        hit = left * right > 0.0
+        pair = jnp.where(left * right > 0.0, left + right * 512.0, 0.0)
+        name = pair[0:bands, :]
+        for place in range(1, blocks // bands):
+            name = name + pair[place * bands:(place + 1) * bands, :]
+        hit = name > 0.0
         ranks = jnp.dot(below, jnp.where(hit, 1.0, 0.0).astype(bf16), preferred_element_type=f32)
-        everything.append(ranks[blocks - 1:blocks, :])
-        keys[group * blocks:(group + 1) * blocks, :] = jnp.where(hit, ranks, 0.0)
-        values[group * blocks:(group + 1) * blocks, :] = value_of(left, right)
+        everything.append(ranks[bands - 1:bands, :])
+        keys[group * bands:(group + 1) * bands, :] = jnp.where(hit, ranks, 0.0)
+        values[group * bands:(group + 1) * bands, :] = value_of(name)
     found = jnp.concatenate(everything + everything[-1:] * (8 - len(everything)), axis=0)
     ahead = jnp.dot(found.astype(bf16), earlier, preferred_element_type=f32) - base.astype(f32)
     counts = jnp.dot(found.astype(bf16), together.astype(bf16), preferred_element_type=f32)
@@ -175,7 +180,7 @@
     def one_depth(level, carry):
         level_f = level.astype(f32)
         for group in range(groups):
-            span = slice(group * blocks, (group + 1) * blocks)
+            span = slice(group * bands, (group + 1) * bands)
             value = jnp.sum(jnp.where(keys[span, :] == level_f + 1.0, values[span, :], 0.0), axis=0, keepdims=True)
             place = jnp.where(found[group:group + 1, :] > level_f, ahead[group:group + 1, :] + level_f, -1.0)
             span = slice(group * deep, (group + 1) * deep)
@@ -228,17 +233,19 @@
             targets.append(meta)
         else:
             targets[-1] = targets[-1] + meta
-    by_col = table[...]
-    by_row = by_col.T.astype(bf16)
-    by_col = by_col.astype(bf16)
+    by_index = table[...].astype(bf16)
+    index = iota((blocks, blocks), 0)
+    order = jnp.where(index % peers * band + index // peers == iota((blocks, blocks), 1), 1.0, 0.0).astype(bf16)
+    by_col = jnp.dot(order, by_index, preferred_element_type=f32).astype(bf16)
+    by_row = lax.dot_general(order, by_index, (((1,), (1,)), ((), ())), preferred_element_type=f32).astype(bf16)
     by_col_ref[...] = by_col
     by_row_ref[...] = by_row
 
-    fixed = iota((blocks, LANES), 0) // band * per_peer + ((iota((blocks, LANES), 1) % SLOT_PITCH) << 16)
+    fixed = iota((peers, LANES), 0) * per_peer + ((iota((peers, LANES), 1) % SLOT_PITCH) << 16)
     fixed = (fixed - (SLOT_PITCH * row_index + 1 + 512)).astype(f32)
     lines, counts = list_products(
         by_col, by_row, [(meta[2:3, :], meta[3:4, :]) for meta in targets],
-        lambda left, right: fixed + left + right * 512.0, base, cap, values, keys, picks,
+        lambda name: name + fixed, base, cap, values, keys, picks,
     )
     codes = jnp.concatenate(lines, axis=0).astype(jnp.int32)
     places_vmem[...] = codes & 511
@@ -268,8 +275,8 @@
     return pl.BlockSpec(shape, lambda i, *_: (0,) * len(shape))
 
 
-def list_scratch(groups, blocks, cap):
-    lists = pltpu.VMEM((groups * blocks, LANES), jnp.float32)
+def list_scratch(groups, peers, cap):
+    lists = pltpu.VMEM((groups * peers, LANES), jnp.float32)
     return [lists, lists, pltpu.VMEM((groups * padded(cap, 8), LANES), jnp.float32)]
 
 
@@ -292,7 +299,7 @@
             out_specs=[HBM] + [whole(shape) for shape, _ in shapes[1:]],
             scratch_shapes=[
                 pltpu.VMEM((blocks, blocks), jnp.float32),
-                *list_scratch(groups, blocks, cap),
+                *list_scratch(groups, peers, cap),
                 pltpu.VMEM((lines, LANES), jnp.int32),
                 pltpu.VMEM(send, jnp.float32),
                 pltpu.SMEM((lines, LANES), jnp.int32),
@@ -312,8 +319,8 @@
     count, strip, _ = piece_refs[0].shape
     cap = right_refs[0].shape[0] - 1
 
-    def place_of(left, right):
-        name = right.astype(jnp.int32) - 1
+    def place_of(name):
+        name = (name.astype(jnp.int32) >> 9) - 1
         return (name - (SLOT_PITCH - count) * (name >> 4)).astype(jnp.float32)
 
     lines, _ = list_products(
@@ -337,7 +344,7 @@
         right_ref[cap, 8:16, :] = peak_ref[...]
 
 
-def collect(tables, mates, peak, pieces, base, cap):
+def collect(tables, mates, peak, pieces, base, peers, cap):
     rows = len(pieces)
     count, strip, order = pieces[0].shape
     right = (cap + 1, strip, order)
@@ -350,7 +357,7 @@
             in_specs=[whole(operand.shape) for operand in operands],
             out_specs=[whole(right)] * rows,
             scratch_shapes=[
-                *list_scratch(1, tables[0].shape[0], cap),
+                *list_scratch(1, peers, cap),
                 pltpu.VMEM((8, LANES), jnp.int32),
                 pltpu.VMEM((rows * count, strip, order), jnp.float32),
                 pltpu.SMEM((8, LANES), jnp.int32),
@@ -468,7 +475,7 @@
     def one_round(base, running):
         send, codes, counts, peak, *tables = plan(strips, base, rows, peers, ROUND_CAP)
         left = lax.all_to_all(send, GROUP, 0, 0, tiled=True)
-        right = shift_all(collect(tables, mates, peak, pieces, base, ROUND_CAP))
+        right = shift_all(collect(tables, mates, peak, pieces, base, peers, ROUND_CAP))
         return multiply_round(left, right, codes, counts, base, running, kept)
 
     summed, most = one_round(jnp.zeros((), jnp.int32), None)

time: 93.1 us -> 92.7 us (level)
  no operation moved by 1% of the time
where the time goes in v8:
time: 92.7 us; the launch traced here: 92.3 us
  starting transfers between devices  41.8 us (45%)
  waiting for transfers between devices  30 us (32%)
  Pallas kernels  18.4 us (20%)
    ppermute x14, starting transfers between devices, shift_all(): lax.ppermute(pieces[by], 'row', [(i, (i + by) % rows) for i in range(rows)])  20 us
    ppermute x14, waiting for transfers between devices, shift_all(): lax.ppermute(pieces[by], 'row', [(i, (i + by) % rows) for i in range(rows)])  12.1 us
    all_to_all x1, starting transfers between devices, local(): strips = lax.all_to_all(strips, GROUP, 0, 0, tiled=True)  11.6 us
    all_to_all x1, waiting for transfers between devices, local(): strips = lax.all_to_all(strips, GROUP, 0, 0, tiled=True)  7.83 us
    all_to_all x1, waiting for transfers between devices, one_round(): left = lax.all_to_all(send, GROUP, 0, 0, tiled=True)  6.9 us
    all_to_all x1, starting transfers between devices, one_round(): left = lax.all_to_all(send, GROUP, 0, 0, tiled=True)  5.71 us
    ppermute x3, starting transfers between devices, swap_rows(): return lax.ppermute(array, 'row', [(i, i ^ by) for i in range(rows)])  4.49 us
    pallas_call x1, Pallas kernels, multiply_round(): pl.pallas_call(functools.partial(product_body, first, len(right)), grid_s...  4.25 us
  transfers between devices with their start and end apart: 19, of which 14 were waited for; matrix products, arithmetic and copies ran while one was open for 1% of the time, Pallas kernels for 9%

profile of v8, /device:TPU:4, one launch (start us, length us, event | category | flops | bytes accessed | tf_op | source)
XLA Modules:
  0.0 92.3 jit_solution(11037668544809261099)
XLA Ops:
  1.0 1.1 %collective-permute-done.7 = f32[4,128]{1,0:T(4,128)S(1)} collective-permute-done((f32[4,128]{1,0:T(4,128)S(1)}, f32[4,128]{1,0:T(4,128)S(1)}, u32[]{:S(2)}, u32[]{:S(2)}) %collective-permute-start.7) | collective-permute-done | bytes 2080 | tf_op jit(solution)/shard_map/ppermute | solution.py:455
  2.1 1.6 %collective-permute-start.8 = (f32[4,128]{1,0:T(4,128)S(1)}, f32[4,128]{1,0:T(4,128)S(1)}, u32[]{:S(2)}, u32[]{:S(2)}) collective-permute-start(f32[4,128]{1,0:T(4,128)S(1)} %add.9), channel_id=1, source_target_pairs={{0,64},{32,96},{64,0},{96,32},{128,192},{160,224},{192,128},{224,1... | collective-permute-start | bytes 6152 | tf_op jit(solution)/shard_map/ppermute | solution.py:455
  3.7 2.2 %shard_map.65.strips_in = f32[32,13,4,128]{3,2,1,0:T(4,128)} custom-call(f32[12,128,128]{2,1,0:T(8,128)} %bitcast.13), custom_call_target="tpu_custom_call" | custom-call | tf_op jit(solution)/shard_map/pallas_call | solution.py:89
  5.9 2.8 %collective-permute-start.9 = (f32[4,128]{1,0:T(4,128)S(1)}, f32[4,128]{1,0:T(4,128)S(1)}, u32[]{:S(2)}, u32[]{:S(2)}) collective-permute-start(f32[4,128]{1,0:T(4,128)S(1)} %add.10.one_ref), channel_id=1, source_target_pairs={{0,192},{32,224},{64,128},{96,160},{128,64},{160,96},{192,0},{224,... | collective-permute-start | bytes 6152 | tf_op jit(solution)/shard_map/ppermute | solution.py:455
  8.7 2.1 %collective-permute-done.9.other_ref = f32[4,128]{1,0:T(4,128)S(1)} collective-permute-done((f32[4,128]{1,0:T(4,128)S(1)}, f32[4,128]{1,0:T(4,128)S(1)}, u32[]{:S(2)}, u32[]{:S(2)}) %collective-permute-start.9) | collective-permute-done | bytes 2080 | tf_op jit(solution)/shard_map/ppermute | solution.py:455
  11.4 11.6 %all-to-all-start.1 = ((f32[32,13,4,128]{3,2,1,0:T(4,128)}), f32[32,13,4,128]{3,2,1,0:T(4,128)S(1)}, u32[]{:S(2)}, u32[]{:S(2)}) async-start(f32[32,13,4,128]{3,2,1,0:T(4,128)} %get-tuple-element.128), calls=%async_computation.1 | async-start | bytes 1703936 | tf_op jit(solution)/shard_map/all_to_all | solution.py:471
  23.0 1.8 %shard_map.67 = (f32[12,16,128]{2,1,0:T(8,128)}, f32[12,16,128]{2,1,0:T(8,128)S(1)}, f32[12,16,128]{2,1,0:T(8,128)S(1)}, f32[12,16,128]{2,1,0:T(8,128)S(1)}, f32...) custom-call(f32[12,128,128]{2,1,0:T(8,128)} %bitcast.14), custom_call_target="tpu_custom_call" | custom-call | tf_op jit(solution)/shard_map/pallas_call | solution.py:136
  25.0 3.5 %collective-permute-start.12 = (f32[12,16,128]{2,1,0:T(8,128)S(1)}, f32[12,16,128]{2,1,0:T(8,128)}, u32[]{:S(2)}, u32[]{:S(2)}) collective-permute-start(f32[12,16,128]{2,1,0:T(8,128)S(1)} %get-tuple-element.132), channel_id=1, source_target_pairs={{0,96},{32,128},{64,160},{96,192},{128,224},{160,0},{192,32},{224,... | collective-permute-start | bytes 294920 | tf_op jit(solution)/shard_map/ppermute | solution.py:450
  29.3 2.7 %collective-permute-start.14 = (f32[12,16,128]{2,1,0:T(8,128)S(1)}, f32[12,16,128]{2,1,0:T(8,128)}, u32[]{:S(2)}, u32[]{:S(2)}) collective-permute-start(f32[12,16,128]{2,1,0:T(8,128)S(1)} %get-tuple-element.134), channel_id=1, source_target_pairs={{0,160},{32,192},{64,224},{96,0},{128,32},{160,64},{192,96},{224,1... | collective-permute-start | bytes 294920 | tf_op jit(solution)/shard_map/ppermute | solution.py:450
  32.2 1.7 %collective-permute-start.16 = (f32[12,16,128]{2,1,0:T(8,128)S(1)}, f32[12,16,128]{2,1,0:T(8,128)}, u32[]{:S(2)}, u32[]{:S(2)}) collective-permute-start(f32[12,16,128]{2,1,0:T(8,128)S(1)} %get-tuple-element.136), channel_id=1, source_target_pairs={{0,224},{32,0},{64,32},{96,64},{128,96},{160,128},{192,160},{224,1... | collective-permute-start | bytes 294920 | tf_op jit(solution)/shard_map/ppermute | solution.py:450
  34.0 1.9 %collective-permute-done.12.refs_3_ = f32[12,16,128]{2,1,0:T(8,128)} collective-permute-done((f32[12,16,128]{2,1,0:T(8,128)S(1)}, f32[12,16,128]{2,1,0:T(8,128)}, u32[]{:S(2)}, u32[]{:S(2)}) %collective-permute-start.12) | collective-permute-done | bytes 98336 | tf_op jit(solution)/shard_map/ppermute | solution.py:450
  37.7 7.8 %all-to-all-done.1 = f32[32,13,4,128]{3,2,1,0:T(4,128)S(1)} async-done(((f32[32,13,4,128]{3,2,1,0:T(4,128)}), f32[32,13,4,128]{3,2,1,0:T(4,128)S(1)}, u32[]{:S(2)}, u32[]{:S(2)}) %all-to-all-start.1) | async-done | bytes 852000 | tf_op jit(solution)/shard_map/all_to_all | solution.py:471
  45.5 4.1 %shard_map.68 = (f32[32,20,4,128]{3,2,1,0:T(4,128)}, s32[8,128]{1,0:T(8,128)S(1)}, s32[8,128]{1,0:T(8,128)S(1)}, f32[8,128]{1,0:T(8,128)S(1)}, bf16[256,256]{1,0...) custom-call(s32[1]{0:T(128)} %constant.2.clone.1.base_ref, f32[416,4,128]{2,1,0:T(4,128)S(1)} %bitcast.11), custom_call_target="tpu_custom_call" | custom-call | tf_op jit(solution)/shard_map/pallas_call | solution.py:293
  49.6 5.7 %all-to-all-start.2 = ((f32[32,20,4,128]{3,2,1,0:T(4,128)}), f32[32,20,4,128]{3,2,1,0:T(4,128)S(1)}, u32[]{:S(2)}, u32[]{:S(2)}) async-start(f32[32,20,4,128]{3,2,1,0:T(4,128)} %get-tuple-element.160), calls=%async_computation.2 | async-start | bytes 2621440 | tf_op jit(solution)/shard_map/all_to_all | solution.py:477
  55.4 3.7 %shard_map.69 = (f32[21,16,128]{2,1,0:T(8,128)S(1)}, f32[21,16,128]{2,1,0:T(8,128)S(1)}, f32[21,16,128]{2,1,0:T(8,128)S(1)}, f32[21,16,128]{2,1,0:T(8,128)}, f32...) custom-call(s32[1]{0:T(128)} %constant.2.clone.1.base_ref, ...), custom_call_target="tpu_custom_call" | custom-call | tf_op jit(solution)/shard_map/pallas_call | solution.py:352
  59.1 3.0 %collective-permute-start.19 = (f32[21,16,128]{2,1,0:T(8,128)}, f32[21,16,128]{2,1,0:T(8,128)S(1)}, u32[]{:S(2)}, u32[]{:S(2)}) collective-permute-start(f32[21,16,128]{2,1,0:T(8,128)} %get-tuple-element.153), channel_id=1, source_target_pairs={{0,96},{32,128},{64,160},{96,192},{128,224},{160,0},{192,32},{224,... | collective-permute-start | bytes 516104 | tf_op jit(solution)/shard_map/ppermute | solution.py:450
  62.1 1.4 %collective-permute-start.20 = (f32[21,16,128]{2,1,0:T(8,128)}, f32[21,16,128]{2,1,0:T(8,128)S(1)}, u32[]{:S(2)}, u32[]{:S(2)}) collective-permute-start(f32[21,16,128]{2,1,0:T(8,128)} %get-tuple-element.154), channel_id=1, source_target_pairs={{0,128},{32,160},{64,192},{96,224},{128,0},{160,32},{192,64},{224,... | collective-permute-start | bytes 516104 | tf_op jit(solution)/shard_map/ppermute | solution.py:450
  63.5 2.3 %collective-permute-start.21 = (f32[21,16,128]{2,1,0:T(8,128)}, f32[21,16,128]{2,1,0:T(8,128)S(1)}, u32[]{:S(2)}, u32[]{:S(2)}) collective-permute-start(f32[21,16,128]{2,1,0:T(8,128)} %get-tuple-element.155), channel_id=1, source_target_pairs={{0,160},{32,192},{64,224},{96,0},{128,32},{160,64},{192,96},{224,1... | collective-permute-start | bytes 516104 | tf_op jit(solution)/shard_map/ppermute | solution.py:450
  67.5 3.2 %collective-permute-start.23 = (f32[21,16,128]{2,1,0:T(8,128)}, f32[21,16,128]{2,1,0:T(8,128)}, u32[]{:S(2)}, u32[]{:S(2)}) collective-permute-start(f32[21,16,128]{2,1,0:T(8,128)} %get-tuple-element.157), channel_id=1, source_target_pairs={{0,224},{32,0},{64,32},{96,64},{128,96},{160,128},{192,160},{224,1... | collective-permute-start | bytes 516104 | tf_op jit(solution)/shard_map/ppermute | solution.py:450
  70.7 3.4 %collective-permute-done.19.refs_3_ = f32[21,16,128]{2,1,0:T(8,128)S(1)} collective-permute-done((f32[21,16,128]{2,1,0:T(8,128)}, f32[21,16,128]{2,1,0:T(8,128)S(1)}, u32[]{:S(2)}, u32[]{:S(2)}) %collective-permute-start.19) | collective-permute-done | bytes 172064 | tf_op jit(solution)/shard_map/ppermute | solution.py:450
  74.1 1.2 %collective-permute-done.20.refs_4_ = f32[21,16,128]{2,1,0:T(8,128)S(1)} collective-permute-done((f32[21,16,128]{2,1,0:T(8,128)}, f32[21,16,128]{2,1,0:T(8,128)S(1)}, u32[]{:S(2)}, u32[]{:S(2)}) %collective-permute-start.20) | collective-permute-done | bytes 172064 | tf_op jit(solution)/shard_map/ppermute | solution.py:450
  75.3 1.8 %collective-permute-done.22.refs_6_ = f32[21,16,128]{2,1,0:T(8,128)S(1)} collective-permute-done((f32[21,16,128]{2,1,0:T(8,128)}, f32[21,16,128]{2,1,0:T(8,128)S(1)}, u32[]{:S(2)}, u32[]{:S(2)}) %collective-permute-start.22) | collective-permute-done | bytes 172064 | tf_op jit(solution)/shard_map/ppermute | solution.py:450
  80.4 6.9 %all-to-all-done.2.left_ref = f32[32,20,4,128]{3,2,1,0:T(4,128)S(1)} async-done(((f32[32,20,4,128]{3,2,1,0:T(4,128)}), f32[32,20,4,128]{3,2,1,0:T(4,128)S(1)}, u32[]{:S(2)}, u32[]{:S(2)}) %all-to-all-start.2) | async-done | bytes 1310752 | tf_op jit(solution)/shard_map/all_to_all | solution.py:477
  87.3 4.2 %shard_map.71 = f32[12,128,128]{2,1,0:T(8,128)} custom-call(s32[2]{0:T(128)S(1)} %pad_add_fusion.1.scalars, s32[8,128]{1,0:T(8,128)S(1)} %get-tuple-element.158.codes, s32[8,128]{1,0:T(8,128)S(1)} %get-tuple-element.159.counts, f32[32,20,4,128]{3,2,1,0:T(4,128)S(1)} %all-to-all-done.2.left_ref, f32[21,16,128]{2,1,0:T(8,128)S(1)} %get-tuple-element.150.refs_0_, ...), custom_call_target="tpu_custom_call" | custom-call | tf_op jit(solution)/shard_map/pallas_call | solution.py:432
  (27 shorter events, 10.3 us)
Async XLA Ops:
  0.9 1.2 %collective-permute-start.7 = (f32[4,128]{1,0:T(4,128)S(1)}, f32[4,128]{1,0:T(4,128)S(1)}, u32[]{:S(2)}, u32[]{:S(2)}) collective-permute-start(f32[4,128]{1,0:T(4,128)S(1)} %get-tuple-element.124), channel_id=1, source_target_pairs={{0,32},{32,0},{64,96},{96,64},{128,160},{160,128},{192,224},{224,1... | collective-permute-start | bytes 6152 | tf_op jit(solution)/shard_map/ppermute | solution.py:455
  2.1 3.8 %collective-permute-start.8 = (f32[4,128]{1,0:T(4,128)S(1)}, f32[4,128]{1,0:T(4,128)S(1)}, u32[]{:S(2)}, u32[]{:S(2)}) collective-permute-start(f32[4,128]{1,0:T(4,128)S(1)} %add.9), channel_id=1, source_target_pairs={{0,64},{32,96},{64,0},{96,32},{128,192},{160,224},{192,128},{224,1... | collective-permute-start | bytes 6152 | tf_op jit(solution)/shard_map/ppermute | solution.py:455
  5.9 4.9 %collective-permute-start.9 = (f32[4,128]{1,0:T(4,128)S(1)}, f32[4,128]{1,0:T(4,128)S(1)}, u32[]{:S(2)}, u32[]{:S(2)}) collective-permute-start(f32[4,128]{1,0:T(4,128)S(1)} %add.10.one_ref), channel_id=1, source_target_pairs={{0,192},{32,224},{64,128},{96,160},{128,64},{160,96},{192,0},{224,... | collective-permute-start | bytes 6152 | tf_op jit(solution)/shard_map/ppermute | solution.py:455
  11.4 34.1 %all-to-all-start.1 = ((f32[32,13,4,128]{3,2,1,0:T(4,128)}), f32[32,13,4,128]{3,2,1,0:T(4,128)S(1)}, u32[]{:S(2)}, u32[]{:S(2)}) async-start(f32[32,13,4,128]{3,2,1,0:T(4,128)} %get-tuple-element.128), calls=%async_computation.1 | async-start | bytes 1703936 | tf_op jit(solution)/shard_map/all_to_all | solution.py:471
  24.9 7.2 %collective-permute-start.10 = (f32[12,16,128]{2,1,0:T(8,128)S(1)}, f32[12,16,128]{2,1,0:T(8,128)}, u32[]{:S(2)}, u32[]{:S(2)}) collective-permute-start(f32[12,16,128]{2,1,0:T(8,128)S(1)} %get-tuple-element.130), channel_id=1, source_target_pairs={{0,32},{32,64},{64,96},{96,128},{128,160},{160,192},{192,224},{224... | collective-permute-start | bytes 294920 | tf_op jit(solution)/shard_map/ppermute | solution.py:450
  24.9 7.4 %collective-permute-start.11 = (f32[12,16,128]{2,1,0:T(8,128)S(1)}, f32[12,16,128]{2,1,0:T(8,128)}, u32[]{:S(2)}, u32[]{:S(2)}) collective-permute-start(f32[12,16,128]{2,1,0:T(8,128)S(1)} %get-tuple-element.131), channel_id=1, source_target_pairs={{0,64},{32,96},{64,128},{96,160},{128,192},{160,224},{192,0},{224,... | collective-permute-start | bytes 294920 | tf_op jit(solution)/shard_map/ppermute | solution.py:450
  25.0 10.9 %collective-permute-start.12 = (f32[12,16,128]{2,1,0:T(8,128)S(1)}, f32[12,16,128]{2,1,0:T(8,128)}, u32[]{:S(2)}, u32[]{:S(2)}) collective-permute-start(f32[12,16,128]{2,1,0:T(8,128)S(1)} %get-tuple-element.132), channel_id=1, source_target_pairs={{0,96},{32,128},{64,160},{96,192},{128,224},{160,0},{192,32},{224,... | collective-permute-start | bytes 294920 | tf_op jit(solution)/shard_map/ppermute | solution.py:450
  28.5 8.5 %collective-permute-start.13 = (f32[12,16,128]{2,1,0:T(8,128)S(1)}, f32[12,16,128]{2,1,0:T(8,128)}, u32[]{:S(2)}, u32[]{:S(2)}) collective-permute-start(f32[12,16,128]{2,1,0:T(8,128)S(1)} %get-tuple-element.133), channel_id=1, source_target_pairs={{0,128},{32,160},{64,192},{96,224},{128,0},{160,32},{192,64},{224,... | collective-permute-start | bytes 294920 | tf_op jit(solution)/shard_map/ppermute | solution.py:450
  29.3 7.7 %collective-permute-start.14 = (f32[12,16,128]{2,1,0:T(8,128)S(1)}, f32[12,16,128]{2,1,0:T(8,128)}, u32[]{:S(2)}, u32[]{:S(2)}) collective-permute-start(f32[12,16,128]{2,1,0:T(8,128)S(1)} %get-tuple-element.134), channel_id=1, source_target_pairs={{0,160},{32,192},{64,224},{96,0},{128,32},{160,64},{192,96},{224,1... | collective-permute-start | bytes 294920 | tf_op jit(solution)/shard_map/ppermute | solution.py:450
  32.1 5.4 %collective-permute-start.15 = (f32[12,16,128]{2,1,0:T(8,128)S(1)}, f32[12,16,128]{2,1,0:T(8,128)}, u32[]{:S(2)}, u32[]{:S(2)}) collective-permute-start(f32[12,16,128]{2,1,0:T(8,128)S(1)} %get-tuple-element.135), channel_id=1, source_target_pairs={{0,192},{32,224},{64,0},{96,32},{128,64},{160,96},{192,128},{224,1... | collective-permute-start | bytes 294920 | tf_op jit(solution)/shard_map/ppermute | solution.py:450
  32.2 5.5 %collective-permute-start.16 = (f32[12,16,128]{2,1,0:T(8,128)S(1)}, f32[12,16,128]{2,1,0:T(8,128)}, u32[]{:S(2)}, u32[]{:S(2)}) collective-permute-start(f32[12,16,128]{2,1,0:T(8,128)S(1)} %get-tuple-element.136), channel_id=1, source_target_pairs={{0,224},{32,0},{64,32},{96,64},{128,96},{160,128},{192,160},{224,1... | collective-permute-start | bytes 294920 | tf_op jit(solution)/shard_map/ppermute | solution.py:450
  49.6 37.7 %all-to-all-start.2 = ((f32[32,20,4,128]{3,2,1,0:T(4,128)}), f32[32,20,4,128]{3,2,1,0:T(4,128)S(1)}, u32[]{:S(2)}, u32[]{:S(2)}) async-start(f32[32,20,4,128]{3,2,1,0:T(4,128)} %get-tuple-element.160), calls=%async_computation.2 | async-start | bytes 2621440 | tf_op jit(solution)/shard_map/all_to_all | solution.py:477
  59.0 7.3 %collective-permute-start.17 = (f32[21,16,128]{2,1,0:T(8,128)S(1)}, f32[21,16,128]{2,1,0:T(8,128)S(1)}, u32[]{:S(2)}, u32[]{:S(2)}) collective-permute-start(f32[21,16,128]{2,1,0:T(8,128)S(1)} %get-tuple-element.151), channel_id=1, source_target_pairs={{0,32},{32,64},{64,96},{96,128},{128,160},{160,192},{192,224},{224... | collective-permute-start | bytes 516104 | tf_op jit(solution)/shard_map/ppermute | solution.py:450
  59.0 8.5 %collective-permute-start.18 = (f32[21,16,128]{2,1,0:T(8,128)S(1)}, f32[21,16,128]{2,1,0:T(8,128)S(1)}, u32[]{:S(2)}, u32[]{:S(2)}) collective-permute-start(f32[21,16,128]{2,1,0:T(8,128)S(1)} %get-tuple-element.152), channel_id=1, source_target_pairs={{0,64},{32,96},{64,128},{96,160},{128,192},{160,224},{192,0},{224,... | collective-permute-start | bytes 516104 | tf_op jit(solution)/shard_map/ppermute | solution.py:450
  59.1 15.0 %collective-permute-start.19 = (f32[21,16,128]{2,1,0:T(8,128)}, f32[21,16,128]{2,1,0:T(8,128)S(1)}, u32[]{:S(2)}, u32[]{:S(2)}) collective-permute-start(f32[21,16,128]{2,1,0:T(8,128)} %get-tuple-element.153), channel_id=1, source_target_pairs={{0,96},{32,128},{64,160},{96,192},{128,224},{160,0},{192,32},{224,... | collective-permute-start | bytes 516104 | tf_op jit(solution)/shard_map/ppermute | solution.py:450
  62.1 13.2 %collective-permute-start.20 = (f32[21,16,128]{2,1,0:T(8,128)}, f32[21,16,128]{2,1,0:T(8,128)S(1)}, u32[]{:S(2)}, u32[]{:S(2)}) collective-permute-start(f32[21,16,128]{2,1,0:T(8,128)} %get-tuple-element.154), channel_id=1, source_target_pairs={{0,128},{32,160},{64,192},{96,224},{128,0},{160,32},{192,64},{224,... | collective-permute-start | bytes 516104 | tf_op jit(solution)/shard_map/ppermute | solution.py:450
  63.5 11.9 %collective-permute-start.21 = (f32[21,16,128]{2,1,0:T(8,128)}, f32[21,16,128]{2,1,0:T(8,128)S(1)}, u32[]{:S(2)}, u32[]{:S(2)}) collective-permute-start(f32[21,16,128]{2,1,0:T(8,128)} %get-tuple-element.155), channel_id=1, source_target_pairs={{0,160},{32,192},{64,224},{96,0},{128,32},{160,64},{192,96},{224,1... | collective-permute-start | bytes 516104 | tf_op jit(solution)/shard_map/ppermute | solution.py:450
  66.3 10.9 %collective-permute-start.22 = (f32[21,16,128]{2,1,0:T(8,128)}, f32[21,16,128]{2,1,0:T(8,128)S(1)}, u32[]{:S(2)}, u32[]{:S(2)}) collective-permute-start(f32[21,16,128]{2,1,0:T(8,128)} %get-tuple-element.156), channel_id=1, source_target_pairs={{0,192},{32,224},{64,0},{96,32},{128,64},{160,96},{192,128},{224,1... | collective-permute-start | bytes 516104 | tf_op jit(solution)/shard_map/ppermute | solution.py:450
  67.5 10.7 %collective-permute-start.23 = (f32[21,16,128]{2,1,0:T(8,128)}, f32[21,16,128]{2,1,0:T(8,128)}, u32[]{:S(2)}, u32[]{:S(2)}) collective-permute-start(f32[21,16,128]{2,1,0:T(8,128)} %get-tuple-element.157), channel_id=1, source_target_pairs={{0,224},{32,0},{64,32},{96,64},{128,96},{160,128},{192,160},{224,1... | collective-permute-start | bytes 516104 | tf_op jit(solution)/shard_map/ppermute | solution.py:450

commit v9 on v8

--- a/solution.py
+++ b/solution.py
@@ -95,9 +95,12 @@
     )(*in_hbm(tiles))
 
 
-def stamp_body(one_ref, other_ref, wanted_ref, strips_in, strips_out, total_ref, meta, sem):
+def stamp_body(*refs):
+    *listed_refs, wanted_ref, strips_in, strips_out, total_ref, meta, sem = refs
     peers, per_peer = strips_out.shape[:2]
-    total = one_ref[...] + other_ref[...]
+    total = listed_refs[0][...]
+    for listed_ref in listed_refs[1:]:
+        total = total + listed_ref[...]
     total_ref[...] = total
     full = jnp.concatenate([total[0:2, :], wanted_ref[...]])
     for peer in range(peers):
@@ -107,18 +110,19 @@
     copy.wait()
 
 
-def stamp(one, other, wanted, strips):
+def stamp(listed, wanted, strips):
     peers, _, strip, order = strips.shape
     vmem = pl.BlockSpec(memory_space=pltpu.VMEM)
+    small = [*listed, wanted]
     return pl.pallas_call(
         stamp_body,
-        in_specs=[vmem, vmem, vmem, HBM],
+        in_specs=[vmem] * len(small) + [HBM],
         out_specs=[HBM, vmem],
-        out_shape=[pltpu.HBM(strips.shape, jnp.float32), jax.ShapeDtypeStruct(one.shape, jnp.float32)],
-        input_output_aliases={3: 0},
+        out_shape=[pltpu.HBM(strips.shape, jnp.float32), jax.ShapeDtypeStruct(listed[0].shape, jnp.float32)],
+        input_output_aliases={len(small): 0},
         scratch_shapes=[pltpu.VMEM((peers, strip, order), jnp.float32), pltpu.SemaphoreType.DMA],
         compiler_params=LIMIT,
-    )(one, other, wanted, *in_hbm(strips))
+    )(*small, *in_hbm(strips))
 
 
 def pack_right_body(tiles_ref, *out_refs):
@@ -451,10 +455,6 @@
     ]
 
 
-def swap_rows(array, rows, by):
-    return lax.ppermute(array, "row", [(i, i ^ by) for i in range(rows)])
-
-
 def local(tile_values, tile_rows, tile_cols, tile_counts, out_rows, out_cols):
     order = tile_values.shape[-1]
     kept = out_rows.shape[-1]
@@ -463,10 +463,9 @@
     tiles = tile_values.reshape(-1, order, order)
 
     listed, wanted = label(tile_rows, tile_cols, tile_counts, out_rows, out_cols)
-    for by in (1, 2):
-        listed = listed + swap_rows(listed, rows, by)
-    listed, strips = lax.optimization_barrier((listed, pack(tiles, peers)))
-    strips, mates = stamp(listed, swap_rows(listed, rows, rows - 2), wanted, strips)
+    listed = listed + lax.ppermute(listed, "row", [(i, i ^ 1) for i in range(rows)])
+    others = [lax.ppermute(listed, "row", [(i, (i + by) % rows) for i in range(rows)]) for by in range(2, rows, 2)]
+    strips, mates = stamp([listed, *others], wanted, pack(tiles, peers))
     pieces = shift_all(pack_right(tiles, rows))
     strips = lax.all_to_all(strips, GROUP, 0, 0, tiled=True)
     strips, pieces = lax.optimization_barrier((strips, pieces))

time: 92.7 us -> 94.4 us (1.018)
  waiting for transfers between devices: 30 us -> 35.6 us
  starting transfers between devices: 41.8 us -> 37.6 us
    ppermute x14, waiting for transfers between devices: 12.1 us -> 16.7 us  [shift_all(): lax.ppermute(pieces[by], 'row', [(i, (i + by) % rows) for i in range(rows)])]
    ppermute x14, starting transfers between devices: 20 us -> 15.6 us  [shift_all(): lax.ppermute(pieces[by], 'row', [(i, (i + by) % rows) for i in range(rows)])]
    all_to_all x1, waiting for transfers between devices: 6.9 us -> 8.83 us  [one_round(): left = lax.all_to_all(send, GROUP, 0, 0, tiled=True)]
    ppermute x3 -> x4, waiting for transfers between devices: 3.21 us -> 2.76 us  [the longest x3 1.62 us: local(): lax.ppermute(listed, 'row', [(i, (i + by) % rows) for i in range(rows)])]
    ppermute x3 -> x4, starting transfers between devices: 4.49 us -> 4.71 us  [the longest x3 4.61 us: local(): lax.ppermute(listed, 'row', [(i, (i + by) % rows) for i in range(rows)])]
  transfers between devices with their start and end apart: 19 -> 20, of which waited for: 14 -> 17; matrix products, arithmetic and copies ran while one was open for 1% -> 1% of each run, Pallas kernels for 9% -> 9%
where the time goes in v9:
time: 94.4 us; the launch traced here: 93.8 us
  starting transfers between devices  37.6 us (40%)
  waiting for transfers between devices  35.6 us (38%)
  Pallas kernels  18.4 us (19%)
    ppermute x14, waiting for transfers between devices, shift_all(): lax.ppermute(pieces[by], 'row', [(i, (i + by) % rows) for i in range(rows)])  16.7 us
    ppermute x14, starting transfers between devices, shift_all(): lax.ppermute(pieces[by], 'row', [(i, (i + by) % rows) for i in range(rows)])  15.6 us
    all_to_all x1, starting transfers between devices, local(): strips = lax.all_to_all(strips, GROUP, 0, 0, tiled=True)  11.6 us
    all_to_all x1, waiting for transfers between devices, one_round(): left = lax.all_to_all(send, GROUP, 0, 0, tiled=True)  8.83 us
    all_to_all x1, waiting for transfers between devices, local(): strips = lax.all_to_all(strips, GROUP, 0, 0, tiled=True)  7.28 us
    all_to_all x1, starting transfers between devices, one_round(): left = lax.all_to_all(send, GROUP, 0, 0, tiled=True)  5.71 us
    ppermute x3, starting transfers between devices, local(): lax.ppermute(listed, 'row', [(i, (i + by) % rows) for i in range(rows)])  4.61 us
    pallas_call x1, Pallas kernels, multiply_round(): pl.pallas_call(functools.partial(product_body, first, len(right)), grid_s...  4.25 us
  transfers between devices with their start and end apart: 20, of which 17 were waited for; matrix products, arithmetic and copies ran while one was open for 1% of the time, Pallas kernels for 9%

profile of v9, /device:TPU:4, one launch (start us, length us, event | category | flops | bytes accessed | tf_op | source)
XLA Modules:
  0.0 93.8 jit_solution(18130503054919310254)
XLA Ops:
  2.1 3.0 %collective-permute-start.10 = (f32[4,128]{1,0:T(4,128)S(1)}, f32[4,128]{1,0:T(4,128)S(1)}, u32[]{:S(2)}, u32[]{:S(2)}) collective-permute-start(f32[4,128]{1,0:T(4,128)S(1)} %add.6.refs_0_), channel_id=1, source_target_pairs={{0,192},{32,224},{64,0},{96,32},{128,64},{160,96},{192,128},{224,1... | collective-permute-start | bytes 6152 | tf_op jit(solution)/shard_map/ppermute | solution.py:467
  6.7 2.2 %shard_map.65.refs_5_ = f32[32,13,4,128]{3,2,1,0:T(4,128)} custom-call(f32[12,128,128]{2,1,0:T(8,128)} %bitcast.13), custom_call_target="tpu_custom_call" | custom-call | tf_op jit(solution)/shard_map/pallas_call | solution.py:89
  8.9 1.3 %collective-permute-done.9.refs_2_ = f32[4,128]{1,0:T(4,128)S(1)} collective-permute-done((f32[4,128]{1,0:T(4,128)S(1)}, f32[4,128]{1,0:T(4,128)S(1)}, u32[]{:S(2)}, u32[]{:S(2)}) %collective-permute-start.9) | collective-permute-done | bytes 2080 | tf_op jit(solution)/shard_map/ppermute | solution.py:467
  11.2 11.6 %all-to-all-start.1 = ((f32[32,13,4,128]{3,2,1,0:T(4,128)}), f32[32,13,4,128]{3,2,1,0:T(4,128)S(1)}, u32[]{:S(2)}, u32[]{:S(2)}) async-start(f32[32,13,4,128]{3,2,1,0:T(4,128)} %get-tuple-element.124), calls=%async_computation.1 | async-start | bytes 1703936 | tf_op jit(solution)/shard_map/all_to_all | solution.py:470
  22.8 1.8 %shard_map.67 = (f32[12,16,128]{2,1,0:T(8,128)}, f32[12,16,128]{2,1,0:T(8,128)S(1)}, f32[12,16,128]{2,1,0:T(8,128)S(1)}, f32[12,16,128]{2,1,0:T(8,128)S(1)}, f32...) custom-call(f32[12,128,128]{2,1,0:T(8,128)} %bitcast.14), custom_call_target="tpu_custom_call" | custom-call | tf_op jit(solution)/shard_map/pallas_call | solution.py:140
  25.0 1.2 %collective-permute-start.13 = (f32[12,16,128]{2,1,0:T(8,128)S(1)}, f32[12,16,128]{2,1,0:T(8,128)}, u32[]{:S(2)}, u32[]{:S(2)}) collective-permute-start(f32[12,16,128]{2,1,0:T(8,128)S(1)} %get-tuple-element.128), channel_id=1, source_target_pairs={{0,96},{32,128},{64,160},{96,192},{128,224},{160,0},{192,32},{224,... | collective-permute-start | bytes 294920 | tf_op jit(solution)/shard_map/ppermute | solution.py:454
  26.2 2.9 %collective-permute-start.14 = (f32[12,16,128]{2,1,0:T(8,128)S(1)}, f32[12,16,128]{2,1,0:T(8,128)}, u32[]{:S(2)}, u32[]{:S(2)}) collective-permute-start(f32[12,16,128]{2,1,0:T(8,128)S(1)} %get-tuple-element.129), channel_id=1, source_target_pairs={{0,128},{32,160},{64,192},{96,224},{128,0},{160,32},{192,64},{224,... | collective-permute-start | bytes 294920 | tf_op jit(solution)/shard_map/ppermute | solution.py:454
  30.5 1.5 %collective-permute-start.16 = (f32[12,16,128]{2,1,0:T(8,128)S(1)}, f32[12,16,128]{2,1,0:T(8,128)}, u32[]{:S(2)}, u32[]{:S(2)}) collective-permute-start(f32[12,16,128]{2,1,0:T(8,128)S(1)} %get-tuple-element.131), channel_id=1, source_target_pairs={{0,192},{32,224},{64,0},{96,32},{128,64},{160,96},{192,128},{224,1... | collective-permute-start | bytes 294920 | tf_op jit(solution)/shard_map/ppermute | solution.py:454
  32.2 1.7 %collective-permute-done.13.refs_3_ = f32[12,16,128]{2,1,0:T(8,128)} collective-permute-done((f32[12,16,128]{2,1,0:T(8,128)S(1)}, f32[12,16,128]{2,1,0:T(8,128)}, u32[]{:S(2)}, u32[]{:S(2)}) %collective-permute-start.13) | collective-permute-done | bytes 98336 | tf_op jit(solution)/shard_map/ppermute | solution.py:454
  33.9 1.1 %collective-permute-done.14.refs_4_ = f32[12,16,128]{2,1,0:T(8,128)} collective-permute-done((f32[12,16,128]{2,1,0:T(8,128)S(1)}, f32[12,16,128]{2,1,0:T(8,128)}, u32[]{:S(2)}, u32[]{:S(2)}) %collective-permute-start.14) | collective-permute-done | bytes 98336 | tf_op jit(solution)/shard_map/ppermute | solution.py:454
  35.0 2.2 %collective-permute-done.16.refs_6_ = f32[12,16,128]{2,1,0:T(8,128)} collective-permute-done((f32[12,16,128]{2,1,0:T(8,128)S(1)}, f32[12,16,128]{2,1,0:T(8,128)}, u32[]{:S(2)}, u32[]{:S(2)}) %collective-permute-start.16) | collective-permute-done | bytes 98336 | tf_op jit(solution)/shard_map/ppermute | solution.py:454
  37.8 7.3 %all-to-all-done.1 = f32[32,13,4,128]{3,2,1,0:T(4,128)S(1)} async-done(((f32[32,13,4,128]{3,2,1,0:T(4,128)}), f32[32,13,4,128]{3,2,1,0:T(4,128)S(1)}, u32[]{:S(2)}, u32[]{:S(2)}) %all-to-all-start.1) | async-done | bytes 852000 | tf_op jit(solution)/shard_map/all_to_all | solution.py:470
  45.1 4.1 %shard_map.68 = (f32[32,20,4,128]{3,2,1,0:T(4,128)}, s32[8,128]{1,0:T(8,128)S(1)}, s32[8,128]{1,0:T(8,128)S(1)}, f32[8,128]{1,0:T(8,128)S(1)}, bf16[256,256]{1,0...) custom-call(s32[1]{0:T(128)} %constant.2.clone.1.base_ref, f32[416,4,128]{2,1,0:T(4,128)S(1)} %bitcast.11), custom_call_target="tpu_custom_call" | custom-call | tf_op jit(solution)/shard_map/pallas_call | solution.py:297
  49.2 5.7 %all-to-all-start.2 = ((f32[32,20,4,128]{3,2,1,0:T(4,128)}), f32[32,20,4,128]{3,2,1,0:T(4,128)S(1)}, u32[]{:S(2)}, u32[]{:S(2)}) async-start(f32[32,20,4,128]{3,2,1,0:T(4,128)} %get-tuple-element.156), calls=%async_computation.2 | async-start | bytes 2621440 | tf_op jit(solution)/shard_map/all_to_all | solution.py:476
  54.9 3.6 %shard_map.69 = (f32[21,16,128]{2,1,0:T(8,128)S(1)}, f32[21,16,128]{2,1,0:T(8,128)S(1)}, f32[21,16,128]{2,1,0:T(8,128)S(1)}, f32[21,16,128]{2,1,0:T(8,128)}, f32...) custom-call(s32[1]{0:T(128)} %constant.2.clone.1.base_ref, ...), custom_call_target="tpu_custom_call" | custom-call | tf_op jit(solution)/shard_map/pallas_call | solution.py:356
  59.7 1.1 %collective-permute-start.20 = (f32[21,16,128]{2,1,0:T(8,128)}, f32[21,16,128]{2,1,0:T(8,128)S(1)}, u32[]{:S(2)}, u32[]{:S(2)}) collective-permute-start(f32[21,16,128]{2,1,0:T(8,128)} %get-tuple-element.149), channel_id=1, source_target_pairs={{0,96},{32,128},{64,160},{96,192},{128,224},{160,0},{192,32},{224,... | collective-permute-start | bytes 516104 | tf_op jit(solution)/shard_map/ppermute | solution.py:454
  60.8 2.9 %collective-permute-start.21 = (f32[21,16,128]{2,1,0:T(8,128)}, f32[21,16,128]{2,1,0:T(8,128)S(1)}, u32[]{:S(2)}, u32[]{:S(2)}) collective-permute-start(f32[21,16,128]{2,1,0:T(8,128)} %get-tuple-element.150), channel_id=1, source_target_pairs={{0,128},{32,160},{64,192},{96,224},{128,0},{160,32},{192,64},{224,... | collective-permute-start | bytes 516104 | tf_op jit(solution)/shard_map/ppermute | solution.py:454
  64.5 1.3 %collective-permute-done.18.refs_1_ = f32[21,16,128]{2,1,0:T(8,128)S(1)} collective-permute-done((f32[21,16,128]{2,1,0:T(8,128)S(1)}, f32[21,16,128]{2,1,0:T(8,128)S(1)}, u32[]{:S(2)}, u32[]{:S(2)}) %collective-permute-start.18) | collective-permute-done | bytes 172064 | tf_op jit(solution)/shard_map/ppermute | solution.py:454
  67.0 2.4 %collective-permute-start.24 = (f32[21,16,128]{2,1,0:T(8,128)}, f32[21,16,128]{2,1,0:T(8,128)}, u32[]{:S(2)}, u32[]{:S(2)}) collective-permute-start(f32[21,16,128]{2,1,0:T(8,128)} %get-tuple-element.153), channel_id=1, source_target_pairs={{0,224},{32,0},{64,32},{96,64},{128,96},{160,128},{192,160},{224,1... | collective-permute-start | bytes 516104 | tf_op jit(solution)/shard_map/ppermute | solution.py:454
  69.4 3.5 %collective-permute-done.20.refs_3_ = f32[21,16,128]{2,1,0:T(8,128)S(1)} collective-permute-done((f32[21,16,128]{2,1,0:T(8,128)}, f32[21,16,128]{2,1,0:T(8,128)S(1)}, u32[]{:S(2)}, u32[]{:S(2)}) %collective-permute-start.20) | collective-permute-done | bytes 172064 | tf_op jit(solution)/shard_map/ppermute | solution.py:454
  72.9 1.2 %collective-permute-done.21.refs_4_ = f32[21,16,128]{2,1,0:T(8,128)S(1)} collective-permute-done((f32[21,16,128]{2,1,0:T(8,128)}, f32[21,16,128]{2,1,0:T(8,128)S(1)}, u32[]{:S(2)}, u32[]{:S(2)}) %collective-permute-start.21) | collective-permute-done | bytes 172064 | tf_op jit(solution)/shard_map/ppermute | solution.py:454
  75.0 1.9 %collective-permute-done.23.refs_6_ = f32[21,16,128]{2,1,0:T(8,128)S(1)} collective-permute-done((f32[21,16,128]{2,1,0:T(8,128)}, f32[21,16,128]{2,1,0:T(8,128)S(1)}, u32[]{:S(2)}, u32[]{:S(2)}) %collective-permute-start.23) | collective-permute-done | bytes 172064 | tf_op jit(solution)/shard_map/ppermute | solution.py:454
  79.9 8.8 %all-to-all-done.2.left_ref = f32[32,20,4,128]{3,2,1,0:T(4,128)S(1)} async-done(((f32[32,20,4,128]{3,2,1,0:T(4,128)}), f32[32,20,4,128]{3,2,1,0:T(4,128)S(1)}, u32[]{:S(2)}, u32[]{:S(2)}) %all-to-all-start.2) | async-done | bytes 1310752 | tf_op jit(solution)/shard_map/all_to_all | solution.py:476
  88.8 4.2 %shard_map.71 = f32[12,128,128]{2,1,0:T(8,128)} custom-call(s32[2]{0:T(128)S(1)} %pad_add_fusion.1.scalars, s32[8,128]{1,0:T(8,128)S(1)} %get-tuple-element.154.codes, s32[8,128]{1,0:T(8,128)S(1)} %get-tuple-element.155.counts, f32[32,20,4,128]{3,2,1,0:T(4,128)S(1)} %all-to-all-done.2.left_ref, f32[21,16,128]{2,1,0:T(8,128)S(1)} %get-tuple-element.146.refs_0_, ...), custom_call_target="tpu_custom_call" | custom-call | tf_op jit(solution)/shard_map/pallas_call | solution.py:436
  (28 shorter events, 14.9 us)
Async XLA Ops:
  0.9 1.2 %collective-permute-start.7 = (f32[4,128]{1,0:T(4,128)S(1)}, f32[4,128]{1,0:T(4,128)S(1)}, u32[]{:S(2)}, u32[]{:S(2)}) collective-permute-start(f32[4,128]{1,0:T(4,128)S(1)} %get-tuple-element.122), channel_id=1, source_target_pairs={{0,32},{32,0},{64,96},{96,64},{128,160},{160,128},{192,224},{224,1... | collective-permute-start | bytes 6152 | tf_op jit(solution)/shard_map/ppermute | solution.py:466
  2.1 6.8 %collective-permute-start.10 = (f32[4,128]{1,0:T(4,128)S(1)}, f32[4,128]{1,0:T(4,128)S(1)}, u32[]{:S(2)}, u32[]{:S(2)}) collective-permute-start(f32[4,128]{1,0:T(4,128)S(1)} %add.6.refs_0_), channel_id=1, source_target_pairs={{0,192},{32,224},{64,0},{96,32},{128,64},{160,96},{192,128},{224,1... | collective-permute-start | bytes 6152 | tf_op jit(solution)/shard_map/ppermute | solution.py:467
  5.1 5.1 %collective-permute-start.9 = (f32[4,128]{1,0:T(4,128)S(1)}, f32[4,128]{1,0:T(4,128)S(1)}, u32[]{:S(2)}, u32[]{:S(2)}) collective-permute-start(f32[4,128]{1,0:T(4,128)S(1)} %add.6.refs_0_), channel_id=1, source_target_pairs={{0,128},{32,160},{64,192},{96,224},{128,0},{160,32},{192,64},{224,... | collective-permute-start | bytes 6152 | tf_op jit(solution)/shard_map/ppermute | solution.py:467
  5.8 4.8 %collective-permute-start.8 = (f32[4,128]{1,0:T(4,128)S(1)}, f32[4,128]{1,0:T(4,128)S(1)}, u32[]{:S(2)}, u32[]{:S(2)}) collective-permute-start(f32[4,128]{1,0:T(4,128)S(1)} %add.6.refs_0_), channel_id=1, source_target_pairs={{0,64},{32,96},{64,128},{96,160},{128,192},{160,224},{192,0},{224,... | collective-permute-start | bytes 6152 | tf_op jit(solution)/shard_map/ppermute | solution.py:467
  11.2 33.8 %all-to-all-start.1 = ((f32[32,13,4,128]{3,2,1,0:T(4,128)}), f32[32,13,4,128]{3,2,1,0:T(4,128)S(1)}, u32[]{:S(2)}, u32[]{:S(2)}) async-start(f32[32,13,4,128]{3,2,1,0:T(4,128)} %get-tuple-element.124), calls=%async_computation.1 | async-start | bytes 1703936 | tf_op jit(solution)/shard_map/all_to_all | solution.py:470
  24.7 5.9 %collective-permute-start.11 = (f32[12,16,128]{2,1,0:T(8,128)S(1)}, f32[12,16,128]{2,1,0:T(8,128)}, u32[]{:S(2)}, u32[]{:S(2)}) collective-permute-start(f32[12,16,128]{2,1,0:T(8,128)S(1)} %get-tuple-element.126), channel_id=1, source_target_pairs={{0,32},{32,64},{64,96},{96,128},{128,160},{160,192},{192,224},{224... | collective-permute-start | bytes 294920 | tf_op jit(solution)/shard_map/ppermute | solution.py:454
  24.7 7.3 %collective-permute-start.12 = (f32[12,16,128]{2,1,0:T(8,128)S(1)}, f32[12,16,128]{2,1,0:T(8,128)}, u32[]{:S(2)}, u32[]{:S(2)}) collective-permute-start(f32[12,16,128]{2,1,0:T(8,128)S(1)} %get-tuple-element.127), channel_id=1, source_target_pairs={{0,64},{32,96},{64,128},{96,160},{128,192},{160,224},{192,0},{224,... | collective-permute-start | bytes 294920 | tf_op jit(solution)/shard_map/ppermute | solution.py:454
  25.0 8.9 %collective-permute-start.13 = (f32[12,16,128]{2,1,0:T(8,128)S(1)}, f32[12,16,128]{2,1,0:T(8,128)}, u32[]{:S(2)}, u32[]{:S(2)}) collective-permute-start(f32[12,16,128]{2,1,0:T(8,128)S(1)} %get-tuple-element.128), channel_id=1, source_target_pairs={{0,96},{32,128},{64,160},{96,192},{128,224},{160,0},{192,32},{224,... | collective-permute-start | bytes 294920 | tf_op jit(solution)/shard_map/ppermute | solution.py:454
  26.2 8.8 %collective-permute-start.14 = (f32[12,16,128]{2,1,0:T(8,128)S(1)}, f32[12,16,128]{2,1,0:T(8,128)}, u32[]{:S(2)}, u32[]{:S(2)}) collective-permute-start(f32[12,16,128]{2,1,0:T(8,128)S(1)} %get-tuple-element.129), channel_id=1, source_target_pairs={{0,128},{32,160},{64,192},{96,224},{128,0},{160,32},{192,64},{224,... | collective-permute-start | bytes 294920 | tf_op jit(solution)/shard_map/ppermute | solution.py:454
  29.1 5.9 %collective-permute-start.15 = (f32[12,16,128]{2,1,0:T(8,128)S(1)}, f32[12,16,128]{2,1,0:T(8,128)}, u32[]{:S(2)}, u32[]{:S(2)}) collective-permute-start(f32[12,16,128]{2,1,0:T(8,128)S(1)} %get-tuple-element.130), channel_id=1, source_target_pairs={{0,160},{32,192},{64,224},{96,0},{128,32},{160,64},{192,96},{224,1... | collective-permute-start | bytes 294920 | tf_op jit(solution)/shard_map/ppermute | solution.py:454
  30.5 6.7 %collective-permute-start.16 = (f32[12,16,128]{2,1,0:T(8,128)S(1)}, f32[12,16,128]{2,1,0:T(8,128)}, u32[]{:S(2)}, u32[]{:S(2)}) collective-permute-start(f32[12,16,128]{2,1,0:T(8,128)S(1)} %get-tuple-element.131), channel_id=1, source_target_pairs={{0,192},{32,224},{64,0},{96,32},{128,64},{160,96},{192,128},{224,1... | collective-permute-start | bytes 294920 | tf_op jit(solution)/shard_map/ppermute | solution.py:454
  32.0 5.8 %collective-permute-start.17 = (f32[12,16,128]{2,1,0:T(8,128)S(1)}, f32[12,16,128]{2,1,0:T(8,128)}, u32[]{:S(2)}, u32[]{:S(2)}) collective-permute-start(f32[12,16,128]{2,1,0:T(8,128)S(1)} %get-tuple-element.132), channel_id=1, source_target_pairs={{0,224},{32,0},{64,32},{96,64},{128,96},{160,128},{192,160},{224,1... | collective-permute-start | bytes 294920 | tf_op jit(solution)/shard_map/ppermute | solution.py:454
  49.2 39.6 %all-to-all-start.2 = ((f32[32,20,4,128]{3,2,1,0:T(4,128)}), f32[32,20,4,128]{3,2,1,0:T(4,128)S(1)}, u32[]{:S(2)}, u32[]{:S(2)}) async-start(f32[32,20,4,128]{3,2,1,0:T(4,128)} %get-tuple-element.156), calls=%async_computation.2 | async-start | bytes 2621440 | tf_op jit(solution)/shard_map/all_to_all | solution.py:476
  58.5 7.3 %collective-permute-start.18 = (f32[21,16,128]{2,1,0:T(8,128)S(1)}, f32[21,16,128]{2,1,0:T(8,128)S(1)}, u32[]{:S(2)}, u32[]{:S(2)}) collective-permute-start(f32[21,16,128]{2,1,0:T(8,128)S(1)} %get-tuple-element.147), channel_id=1, source_target_pairs={{0,32},{32,64},{64,96},{96,128},{128,160},{160,192},{192,224},{224... | collective-permute-start | bytes 516104 | tf_op jit(solution)/shard_map/ppermute | solution.py:454
  58.5 8.5 %collective-permute-start.19 = (f32[21,16,128]{2,1,0:T(8,128)S(1)}, f32[21,16,128]{2,1,0:T(8,128)S(1)}, u32[]{:S(2)}, u32[]{:S(2)}) collective-permute-start(f32[21,16,128]{2,1,0:T(8,128)S(1)} %get-tuple-element.148), channel_id=1, source_target_pairs={{0,64},{32,96},{64,128},{96,160},{128,192},{160,224},{192,0},{224,... | collective-permute-start | bytes 516104 | tf_op jit(solution)/shard_map/ppermute | solution.py:454
  59.7 13.3 %collective-permute-start.20 = (f32[21,16,128]{2,1,0:T(8,128)}, f32[21,16,128]{2,1,0:T(8,128)S(1)}, u32[]{:S(2)}, u32[]{:S(2)}) collective-permute-start(f32[21,16,128]{2,1,0:T(8,128)} %get-tuple-element.149), channel_id=1, source_target_pairs={{0,96},{32,128},{64,160},{96,192},{128,224},{160,0},{192,32},{224,... | collective-permute-start | bytes 516104 | tf_op jit(solution)/shard_map/ppermute | solution.py:454
  60.8 13.3 %collective-permute-start.21 = (f32[21,16,128]{2,1,0:T(8,128)}, f32[21,16,128]{2,1,0:T(8,128)S(1)}, u32[]{:S(2)}, u32[]{:S(2)}) collective-permute-start(f32[21,16,128]{2,1,0:T(8,128)} %get-tuple-element.150), channel_id=1, source_target_pairs={{0,128},{32,160},{64,192},{96,224},{128,0},{160,32},{192,64},{224,... | collective-permute-start | bytes 516104 | tf_op jit(solution)/shard_map/ppermute | solution.py:454
  63.7 11.2 %collective-permute-start.22 = (f32[21,16,128]{2,1,0:T(8,128)}, f32[21,16,128]{2,1,0:T(8,128)S(1)}, u32[]{:S(2)}, u32[]{:S(2)}) collective-permute-start(f32[21,16,128]{2,1,0:T(8,128)} %get-tuple-element.151), channel_id=1, source_target_pairs={{0,160},{32,192},{64,224},{96,0},{128,32},{160,64},{192,96},{224,1... | collective-permute-start | bytes 516104 | tf_op jit(solution)/shard_map/ppermute | solution.py:454
  65.8 11.0 %collective-permute-start.23 = (f32[21,16,128]{2,1,0:T(8,128)}, f32[21,16,128]{2,1,0:T(8,128)S(1)}, u32[]{:S(2)}, u32[]{:S(2)}) collective-permute-start(f32[21,16,128]{2,1,0:T(8,128)} %get-tuple-element.152), channel_id=1, source_target_pairs={{0,192},{32,224},{64,0},{96,32},{128,64},{160,96},{192,128},{224,1... | collective-permute-start | bytes 516104 | tf_op jit(solution)/shard_map/ppermute | solution.py:454
  67.0 10.7 %collective-permute-start.24 = (f32[21,16,128]{2,1,0:T(8,128)}, f32[21,16,128]{2,1,0:T(8,128)}, u32[]{:S(2)}, u32[]{:S(2)}) collective-permute-start(f32[21,16,128]{2,1,0:T(8,128)} %get-tuple-element.153), channel_id=1, source_target_pairs={{0,224},{32,0},{64,32},{96,64},{128,96},{160,128},{192,160},{224,1... | collective-permute-start | bytes 516104 | tf_op jit(solution)/shard_map/ppermute | solution.py:454

commit v10 on v8

--- a/solution.py
+++ b/solution.py
@@ -380,8 +380,9 @@
 
 def product_body(first, rows, scalars, codes, counts, left_ref, *refs):
     right_refs, refs = refs[:rows], refs[rows:]
-    out_ref, right = refs[-2:]
+    out_hbm, right, out_ref, sems = refs[-4:]
     out_ref[...] = jnp.zeros_like(out_ref) if first else refs[0][...]
+    kept = out_ref.shape[0]
     row_index, own, base = lax.axis_index("row"), lax.axis_index(GROUP), scalars[0]
     peers, cap = left_ref.shape[:2]
     tall_strip = right_refs[0].shape[1]
@@ -407,8 +408,16 @@
     def target(at):
         return codes[line + (at >> 4), lane + (at & (SLOT_PITCH - 1))] >> 16
 
-    def several(step, carry):
+    def write(tile):
+        return pltpu.make_async_copy(out_ref.at[tile], out_hbm.at[tile], sems.at[tile])
+
+    def start(tile, carry):
+        write(tile).start()
+        return carry
+
+    def several(step, finished):
         at = TOGETHER * step
+        lax.fori_loop(finished, target(at), start, 0)
         sums = [product(at + n, n) for n in range(TOGETHER)]
         out_ref[target(at)] += sums[0]
         for n in range(1, TOGETHER):
@@ -416,9 +425,12 @@
             def _():
                 out_ref[target(at + n)] += sums[n]
 
-        return carry
-
-    lax.fori_loop(0, (todo + TOGETHER - 1) // TOGETHER, several, 0)
+        return target(at)
+
+    finished = lax.fori_loop(0, (todo + TOGETHER - 1) // TOGETHER, several, jnp.int32(0))
+    lax.fori_loop(finished, kept, start, 0)
+    for tile in range(kept):
+        write(tile).wait()
 
 
 def multiply_round(left, right, codes, counts, base, running, kept):
@@ -435,10 +447,14 @@
             num_scalar_prefetch=3,
             grid=(1,),
             in_specs=[whole(operand.shape) for operand in operands],
-            out_specs=whole(tiles),
-            scratch_shapes=[pltpu.VMEM((TOGETHER, order, order), jnp.float32)],
+            out_specs=HBM,
+            scratch_shapes=[
+                pltpu.VMEM((TOGETHER, order, order), jnp.float32),
+                pltpu.VMEM(tiles, jnp.float32),
+                pltpu.SemaphoreType.DMA((kept,)),
+            ],
         ),
-        out_shape=jax.ShapeDtypeStruct(tiles, jnp.float32),
+        out_shape=pltpu.HBM(tiles, jnp.float32),
         compiler_params=LIMIT,
     )(jnp.stack([base, most]), codes, counts, *operands)
     return summed, most

time: 92.7 us -> 93 us (level)
  no operation moved by 1% of the time
where the time goes in v10:
time: 93 us; the launch traced here: 92.6 us
  starting transfers between devices  41.7 us (45%)
  waiting for transfers between devices  30 us (32%)
  Pallas kernels  18.7 us (20%)
    ppermute x14, starting transfers between devices, shift_all(): lax.ppermute(pieces[by], 'row', [(i, (i + by) % rows) for i in range(rows)])  19.9 us
    ppermute x14, waiting for transfers between devices, shift_all(): lax.ppermute(pieces[by], 'row', [(i, (i + by) % rows) for i in range(rows)])  12.1 us
    all_to_all x1, starting transfers between devices, local(): strips = lax.all_to_all(strips, GROUP, 0, 0, tiled=True)  11.6 us
    all_to_all x1, waiting for transfers between devices, local(): strips = lax.all_to_all(strips, GROUP, 0, 0, tiled=True)  7.83 us
    all_to_all x1, waiting for transfers between devices, one_round(): left = lax.all_to_all(send, GROUP, 0, 0, tiled=True)  6.88 us
    all_to_all x1, starting transfers between devices, one_round(): left = lax.all_to_all(send, GROUP, 0, 0, tiled=True)  5.71 us
    pallas_call x1, Pallas kernels, multiply_round(): pl.pallas_call(functools.partial(product_body, first, len(right)), grid_s...  4.51 us
    ppermute x3, starting transfers between devices, swap_rows(): return lax.ppermute(array, 'row', [(i, i ^ by) for i in range(rows)])  4.49 us
  transfers between devices with their start and end apart: 19, of which 14 were waited for; matrix products, arithmetic and copies ran while one was open for 1% of the time, Pallas kernels for 9%

profile of v10, /device:TPU:4, one launch (start us, length us, event | category | flops | bytes accessed | tf_op | source)
XLA Modules:
  0.0 92.6 jit_solution(6704164306708217985)
XLA Ops:
  1.0 1.1 %collective-permute-done.7 = f32[4,128]{1,0:T(4,128)S(1)} collective-permute-done((f32[4,128]{1,0:T(4,128)S(1)}, f32[4,128]{1,0:T(4,128)S(1)}, u32[]{:S(2)}, u32[]{:S(2)}) %collective-permute-start.7) | collective-permute-done | bytes 2080 | tf_op jit(solution)/shard_map/ppermute | solution.py:471
  2.1 1.6 %collective-permute-start.8 = (f32[4,128]{1,0:T(4,128)S(1)}, f32[4,128]{1,0:T(4,128)S(1)}, u32[]{:S(2)}, u32[]{:S(2)}) collective-permute-start(f32[4,128]{1,0:T(4,128)S(1)} %add.9), channel_id=1, source_target_pairs={{0,64},{32,96},{64,0},{96,32},{128,192},{160,224},{192,128},{224,1... | collective-permute-start | bytes 6152 | tf_op jit(solution)/shard_map/ppermute | solution.py:471
  3.7 2.2 %shard_map.65.strips_in = f32[32,13,4,128]{3,2,1,0:T(4,128)} custom-call(f32[12,128,128]{2,1,0:T(8,128)} %bitcast.13), custom_call_target="tpu_custom_call" | custom-call | tf_op jit(solution)/shard_map/pallas_call | solution.py:89
  5.9 2.8 %collective-permute-start.9 = (f32[4,128]{1,0:T(4,128)S(1)}, f32[4,128]{1,0:T(4,128)S(1)}, u32[]{:S(2)}, u32[]{:S(2)}) collective-permute-start(f32[4,128]{1,0:T(4,128)S(1)} %add.10.one_ref), channel_id=1, source_target_pairs={{0,192},{32,224},{64,128},{96,160},{128,64},{160,96},{192,0},{224,... | collective-permute-start | bytes 6152 | tf_op jit(solution)/shard_map/ppermute | solution.py:471
  8.7 2.1 %collective-permute-done.9.other_ref = f32[4,128]{1,0:T(4,128)S(1)} collective-permute-done((f32[4,128]{1,0:T(4,128)S(1)}, f32[4,128]{1,0:T(4,128)S(1)}, u32[]{:S(2)}, u32[]{:S(2)}) %collective-permute-start.9) | collective-permute-done | bytes 2080 | tf_op jit(solution)/shard_map/ppermute | solution.py:471
  11.4 11.6 %all-to-all-start.1 = ((f32[32,13,4,128]{3,2,1,0:T(4,128)}), f32[32,13,4,128]{3,2,1,0:T(4,128)S(1)}, u32[]{:S(2)}, u32[]{:S(2)}) async-start(f32[32,13,4,128]{3,2,1,0:T(4,128)} %get-tuple-element.128), calls=%async_computation.1 | async-start | bytes 1703936 | tf_op jit(solution)/shard_map/all_to_all | solution.py:487
  23.0 1.8 %shard_map.67 = (f32[12,16,128]{2,1,0:T(8,128)}, f32[12,16,128]{2,1,0:T(8,128)S(1)}, f32[12,16,128]{2,1,0:T(8,128)S(1)}, f32[12,16,128]{2,1,0:T(8,128)S(1)}, f32...) custom-call(f32[12,128,128]{2,1,0:T(8,128)} %bitcast.14), custom_call_target="tpu_custom_call" | custom-call | tf_op jit(solution)/shard_map/pallas_call | solution.py:136
  25.0 3.5 %collective-permute-start.12 = (f32[12,16,128]{2,1,0:T(8,128)S(1)}, f32[12,16,128]{2,1,0:T(8,128)}, u32[]{:S(2)}, u32[]{:S(2)}) collective-permute-start(f32[12,16,128]{2,1,0:T(8,128)S(1)} %get-tuple-element.132), channel_id=1, source_target_pairs={{0,96},{32,128},{64,160},{96,192},{128,224},{160,0},{192,32},{224,... | collective-permute-start | bytes 294920 | tf_op jit(solution)/shard_map/ppermute | solution.py:466
  29.3 2.7 %collective-permute-start.14 = (f32[12,16,128]{2,1,0:T(8,128)S(1)}, f32[12,16,128]{2,1,0:T(8,128)}, u32[]{:S(2)}, u32[]{:S(2)}) collective-permute-start(f32[12,16,128]{2,1,0:T(8,128)S(1)} %get-tuple-element.134), channel_id=1, source_target_pairs={{0,160},{32,192},{64,224},{96,0},{128,32},{160,64},{192,96},{224,1... | collective-permute-start | bytes 294920 | tf_op jit(solution)/shard_map/ppermute | solution.py:466
  32.2 1.7 %collective-permute-start.16 = (f32[12,16,128]{2,1,0:T(8,128)S(1)}, f32[12,16,128]{2,1,0:T(8,128)}, u32[]{:S(2)}, u32[]{:S(2)}) collective-permute-start(f32[12,16,128]{2,1,0:T(8,128)S(1)} %get-tuple-element.136), channel_id=1, source_target_pairs={{0,224},{32,0},{64,32},{96,64},{128,96},{160,128},{192,160},{224,1... | collective-permute-start | bytes 294920 | tf_op jit(solution)/shard_map/ppermute | solution.py:466
  34.0 1.9 %collective-permute-done.12.refs_3_ = f32[12,16,128]{2,1,0:T(8,128)} collective-permute-done((f32[12,16,128]{2,1,0:T(8,128)S(1)}, f32[12,16,128]{2,1,0:T(8,128)}, u32[]{:S(2)}, u32[]{:S(2)}) %collective-permute-start.12) | collective-permute-done | bytes 98336 | tf_op jit(solution)/shard_map/ppermute | solution.py:466
  37.7 7.8 %all-to-all-done.1 = f32[32,13,4,128]{3,2,1,0:T(4,128)S(1)} async-done(((f32[32,13,4,128]{3,2,1,0:T(4,128)}), f32[32,13,4,128]{3,2,1,0:T(4,128)S(1)}, u32[]{:S(2)}, u32[]{:S(2)}) %all-to-all-start.1) | async-done | bytes 852000 | tf_op jit(solution)/shard_map/all_to_all | solution.py:487
  45.5 4.1 %shard_map.68 = (f32[32,20,4,128]{3,2,1,0:T(4,128)}, s32[8,128]{1,0:T(8,128)S(1)}, s32[8,128]{1,0:T(8,128)S(1)}, f32[8,128]{1,0:T(8,128)S(1)}, bf16[256,256]{1,0...) custom-call(s32[1]{0:T(128)} %constant.2.clone.1.base_ref, f32[416,4,128]{2,1,0:T(4,128)S(1)} %bitcast.11), custom_call_target="tpu_custom_call" | custom-call | tf_op jit(solution)/shard_map/pallas_call | solution.py:293
  49.7 5.7 %all-to-all-start.2 = ((f32[32,20,4,128]{3,2,1,0:T(4,128)}), f32[32,20,4,128]{3,2,1,0:T(4,128)S(1)}, u32[]{:S(2)}, u32[]{:S(2)}) async-start(f32[32,20,4,128]{3,2,1,0:T(4,128)} %get-tuple-element.160), calls=%async_computation.2 | async-start | bytes 2621440 | tf_op jit(solution)/shard_map/all_to_all | solution.py:493
  55.4 3.7 %shard_map.69 = (f32[21,16,128]{2,1,0:T(8,128)S(1)}, f32[21,16,128]{2,1,0:T(8,128)S(1)}, f32[21,16,128]{2,1,0:T(8,128)S(1)}, f32[21,16,128]{2,1,0:T(8,128)}, f32...) custom-call(s32[1]{0:T(128)} %constant.2.clone.1.base_ref, ...), custom_call_target="tpu_custom_call" | custom-call | tf_op jit(solution)/shard_map/pallas_call | solution.py:352
  59.2 2.9 %collective-permute-start.19 = (f32[21,16,128]{2,1,0:T(8,128)}, f32[21,16,128]{2,1,0:T(8,128)S(1)}, u32[]{:S(2)}, u32[]{:S(2)}) collective-permute-start(f32[21,16,128]{2,1,0:T(8,128)} %get-tuple-element.153), channel_id=1, source_target_pairs={{0,96},{32,128},{64,160},{96,192},{128,224},{160,0},{192,32},{224,... | collective-permute-start | bytes 516104 | tf_op jit(solution)/shard_map/ppermute | solution.py:466
  62.1 1.4 %collective-permute-start.20 = (f32[21,16,128]{2,1,0:T(8,128)}, f32[21,16,128]{2,1,0:T(8,128)S(1)}, u32[]{:S(2)}, u32[]{:S(2)}) collective-permute-start(f32[21,16,128]{2,1,0:T(8,128)} %get-tuple-element.154), channel_id=1, source_target_pairs={{0,128},{32,160},{64,192},{96,224},{128,0},{160,32},{192,64},{224,... | collective-permute-start | bytes 516104 | tf_op jit(solution)/shard_map/ppermute | solution.py:466
  63.5 2.3 %collective-permute-start.21 = (f32[21,16,128]{2,1,0:T(8,128)}, f32[21,16,128]{2,1,0:T(8,128)S(1)}, u32[]{:S(2)}, u32[]{:S(2)}) collective-permute-start(f32[21,16,128]{2,1,0:T(8,128)} %get-tuple-element.155), channel_id=1, source_target_pairs={{0,160},{32,192},{64,224},{96,0},{128,32},{160,64},{192,96},{224,1... | collective-permute-start | bytes 516104 | tf_op jit(solution)/shard_map/ppermute | solution.py:466
  67.6 3.1 %collective-permute-start.23 = (f32[21,16,128]{2,1,0:T(8,128)}, f32[21,16,128]{2,1,0:T(8,128)}, u32[]{:S(2)}, u32[]{:S(2)}) collective-permute-start(f32[21,16,128]{2,1,0:T(8,128)} %get-tuple-element.157), channel_id=1, source_target_pairs={{0,224},{32,0},{64,32},{96,64},{128,96},{160,128},{192,160},{224,1... | collective-permute-start | bytes 516104 | tf_op jit(solution)/shard_map/ppermute | solution.py:466
  70.7 3.4 %collective-permute-done.19.refs_3_ = f32[21,16,128]{2,1,0:T(8,128)S(1)} collective-permute-done((f32[21,16,128]{2,1,0:T(8,128)}, f32[21,16,128]{2,1,0:T(8,128)S(1)}, u32[]{:S(2)}, u32[]{:S(2)}) %collective-permute-start.19) | collective-permute-done | bytes 172064 | tf_op jit(solution)/shard_map/ppermute | solution.py:466
  74.1 1.2 %collective-permute-done.20.refs_4_ = f32[21,16,128]{2,1,0:T(8,128)S(1)} collective-permute-done((f32[21,16,128]{2,1,0:T(8,128)}, f32[21,16,128]{2,1,0:T(8,128)S(1)}, u32[]{:S(2)}, u32[]{:S(2)}) %collective-permute-start.20) | collective-permute-done | bytes 172064 | tf_op jit(solution)/shard_map/ppermute | solution.py:466
  75.3 1.8 %collective-permute-done.22.refs_6_ = f32[21,16,128]{2,1,0:T(8,128)S(1)} collective-permute-done((f32[21,16,128]{2,1,0:T(8,128)}, f32[21,16,128]{2,1,0:T(8,128)S(1)}, u32[]{:S(2)}, u32[]{:S(2)}) %collective-permute-start.22) | collective-permute-done | bytes 172064 | tf_op jit(solution)/shard_map/ppermute | solution.py:466
  80.4 6.9 %all-to-all-done.2.left_ref = f32[32,20,4,128]{3,2,1,0:T(4,128)S(1)} async-done(((f32[32,20,4,128]{3,2,1,0:T(4,128)}), f32[32,20,4,128]{3,2,1,0:T(4,128)S(1)}, u32[]{:S(2)}, u32[]{:S(2)}) %all-to-all-start.2) | async-done | bytes 1310752 | tf_op jit(solution)/shard_map/all_to_all | solution.py:493
  87.3 4.5 %shard_map.71 = f32[12,128,128]{2,1,0:T(8,128)} custom-call(s32[2]{0:T(128)S(1)} %pad_add_fusion.1.scalars, s32[8,128]{1,0:T(8,128)S(1)} %get-tuple-element.158.codes, s32[8,128]{1,0:T(8,128)S(1)} %get-tuple-element.159.counts, f32[32,20,4,128]{3,2,1,0:T(4,128)S(1)} %all-to-all-done.2.left_ref, f32[21,16,128]{2,1,0:T(8,128)S(1)} %get-tuple-element.150.refs_0_, ...), custom_call_target="tpu_custom_call" | custom-call | tf_op jit(solution)/shard_map/pallas_call | solution.py:444
  (27 shorter events, 10.4 us)
Async XLA Ops:
  0.9 1.2 %collective-permute-start.7 = (f32[4,128]{1,0:T(4,128)S(1)}, f32[4,128]{1,0:T(4,128)S(1)}, u32[]{:S(2)}, u32[]{:S(2)}) collective-permute-start(f32[4,128]{1,0:T(4,128)S(1)} %get-tuple-element.124), channel_id=1, source_target_pairs={{0,32},{32,0},{64,96},{96,64},{128,160},{160,128},{192,224},{224,1... | collective-permute-start | bytes 6152 | tf_op jit(solution)/shard_map/ppermute | solution.py:471
  2.1 3.8 %collective-permute-start.8 = (f32[4,128]{1,0:T(4,128)S(1)}, f32[4,128]{1,0:T(4,128)S(1)}, u32[]{:S(2)}, u32[]{:S(2)}) collective-permute-start(f32[4,128]{1,0:T(4,128)S(1)} %add.9), channel_id=1, source_target_pairs={{0,64},{32,96},{64,0},{96,32},{128,192},{160,224},{192,128},{224,1... | collective-permute-start | bytes 6152 | tf_op jit(solution)/shard_map/ppermute | solution.py:471
  5.9 4.9 %collective-permute-start.9 = (f32[4,128]{1,0:T(4,128)S(1)}, f32[4,128]{1,0:T(4,128)S(1)}, u32[]{:S(2)}, u32[]{:S(2)}) collective-permute-start(f32[4,128]{1,0:T(4,128)S(1)} %add.10.one_ref), channel_id=1, source_target_pairs={{0,192},{32,224},{64,128},{96,160},{128,64},{160,96},{192,0},{224,... | collective-permute-start | bytes 6152 | tf_op jit(solution)/shard_map/ppermute | solution.py:471
  11.4 34.1 %all-to-all-start.1 = ((f32[32,13,4,128]{3,2,1,0:T(4,128)}), f32[32,13,4,128]{3,2,1,0:T(4,128)S(1)}, u32[]{:S(2)}, u32[]{:S(2)}) async-start(f32[32,13,4,128]{3,2,1,0:T(4,128)} %get-tuple-element.128), calls=%async_computation.1 | async-start | bytes 1703936 | tf_op jit(solution)/shard_map/all_to_all | solution.py:487
  24.9 7.2 %collective-permute-start.10 = (f32[12,16,128]{2,1,0:T(8,128)S(1)}, f32[12,16,128]{2,1,0:T(8,128)}, u32[]{:S(2)}, u32[]{:S(2)}) collective-permute-start(f32[12,16,128]{2,1,0:T(8,128)S(1)} %get-tuple-element.130), channel_id=1, source_target_pairs={{0,32},{32,64},{64,96},{96,128},{128,160},{160,192},{192,224},{224... | collective-permute-start | bytes 294920 | tf_op jit(solution)/shard_map/ppermute | solution.py:466
  24.9 7.4 %collective-permute-start.11 = (f32[12,16,128]{2,1,0:T(8,128)S(1)}, f32[12,16,128]{2,1,0:T(8,128)}, u32[]{:S(2)}, u32[]{:S(2)}) collective-permute-start(f32[12,16,128]{2,1,0:T(8,128)S(1)} %get-tuple-element.131), channel_id=1, source_target_pairs={{0,64},{32,96},{64,128},{96,160},{128,192},{160,224},{192,0},{224,... | collective-permute-start | bytes 294920 | tf_op jit(solution)/shard_map/ppermute | solution.py:466
  25.0 10.9 %collective-permute-start.12 = (f32[12,16,128]{2,1,0:T(8,128)S(1)}, f32[12,16,128]{2,1,0:T(8,128)}, u32[]{:S(2)}, u32[]{:S(2)}) collective-permute-start(f32[12,16,128]{2,1,0:T(8,128)S(1)} %get-tuple-element.132), channel_id=1, source_target_pairs={{0,96},{32,128},{64,160},{96,192},{128,224},{160,0},{192,32},{224,... | collective-permute-start | bytes 294920 | tf_op jit(solution)/shard_map/ppermute | solution.py:466
  28.5 8.5 %collective-permute-start.13 = (f32[12,16,128]{2,1,0:T(8,128)S(1)}, f32[12,16,128]{2,1,0:T(8,128)}, u32[]{:S(2)}, u32[]{:S(2)}) collective-permute-start(f32[12,16,128]{2,1,0:T(8,128)S(1)} %get-tuple-element.133), channel_id=1, source_target_pairs={{0,128},{32,160},{64,192},{96,224},{128,0},{160,32},{192,64},{224,... | collective-permute-start | bytes 294920 | tf_op jit(solution)/shard_map/ppermute | solution.py:466
  29.3 7.7 %collective-permute-start.14 = (f32[12,16,128]{2,1,0:T(8,128)S(1)}, f32[12,16,128]{2,1,0:T(8,128)}, u32[]{:S(2)}, u32[]{:S(2)}) collective-permute-start(f32[12,16,128]{2,1,0:T(8,128)S(1)} %get-tuple-element.134), channel_id=1, source_target_pairs={{0,160},{32,192},{64,224},{96,0},{128,32},{160,64},{192,96},{224,1... | collective-permute-start | bytes 294920 | tf_op jit(solution)/shard_map/ppermute | solution.py:466
  32.1 5.4 %collective-permute-start.15 = (f32[12,16,128]{2,1,0:T(8,128)S(1)}, f32[12,16,128]{2,1,0:T(8,128)}, u32[]{:S(2)}, u32[]{:S(2)}) collective-permute-start(f32[12,16,128]{2,1,0:T(8,128)S(1)} %get-tuple-element.135), channel_id=1, source_target_pairs={{0,192},{32,224},{64,0},{96,32},{128,64},{160,96},{192,128},{224,1... | collective-permute-start | bytes 294920 | tf_op jit(solution)/shard_map/ppermute | solution.py:466
  32.2 5.5 %collective-permute-start.16 = (f32[12,16,128]{2,1,0:T(8,128)S(1)}, f32[12,16,128]{2,1,0:T(8,128)}, u32[]{:S(2)}, u32[]{:S(2)}) collective-permute-start(f32[12,16,128]{2,1,0:T(8,128)S(1)} %get-tuple-element.136), channel_id=1, source_target_pairs={{0,224},{32,0},{64,32},{96,64},{128,96},{160,128},{192,160},{224,1... | collective-permute-start | bytes 294920 | tf_op jit(solution)/shard_map/ppermute | solution.py:466
  49.7 37.6 %all-to-all-start.2 = ((f32[32,20,4,128]{3,2,1,0:T(4,128)}), f32[32,20,4,128]{3,2,1,0:T(4,128)S(1)}, u32[]{:S(2)}, u32[]{:S(2)}) async-start(f32[32,20,4,128]{3,2,1,0:T(4,128)} %get-tuple-element.160), calls=%async_computation.2 | async-start | bytes 2621440 | tf_op jit(solution)/shard_map/all_to_all | solution.py:493
  59.0 7.3 %collective-permute-start.17 = (f32[21,16,128]{2,1,0:T(8,128)S(1)}, f32[21,16,128]{2,1,0:T(8,128)S(1)}, u32[]{:S(2)}, u32[]{:S(2)}) collective-permute-start(f32[21,16,128]{2,1,0:T(8,128)S(1)} %get-tuple-element.151), channel_id=1, source_target_pairs={{0,32},{32,64},{64,96},{96,128},{128,160},{160,192},{192,224},{224... | collective-permute-start | bytes 516104 | tf_op jit(solution)/shard_map/ppermute | solution.py:466
  59.1 8.5 %collective-permute-start.18 = (f32[21,16,128]{2,1,0:T(8,128)S(1)}, f32[21,16,128]{2,1,0:T(8,128)S(1)}, u32[]{:S(2)}, u32[]{:S(2)}) collective-permute-start(f32[21,16,128]{2,1,0:T(8,128)S(1)} %get-tuple-element.152), channel_id=1, source_target_pairs={{0,64},{32,96},{64,128},{96,160},{128,192},{160,224},{192,0},{224,... | collective-permute-start | bytes 516104 | tf_op jit(solution)/shard_map/ppermute | solution.py:466
  59.2 14.9 %collective-permute-start.19 = (f32[21,16,128]{2,1,0:T(8,128)}, f32[21,16,128]{2,1,0:T(8,128)S(1)}, u32[]{:S(2)}, u32[]{:S(2)}) collective-permute-start(f32[21,16,128]{2,1,0:T(8,128)} %get-tuple-element.153), channel_id=1, source_target_pairs={{0,96},{32,128},{64,160},{96,192},{128,224},{160,0},{192,32},{224,... | collective-permute-start | bytes 516104 | tf_op jit(solution)/shard_map/ppermute | solution.py:466
  62.1 13.2 %collective-permute-start.20 = (f32[21,16,128]{2,1,0:T(8,128)}, f32[21,16,128]{2,1,0:T(8,128)S(1)}, u32[]{:S(2)}, u32[]{:S(2)}) collective-permute-start(f32[21,16,128]{2,1,0:T(8,128)} %get-tuple-element.154), channel_id=1, source_target_pairs={{0,128},{32,160},{64,192},{96,224},{128,0},{160,32},{192,64},{224,... | collective-permute-start | bytes 516104 | tf_op jit(solution)/shard_map/ppermute | solution.py:466
  63.5 11.8 %collective-permute-start.21 = (f32[21,16,128]{2,1,0:T(8,128)}, f32[21,16,128]{2,1,0:T(8,128)S(1)}, u32[]{:S(2)}, u32[]{:S(2)}) collective-permute-start(f32[21,16,128]{2,1,0:T(8,128)} %get-tuple-element.155), channel_id=1, source_target_pairs={{0,160},{32,192},{64,224},{96,0},{128,32},{160,64},{192,96},{224,1... | collective-permute-start | bytes 516104 | tf_op jit(solution)/shard_map/ppermute | solution.py:466
  66.3 10.8 %collective-permute-start.22 = (f32[21,16,128]{2,1,0:T(8,128)}, f32[21,16,128]{2,1,0:T(8,128)S(1)}, u32[]{:S(2)}, u32[]{:S(2)}) collective-permute-start(f32[21,16,128]{2,1,0:T(8,128)} %get-tuple-element.156), channel_id=1, source_target_pairs={{0,192},{32,224},{64,0},{96,32},{128,64},{160,96},{192,128},{224,1... | collective-permute-start | bytes 516104 | tf_op jit(solution)/shard_map/ppermute | solution.py:466
  67.6 10.7 %collective-permute-start.23 = (f32[21,16,128]{2,1,0:T(8,128)}, f32[21,16,128]{2,1,0:T(8,128)}, u32[]{:S(2)}, u32[]{:S(2)}) collective-permute-start(f32[21,16,128]{2,1,0:T(8,128)} %get-tuple-element.157), channel_id=1, source_target_pairs={{0,224},{32,0},{64,32},{96,64},{128,96},{160,128},{192,160},{224,1... | collective-permute-start | bytes 516104 | tf_op jit(solution)/shard_map/ppermute | solution.py:466

commit v11 on v8

--- a/solution.py
+++ b/solution.py
@@ -466,8 +466,9 @@
     for by in (1, 2):
         listed = listed + swap_rows(listed, rows, by)
     listed, strips = lax.optimization_barrier((listed, pack(tiles, peers)))
+    strips, right_strips = lax.optimization_barrier((strips, pack_right(tiles, rows)))
     strips, mates = stamp(listed, swap_rows(listed, rows, rows - 2), wanted, strips)
-    pieces = shift_all(pack_right(tiles, rows))
+    pieces = shift_all(right_strips)
     strips = lax.all_to_all(strips, GROUP, 0, 0, tiled=True)
     strips, pieces = lax.optimization_barrier((strips, pieces))
     strips = strips.reshape(-1, order // peers, order)

time: 92.7 us -> 93.4 us (level)
  waiting for transfers between devices: 30 us -> 31.2 us
    all_to_all x1, waiting for transfers between devices: 7.83 us -> 9.71 us  [local(): strips = lax.all_to_all(strips, GROUP, 0, 0, tiled=True)]
    ppermute x3, waiting for transfers between devices: 3.21 us -> 1.4 us  [swap_rows(): return lax.ppermute(array, 'row', [(i, i ^ by) for i in range(rows)])]
where the time goes in v11:
time: 93.4 us; the launch traced here: 93 us
  starting transfers between devices  41.4 us (44%)
  waiting for transfers between devices  31.2 us (33%)
  Pallas kernels  18.2 us (19%)
    ppermute x14, starting transfers between devices, shift_all(): lax.ppermute(pieces[by], 'row', [(i, (i + by) % rows) for i in range(rows)])  19.6 us
    ppermute x14, waiting for transfers between devices, shift_all(): lax.ppermute(pieces[by], 'row', [(i, (i + by) % rows) for i in range(rows)])  12.5 us
    all_to_all x1, starting transfers between devices, local(): strips = lax.all_to_all(strips, GROUP, 0, 0, tiled=True)  11.6 us
    all_to_all x1, waiting for transfers between devices, local(): strips = lax.all_to_all(strips, GROUP, 0, 0, tiled=True)  9.71 us
    all_to_all x1, waiting for transfers between devices, one_round(): left = lax.all_to_all(send, GROUP, 0, 0, tiled=True)  7.64 us
    all_to_all x1, starting transfers between devices, one_round(): left = lax.all_to_all(send, GROUP, 0, 0, tiled=True)  5.71 us
    ppermute x3, starting transfers between devices, swap_rows(): return lax.ppermute(array, 'row', [(i, i ^ by) for i in range(rows)])  4.49 us
    pallas_call x1, Pallas kernels, plan(): pl.pallas_call(functools.partial(plan_body, rows), grid_spec=pltpu.Prefet...  4.13 us
  transfers between devices with their start and end apart: 19, of which 14 were waited for; matrix products, arithmetic and copies ran while one was open for 1% of the time, Pallas kernels for 9%

profile of v11, /device:TPU:4, one launch (start us, length us, event | category | flops | bytes accessed | tf_op | source)
XLA Modules:
  0.0 93.0 jit_solution(7133058349831690671)
XLA Ops:
  2.1 1.6 %collective-permute-start.8 = (f32[4,128]{1,0:T(4,128)S(1)}, f32[4,128]{1,0:T(4,128)S(1)}, u32[]{:S(2)}, u32[]{:S(2)}) collective-permute-start(f32[4,128]{1,0:T(4,128)S(1)} %add.9), channel_id=1, source_target_pairs={{0,64},{32,96},{64,0},{96,32},{128,192},{160,224},{192,128},{224,1... | collective-permute-start | bytes 6152 | tf_op jit(solution)/shard_map/ppermute | solution.py:455
  3.7 2.2 %shard_map.65.strips_in = f32[32,13,4,128]{3,2,1,0:T(4,128)} custom-call(f32[12,128,128]{2,1,0:T(8,128)} %bitcast.13), custom_call_target="tpu_custom_call" | custom-call | tf_op jit(solution)/shard_map/pallas_call | solution.py:89
  5.9 2.8 %collective-permute-start.9 = (f32[4,128]{1,0:T(4,128)S(1)}, f32[4,128]{1,0:T(4,128)S(1)}, u32[]{:S(2)}, u32[]{:S(2)}) collective-permute-start(f32[4,128]{1,0:T(4,128)S(1)} %add.10.one_ref), channel_id=1, source_target_pairs={{0,192},{32,224},{64,128},{96,160},{128,64},{160,96},{192,0},{224,... | collective-permute-start | bytes 6152 | tf_op jit(solution)/shard_map/ppermute | solution.py:455
  8.7 1.8 %shard_map.66 = (f32[12,16,128]{2,1,0:T(8,128)}, f32[12,16,128]{2,1,0:T(8,128)S(1)}, f32[12,16,128]{2,1,0:T(8,128)S(1)}, f32[12,16,128]{2,1,0:T(8,128)S(1)}, f32...) custom-call(f32[12,128,128]{2,1,0:T(8,128)} %bitcast.14), custom_call_target="tpu_custom_call" | custom-call | tf_op jit(solution)/shard_map/pallas_call | solution.py:136
  11.4 11.6 %all-to-all-start.1 = ((f32[32,13,4,128]{3,2,1,0:T(4,128)}), f32[32,13,4,128]{3,2,1,0:T(4,128)S(1)}, u32[]{:S(2)}, u32[]{:S(2)}) async-start(f32[32,13,4,128]{3,2,1,0:T(4,128)} %get-tuple-element.146), calls=%async_computation.1 | async-start | bytes 1703936 | tf_op jit(solution)/shard_map/all_to_all | solution.py:472
  23.2 3.4 %collective-permute-start.12 = (f32[12,16,128]{2,1,0:T(8,128)S(1)}, f32[12,16,128]{2,1,0:T(8,128)}, u32[]{:S(2)}, u32[]{:S(2)}) collective-permute-start(f32[12,16,128]{2,1,0:T(8,128)S(1)} %get-tuple-element.150), channel_id=1, source_target_pairs={{0,96},{32,128},{64,160},{96,192},{128,224},{160,0},{192,32},{224,... | collective-permute-start | bytes 294920 | tf_op jit(solution)/shard_map/ppermute | solution.py:450
  27.5 2.8 %collective-permute-start.14 = (f32[12,16,128]{2,1,0:T(8,128)S(1)}, f32[12,16,128]{2,1,0:T(8,128)}, u32[]{:S(2)}, u32[]{:S(2)}) collective-permute-start(f32[12,16,128]{2,1,0:T(8,128)S(1)} %get-tuple-element.152), channel_id=1, source_target_pairs={{0,160},{32,192},{64,224},{96,0},{128,32},{160,64},{192,96},{224,1... | collective-permute-start | bytes 294920 | tf_op jit(solution)/shard_map/ppermute | solution.py:450
  30.5 1.6 %collective-permute-start.16 = (f32[12,16,128]{2,1,0:T(8,128)S(1)}, f32[12,16,128]{2,1,0:T(8,128)}, u32[]{:S(2)}, u32[]{:S(2)}) collective-permute-start(f32[12,16,128]{2,1,0:T(8,128)S(1)} %get-tuple-element.154), channel_id=1, source_target_pairs={{0,224},{32,0},{64,32},{96,64},{128,96},{160,128},{192,160},{224,1... | collective-permute-start | bytes 294920 | tf_op jit(solution)/shard_map/ppermute | solution.py:450
  32.1 1.9 %collective-permute-done.12.refs_3_ = f32[12,16,128]{2,1,0:T(8,128)} collective-permute-done((f32[12,16,128]{2,1,0:T(8,128)S(1)}, f32[12,16,128]{2,1,0:T(8,128)}, u32[]{:S(2)}, u32[]{:S(2)}) %collective-permute-start.12) | collective-permute-done | bytes 98336 | tf_op jit(solution)/shard_map/ppermute | solution.py:450
  34.0 1.2 %collective-permute-done.13.refs_4_ = f32[12,16,128]{2,1,0:T(8,128)} collective-permute-done((f32[12,16,128]{2,1,0:T(8,128)S(1)}, f32[12,16,128]{2,1,0:T(8,128)}, u32[]{:S(2)}, u32[]{:S(2)}) %collective-permute-start.13) | collective-permute-done | bytes 98336 | tf_op jit(solution)/shard_map/ppermute | solution.py:450
  35.9 9.7 %all-to-all-done.1 = f32[32,13,4,128]{3,2,1,0:T(4,128)S(1)} async-done(((f32[32,13,4,128]{3,2,1,0:T(4,128)}), f32[32,13,4,128]{3,2,1,0:T(4,128)S(1)}, u32[]{:S(2)}, u32[]{:S(2)}) %all-to-all-start.1) | async-done | bytes 852000 | tf_op jit(solution)/shard_map/all_to_all | solution.py:472
  45.6 4.1 %shard_map.68 = (f32[32,20,4,128]{3,2,1,0:T(4,128)}, s32[8,128]{1,0:T(8,128)S(1)}, s32[8,128]{1,0:T(8,128)S(1)}, f32[8,128]{1,0:T(8,128)S(1)}, bf16[256,256]{1,0...) custom-call(s32[1]{0:T(128)} %constant.2.clone.1.base_ref, f32[416,4,128]{2,1,0:T(4,128)S(1)} %bitcast.11), custom_call_target="tpu_custom_call" | custom-call | tf_op jit(solution)/shard_map/pallas_call | solution.py:293
  49.7 5.7 %all-to-all-start.2 = ((f32[32,20,4,128]{3,2,1,0:T(4,128)}), f32[32,20,4,128]{3,2,1,0:T(4,128)S(1)}, u32[]{:S(2)}, u32[]{:S(2)}) async-start(f32[32,20,4,128]{3,2,1,0:T(4,128)} %get-tuple-element.178), calls=%async_computation.2 | async-start | bytes 2621440 | tf_op jit(solution)/shard_map/all_to_all | solution.py:478
  55.5 3.7 %shard_map.69 = (f32[21,16,128]{2,1,0:T(8,128)S(1)}, f32[21,16,128]{2,1,0:T(8,128)S(1)}, f32[21,16,128]{2,1,0:T(8,128)S(1)}, f32[21,16,128]{2,1,0:T(8,128)}, f32...) custom-call(s32[1]{0:T(128)} %constant.2.clone.1.base_ref, ...), custom_call_target="tpu_custom_call" | custom-call | tf_op jit(solution)/shard_map/pallas_call | solution.py:352
  59.8 2.3 %collective-permute-start.19 = (f32[21,16,128]{2,1,0:T(8,128)}, f32[21,16,128]{2,1,0:T(8,128)S(1)}, u32[]{:S(2)}, u32[]{:S(2)}) collective-permute-start(f32[21,16,128]{2,1,0:T(8,128)} %get-tuple-element.171), channel_id=1, source_target_pairs={{0,96},{32,128},{64,160},{96,192},{128,224},{160,0},{192,32},{224,... | collective-permute-start | bytes 516104 | tf_op jit(solution)/shard_map/ppermute | solution.py:450
  62.1 1.7 %collective-permute-start.20 = (f32[21,16,128]{2,1,0:T(8,128)}, f32[21,16,128]{2,1,0:T(8,128)S(1)}, u32[]{:S(2)}, u32[]{:S(2)}) collective-permute-start(f32[21,16,128]{2,1,0:T(8,128)} %get-tuple-element.172), channel_id=1, source_target_pairs={{0,128},{32,160},{64,192},{96,224},{128,0},{160,32},{192,64},{224,... | collective-permute-start | bytes 516104 | tf_op jit(solution)/shard_map/ppermute | solution.py:450
  63.8 1.9 %collective-permute-start.21 = (f32[21,16,128]{2,1,0:T(8,128)}, f32[21,16,128]{2,1,0:T(8,128)S(1)}, u32[]{:S(2)}, u32[]{:S(2)}) collective-permute-start(f32[21,16,128]{2,1,0:T(8,128)} %get-tuple-element.173), channel_id=1, source_target_pairs={{0,160},{32,192},{64,224},{96,0},{128,32},{160,64},{192,96},{224,1... | collective-permute-start | bytes 516104 | tf_op jit(solution)/shard_map/ppermute | solution.py:450
  67.6 3.1 %collective-permute-start.23 = (f32[21,16,128]{2,1,0:T(8,128)}, f32[21,16,128]{2,1,0:T(8,128)}, u32[]{:S(2)}, u32[]{:S(2)}) collective-permute-start(f32[21,16,128]{2,1,0:T(8,128)} %get-tuple-element.175), channel_id=1, source_target_pairs={{0,224},{32,0},{64,32},{96,64},{128,96},{160,128},{192,160},{224,1... | collective-permute-start | bytes 516104 | tf_op jit(solution)/shard_map/ppermute | solution.py:450
  70.7 3.4 %collective-permute-done.19.refs_3_ = f32[21,16,128]{2,1,0:T(8,128)S(1)} collective-permute-done((f32[21,16,128]{2,1,0:T(8,128)}, f32[21,16,128]{2,1,0:T(8,128)S(1)}, u32[]{:S(2)}, u32[]{:S(2)}) %collective-permute-start.19) | collective-permute-done | bytes 172064 | tf_op jit(solution)/shard_map/ppermute | solution.py:450
  74.1 1.2 %collective-permute-done.20.refs_4_ = f32[21,16,128]{2,1,0:T(8,128)S(1)} collective-permute-done((f32[21,16,128]{2,1,0:T(8,128)}, f32[21,16,128]{2,1,0:T(8,128)S(1)}, u32[]{:S(2)}, u32[]{:S(2)}) %collective-permute-start.20) | collective-permute-done | bytes 172064 | tf_op jit(solution)/shard_map/ppermute | solution.py:450
  75.3 1.8 %collective-permute-done.22.refs_6_ = f32[21,16,128]{2,1,0:T(8,128)S(1)} collective-permute-done((f32[21,16,128]{2,1,0:T(8,128)}, f32[21,16,128]{2,1,0:T(8,128)S(1)}, u32[]{:S(2)}, u32[]{:S(2)}) %collective-permute-start.22) | collective-permute-done | bytes 172064 | tf_op jit(solution)/shard_map/ppermute | solution.py:450
  77.1 1.2 %collective-permute-done.23.refs_7_ = f32[21,16,128]{2,1,0:T(8,128)} collective-permute-done((f32[21,16,128]{2,1,0:T(8,128)}, f32[21,16,128]{2,1,0:T(8,128)}, u32[]{:S(2)}, u32[]{:S(2)}) %collective-permute-start.23) | collective-permute-done | bytes 172064 | tf_op jit(solution)/shard_map/ppermute | solution.py:450
  80.5 7.6 %all-to-all-done.2.left_ref = f32[32,20,4,128]{3,2,1,0:T(4,128)S(1)} async-done(((f32[32,20,4,128]{3,2,1,0:T(4,128)}), f32[32,20,4,128]{3,2,1,0:T(4,128)S(1)}, u32[]{:S(2)}, u32[]{:S(2)}) %all-to-all-start.2) | async-done | bytes 1310752 | tf_op jit(solution)/shard_map/all_to_all | solution.py:478
  88.1 4.0 %shard_map.71 = f32[12,128,128]{2,1,0:T(8,128)} custom-call(s32[2]{0:T(128)S(1)} %pad_add_fusion.1.scalars, s32[8,128]{1,0:T(8,128)S(1)} %get-tuple-element.176.codes, s32[8,128]{1,0:T(8,128)S(1)} %get-tuple-element.177.counts, f32[32,20,4,128]{3,2,1,0:T(4,128)S(1)} %all-to-all-done.2.left_ref, f32[21,16,128]{2,1,0:T(8,128)S(1)} %get-tuple-element.168.refs_0_, ...), custom_call_target="tpu_custom_call" | custom-call | tf_op jit(solution)/shard_map/pallas_call | solution.py:432
  (27 shorter events, 10.2 us)
Async XLA Ops:
  0.9 1.2 %collective-permute-start.7 = (f32[4,128]{1,0:T(4,128)S(1)}, f32[4,128]{1,0:T(4,128)S(1)}, u32[]{:S(2)}, u32[]{:S(2)}) collective-permute-start(f32[4,128]{1,0:T(4,128)S(1)} %get-tuple-element.133), channel_id=1, source_target_pairs={{0,32},{32,0},{64,96},{96,64},{128,160},{160,128},{192,224},{224,1... | collective-permute-start | bytes 6152 | tf_op jit(solution)/shard_map/ppermute | solution.py:455
  2.1 3.8 %collective-permute-start.8 = (f32[4,128]{1,0:T(4,128)S(1)}, f32[4,128]{1,0:T(4,128)S(1)}, u32[]{:S(2)}, u32[]{:S(2)}) collective-permute-start(f32[4,128]{1,0:T(4,128)S(1)} %add.9), channel_id=1, source_target_pairs={{0,64},{32,96},{64,0},{96,32},{128,192},{160,224},{192,128},{224,1... | collective-permute-start | bytes 6152 | tf_op jit(solution)/shard_map/ppermute | solution.py:455
  5.9 4.9 %collective-permute-start.9 = (f32[4,128]{1,0:T(4,128)S(1)}, f32[4,128]{1,0:T(4,128)S(1)}, u32[]{:S(2)}, u32[]{:S(2)}) collective-permute-start(f32[4,128]{1,0:T(4,128)S(1)} %add.10.one_ref), channel_id=1, source_target_pairs={{0,192},{32,224},{64,128},{96,160},{128,64},{160,96},{192,0},{224,... | collective-permute-start | bytes 6152 | tf_op jit(solution)/shard_map/ppermute | solution.py:455
  11.4 34.2 %all-to-all-start.1 = ((f32[32,13,4,128]{3,2,1,0:T(4,128)}), f32[32,13,4,128]{3,2,1,0:T(4,128)S(1)}, u32[]{:S(2)}, u32[]{:S(2)}) async-start(f32[32,13,4,128]{3,2,1,0:T(4,128)} %get-tuple-element.146), calls=%async_computation.1 | async-start | bytes 1703936 | tf_op jit(solution)/shard_map/all_to_all | solution.py:472
  23.0 7.3 %collective-permute-start.10 = (f32[12,16,128]{2,1,0:T(8,128)S(1)}, f32[12,16,128]{2,1,0:T(8,128)}, u32[]{:S(2)}, u32[]{:S(2)}) collective-permute-start(f32[12,16,128]{2,1,0:T(8,128)S(1)} %get-tuple-element.148), channel_id=1, source_target_pairs={{0,32},{32,64},{64,96},{96,128},{128,160},{160,192},{192,224},{224... | collective-permute-start | bytes 294920 | tf_op jit(solution)/shard_map/ppermute | solution.py:450
  23.1 7.4 %collective-permute-start.11 = (f32[12,16,128]{2,1,0:T(8,128)S(1)}, f32[12,16,128]{2,1,0:T(8,128)}, u32[]{:S(2)}, u32[]{:S(2)}) collective-permute-start(f32[12,16,128]{2,1,0:T(8,128)S(1)} %get-tuple-element.149), channel_id=1, source_target_pairs={{0,64},{32,96},{64,128},{96,160},{128,192},{160,224},{192,0},{224,... | collective-permute-start | bytes 294920 | tf_op jit(solution)/shard_map/ppermute | solution.py:450
  23.2 10.8 %collective-permute-start.12 = (f32[12,16,128]{2,1,0:T(8,128)S(1)}, f32[12,16,128]{2,1,0:T(8,128)}, u32[]{:S(2)}, u32[]{:S(2)}) collective-permute-start(f32[12,16,128]{2,1,0:T(8,128)S(1)} %get-tuple-element.150), channel_id=1, source_target_pairs={{0,96},{32,128},{64,160},{96,192},{128,224},{160,0},{192,32},{224,... | collective-permute-start | bytes 294920 | tf_op jit(solution)/shard_map/ppermute | solution.py:450
  26.7 8.6 %collective-permute-start.13 = (f32[12,16,128]{2,1,0:T(8,128)S(1)}, f32[12,16,128]{2,1,0:T(8,128)}, u32[]{:S(2)}, u32[]{:S(2)}) collective-permute-start(f32[12,16,128]{2,1,0:T(8,128)S(1)} %get-tuple-element.151), channel_id=1, source_target_pairs={{0,128},{32,160},{64,192},{96,224},{128,0},{160,32},{192,64},{224,... | collective-permute-start | bytes 294920 | tf_op jit(solution)/shard_map/ppermute | solution.py:450
  27.5 7.7 %collective-permute-start.14 = (f32[12,16,128]{2,1,0:T(8,128)S(1)}, f32[12,16,128]{2,1,0:T(8,128)}, u32[]{:S(2)}, u32[]{:S(2)}) collective-permute-start(f32[12,16,128]{2,1,0:T(8,128)S(1)} %get-tuple-element.152), channel_id=1, source_target_pairs={{0,160},{32,192},{64,224},{96,0},{128,32},{160,64},{192,96},{224,1... | collective-permute-start | bytes 294920 | tf_op jit(solution)/shard_map/ppermute | solution.py:450
  30.3 5.4 %collective-permute-start.15 = (f32[12,16,128]{2,1,0:T(8,128)S(1)}, f32[12,16,128]{2,1,0:T(8,128)}, u32[]{:S(2)}, u32[]{:S(2)}) collective-permute-start(f32[12,16,128]{2,1,0:T(8,128)S(1)} %get-tuple-element.153), channel_id=1, source_target_pairs={{0,192},{32,224},{64,0},{96,32},{128,64},{160,96},{192,128},{224,1... | collective-permute-start | bytes 294920 | tf_op jit(solution)/shard_map/ppermute | solution.py:450
  30.5 5.4 %collective-permute-start.16 = (f32[12,16,128]{2,1,0:T(8,128)S(1)}, f32[12,16,128]{2,1,0:T(8,128)}, u32[]{:S(2)}, u32[]{:S(2)}) collective-permute-start(f32[12,16,128]{2,1,0:T(8,128)S(1)} %get-tuple-element.154), channel_id=1, source_target_pairs={{0,224},{32,0},{64,32},{96,64},{128,96},{160,128},{192,160},{224,1... | collective-permute-start | bytes 294920 | tf_op jit(solution)/shard_map/ppermute | solution.py:450
  49.7 38.4 %all-to-all-start.2 = ((f32[32,20,4,128]{3,2,1,0:T(4,128)}), f32[32,20,4,128]{3,2,1,0:T(4,128)S(1)}, u32[]{:S(2)}, u32[]{:S(2)}) async-start(f32[32,20,4,128]{3,2,1,0:T(4,128)} %get-tuple-element.178), calls=%async_computation.2 | async-start | bytes 2621440 | tf_op jit(solution)/shard_map/all_to_all | solution.py:478
  59.1 7.3 %collective-permute-start.17 = (f32[21,16,128]{2,1,0:T(8,128)S(1)}, f32[21,16,128]{2,1,0:T(8,128)S(1)}, u32[]{:S(2)}, u32[]{:S(2)}) collective-permute-start(f32[21,16,128]{2,1,0:T(8,128)S(1)} %get-tuple-element.169), channel_id=1, source_target_pairs={{0,32},{32,64},{64,96},{96,128},{128,160},{160,192},{192,224},{224... | collective-permute-start | bytes 516104 | tf_op jit(solution)/shard_map/ppermute | solution.py:450
  59.2 8.5 %collective-permute-start.18 = (f32[21,16,128]{2,1,0:T(8,128)S(1)}, f32[21,16,128]{2,1,0:T(8,128)S(1)}, u32[]{:S(2)}, u32[]{:S(2)}) collective-permute-start(f32[21,16,128]{2,1,0:T(8,128)S(1)} %get-tuple-element.170), channel_id=1, source_target_pairs={{0,64},{32,96},{64,128},{96,160},{128,192},{160,224},{192,0},{224,... | collective-permute-start | bytes 516104 | tf_op jit(solution)/shard_map/ppermute | solution.py:450
  59.8 14.3 %collective-permute-start.19 = (f32[21,16,128]{2,1,0:T(8,128)}, f32[21,16,128]{2,1,0:T(8,128)S(1)}, u32[]{:S(2)}, u32[]{:S(2)}) collective-permute-start(f32[21,16,128]{2,1,0:T(8,128)} %get-tuple-element.171), channel_id=1, source_target_pairs={{0,96},{32,128},{64,160},{96,192},{128,224},{160,0},{192,32},{224,... | collective-permute-start | bytes 516104 | tf_op jit(solution)/shard_map/ppermute | solution.py:450
  62.1 13.2 %collective-permute-start.20 = (f32[21,16,128]{2,1,0:T(8,128)}, f32[21,16,128]{2,1,0:T(8,128)S(1)}, u32[]{:S(2)}, u32[]{:S(2)}) collective-permute-start(f32[21,16,128]{2,1,0:T(8,128)} %get-tuple-element.172), channel_id=1, source_target_pairs={{0,128},{32,160},{64,192},{96,224},{128,0},{160,32},{192,64},{224,... | collective-permute-start | bytes 516104 | tf_op jit(solution)/shard_map/ppermute | solution.py:450
  63.8 11.5 %collective-permute-start.21 = (f32[21,16,128]{2,1,0:T(8,128)}, f32[21,16,128]{2,1,0:T(8,128)S(1)}, u32[]{:S(2)}, u32[]{:S(2)}) collective-permute-start(f32[21,16,128]{2,1,0:T(8,128)} %get-tuple-element.173), channel_id=1, source_target_pairs={{0,160},{32,192},{64,224},{96,0},{128,32},{160,64},{192,96},{224,1... | collective-permute-start | bytes 516104 | tf_op jit(solution)/shard_map/ppermute | solution.py:450
  66.4 10.7 %collective-permute-start.22 = (f32[21,16,128]{2,1,0:T(8,128)}, f32[21,16,128]{2,1,0:T(8,128)S(1)}, u32[]{:S(2)}, u32[]{:S(2)}) collective-permute-start(f32[21,16,128]{2,1,0:T(8,128)} %get-tuple-element.174), channel_id=1, source_target_pairs={{0,192},{32,224},{64,0},{96,32},{128,64},{160,96},{192,128},{224,1... | collective-permute-start | bytes 516104 | tf_op jit(solution)/shard_map/ppermute | solution.py:450
  67.6 10.7 %collective-permute-start.23 = (f32[21,16,128]{2,1,0:T(8,128)}, f32[21,16,128]{2,1,0:T(8,128)}, u32[]{:S(2)}, u32[]{:S(2)}) collective-permute-start(f32[21,16,128]{2,1,0:T(8,128)} %get-tuple-element.175), channel_id=1, source_target_pairs={{0,224},{32,0},{64,32},{96,64},{128,96},{160,128},{192,160},{224,1... | collective-permute-start | bytes 516104 | tf_op jit(solution)/shard_map/ppermute | solution.py:450

commit v12 on v8

--- a/solution.py
+++ b/solution.py
@@ -258,16 +258,16 @@
     copy.wait()
 
     def one_group(group):
-        part = pl.ds(group * PER_GROUP, PER_GROUP)
+        part = pl.ds(group * PER_GROUP // 2, PER_GROUP // 2)
         return pltpu.make_async_copy(send.at[part], send_ref.at[part], send_sems.at[group])
 
-    for group in range(groups):
-        for peer in range(group * PER_GROUP, (group + 1) * PER_GROUP):
-            line, first = group * halves, peer % PER_GROUP * SLOT_PITCH
+    for group in range(2 * groups):
+        for peer in range(group * PER_GROUP // 2, (group + 1) * PER_GROUP // 2):
+            line, first = peer // PER_GROUP * halves, peer % PER_GROUP * SLOT_PITCH
             for at in range(cap):
                 send[peer, at] = strips_ref[places[line + at // SLOT_PITCH, first + at % SLOT_PITCH]]
         one_group(group).start()
-    for group in range(groups):
+    for group in range(2 * groups):
         one_group(group).wait()
 
 
@@ -304,7 +304,7 @@
                 pltpu.VMEM(send, jnp.float32),
                 pltpu.SMEM((lines, LANES), jnp.int32),
                 pltpu.SemaphoreType.DMA,
-                pltpu.SemaphoreType.DMA((groups,)),
+                pltpu.SemaphoreType.DMA((2 * groups,)),
             ],
         ),
         out_shape=[pltpu.HBM(*shapes[0])] + [jax.ShapeDtypeStruct(*shape) for shape in shapes[1:]],

time: 92.7 us -> 92.7 us (level)
  no operation moved by 1% of the time
where the time goes in v12:
time: 92.7 us; the launch traced here: 92.1 us
  starting transfers between devices  41.8 us (45%)
  waiting for transfers between devices  30 us (32%)
  Pallas kernels  18.2 us (20%)
    ppermute x14, starting transfers between devices, shift_all(): lax.ppermute(pieces[by], 'row', [(i, (i + by) % rows) for i in range(rows)])  20 us
    ppermute x14, waiting for transfers between devices, shift_all(): lax.ppermute(pieces[by], 'row', [(i, (i + by) % rows) for i in range(rows)])  12.1 us
    all_to_all x1, starting transfers between devices, local(): strips = lax.all_to_all(strips, GROUP, 0, 0, tiled=True)  11.6 us
    all_to_all x1, waiting for transfers between devices, local(): strips = lax.all_to_all(strips, GROUP, 0, 0, tiled=True)  7.83 us
    all_to_all x1, waiting for transfers between devices, one_round(): left = lax.all_to_all(send, GROUP, 0, 0, tiled=True)  6.88 us
    all_to_all x1, starting transfers between devices, one_round(): left = lax.all_to_all(send, GROUP, 0, 0, tiled=True)  5.71 us
    ppermute x3, starting transfers between devices, swap_rows(): return lax.ppermute(array, 'row', [(i, i ^ by) for i in range(rows)])  4.49 us
    pallas_call x1, Pallas kernels, plan(): pl.pallas_call(functools.partial(plan_body, rows), grid_spec=pltpu.Prefet...  4.08 us
  transfers between devices with their start and end apart: 19, of which 14 were waited for; matrix products, arithmetic and copies ran while one was open for 1% of the time, Pallas kernels for 9%

profile of v12, /device:TPU:4, one launch (start us, length us, event | category | flops | bytes accessed | tf_op | source)
XLA Modules:
  0.0 92.1 jit_solution(15413802567122540960)
XLA Ops:
  1.0 1.1 %collective-permute-done.7 = f32[4,128]{1,0:T(4,128)S(1)} collective-permute-done((f32[4,128]{1,0:T(4,128)S(1)}, f32[4,128]{1,0:T(4,128)S(1)}, u32[]{:S(2)}, u32[]{:S(2)}) %collective-permute-start.7) | collective-permute-done | bytes 2080 | tf_op jit(solution)/shard_map/ppermute | solution.py:455
  2.1 1.6 %collective-permute-start.8 = (f32[4,128]{1,0:T(4,128)S(1)}, f32[4,128]{1,0:T(4,128)S(1)}, u32[]{:S(2)}, u32[]{:S(2)}) collective-permute-start(f32[4,128]{1,0:T(4,128)S(1)} %add.9), channel_id=1, source_target_pairs={{0,64},{32,96},{64,0},{96,32},{128,192},{160,224},{192,128},{224,1... | collective-permute-start | bytes 6152 | tf_op jit(solution)/shard_map/ppermute | solution.py:455
  3.7 2.2 %shard_map.65.strips_in = f32[32,13,4,128]{3,2,1,0:T(4,128)} custom-call(f32[12,128,128]{2,1,0:T(8,128)} %bitcast.13), custom_call_target="tpu_custom_call" | custom-call | tf_op jit(solution)/shard_map/pallas_call | solution.py:89
  5.9 2.8 %collective-permute-start.9 = (f32[4,128]{1,0:T(4,128)S(1)}, f32[4,128]{1,0:T(4,128)S(1)}, u32[]{:S(2)}, u32[]{:S(2)}) collective-permute-start(f32[4,128]{1,0:T(4,128)S(1)} %add.10.one_ref), channel_id=1, source_target_pairs={{0,192},{32,224},{64,128},{96,160},{128,64},{160,96},{192,0},{224,... | collective-permute-start | bytes 6152 | tf_op jit(solution)/shard_map/ppermute | solution.py:455
  8.7 2.1 %collective-permute-done.9.other_ref = f32[4,128]{1,0:T(4,128)S(1)} collective-permute-done((f32[4,128]{1,0:T(4,128)S(1)}, f32[4,128]{1,0:T(4,128)S(1)}, u32[]{:S(2)}, u32[]{:S(2)}) %collective-permute-start.9) | collective-permute-done | bytes 2080 | tf_op jit(solution)/shard_map/ppermute | solution.py:455
  11.4 11.6 %all-to-all-start.1 = ((f32[32,13,4,128]{3,2,1,0:T(4,128)}), f32[32,13,4,128]{3,2,1,0:T(4,128)S(1)}, u32[]{:S(2)}, u32[]{:S(2)}) async-start(f32[32,13,4,128]{3,2,1,0:T(4,128)} %get-tuple-element.128), calls=%async_computation.1 | async-start | bytes 1703936 | tf_op jit(solution)/shard_map/all_to_all | solution.py:471
  23.0 1.8 %shard_map.67 = (f32[12,16,128]{2,1,0:T(8,128)}, f32[12,16,128]{2,1,0:T(8,128)S(1)}, f32[12,16,128]{2,1,0:T(8,128)S(1)}, f32[12,16,128]{2,1,0:T(8,128)S(1)}, f32...) custom-call(f32[12,128,128]{2,1,0:T(8,128)} %bitcast.14), custom_call_target="tpu_custom_call" | custom-call | tf_op jit(solution)/shard_map/pallas_call | solution.py:136
  25.0 3.5 %collective-permute-start.12 = (f32[12,16,128]{2,1,0:T(8,128)S(1)}, f32[12,16,128]{2,1,0:T(8,128)}, u32[]{:S(2)}, u32[]{:S(2)}) collective-permute-start(f32[12,16,128]{2,1,0:T(8,128)S(1)} %get-tuple-element.132), channel_id=1, source_target_pairs={{0,96},{32,128},{64,160},{96,192},{128,224},{160,0},{192,32},{224,... | collective-permute-start | bytes 294920 | tf_op jit(solution)/shard_map/ppermute | solution.py:450
  29.3 2.7 %collective-permute-start.14 = (f32[12,16,128]{2,1,0:T(8,128)S(1)}, f32[12,16,128]{2,1,0:T(8,128)}, u32[]{:S(2)}, u32[]{:S(2)}) collective-permute-start(f32[12,16,128]{2,1,0:T(8,128)S(1)} %get-tuple-element.134), channel_id=1, source_target_pairs={{0,160},{32,192},{64,224},{96,0},{128,32},{160,64},{192,96},{224,1... | collective-permute-start | bytes 294920 | tf_op jit(solution)/shard_map/ppermute | solution.py:450
  32.2 1.7 %collective-permute-start.16 = (f32[12,16,128]{2,1,0:T(8,128)S(1)}, f32[12,16,128]{2,1,0:T(8,128)}, u32[]{:S(2)}, u32[]{:S(2)}) collective-permute-start(f32[12,16,128]{2,1,0:T(8,128)S(1)} %get-tuple-element.136), channel_id=1, source_target_pairs={{0,224},{32,0},{64,32},{96,64},{128,96},{160,128},{192,160},{224,1... | collective-permute-start | bytes 294920 | tf_op jit(solution)/shard_map/ppermute | solution.py:450
  34.0 1.9 %collective-permute-done.12.refs_3_ = f32[12,16,128]{2,1,0:T(8,128)} collective-permute-done((f32[12,16,128]{2,1,0:T(8,128)S(1)}, f32[12,16,128]{2,1,0:T(8,128)}, u32[]{:S(2)}, u32[]{:S(2)}) %collective-permute-start.12) | collective-permute-done | bytes 98336 | tf_op jit(solution)/shard_map/ppermute | solution.py:450
  37.7 7.8 %all-to-all-done.1 = f32[32,13,4,128]{3,2,1,0:T(4,128)S(1)} async-done(((f32[32,13,4,128]{3,2,1,0:T(4,128)}), f32[32,13,4,128]{3,2,1,0:T(4,128)S(1)}, u32[]{:S(2)}, u32[]{:S(2)}) %all-to-all-start.1) | async-done | bytes 852000 | tf_op jit(solution)/shard_map/all_to_all | solution.py:471
  45.5 4.1 %shard_map.68 = (f32[32,20,4,128]{3,2,1,0:T(4,128)}, s32[8,128]{1,0:T(8,128)S(1)}, s32[8,128]{1,0:T(8,128)S(1)}, f32[8,128]{1,0:T(8,128)S(1)}, bf16[256,256]{1,0...) custom-call(s32[1]{0:T(128)} %constant.2.clone.1.base_ref, f32[416,4,128]{2,1,0:T(4,128)S(1)} %bitcast.11), custom_call_target="tpu_custom_call" | custom-call | tf_op jit(solution)/shard_map/pallas_call | solution.py:293
  49.6 5.7 %all-to-all-start.2 = ((f32[32,20,4,128]{3,2,1,0:T(4,128)}), f32[32,20,4,128]{3,2,1,0:T(4,128)S(1)}, u32[]{:S(2)}, u32[]{:S(2)}) async-start(f32[32,20,4,128]{3,2,1,0:T(4,128)} %get-tuple-element.160), calls=%async_computation.2 | async-start | bytes 2621440 | tf_op jit(solution)/shard_map/all_to_all | solution.py:477
  55.3 3.7 %shard_map.69 = (f32[21,16,128]{2,1,0:T(8,128)S(1)}, f32[21,16,128]{2,1,0:T(8,128)S(1)}, f32[21,16,128]{2,1,0:T(8,128)S(1)}, f32[21,16,128]{2,1,0:T(8,128)}, f32...) custom-call(s32[1]{0:T(128)} %constant.2.clone.1.base_ref, ...), custom_call_target="tpu_custom_call" | custom-call | tf_op jit(solution)/shard_map/pallas_call | solution.py:352
  59.1 3.0 %collective-permute-start.19 = (f32[21,16,128]{2,1,0:T(8,128)}, f32[21,16,128]{2,1,0:T(8,128)S(1)}, u32[]{:S(2)}, u32[]{:S(2)}) collective-permute-start(f32[21,16,128]{2,1,0:T(8,128)} %get-tuple-element.153), channel_id=1, source_target_pairs={{0,96},{32,128},{64,160},{96,192},{128,224},{160,0},{192,32},{224,... | collective-permute-start | bytes 516104 | tf_op jit(solution)/shard_map/ppermute | solution.py:450
  62.1 1.4 %collective-permute-start.20 = (f32[21,16,128]{2,1,0:T(8,128)}, f32[21,16,128]{2,1,0:T(8,128)S(1)}, u32[]{:S(2)}, u32[]{:S(2)}) collective-permute-start(f32[21,16,128]{2,1,0:T(8,128)} %get-tuple-element.154), channel_id=1, source_target_pairs={{0,128},{32,160},{64,192},{96,224},{128,0},{160,32},{192,64},{224,... | collective-permute-start | bytes 516104 | tf_op jit(solution)/shard_map/ppermute | solution.py:450
  63.5 2.3 %collective-permute-start.21 = (f32[21,16,128]{2,1,0:T(8,128)}, f32[21,16,128]{2,1,0:T(8,128)S(1)}, u32[]{:S(2)}, u32[]{:S(2)}) collective-permute-start(f32[21,16,128]{2,1,0:T(8,128)} %get-tuple-element.155), channel_id=1, source_target_pairs={{0,160},{32,192},{64,224},{96,0},{128,32},{160,64},{192,96},{224,1... | collective-permute-start | bytes 516104 | tf_op jit(solution)/shard_map/ppermute | solution.py:450
  67.5 3.2 %collective-permute-start.23 = (f32[21,16,128]{2,1,0:T(8,128)}, f32[21,16,128]{2,1,0:T(8,128)}, u32[]{:S(2)}, u32[]{:S(2)}) collective-permute-start(f32[21,16,128]{2,1,0:T(8,128)} %get-tuple-element.157), channel_id=1, source_target_pairs={{0,224},{32,0},{64,32},{96,64},{128,96},{160,128},{192,160},{224,1... | collective-permute-start | bytes 516104 | tf_op jit(solution)/shard_map/ppermute | solution.py:450
  70.7 3.4 %collective-permute-done.19.refs_3_ = f32[21,16,128]{2,1,0:T(8,128)S(1)} collective-permute-done((f32[21,16,128]{2,1,0:T(8,128)}, f32[21,16,128]{2,1,0:T(8,128)S(1)}, u32[]{:S(2)}, u32[]{:S(2)}) %collective-permute-start.19) | collective-permute-done | bytes 172064 | tf_op jit(solution)/shard_map/ppermute | solution.py:450
  74.1 1.2 %collective-permute-done.20.refs_4_ = f32[21,16,128]{2,1,0:T(8,128)S(1)} collective-permute-done((f32[21,16,128]{2,1,0:T(8,128)}, f32[21,16,128]{2,1,0:T(8,128)S(1)}, u32[]{:S(2)}, u32[]{:S(2)}) %collective-permute-start.20) | collective-permute-done | bytes 172064 | tf_op jit(solution)/shard_map/ppermute | solution.py:450
  75.3 1.8 %collective-permute-done.22.refs_6_ = f32[21,16,128]{2,1,0:T(8,128)S(1)} collective-permute-done((f32[21,16,128]{2,1,0:T(8,128)}, f32[21,16,128]{2,1,0:T(8,128)S(1)}, u32[]{:S(2)}, u32[]{:S(2)}) %collective-permute-start.22) | collective-permute-done | bytes 172064 | tf_op jit(solution)/shard_map/ppermute | solution.py:450
  80.4 6.9 %all-to-all-done.2.left_ref = f32[32,20,4,128]{3,2,1,0:T(4,128)S(1)} async-done(((f32[32,20,4,128]{3,2,1,0:T(4,128)}), f32[32,20,4,128]{3,2,1,0:T(4,128)S(1)}, u32[]{:S(2)}, u32[]{:S(2)}) %all-to-all-start.2) | async-done | bytes 1310752 | tf_op jit(solution)/shard_map/all_to_all | solution.py:477
  87.3 4.0 %shard_map.71 = f32[12,128,128]{2,1,0:T(8,128)} custom-call(s32[2]{0:T(128)S(1)} %pad_add_fusion.1.scalars, s32[8,128]{1,0:T(8,128)S(1)} %get-tuple-element.158.codes, s32[8,128]{1,0:T(8,128)S(1)} %get-tuple-element.159.counts, f32[32,20,4,128]{3,2,1,0:T(4,128)S(1)} %all-to-all-done.2.left_ref, f32[21,16,128]{2,1,0:T(8,128)S(1)} %get-tuple-element.150.refs_0_, ...), custom_call_target="tpu_custom_call" | custom-call | tf_op jit(solution)/shard_map/pallas_call | solution.py:432
  (27 shorter events, 10.4 us)
Async XLA Ops:
  0.9 1.2 %collective-permute-start.7 = (f32[4,128]{1,0:T(4,128)S(1)}, f32[4,128]{1,0:T(4,128)S(1)}, u32[]{:S(2)}, u32[]{:S(2)}) collective-permute-start(f32[4,128]{1,0:T(4,128)S(1)} %get-tuple-element.124), channel_id=1, source_target_pairs={{0,32},{32,0},{64,96},{96,64},{128,160},{160,128},{192,224},{224,1... | collective-permute-start | bytes 6152 | tf_op jit(solution)/shard_map/ppermute | solution.py:455
  2.1 3.8 %collective-permute-start.8 = (f32[4,128]{1,0:T(4,128)S(1)}, f32[4,128]{1,0:T(4,128)S(1)}, u32[]{:S(2)}, u32[]{:S(2)}) collective-permute-start(f32[4,128]{1,0:T(4,128)S(1)} %add.9), channel_id=1, source_target_pairs={{0,64},{32,96},{64,0},{96,32},{128,192},{160,224},{192,128},{224,1... | collective-permute-start | bytes 6152 | tf_op jit(solution)/shard_map/ppermute | solution.py:455
  5.9 4.9 %collective-permute-start.9 = (f32[4,128]{1,0:T(4,128)S(1)}, f32[4,128]{1,0:T(4,128)S(1)}, u32[]{:S(2)}, u32[]{:S(2)}) collective-permute-start(f32[4,128]{1,0:T(4,128)S(1)} %add.10.one_ref), channel_id=1, source_target_pairs={{0,192},{32,224},{64,128},{96,160},{128,64},{160,96},{192,0},{224,... | collective-permute-start | bytes 6152 | tf_op jit(solution)/shard_map/ppermute | solution.py:455
  11.4 34.1 %all-to-all-start.1 = ((f32[32,13,4,128]{3,2,1,0:T(4,128)}), f32[32,13,4,128]{3,2,1,0:T(4,128)S(1)}, u32[]{:S(2)}, u32[]{:S(2)}) async-start(f32[32,13,4,128]{3,2,1,0:T(4,128)} %get-tuple-element.128), calls=%async_computation.1 | async-start | bytes 1703936 | tf_op jit(solution)/shard_map/all_to_all | solution.py:471
  24.9 7.2 %collective-permute-start.10 = (f32[12,16,128]{2,1,0:T(8,128)S(1)}, f32[12,16,128]{2,1,0:T(8,128)}, u32[]{:S(2)}, u32[]{:S(2)}) collective-permute-start(f32[12,16,128]{2,1,0:T(8,128)S(1)} %get-tuple-element.130), channel_id=1, source_target_pairs={{0,32},{32,64},{64,96},{96,128},{128,160},{160,192},{192,224},{224... | collective-permute-start | bytes 294920 | tf_op jit(solution)/shard_map/ppermute | solution.py:450
  24.9 7.4 %collective-permute-start.11 = (f32[12,16,128]{2,1,0:T(8,128)S(1)}, f32[12,16,128]{2,1,0:T(8,128)}, u32[]{:S(2)}, u32[]{:S(2)}) collective-permute-start(f32[12,16,128]{2,1,0:T(8,128)S(1)} %get-tuple-element.131), channel_id=1, source_target_pairs={{0,64},{32,96},{64,128},{96,160},{128,192},{160,224},{192,0},{224,... | collective-permute-start | bytes 294920 | tf_op jit(solution)/shard_map/ppermute | solution.py:450
  25.0 10.9 %collective-permute-start.12 = (f32[12,16,128]{2,1,0:T(8,128)S(1)}, f32[12,16,128]{2,1,0:T(8,128)}, u32[]{:S(2)}, u32[]{:S(2)}) collective-permute-start(f32[12,16,128]{2,1,0:T(8,128)S(1)} %get-tuple-element.132), channel_id=1, source_target_pairs={{0,96},{32,128},{64,160},{96,192},{128,224},{160,0},{192,32},{224,... | collective-permute-start | bytes 294920 | tf_op jit(solution)/shard_map/ppermute | solution.py:450
  28.5 8.5 %collective-permute-start.13 = (f32[12,16,128]{2,1,0:T(8,128)S(1)}, f32[12,16,128]{2,1,0:T(8,128)}, u32[]{:S(2)}, u32[]{:S(2)}) collective-permute-start(f32[12,16,128]{2,1,0:T(8,128)S(1)} %get-tuple-element.133), channel_id=1, source_target_pairs={{0,128},{32,160},{64,192},{96,224},{128,0},{160,32},{192,64},{224,... | collective-permute-start | bytes 294920 | tf_op jit(solution)/shard_map/ppermute | solution.py:450
  29.3 7.7 %collective-permute-start.14 = (f32[12,16,128]{2,1,0:T(8,128)S(1)}, f32[12,16,128]{2,1,0:T(8,128)}, u32[]{:S(2)}, u32[]{:S(2)}) collective-permute-start(f32[12,16,128]{2,1,0:T(8,128)S(1)} %get-tuple-element.134), channel_id=1, source_target_pairs={{0,160},{32,192},{64,224},{96,0},{128,32},{160,64},{192,96},{224,1... | collective-permute-start | bytes 294920 | tf_op jit(solution)/shard_map/ppermute | solution.py:450
  32.1 5.4 %collective-permute-start.15 = (f32[12,16,128]{2,1,0:T(8,128)S(1)}, f32[12,16,128]{2,1,0:T(8,128)}, u32[]{:S(2)}, u32[]{:S(2)}) collective-permute-start(f32[12,16,128]{2,1,0:T(8,128)S(1)} %get-tuple-element.135), channel_id=1, source_target_pairs={{0,192},{32,224},{64,0},{96,32},{128,64},{160,96},{192,128},{224,1... | collective-permute-start | bytes 294920 | tf_op jit(solution)/shard_map/ppermute | solution.py:450
  32.2 5.5 %collective-permute-start.16 = (f32[12,16,128]{2,1,0:T(8,128)S(1)}, f32[12,16,128]{2,1,0:T(8,128)}, u32[]{:S(2)}, u32[]{:S(2)}) collective-permute-start(f32[12,16,128]{2,1,0:T(8,128)S(1)} %get-tuple-element.136), channel_id=1, source_target_pairs={{0,224},{32,0},{64,32},{96,64},{128,96},{160,128},{192,160},{224,1... | collective-permute-start | bytes 294920 | tf_op jit(solution)/shard_map/ppermute | solution.py:450
  49.6 37.6 %all-to-all-start.2 = ((f32[32,20,4,128]{3,2,1,0:T(4,128)}), f32[32,20,4,128]{3,2,1,0:T(4,128)S(1)}, u32[]{:S(2)}, u32[]{:S(2)}) async-start(f32[32,20,4,128]{3,2,1,0:T(4,128)} %get-tuple-element.160), calls=%async_computation.2 | async-start | bytes 2621440 | tf_op jit(solution)/shard_map/all_to_all | solution.py:477
  59.0 7.3 %collective-permute-start.17 = (f32[21,16,128]{2,1,0:T(8,128)S(1)}, f32[21,16,128]{2,1,0:T(8,128)S(1)}, u32[]{:S(2)}, u32[]{:S(2)}) collective-permute-start(f32[21,16,128]{2,1,0:T(8,128)S(1)} %get-tuple-element.151), channel_id=1, source_target_pairs={{0,32},{32,64},{64,96},{96,128},{128,160},{160,192},{192,224},{224... | collective-permute-start | bytes 516104 | tf_op jit(solution)/shard_map/ppermute | solution.py:450
  59.0 8.5 %collective-permute-start.18 = (f32[21,16,128]{2,1,0:T(8,128)S(1)}, f32[21,16,128]{2,1,0:T(8,128)S(1)}, u32[]{:S(2)}, u32[]{:S(2)}) collective-permute-start(f32[21,16,128]{2,1,0:T(8,128)S(1)} %get-tuple-element.152), channel_id=1, source_target_pairs={{0,64},{32,96},{64,128},{96,160},{128,192},{160,224},{192,0},{224,... | collective-permute-start | bytes 516104 | tf_op jit(solution)/shard_map/ppermute | solution.py:450
  59.1 15.0 %collective-permute-start.19 = (f32[21,16,128]{2,1,0:T(8,128)}, f32[21,16,128]{2,1,0:T(8,128)S(1)}, u32[]{:S(2)}, u32[]{:S(2)}) collective-permute-start(f32[21,16,128]{2,1,0:T(8,128)} %get-tuple-element.153), channel_id=1, source_target_pairs={{0,96},{32,128},{64,160},{96,192},{128,224},{160,0},{192,32},{224,... | collective-permute-start | bytes 516104 | tf_op jit(solution)/shard_map/ppermute | solution.py:450
  62.1 13.2 %collective-permute-start.20 = (f32[21,16,128]{2,1,0:T(8,128)}, f32[21,16,128]{2,1,0:T(8,128)S(1)}, u32[]{:S(2)}, u32[]{:S(2)}) collective-permute-start(f32[21,16,128]{2,1,0:T(8,128)} %get-tuple-element.154), channel_id=1, source_target_pairs={{0,128},{32,160},{64,192},{96,224},{128,0},{160,32},{192,64},{224,... | collective-permute-start | bytes 516104 | tf_op jit(solution)/shard_map/ppermute | solution.py:450
  63.5 11.9 %collective-permute-start.21 = (f32[21,16,128]{2,1,0:T(8,128)}, f32[21,16,128]{2,1,0:T(8,128)S(1)}, u32[]{:S(2)}, u32[]{:S(2)}) collective-permute-start(f32[21,16,128]{2,1,0:T(8,128)} %get-tuple-element.155), channel_id=1, source_target_pairs={{0,160},{32,192},{64,224},{96,0},{128,32},{160,64},{192,96},{224,1... | collective-permute-start | bytes 516104 | tf_op jit(solution)/shard_map/ppermute | solution.py:450
  66.3 10.8 %collective-permute-start.22 = (f32[21,16,128]{2,1,0:T(8,128)}, f32[21,16,128]{2,1,0:T(8,128)S(1)}, u32[]{:S(2)}, u32[]{:S(2)}) collective-permute-start(f32[21,16,128]{2,1,0:T(8,128)} %get-tuple-element.156), channel_id=1, source_target_pairs={{0,192},{32,224},{64,0},{96,32},{128,64},{160,96},{192,128},{224,1... | collective-permute-start | bytes 516104 | tf_op jit(solution)/shard_map/ppermute | solution.py:450
  67.5 10.7 %collective-permute-start.23 = (f32[21,16,128]{2,1,0:T(8,128)}, f32[21,16,128]{2,1,0:T(8,128)}, u32[]{:S(2)}, u32[]{:S(2)}) collective-permute-start(f32[21,16,128]{2,1,0:T(8,128)} %get-tuple-element.157), channel_id=1, source_target_pairs={{0,224},{32,0},{64,32},{96,64},{128,96},{160,128},{192,160},{224,1... | collective-permute-start | bytes 516104 | tf_op jit(solution)/shard_map/ppermute | solution.py:450
